TPU v7x, 32 devices: a whole 2x2x4 slice. The times are simulated.
32 devices in a mesh: tm: 4 (over z), row: 2 (over core), col: 4 (over y, x).
Axes of the slice: x: 2, y: 2, z: 4, core: 2. Of those that a mesh axis runs over, the one named last changes fastest.
Arguments:
- features: bfloat16 [8, 32, 128, 128], P('tm', 'row', 'col'), may hold values from -65 to 65
- conv_first: bfloat16 [3, 3, 3, 128, 128], replicated, may hold values from -0.109375 to 0.109375
- conv_second: bfloat16 [3, 3, 3, 128, 128], replicated, may hold values from -0.109375 to 0.109375
- out_grad: bfloat16 [8, 32, 128, 128], P('tm', 'row', 'col'), may hold values from -6 to 6
Outputs:
- result: bfloat16 [8, 32, 128, 128], P('tm', 'row', 'col')
- feature_grad: bfloat16 [8, 32, 128, 128], P('tm', 'row', 'col')
- first_grad: bfloat16 [3, 3, 3, 128, 128], replicated
- second_grad: bfloat16 [3, 3, 3, 128, 128], replicated
All inputs are finite; a program needn't handle non-finite values.
Results may differ from a plain program's by a relative error of at most 0.0068.
Values may be sent and summed in bfloat16 or wider, within the bound.
No kernel may reach another device: no remote copies, remote signals or barrier semaphores. Data moves between devices by JAX's collectives and lax.ppermute only.
A program may use at most 64 MiB of HBM per device.

v0:
```python
import math

import jax
import jax.numpy as jnp
from jax import lax
from jax.sharding import PartitionSpec as P

GROUPS = 32


EPSILON = 1e-06
NUMBERS = ("NDHWC", "DHWIO", "NDHWC")
SWAPPED = ("CDHWN", "DHWIO", "CDHWN")


def extended(cells, sides, width):
    for axis, dim in sides:
        count = lax.axis_size(axis)
        ends = count - 1
        head = lax.slice_in_dim(cells, 0, width, axis=dim)
        tail = lax.slice_in_dim(cells, cells.shape[dim] - width, cells.shape[dim], axis=dim)
        cells = jnp.concatenate(
            [
                lax.ppermute(tail, axis, [(i, (i + 1) % count) for i in range(ends)]),
                cells,
                lax.ppermute(head, axis, [((i + 1) % count, i) for i in range(ends)]),
            ],
            axis=dim,
        )
    return cells


def passed_along(shard, axis, by):
    peers = lax.axis_size(axis)
    pairs = [(i, i + by) for i in range(peers) if 0 <= i + by < peers]
    return lax.ppermute(shard, axis, pairs)


def conv_valid(window, kernel):
    return lax.conv_general_dilated(
        window[None],
        kernel,
        (1, 1, 1),
        "VALID",
        dimension_numbers=NUMBERS,
        preferred_element_type=jnp.float32,
    )[0]


def flipped(kernel):
    return jnp.transpose(jnp.flip(kernel, (0, 1, 2)), (0, 1, 2, 4, 3))


def window(values, step):
    rimmed = extended(values, (("row", 1), ("col", 2)), 1)
    if step > 0:
        piece = rimmed[-2:]
    else:
        piece = rimmed[:2]
    neighbour = passed_along(piece, "tm", step)
    if step > 0:
        return jnp.concatenate([neighbour, rimmed], 0)
    return jnp.concatenate([rimmed, neighbour], 0)


def group_sum(values):
    per_group = values.shape[3] // GROUPS
    return values.sum((1, 2)).reshape(values.shape[0], GROUPS, per_group).sum(2)


def widen(stat, per_group):
    return jnp.repeat(stat, per_group, axis=1)[:, None, None, :]


def tile_count(values):
    return (
        values.shape[1]
        * values.shape[2]
        * lax.axis_size("row")
        * lax.axis_size("col")
        * (values.shape[3] // GROUPS)
    )


def norm_act(raw):
    values = raw.astype(jnp.float32)
    per_group = values.shape[3] // GROUPS
    count = tile_count(values)
    group_mean = lax.psum(group_sum(values), ("row", "col")) / count
    centred = values - widen(group_mean, per_group)
    spread = lax.psum(group_sum(centred * centred), ("row", "col")) / count
    inv_std = widen(lax.rsqrt(spread + EPSILON), per_group)
    normed = centred * inv_std
    return ((normed * jax.nn.sigmoid(normed)).astype(jnp.bfloat16), normed, inv_std)


def norm_back(grad_act, normed, inv_std):
    per_group = normed.shape[3] // GROUPS
    count = tile_count(normed)
    sigmoid_z = jax.nn.sigmoid(normed)
    grad_norm = grad_act * sigmoid_z * (1.0 + normed * (1.0 - sigmoid_z))
    first_total, second_total = lax.psum(
        (group_sum(grad_norm), group_sum(grad_norm * normed)), ("row", "col")
    )
    first_mean = widen(first_total / count, per_group)
    second_mean = widen(second_total / count, per_group)
    return inv_std * (grad_norm - first_mean - normed * second_mean)


def weight_grad(padded, grad):
    summed = lax.conv_general_dilated(
        padded[None],
        grad[:, :, :, None, :],
        (1, 1, 1),
        "VALID",
        dimension_numbers=SWAPPED,
        preferred_element_type=jnp.float32,
    )
    return jnp.transpose(summed, (1, 2, 3, 4, 0))


def on_device(features, conv_first, conv_second, out_grad):
    cells = (
        features.shape[0]
        * features.shape[1]
        * features.shape[2]
        * lax.axis_size("tm")
        * lax.axis_size("row")
        * lax.axis_size("col")
    )
    factor = 1.0 / math.sqrt(cells)
    act_first, norm_first, std_first = norm_act(features)
    pad_first = window(act_first, 1)
    hidden = conv_valid(pad_first, conv_first).astype(jnp.bfloat16)
    act_second, norm_second, std_second = norm_act(hidden)
    pad_second = window(act_second, 1)
    branch = conv_valid(pad_second, conv_second)
    result = (features.astype(jnp.float32) + branch).astype(jnp.bfloat16)
    grad_window = window(out_grad, -1)
    second_term = weight_grad(pad_second, out_grad)
    grad_act2 = conv_valid(grad_window, flipped(conv_second))
    hidden_grad = norm_back(grad_act2, norm_second, std_second).astype(jnp.bfloat16)
    hidden_window = window(hidden_grad, -1)
    grad_act1 = conv_valid(hidden_window, flipped(conv_first))
    first_term = weight_grad(pad_first, hidden_grad)
    feature_grad = (
        out_grad.astype(jnp.float32) + norm_back(grad_act1, norm_first, std_first)
    ).astype(jnp.bfloat16)
    first_total, second_total = lax.psum((first_term, second_term), ("tm", "row", "col"))
    first_grad = (first_total * factor).astype(jnp.bfloat16)
    second_grad = (second_total * factor).astype(jnp.bfloat16)
    return (result, feature_grad, first_grad, second_grad)


def solution(mesh):
    in_specs = (P("tm", "row", "col", None), P(), P(), P("tm", "row", "col", None))
    out_specs = (P("tm", "row", "col", None), P("tm", "row", "col", None), P(), P())
    return jax.shard_map(
        on_device, mesh=mesh, in_specs=in_specs, out_specs=out_specs, check_vma=False
    )
```

profile of v0, /device:TPU:0, one launch (start us, length us, event | category | flops | bytes accessed | tf_op | source)
XLA Modules:
  0.0 334.4 jit_solution(3689381599951502855)
XLA Ops:
  8.6 15.8 %psum.70 = f32[2,32]{1,0:T(2,128)S(1)} all-reduce(f32[2,32]{1,0:T(2,128)S(1)} %reduce_sum.145), channel_id=1, replica_groups=mesh['tm'=4,'row'=2,'col'=4] {'row','col'}, use_global_device_ids=true, to_apply=%region_2.0 | all-reduce | flops 64 | bytes 512 | tf_op jit(solution)/shard_map/psum | solution.py:89
  25.8 14.2 %psum.71 = f32[2,32]{1,0:T(2,128)S(1)} all-reduce(f32[2,32]{1,0:T(2,128)S(1)} %reduce_sum.147), channel_id=1, replica_groups=mesh['tm'=4,'row'=2,'col'=4] {'row','col'}, use_global_device_ids=true, to_apply=%region_5.0 | all-reduce | flops 64 | bytes 512 | tf_op jit(solution)/shard_map/psum | solution.py:91
  43.3 3.0 collective-permute-start
  51.0 4.8 %collective-permute-start.2 = (bf16[2,18,1,128]{3,1,2,0:T(8,128)(2,1)S(1)}, bf16[2,18,1,128]{3,1,2,0:T(8,128)(2,1)S(1)}, u32[]{:S(2)}, u32[]{:S(2)}) collective-permute-start(bf16[2,18,1,128]{3,1,2,0:T(8,128)(2,1)S(1)} %get-tuple-element.30), channel_id=1, source_target_pairs={{0,1},{1,2},{2,3},{4,5},{5,6},{6,7},{8,9},{9,10},{10,11},{12,13},{... | collective-permute-start | bytes 27656 | tf_op jit(solution)/shard_map/ppermute | solution.py:24
  57.4 3.5 %collective-permute-start.4 = (bf16[2,18,34,128]{3,1,2,0:T(8,128)(2,1)S(1)}, bf16[2,18,34,128]{3,1,2,0:T(8,128)(2,1)S(1)}, u32[]{:S(2)}, u32[]{:S(2)}) collective-permute-start(bf16[2,18,34,128]{3,1,2,0:T(8,128)(2,1)S(1)} %pad_maximum_fusion), channel_id=1, source_target_pairs={{0,8},{8,16},{16,24},{1,9},{9,17},{17,25},{2,10},{10,18},{18,26},{... | collective-permute-start | bytes 940040 | tf_op jit(solution)/shard_map/ppermute | solution.py:36
  62.2 5.4 %collective-permute-start.12 = (bf16[2,18,1,128]{3,2,1,0:T(2,128)(2,1)S(1)}, bf16[2,18,1,128]{3,2,1,0:T(2,128)(2,1)S(1)}, u32[]{:S(2)}, u32[]{:S(2)}) collective-permute-start(bf16[2,18,1,128]{3,2,1,0:T(2,128)(2,1)S(1)} %get-tuple-element.32), channel_id=1, source_target_pairs={{0,1},{1,2},{2,3},{4,5},{5,6},{6,7},{8,9},{9,10},{10,11},{12,13},{... | collective-permute-start | bytes 27656 | tf_op jit(solution)/shard_map/ppermute | solution.py:24
  72.5 2.5 select_reduce_fusion
  75.3 17.4 %psum.72 = f32[2,32]{1,0:T(2,128)S(1)} all-reduce(f32[2,32]{1,0:T(2,128)S(1)} %reduce_sum.149), channel_id=1, replica_groups=mesh['tm'=4,'row'=2,'col'=4] {'row','col'}, use_global_device_ids=true, to_apply=%region_8.0 | all-reduce | flops 64 | bytes 512 | tf_op jit(solution)/shard_map/psum | solution.py:89
  93.1 14.5 %psum.73 = f32[2,32]{1,0:T(2,128)S(1)} all-reduce(f32[2,32]{1,0:T(2,128)S(1)} %reduce_sum.151), channel_id=1, replica_groups=mesh['tm'=4,'row'=2,'col'=4] {'row','col'}, use_global_device_ids=true, to_apply=%region_11.0 | all-reduce | flops 64 | bytes 512 | tf_op jit(solution)/shard_map/psum | solution.py:91
  109.5 2.5 convolution_select_fusion.1
  112.8 14.7 %all-reduce.2 = (f32[2,32]{1,0:T(2,128)S(1)}, f32[2,32]{1,0:T(2,128)S(1)}) all-reduce(f32[2,32]{1,0:T(2,128)S(1)} %reduce_sum.155, f32[2,32]{1,0:T(2,128)S(1)} %reduce_sum.153), channel_id=1, replica_groups=mesh['tm'=4,'row'=2,'col'=4] {'row','col'}, use_global_device_ids=true, to_apply=%region_17.18 | all-reduce | flops 128 | bytes 1024 | tf_op jit(solution)/shard_map/psum | solution.py:102
  129.7 3.0 collective-permute-start.15
  134.1 3.0 collective-permute-start.5
  139.3 4.5 %collective-permute-start.7 = (bf16[2,18,1,128]{3,1,2,0:T(8,128)(2,1)S(1)}, bf16[2,18,1,128]{3,1,2,0:T(8,128)(2,1)S(1)}, u32[]{:S(2)}, u32[]{:S(2)}) collective-permute-start(bf16[2,18,1,128]{3,1,2,0:T(8,128)(2,1)S(1)} %get-tuple-element.28), channel_id=1, source_target_pairs={{0,1},{1,2},{2,3},{4,5},{5,6},{6,7},{8,9},{9,10},{10,11},{12,13},{... | collective-permute-start | bytes 27656 | tf_op jit(solution)/shard_map/ppermute | solution.py:24
  145.8 5.8 %collective-permute-start.17 = (bf16[2,18,1,128]{3,1,2,0:T(8,128)(2,1)}, bf16[2,18,1,128]{3,1,2,0:T(8,128)(2,1)}, u32[]{:S(2)}, u32[]{:S(2)}) collective-permute-start(bf16[2,18,1,128]{3,1,2,0:T(8,128)(2,1)} %get-tuple-element.26), channel_id=1, source_target_pairs={{0,1},{1,2},{2,3},{4,5},{5,6},{6,7},{8,9},{9,10},{10,11},{12,13},{... | collective-permute-start | bytes 27656 | tf_op jit(solution)/shard_map/ppermute | solution.py:24
  152.6 5.5 %collective-permute-start.9 = (bf16[2,18,34,128]{3,1,2,0:T(8,128)(2,1)}, bf16[2,18,34,128]{3,1,2,0:T(8,128)(2,1)}, u32[]{:S(2)}, u32[]{:S(2)}) collective-permute-start(bf16[2,18,34,128]{3,1,2,0:T(8,128)(2,1)} %pad_maximum_fusion.1), channel_id=1, source_target_pairs={{0,8},{8,16},{16,24},{1,9},{9,17},{17,25},{2,10},{10,18},{18,26},{... | collective-permute-start | bytes 940040 | tf_op jit(solution)/shard_map/ppermute | solution.py:36
  158.1 9.0 %fusion.6 = f32[3,3,3,128,128]{4,3,2,1,0:T(8,128)} fusion(bf16[1,4,18,34,128]{4,2,3,1,0:T(8,128)(2,1)S(1)} %copy-done.11, bf16[2,16,32,1,128]{4,1,2,0,3:T(8,128)(2,1)S(1)} %fusion.67), kind=kOutput, calls=%fused_computation.9 | convolution fusion | flops 905969664 | bytes 2658304 | tf_op jit(solution)/shard_map/transpose | solution.py:119
  170.5 2.3 fusion.89
  172.8 9.0 %fusion.4 = f32[3,3,3,128,128]{4,3,2,1,0:T(8,128)} fusion(bf16[1,4,18,34,128]{4,2,3,1,0:T(8,128)(2,1)S(1)} %get-tuple-element.20, bf16[2,16,32,1,128]{4,2,1,0,3:T(8,128)(2,1)S(1)} %bitcast.93), kind=kOutput, calls=%fused_computation.7 | convolution fusion | flops 905969664 | bytes 2658304 | tf_op jit(solution)/shard_map/transpose | solution.py:119
  184.7 2.5 convolution_select_fusion
  188.1 15.5 %all-reduce.1 = (f32[2,32]{1,0:T(2,128)S(1)}, f32[2,32]{1,0:T(2,128)S(1)}) all-reduce(f32[2,32]{1,0:T(2,128)S(1)} %reduce_sum.159, f32[2,32]{1,0:T(2,128)S(1)} %reduce_sum.157), channel_id=1, replica_groups=mesh['tm'=4,'row'=2,'col'=4] {'row','col'}, use_global_device_ids=true, to_apply=%region_23.24 | all-reduce | flops 128 | bytes 1024 | tf_op jit(solution)/shard_map/psum | solution.py:102
  205.2 2.5 convolution_select_fusion.2
  209.6 114.0 %all-reduce.5.cloned.1.call-done = (f32[3,3,3,128,128]{4,3,2,1,0:T(8,128)}, f32[3,3,3,128,128]{4,3,2,1,0:T(8,128)}) async-done(((f32[3,3,3,128,128]{4,3,2,1,0:T(8,128)}, f32[3,3,3,128,128]{4,3,2,1,0:T(8,128)}), (f32[3,3,3,128,128]{4,3,2,1,0:T(8,128)}, f32[3,3,3,128,128]{4,3,2,1,0:T(8,128)})) %all-reduce.5.cloned.1.call-update) | async-done | bytes 3538960 | tf_op jit(solution)/shard_map/psum | solution.py:149
  323.6 2.8 multiply_convert_fusion.1
  (176 shorter events, 41.8 us)
Async XLA Ops:
  7.2 65.1 %copy-start = (bf16[3,3,3,128,128]{4,3,2,1,0:T(8,128)(2,1)S(1)}, bf16[3,3,3,128,128]{4,3,2,1,0:T(8,128)(2,1)}, u32[]{:S(2)}) copy-start(bf16[3,3,3,128,128]{4,3,2,1,0:T(8,128)(2,1)} %param.5) | copy-start | bytes 2654212
  7.2 48.6 %copy-start.9 = (bf16[2,16,32,128]{3,2,1,0:T(8,128)(2,1)S(1)}, bf16[2,16,32,128]{3,2,1,0:T(8,128)(2,1)}, u32[]{:S(2)}) copy-start(bf16[2,16,32,128]{3,2,1,0:T(8,128)(2,1)} %param.7) | copy-start | bytes 786436
  7.2 316.4 %all-reduce.5.cloned.1.call-start = ((), (), s32[]{:S(2)}) async-start(), calls=%async_computation | async-start | bytes 7077888 | tf_op jit(solution)/shard_map/psum | solution.py:149
  42.0 7.7 %collective-permute-start.1 = (bf16[2,1,32,128]{3,1,2,0:T(2,128)(2,1)S(1)}, bf16[2,1,32,128]{3,1,2,0:T(2,128)(2,1)S(1)}, u32[]{:S(2)}, u32[]{:S(2)}) collective-permute-start(bf16[2,1,32,128]{3,1,2,0:T(2,128)(2,1)S(1)} %get-tuple-element.43), channel_id=1, source_target_pairs={{4,0},{5,1},{6,2},{7,3},{12,8},{13,9},{14,10},{15,11},{20,16},{21,... | collective-permute-start | bytes 49160 | tf_op jit(solution)/shard_map/ppermute | solution.py:26
  43.3 6.4 %collective-permute-start = (bf16[2,1,32,128]{3,1,2,0:T(2,128)(2,1)S(1)}, bf16[2,1,32,128]{3,1,2,0:T(2,128)(2,1)S(1)}, u32[]{:S(2)}, u32[]{:S(2)}) collective-permute-start(bf16[2,1,32,128]{3,1,2,0:T(2,128)(2,1)S(1)} %get-tuple-element.42), channel_id=1, source_target_pairs={{0,4},{1,5},{2,6},{3,7},{8,12},{9,13},{10,14},{11,15},{16,20},{17,... | collective-permute-start | bytes 49160 | tf_op jit(solution)/shard_map/ppermute | solution.py:24
  47.0 8.8 %collective-permute-start.10 = (bf16[2,1,32,128]{3,2,1,0:T(8,128)(2,1)S(1)}, bf16[2,1,32,128]{3,2,1,0:T(8,128)(2,1)S(1)}, u32[]{:S(2)}, u32[]{:S(2)}) collective-permute-start(bf16[2,1,32,128]{3,2,1,0:T(8,128)(2,1)S(1)} %get-tuple-element.39), channel_id=1, source_target_pairs={{0,4},{1,5},{2,6},{3,7},{8,12},{9,13},{10,14},{11,15},{16,20},{17,... | collective-permute-start | bytes 49160 | tf_op jit(solution)/shard_map/ppermute | solution.py:24
  48.3 7.5 %collective-permute-start.11 = (bf16[2,1,32,128]{3,2,1,0:T(8,128)(2,1)S(1)}, bf16[2,1,32,128]{3,2,1,0:T(8,128)(2,1)S(1)}, u32[]{:S(2)}, u32[]{:S(2)}) collective-permute-start(bf16[2,1,32,128]{3,2,1,0:T(8,128)(2,1)S(1)} %get-tuple-element.38), channel_id=1, source_target_pairs={{4,0},{5,1},{6,2},{7,3},{12,8},{13,9},{14,10},{15,11},{20,16},{21,... | collective-permute-start | bytes 49160 | tf_op jit(solution)/shard_map/ppermute | solution.py:26
  49.7 6.2 %collective-permute-start.3 = (bf16[2,18,1,128]{3,1,2,0:T(8,128)(2,1)S(1)}, bf16[2,18,1,128]{3,1,2,0:T(8,128)(2,1)S(1)}, u32[]{:S(2)}, u32[]{:S(2)}) collective-permute-start(bf16[2,18,1,128]{3,1,2,0:T(8,128)(2,1)S(1)} %get-tuple-element.31), channel_id=1, source_target_pairs={{1,0},{2,1},{3,2},{5,4},{6,5},{7,6},{9,8},{10,9},{11,10},{13,12},{... | collective-permute-start | bytes 27656 | tf_op jit(solution)/shard_map/ppermute | solution.py:26
  51.0 6.2 %collective-permute-start.2 = (bf16[2,18,1,128]{3,1,2,0:T(8,128)(2,1)S(1)}, bf16[2,18,1,128]{3,1,2,0:T(8,128)(2,1)S(1)}, u32[]{:S(2)}, u32[]{:S(2)}) collective-permute-start(bf16[2,18,1,128]{3,1,2,0:T(8,128)(2,1)S(1)} %get-tuple-element.30), channel_id=1, source_target_pairs={{0,1},{1,2},{2,3},{4,5},{5,6},{6,7},{8,9},{9,10},{10,11},{12,13},{... | collective-permute-start | bytes 27656 | tf_op jit(solution)/shard_map/ppermute | solution.py:24
  57.4 13.2 %collective-permute-start.4 = (bf16[2,18,34,128]{3,1,2,0:T(8,128)(2,1)S(1)}, bf16[2,18,34,128]{3,1,2,0:T(8,128)(2,1)S(1)}, u32[]{:S(2)}, u32[]{:S(2)}) collective-permute-start(bf16[2,18,34,128]{3,1,2,0:T(8,128)(2,1)S(1)} %pad_maximum_fusion), channel_id=1, source_target_pairs={{0,8},{8,16},{16,24},{1,9},{9,17},{17,25},{2,10},{10,18},{18,26},{... | collective-permute-start | bytes 940040 | tf_op jit(solution)/shard_map/ppermute | solution.py:36
  60.9 6.8 %collective-permute-start.13 = (bf16[2,18,1,128]{3,2,1,0:T(2,128)(2,1)S(1)}, bf16[2,18,1,128]{3,2,1,0:T(2,128)(2,1)S(1)}, u32[]{:S(2)}, u32[]{:S(2)}) collective-permute-start(bf16[2,18,1,128]{3,2,1,0:T(2,128)(2,1)S(1)} %get-tuple-element.33), channel_id=1, source_target_pairs={{1,0},{2,1},{3,2},{5,4},{6,5},{7,6},{9,8},{10,9},{11,10},{13,12},{... | collective-permute-start | bytes 27656 | tf_op jit(solution)/shard_map/ppermute | solution.py:26
  62.2 6.9 %collective-permute-start.12 = (bf16[2,18,1,128]{3,2,1,0:T(2,128)(2,1)S(1)}, bf16[2,18,1,128]{3,2,1,0:T(2,128)(2,1)S(1)}, u32[]{:S(2)}, u32[]{:S(2)}) collective-permute-start(bf16[2,18,1,128]{3,2,1,0:T(2,128)(2,1)S(1)} %get-tuple-element.32), channel_id=1, source_target_pairs={{0,1},{1,2},{2,3},{4,5},{5,6},{6,7},{8,9},{9,10},{10,11},{12,13},{... | collective-permute-start | bytes 27656 | tf_op jit(solution)/shard_map/ppermute | solution.py:24
  69.3 38.5 %collective-permute-start.14 = (bf16[2,18,34,128]{3,2,1,0:T(8,128)(2,1)S(1)}, bf16[2,18,34,128]{3,2,1,0:T(8,128)(2,1)S(1)}, u32[]{:S(2)}, u32[]{:S(2)}) collective-permute-start(bf16[2,18,34,128]{3,2,1,0:T(8,128)(2,1)S(1)} %pad_maximum_fusion.3), channel_id=1, source_target_pairs={{8,0},{16,8},{24,16},{9,1},{17,9},{25,17},{10,2},{18,10},{26,18},{... | collective-permute-start | bytes 940040 | tf_op jit(solution)/shard_map/ppermute | solution.py:36
  128.2 29.9 %copy-start.5 = (bf16[2,16,32,128]{3,1,2,0:T(8,128)(2,1)}, bf16[2,16,32,128]{3,1,2,0:T(8,128)(2,1)S(1)}, u32[]{:S(2)}) copy-start(bf16[2,16,32,128]{3,1,2,0:T(8,128)(2,1)S(1)} %get-tuple-element.25) | copy-start | bytes 786436
  128.3 15.6 %collective-permute-start.16 = (bf16[2,1,32,128]{3,1,2,0:T(2,128)(2,1)S(1)}, bf16[2,1,32,128]{3,1,2,0:T(2,128)(2,1)S(1)}, u32[]{:S(2)}, u32[]{:S(2)}) collective-permute-start(bf16[2,1,32,128]{3,1,2,0:T(2,128)(2,1)S(1)} %get-tuple-element.37), channel_id=1, source_target_pairs={{4,0},{5,1},{6,2},{7,3},{12,8},{13,9},{14,10},{15,11},{20,16},{21,... | collective-permute-start | bytes 49160 | tf_op jit(solution)/shard_map/ppermute | solution.py:26
  129.7 14.2 %collective-permute-start.15 = (bf16[2,1,32,128]{3,1,2,0:T(2,128)(2,1)S(1)}, bf16[2,1,32,128]{3,1,2,0:T(2,128)(2,1)S(1)}, u32[]{:S(2)}, u32[]{:S(2)}) collective-permute-start(bf16[2,1,32,128]{3,1,2,0:T(2,128)(2,1)S(1)} %get-tuple-element.36), channel_id=1, source_target_pairs={{0,4},{1,5},{2,6},{3,7},{8,12},{9,13},{10,14},{11,15},{16,20},{17,... | collective-permute-start | bytes 49160 | tf_op jit(solution)/shard_map/ppermute | solution.py:24
  132.8 4.7 %collective-permute-start.6 = (bf16[2,1,32,128]{3,1,2,0:T(2,128)(2,1)S(1)}, bf16[2,1,32,128]{3,1,2,0:T(2,128)(2,1)S(1)}, u32[]{:S(2)}, u32[]{:S(2)}) collective-permute-start(bf16[2,1,32,128]{3,1,2,0:T(2,128)(2,1)S(1)} %get-tuple-element.41), channel_id=1, source_target_pairs={{4,0},{5,1},{6,2},{7,3},{12,8},{13,9},{14,10},{15,11},{20,16},{21,... | collective-permute-start | bytes 49160 | tf_op jit(solution)/shard_map/ppermute | solution.py:26
  134.1 3.9 %collective-permute-start.5 = (bf16[2,1,32,128]{3,1,2,0:T(2,128)(2,1)S(1)}, bf16[2,1,32,128]{3,1,2,0:T(2,128)(2,1)S(1)}, u32[]{:S(2)}, u32[]{:S(2)}) collective-permute-start(bf16[2,1,32,128]{3,1,2,0:T(2,128)(2,1)S(1)} %get-tuple-element.40), channel_id=1, source_target_pairs={{0,4},{1,5},{2,6},{3,7},{8,12},{9,13},{10,14},{11,15},{16,20},{17,... | collective-permute-start | bytes 49160 | tf_op jit(solution)/shard_map/ppermute | solution.py:24
  138.0 13.6 %collective-permute-start.8 = (bf16[2,18,1,128]{3,1,2,0:T(8,128)(2,1)S(1)}, bf16[2,18,1,128]{3,1,2,0:T(8,128)(2,1)S(1)}, u32[]{:S(2)}, u32[]{:S(2)}) collective-permute-start(bf16[2,18,1,128]{3,1,2,0:T(8,128)(2,1)S(1)} %get-tuple-element.29), channel_id=1, source_target_pairs={{1,0},{2,1},{3,2},{5,4},{6,5},{7,6},{9,8},{10,9},{11,10},{13,12},{... | collective-permute-start | bytes 27656 | tf_op jit(solution)/shard_map/ppermute | solution.py:26
  139.3 12.3 %collective-permute-start.7 = (bf16[2,18,1,128]{3,1,2,0:T(8,128)(2,1)S(1)}, bf16[2,18,1,128]{3,1,2,0:T(8,128)(2,1)S(1)}, u32[]{:S(2)}, u32[]{:S(2)}) collective-permute-start(bf16[2,18,1,128]{3,1,2,0:T(8,128)(2,1)S(1)} %get-tuple-element.28), channel_id=1, source_target_pairs={{0,1},{1,2},{2,3},{4,5},{5,6},{6,7},{8,9},{9,10},{10,11},{12,13},{... | collective-permute-start | bytes 27656 | tf_op jit(solution)/shard_map/ppermute | solution.py:24
  144.5 22.6 %collective-permute-start.18 = (bf16[2,18,1,128]{3,1,2,0:T(8,128)(2,1)}, bf16[2,18,1,128]{3,1,2,0:T(8,128)(2,1)}, u32[]{:S(2)}, u32[]{:S(2)}) collective-permute-start(bf16[2,18,1,128]{3,1,2,0:T(8,128)(2,1)} %get-tuple-element.27), channel_id=1, source_target_pairs={{1,0},{2,1},{3,2},{5,4},{6,5},{7,6},{9,8},{10,9},{11,10},{13,12},{... | collective-permute-start | bytes 27656 | tf_op jit(solution)/shard_map/ppermute | solution.py:26
  145.8 21.3 %collective-permute-start.17 = (bf16[2,18,1,128]{3,1,2,0:T(8,128)(2,1)}, bf16[2,18,1,128]{3,1,2,0:T(8,128)(2,1)}, u32[]{:S(2)}, u32[]{:S(2)}) collective-permute-start(bf16[2,18,1,128]{3,1,2,0:T(8,128)(2,1)} %get-tuple-element.26), channel_id=1, source_target_pairs={{0,1},{1,2},{2,3},{4,5},{5,6},{6,7},{8,9},{9,10},{10,11},{12,13},{... | collective-permute-start | bytes 27656 | tf_op jit(solution)/shard_map/ppermute | solution.py:24
  152.6 17.9 %collective-permute-start.9 = (bf16[2,18,34,128]{3,1,2,0:T(8,128)(2,1)}, bf16[2,18,34,128]{3,1,2,0:T(8,128)(2,1)}, u32[]{:S(2)}, u32[]{:S(2)}) collective-permute-start(bf16[2,18,34,128]{3,1,2,0:T(8,128)(2,1)} %pad_maximum_fusion.1), channel_id=1, source_target_pairs={{0,8},{8,16},{16,24},{1,9},{9,17},{17,25},{2,10},{10,18},{18,26},{... | collective-permute-start | bytes 940040 | tf_op jit(solution)/shard_map/ppermute | solution.py:36
  169.0 13.0 %collective-permute-start.19 = (bf16[2,18,34,128]{3,1,2,0:T(8,128)(2,1)}, bf16[2,18,34,128]{3,1,2,0:T(8,128)(2,1)}, u32[]{:S(2)}, u32[]{:S(2)}) collective-permute-start(bf16[2,18,34,128]{3,1,2,0:T(8,128)(2,1)} %pad_maximum_fusion.2), channel_id=1, source_target_pairs={{8,0},{16,8},{24,16},{9,1},{17,9},{25,17},{10,2},{18,10},{26,18},{... | collective-permute-start | bytes 940040 | tf_op jit(solution)/shard_map/ppermute | solution.py:36
  (25 other events, 259.3 us)
Sparse Core Ops, SparseCore 0:
  181.9 141.6 all-reduce.4
where the time goes:
time: 335 us; the launch traced here: 334 us
  waiting for transfers between devices  117 us (35%)
  blocking collectives  92 us (27%)
  starting transfers between devices  53.2 us (16%)
  matrix products  27.9 us (8%)
  other arithmetic  18.4 us (5%)
  between operations  14.9 us (4%)
  local copies, waits for them, and re-layouts  10.5 us (3%)
    psum x1, waiting for transfers between devices, on_device(): lax.psum((first_term, second_term), ('tm', 'row', 'col'))  114 us
    psum x2, blocking collectives, norm_act(): group_mean = lax.psum(group_sum(values), ('row', 'col')) / count  33.1 us
    ppermute x8, starting transfers between devices, extended(): lax.ppermute(tail, axis, [(i, (i + 1) % count) for i in range(ends)])  30.9 us
    psum x2, blocking collectives, norm_back(): lax.psum((group_sum(grad_norm), group_sum(grad_norm * normed)), ('row', '...  30.2 us
    psum x2, blocking collectives, norm_act(): spread = lax.psum(group_sum(centred * centred), ('row', 'col')) / count  28.7 us
    transpose x2, matrix products, weight_grad(): return jnp.transpose(summed, (1, 2, 3, 4, 0))  18 us
    ppermute x4, starting transfers between devices, passed_along(): return lax.ppermute(shard, axis, pairs)  11.8 us
    ppermute x8, starting transfers between devices, extended(): lax.ppermute(head, axis, [((i + 1) % count, i) for i in range(ends)])  10.5 us
  transfers between devices with their start and end apart: 21, of which 5 were waited for; matrix products, arithmetic and copies ran while one was open for 12% of the time, Pallas kernels for 0%

commit v1 on v0

v1 whole, which is shorter than its diff:
```python
import math

import jax
import jax.numpy as jnp
from jax import lax
from jax.sharding import PartitionSpec as P

GROUPS = 32


EPSILON = 1e-06
NUMBERS = ("NDHWC", "DHWIO", "NDHWC")
SWAPPED = ("CDHWN", "DHWIO", "CDHWN")


def conv_valid(window, kernel):
    return lax.conv_general_dilated(
        window[None],
        kernel,
        (1, 1, 1),
        "VALID",
        dimension_numbers=NUMBERS,
        preferred_element_type=jnp.float32,
    )[0]


def flipped(kernel):
    return jnp.transpose(jnp.flip(kernel, (0, 1, 2)), (0, 1, 2, 4, 3))


def weight_grad(padded, grad):
    summed = lax.conv_general_dilated(
        padded[None],
        grad[:, :, :, None, :],
        (1, 1, 1),
        "VALID",
        dimension_numbers=SWAPPED,
        preferred_element_type=jnp.float32,
    )
    return jnp.transpose(summed, (1, 2, 3, 4, 0))


def split3(stat):
    high = lax.reduce_precision(stat, 8, 7)
    rest = stat - high
    middle = lax.reduce_precision(rest, 8, 7)
    return jnp.stack([high, middle, rest - middle]).astype(jnp.bfloat16)


def join3(parts):
    terms = parts.astype(jnp.float32)
    return terms[0] + (terms[1] + terms[2])


def group_total(stat):
    chans = stat.shape[-1]
    per_group = chans // GROUPS
    ids = jnp.arange(chans) // per_group
    same = (ids[:, None] == ids[None, :]).astype(jnp.float32)
    flat = stat.reshape(-1, chans)
    return jnp.dot(flat, same, precision=lax.Precision.HIGHEST).reshape(stat.shape)


def local_stats(values):
    mean = values.mean((1, 2))
    centred = values - mean[:, None, None, :]
    return jnp.stack([mean, (centred * centred).sum((1, 2))])


def rows_of(*pieces):
    return jnp.concatenate([p.reshape(-1, p.shape[-1]) for p in pieces], 0)


def unrows(flat, shapes):
    out, at = [], 0
    for shape in shapes:
        count = math.prod(shape[:-1])
        out.append(flat[at : at + count].reshape(shape))
        at += count
    return out


def row_swap(values):
    return lax.ppermute(values, "row", [(0, 1), (1, 0)])


def exchange(arrays, rims, stats, cells):
    upper = lax.axis_index("row") == 0
    edges = [
        jnp.where(upper, a[:, a.shape[1] - rim :], a[:, :rim]) for a, rim in zip(arrays, rims)
    ]
    parts = split3(stats)
    got = unrows(row_swap(rows_of(*edges, parts)), [e.shape for e in edges] + [parts.shape])
    arrays = [
        jnp.concatenate(
            [
                jnp.where(upper, jnp.zeros_like(rim), rim),
                a,
                jnp.where(upper, rim, jnp.zeros_like(rim)),
            ],
            1,
        )
        for a, rim in zip(arrays, got)
    ]
    other = join3(got[-1])
    delta = stats[0] - other[0]
    stats = jnp.stack(
        [0.5 * (stats[0] + other[0]), stats[1] + other[1] + (0.5 * cells) * delta * delta]
    )

    count = lax.axis_size("col")
    here = lax.axis_index("col")
    heads = [a[:, :, :rim] for a, rim in zip(arrays, rims)]
    tails = [a[:, :, a.shape[2] - rim :] for a, rim in zip(arrays, rims)]
    shapes = [h.shape for h in heads]
    head, tail = rows_of(*heads), rows_of(*tails)
    parts = split3(stats)
    target = jnp.arange(count)[:, None, None]
    nothing = jnp.zeros_like(head)
    slots = jnp.where(target == here + 1, tail, jnp.where(target == here - 1, head, nothing))
    flat_parts = rows_of(parts)
    slots = jnp.concatenate(
        [slots, jnp.broadcast_to(flat_parts[None], (count,) + flat_parts.shape)], 1
    )
    got = lax.all_to_all(slots, "col", 0, 0)
    edge = head.shape[0]
    left = lax.dynamic_index_in_dim(got, jnp.maximum(here - 1, 0), 0, False)[:edge]
    right = lax.dynamic_index_in_dim(got, jnp.minimum(here + 1, count - 1), 0, False)[:edge]
    left = unrows(jnp.where(here > 0, left, nothing), shapes)
    right = unrows(jnp.where(here < count - 1, right, nothing), shapes)
    arrays = [jnp.concatenate([lo, a, hi], 2) for lo, a, hi in zip(left, arrays, right)]

    terms = got[:, edge:].reshape((count,) + parts.shape).astype(jnp.float32)
    means, squares = jnp.moveaxis(terms[:, 0] + (terms[:, 1] + terms[:, 2]), 1, 0)
    per_group = stats.shape[-1] // GROUPS
    pieces = count * per_group
    mean = group_total(means.sum(0)) / pieces
    off = means - mean[None]
    spread = group_total((squares + (2.0 * cells) * off * off).sum(0)) / (2.0 * cells * pieces)
    return arrays, mean[:, None, None, :], lax.rsqrt(spread + EPSILON)[:, None, None, :]


def inside(frame, rim):
    high, wide = frame.shape[1] - 2 * rim, frame.shape[2] - 2 * rim
    rows = lax.axis_index("row") * high + jnp.arange(-rim, high + rim)
    cols = lax.axis_index("col") * wide + jnp.arange(-rim, wide + rim)
    in_rows = (rows >= 0) & (rows < high * lax.axis_size("row"))
    in_cols = (cols >= 0) & (cols < wide * lax.axis_size("col"))
    return (in_rows[:, None] & in_cols[None, :])[None, :, :, None]


def frame_means(sums, cells):
    peers = lax.axis_size("row") * lax.axis_size("col")
    slots = jnp.broadcast_to(sums[None], (peers,) + sums.shape)
    total = lax.all_to_all(slots, ("row", "col"), 0, 0).sum(0)
    return group_total(total) / (cells * peers * (sums.shape[-1] // GROUPS))


def later(values, by):
    peers = lax.axis_size("tm")
    pairs = [(i, i + by) for i in range(peers) if 0 <= i + by < peers]
    return lax.ppermute(values, "tm", pairs)


def back_sums(act_grad, normed):
    sigmoid_z = jax.nn.sigmoid(normed)
    return act_grad * sigmoid_z * (1.0 + normed * (1.0 - sigmoid_z))


def scatter_sum(values, axis):
    peers = lax.axis_size(axis)
    share = -(-values.shape[0] // peers)
    values = jnp.pad(values, ((0, share * peers - values.shape[0]), (0, 0)))
    slots = values.reshape(peers, share, values.shape[1]).astype(jnp.bfloat16)
    return lax.all_to_all(slots, axis, 0, 0).astype(jnp.float32).sum(0)


def gather_shares(share, axis, rows):
    peers = lax.axis_size(axis)
    slots = jnp.broadcast_to(share[None], (peers,) + share.shape)
    return lax.all_to_all(slots, axis, 0, 0).reshape(-1, share.shape[1])[:rows]


def summed_kernels(first_term, second_term, factor):
    shape = first_term.shape
    chans = shape[-1]
    first_term, second_term = first_term.reshape(-1, chans), second_term.reshape(-1, chans)
    upper = lax.axis_index("row") == 0
    keep = jnp.where(upper, first_term, second_term)
    give = jnp.where(upper, second_term, first_term).astype(jnp.bfloat16)
    keep = keep + row_swap(give).astype(jnp.float32)
    by_col = scatter_sum(keep, "col")
    by_tm = scatter_sum(by_col, "tm")
    done = (by_tm * factor).astype(jnp.bfloat16)
    done = gather_shares(done, "tm", by_col.shape[0])
    done = gather_shares(done, "col", keep.shape[0])
    other = row_swap(done)
    return (
        jnp.where(upper, done, other).reshape(shape),
        jnp.where(upper, other, done).reshape(shape),
    )


def on_device(features, conv_first, conv_second, out_grad):
    frames, high, wide, _ = features.shape
    cells = high * wide
    every = cells * frames * lax.axis_size("tm") * lax.axis_size("row") * lax.axis_size("col")
    factor = 1.0 / math.sqrt(every)

    stats = local_stats(features.astype(jnp.float32))
    (wide_features, wide_grad), mean_first, std_first = exchange(
        [features, out_grad], [1, 2], stats, cells
    )
    normed = (wide_features.astype(jnp.float32) - mean_first) * std_first
    act_first = normed * jax.nn.sigmoid(normed)
    rim_ok = inside(act_first, 1)
    act_first = jnp.where(rim_ok, act_first, 0.0).astype(jnp.bfloat16)
    pad_first = jnp.concatenate([later(act_first[-2:], 1), act_first], 0)
    grad_window = jnp.concatenate([wide_grad, later(wide_grad[:2], -1)], 0)

    hidden = conv_valid(pad_first, conv_first).astype(jnp.bfloat16)
    grad_act2 = conv_valid(grad_window, flipped(conv_second))
    stats = local_stats(hidden.astype(jnp.float32))
    (wide_hidden,), mean_second, std_second = exchange([hidden], [1], stats, cells)
    normed = (wide_hidden.astype(jnp.float32) - mean_second) * std_second
    act_second = normed * jax.nn.sigmoid(normed)
    act_second = jnp.where(rim_ok, act_second, 0.0).astype(jnp.bfloat16)
    core = (slice(None), slice(1, -1), slice(1, -1))

    q = back_sums(grad_act2, normed)
    sums = jnp.stack([q[core].sum((1, 2)), (q * normed)[core].sum((1, 2))])
    means = frame_means(sums, cells)[:, :, None, None, :]
    hidden_grad = std_second * (q - means[0] - normed * means[1])
    hidden_grad = jnp.where(rim_ok, hidden_grad, 0.0).astype(jnp.bfloat16)

    hidden_window = jnp.concatenate([hidden_grad, later(hidden_grad[:2], -1)], 0)
    pad_second = jnp.concatenate([later(act_second[-2:], 1), act_second], 0)
    first_term = weight_grad(pad_first, hidden_grad[core])
    second_term = jnp.flip(weight_grad(grad_window[core], act_second[core]), (0, 1, 2))
    second_term = jnp.swapaxes(second_term, 3, 4)

    branch = conv_valid(pad_second, conv_second)
    result = (features.astype(jnp.float32) + branch).astype(jnp.bfloat16)

    grad_act1 = conv_valid(hidden_window, flipped(conv_first))
    normed = (features.astype(jnp.float32) - mean_first) * std_first
    q = back_sums(grad_act1, normed)
    means = frame_means(jnp.stack([q.sum((1, 2)), (q * normed).sum((1, 2))]), cells)
    means = means[:, :, None, None, :]
    feature_grad = std_first * (q - means[0] - normed * means[1])
    feature_grad = (out_grad.astype(jnp.float32) + feature_grad).astype(jnp.bfloat16)

    first_grad, second_grad = summed_kernels(first_term, second_term, factor)
    return (result, feature_grad, first_grad, second_grad)


def solution(mesh):
    in_specs = (P("tm", "row", "col", None), P(), P(), P("tm", "row", "col", None))
    out_specs = (P("tm", "row", "col", None), P("tm", "row", "col", None), P(), P())
    return jax.shard_map(
        on_device, mesh=mesh, in_specs=in_specs, out_specs=out_specs, check_vma=False
    )
```

time: 335 us -> 156 us (0.47)
  blocking collectives: 92 us -> 15.6 us
  waiting for transfers between devices: 117 us -> 40.7 us
  starting transfers between devices: 53.2 us -> 37.8 us
  between operations: 14.9 us -> 1.64 us
    psum x1 -> x0, waiting for transfers between devices: 114 us -> none  [on_device(): lax.psum((first_term, second_term), ('tm', 'row', 'col'))]
    psum x6 -> x0, blocking collectives: 92 us -> none  [the longest x2 33.1 us: norm_act(): group_mean = lax.psum(group_sum(values), ('row', 'col')) / count]
    ppermute x20 -> x8, starting transfers between devices: 53.2 us -> 11.1 us  [the longest x4 9.97 us: later(): return lax.ppermute(values, 'tm', pairs)]
    all_to_all x0 -> x7, starting transfers between devices: none -> 26.7 us  [the longest x2 8.34 us: exchange(): got = lax.all_to_all(slots, 'col', 0, 0)]
    all_to_all x0 -> x7, waiting for transfers between devices: none -> 21.9 us  [the longest x1 7.16 us: scatter_sum(): return lax.all_to_all(slots, axis, 0, 0).astype(jnp.float32).sum(0)]
    all_to_all x0 -> x1, blocking collectives: none -> 15.6 us  [scatter_sum(): return lax.all_to_all(slots, axis, 0, 0).astype(jnp.float32).sum(0)]
    ppermute x20 -> x8, waiting for transfers between devices: 3.41 us -> 18.7 us  [the longest x4 15.6 us: later(): return lax.ppermute(values, 'tm', pairs)]
    select_n x0 -> x12, other arithmetic: none -> 4.32 us  [the longest x1 2.49 us: summed_kernels(): jnp.where(upper, other, done).reshape(shape)]
  transfers between devices with their start and end apart: 21 -> 15, of which waited for: 5 -> 10; matrix products, arithmetic and copies ran while one was open for 12% -> 15% of each run, Pallas kernels for 0% -> 0%
where the time goes in v1:
time: 156 us; the launch traced here: 155 us
  waiting for transfers between devices  40.7 us (26%)
  starting transfers between devices  37.8 us (24%)
  matrix products  29.8 us (19%)
  other arithmetic  16.2 us (10%)
  blocking collectives  15.6 us (10%)
  local copies, waits for them, and re-layouts  13 us (8%)
  between operations  1.64 us (1%)
    ppermute x4, waiting for transfers between devices, later(): return lax.ppermute(values, 'tm', pairs)  15.6 us
    all_to_all x1, blocking collectives, scatter_sum(): return lax.all_to_all(slots, axis, 0, 0).astype(jnp.float32).sum(0)  15.6 us
    transpose x2, matrix products, weight_grad(): return jnp.transpose(summed, (1, 2, 3, 4, 0))  15.4 us
    conv_general_dilated x4, matrix products, conv_valid(): lax.conv_general_dilated(window[None], kernel, (1, 1, 1), 'VALID', dimens...  12.5 us
    ppermute x4, starting transfers between devices, later(): return lax.ppermute(values, 'tm', pairs)  9.97 us
    all_to_all x2, starting transfers between devices, exchange(): got = lax.all_to_all(slots, 'col', 0, 0)  8.34 us
    all_to_all x2, starting transfers between devices, frame_means(): total = lax.all_to_all(slots, ('row', 'col'), 0, 0).sum(0)  7.47 us
    all_to_all x1, waiting for transfers between devices, scatter_sum(): return lax.all_to_all(slots, axis, 0, 0).astype(jnp.float32).sum(0)  7.16 us
  transfers between devices with their start and end apart: 15, of which 10 were waited for; matrix products, arithmetic and copies ran while one was open for 15% of the time, Pallas kernels for 0%

profile of v1, /device:TPU:0, one launch (start us, length us, event | category | flops | bytes accessed | tf_op | source)
XLA Modules:
  0.0 154.7 jit_solution(14753460175597179317)
XLA Ops:
  7.8 5.1 %all-to-all-start = ((bf16[4,128,128]{2,1,0:T(8,128)(2,1)}), bf16[4,128,128]{2,1,0:T(8,128)(2,1)S(1)}, u32[]{:S(2)}, u32[]{:S(2)}) async-start(bf16[4,128,128]{2,1,0:T(8,128)(2,1)} %pad_maximum_fusion.3), calls=%async_computation | async-start | bytes 262144 | tf_op jit(solution)/shard_map/all_to_all | solution.py:125
  12.9 5.0 %all-to-all-done = bf16[4,128,128]{2,1,0:T(8,128)(2,1)S(1)} async-done(((bf16[4,128,128]{2,1,0:T(8,128)(2,1)}), bf16[4,128,128]{2,1,0:T(8,128)(2,1)S(1)}, u32[]{:S(2)}, u32[]{:S(2)}) %all-to-all-start) | async-done | bytes 131104 | tf_op jit(solution)/shard_map/all_to_all | solution.py:125
  19.0 3.5 %collective-permute-start.1 = (bf16[2,18,34,128]{3,2,0,1:T(8,128)(2,1)S(1)}, bf16[2,18,34,128]{3,2,0,1:T(8,128)(2,1)S(1)}, u32[]{:S(2)}, u32[]{:S(2)}) collective-permute-start(bf16[2,18,34,128]{3,2,0,1:T(8,128)(2,1)S(1)} %select_convert_fusion.2), channel_id=1, source_target_pairs={{0,8},{8,16},{16,24},{1,9},{9,17},{17,25},{2,10},{10,18},{18,26},{... | collective-permute-start | bytes 940040 | tf_op jit(solution)/shard_map/ppermute | solution.py:162
  22.5 6.7 %collective-permute-done.1 = bf16[2,18,34,128]{3,2,0,1:T(8,128)(2,1)S(1)} collective-permute-done((bf16[2,18,34,128]{3,2,0,1:T(8,128)(2,1)S(1)}, bf16[2,18,34,128]{3,2,0,1:T(8,128)(2,1)S(1)}, u32[]{:S(2)}, u32[]{:S(2)}) %collective-permute-start.1) | collective-permute-done | bytes 313376 | tf_op jit(solution)/shard_map/ppermute | solution.py:162
  31.6 2.5 %fusion.10 = bf16[2,16,8,5,128]{4,2,3,1,0:T(8,128)(2,1)S(1)} fusion(bf16[3,3,3,128,128]{4,3,2,1,0:T(8,128)(2,1)S(1)} %copy-done.15, bf16[4,18,1,7,2,128]{5,3,4,1,0,2:T(8,128)(2,1)S(1)} %slice.254, bf16[4,18,1,8,5,128]{5,3,4,1,0,2:T(8,128)(2,1)S(1)} %copy.259, pred[8,5]{0,1:T(8,128)(4,1)S(1)} %copy-done.16), kind=kOutput, calls=%fused_computation.19 | convolution fusion | flops 1135886336 | bytes 2207784 | tf_op jit(solution)/shard_map/conv_general_dilated | solution.py:17
  37.0 3.3 %all-to-all-start.1 = ((bf16[4,48,128]{2,1,0:T(8,128)(2,1)}), bf16[4,48,128]{2,1,0:T(8,128)(2,1)S(1)}, u32[]{:S(2)}, u32[]{:S(2)}) async-start(bf16[4,48,128]{2,1,0:T(8,128)(2,1)} %pad_maximum_fusion.5), calls=%async_computation.1 | async-start | bytes 98304 | tf_op jit(solution)/shard_map/all_to_all | solution.py:125
  40.3 9.0 %collective-permute-done.4 = bf16[2,20,36,128]{3,2,1,0:T(8,128)(2,1)S(1)} collective-permute-done((bf16[2,20,36,128]{3,2,1,0:T(8,128)(2,1)S(1)}, bf16[2,20,36,128]{3,2,1,0:T(8,128)(2,1)S(1)}, u32[]{:S(2)}, u32[]{:S(2)}) %collective-permute-start.4) | collective-permute-done | bytes 368672 | tf_op jit(solution)/shard_map/ppermute | solution.py:162
  50.6 2.8 %convolution_select_fusion = f32[2,18,8,5,128]{4,2,3,1,0:T(8,128)S(1)} fusion(bf16[3,3,3,128,128]{4,3,2,1,0:T(8,128)(2,1)S(1)} %copy-done, bf16[4,20,1,7,2,128]{5,3,4,1,0,2:T(8,128)(2,1)S(1)} %slice.271, bf16[4,20,1,8,5,128]{5,3,4,1,0,2:T(8,128)(2,1)S(1)} %copy.274, pred[8,5]{0,1:T(8,128)(4,1)S(1)} %copy-done.18), kind=kOutput, calls=%fused_computation.15 | convolution fusion | flops 1277644800 | bytes 2727976 | tf_op jit(solution)/shard_map/conv_general_dilated | solution.py:17
  56.0 3.5 %all-to-all-start.2 = ((f32[8,2,2,128]{3,2,1,0:T(2,128)}), f32[8,2,2,128]{3,2,1,0:T(2,128)S(1)}, u32[]{:S(2)}, u32[]{:S(2)}) async-start(f32[8,2,2,128]{3,2,1,0:T(2,128)} %broadcast_in_dim.185), calls=%async_computation.2 | async-start | bytes 32768 | tf_op jit(solution)/shard_map/all_to_all | solution.py:155
  60.6 3.3 %all-to-all-done.2 = f32[8,2,2,128]{3,2,1,0:T(2,128)S(1)} async-done(((f32[8,2,2,128]{3,2,1,0:T(2,128)}), f32[8,2,2,128]{3,2,1,0:T(2,128)S(1)}, u32[]{:S(2)}, u32[]{:S(2)}) %all-to-all-start.2) | async-done | bytes 16416 | tf_op jit(solution)/shard_map/all_to_all | solution.py:155
  65.8 7.1 %fusion.6 = f32[3,3,3,128,128]{3,4,2,1,0:T(8,128)S(1)} fusion(bf16[1,4,18,34,128]{4,3,2,1,0:T(8,128)(2,1)S(1)} %copy-done.10, bf16[2,16,32,1,128]{4,2,0,1,3:T(8,128)(2,1)S(1)} %slice_bitcast_fusion.3), kind=kOutput, calls=%fused_computation.11 | convolution fusion | flops 905969664 | bytes 2658304 | tf_op jit(solution)/shard_map/transpose | solution.py:40
  73.0 8.3 %bitcast_select_fusion.1 = (f32[3,3,3,128,128]{4,3,2,1,0:T(8,128)S(1)}, bf16[3,3,3,128,128]{4,3,2,1,0:T(8,128)(2,1)S(1)}) fusion(f32[3,3,3,128,128]{3,4,2,1,0:T(8,128)S(1)} %fusion.6, pred[]{:T(512)S(6)} %eq.111, bf16[2,16,32,1,128]{4,2,0,1,3:T(8,128)(2,1)S(1)} %slice_bitcast_fusion.4, bf16[1,4,18,34,128]{4,3,1,2,0:T(8,128)(2,1)S(1)} %copy-done.9), kind=kOutput, calls=%fused_computation.9 | convolution fusion | flops 906854400 | bytes 5312513 | tf_op jit(solution)/shard_map/transpose | solution.py:40
  81.7 2.3 %collective-permute-done.6 = bf16[3456,128]{1,0:T(8,128)(2,1)S(1)} collective-permute-done((bf16[3456,128]{1,0:T(8,128)(2,1)S(1)}, bf16[3456,128]{1,0:T(8,128)(2,1)S(1)}, u32[]{:S(2)}, u32[]{:S(2)}) %collective-permute-start.6) | collective-permute-done | bytes 884768 | tf_op jit(solution)/shard_map/ppermute | solution.py:84
  84.2 15.6 %all_to_all.40 = bf16[4,864,128]{2,1,0:T(8,128)(2,1)S(1)} all-to-all(bf16[4,864,128]{2,1,0:T(8,128)(2,1)S(1)} %bitcast.179), channel_id=1, replica_groups=mesh['tm'=4,'row'=2,'col'=4] {'col'}, dimensions={0} | all-to-all | bytes 1769472 | tf_op jit(solution)/shard_map/all_to_all | solution.py:175
  100.6 4.0 %all-to-all-start.5 = ((bf16[4,216,128]{2,1,0:T(8,128)(2,1)}), bf16[4,216,128]{2,1,0:T(8,128)(2,1)S(1)}, u32[]{:S(2)}, u32[]{:S(2)}) async-start(bf16[4,216,128]{2,1,0:T(8,128)(2,1)} %bitcast.74), calls=%async_computation.5 | async-start | bytes 442368 | tf_op jit(solution)/shard_map/all_to_all | solution.py:175
  105.9 7.2 %all-to-all-done.5 = bf16[4,216,128]{2,1,0:T(8,128)(2,1)S(1)} async-done(((bf16[4,216,128]{2,1,0:T(8,128)(2,1)}), bf16[4,216,128]{2,1,0:T(8,128)(2,1)S(1)}, u32[]{:S(2)}, u32[]{:S(2)}) %all-to-all-start.5) | async-done | bytes 221216 | tf_op jit(solution)/shard_map/all_to_all | solution.py:175
  113.9 3.4 %all-to-all-start.6 = ((bf16[4,216,128]{2,1,0:T(8,128)(2,1)}), bf16[4,216,128]{2,1,0:T(8,128)(2,1)S(1)}, u32[]{:S(2)}, u32[]{:S(2)}) async-start(bf16[4,216,128]{2,1,0:T(8,128)(2,1)} %broadcast_in_dim.191), calls=%async_computation.6 | async-start | bytes 442368 | tf_op jit(solution)/shard_map/all_to_all | solution.py:181
  117.3 3.9 %collective-permute-start.3 = (bf16[2,18,34,128]{3,2,0,1:T(8,128)(2,1)S(1)}, bf16[2,18,34,128]{3,2,0,1:T(8,128)(2,1)S(1)}, u32[]{:S(2)}, u32[]{:S(2)}) collective-permute-start(bf16[2,18,34,128]{3,2,0,1:T(8,128)(2,1)S(1)} %copy-done.6), channel_id=1, source_target_pairs={{0,8},{8,16},{16,24},{1,9},{9,17},{17,25},{2,10},{10,18},{18,26},{... | collective-permute-start | bytes 940040 | tf_op jit(solution)/shard_map/ppermute | solution.py:162
  125.1 3.5 %all-to-all-start.7 = ((bf16[4,864,128]{2,1,0:T(8,128)(2,1)}), bf16[4,864,128]{2,1,0:T(8,128)(2,1)S(1)}, u32[]{:S(2)}, u32[]{:S(2)}) async-start(bf16[4,864,128]{2,1,0:T(8,128)(2,1)} %broadcast_in_dim.193), calls=%async_computation.7 | async-start | bytes 1769472 | tf_op jit(solution)/shard_map/all_to_all | solution.py:181
  128.6 3.8 %convolution_select_fusion.1 = f32[2,16,8,5,128]{4,2,3,1,0:T(8,128)S(1)} fusion(bf16[3,3,3,128,128]{4,3,2,1,0:T(8,128)(2,1)} %param.5, bf16[4,18,1,7,2,128]{5,3,4,1,0,2:T(8,128)(2,1)} %slice.278, bf16[4,18,1,8,5,128]{5,3,4,1,0,2:T(8,128)(2,1)S(1)} %copy.280, pred[8,5]{0,1:T(8,128)(4,1)S(1)} %copy-done.17), kind=kOutput, calls=%fused_computation.16 | convolution fusion | flops 1135722496 | bytes 2535464 | tf_op jit(solution)/shard_map/conv_general_dilated | solution.py:17
  134.4 4.3 %all-to-all-done.7 = bf16[4,864,128]{2,1,0:T(8,128)(2,1)S(1)} async-done(((bf16[4,864,128]{2,1,0:T(8,128)(2,1)}), bf16[4,864,128]{2,1,0:T(8,128)(2,1)S(1)}, u32[]{:S(2)}, u32[]{:S(2)}) %all-to-all-start.7) | async-done | bytes 884768 | tf_op jit(solution)/shard_map/all_to_all | solution.py:181
  139.3 4.0 %all-to-all-start.3 = ((f32[8,2,2,128]{3,2,1,0:T(2,128)}), f32[8,2,2,128]{3,2,1,0:T(2,128)}, u32[]{:S(2)}, u32[]{:S(2)}) async-start(f32[8,2,2,128]{3,2,1,0:T(2,128)} %broadcast_in_dim.187), calls=%async_computation.3 | async-start | bytes 32768 | tf_op jit(solution)/shard_map/all_to_all | solution.py:155
  143.7 3.4 %convolution_select_fusion.2 = f32[2,16,8,5,128]{4,2,3,1,0:T(8,128)S(1)} fusion(bf16[3,3,3,128,128]{4,3,2,1,0:T(8,128)(2,1)S(1)} %copy-done, bf16[4,18,1,7,2,128]{5,3,4,1,0,2:T(8,128)(2,1)} %slice.267, bf16[4,18,1,8,5,128]{5,3,4,1,0,2:T(8,128)(2,1)S(1)} %copy.269, pred[8,5]{0,1:T(8,128)(4,1)} %constant.122), kind=kOutput, calls=%fused_computation.17 | convolution fusion | flops 1135722496 | bytes 2535464 | tf_op jit(solution)/shard_map/conv_general_dilated | solution.py:17
  152.2 2.5 %broadcast_select_fusion = (bf16[3456,128]{1,0:T(8,128)(2,1)}, bf16[3456,128]{1,0:T(8,128)(2,1)}) fusion(bf16[3456,128]{1,0:T(8,128)(2,1)} %collective-permute-done.7, pred[]{:T(512)S(6)} %eq.111, bf16[4,864,128]{2,1,0:T(8,128)(2,1)S(1)} %all-to-all-done.7), kind=kLoop, calls=%fused_computation.54 | loop fusion | flops 884736 | bytes 3538945 | tf_op jit(solution)/shard_map/jit(_where)/select_n | solution.py:200
  (196 shorter events, 35.3 us)
Async XLA Ops:
  0.6 49.8 %copy-start = (bf16[3,3,3,128,128]{4,3,2,1,0:T(8,128)(2,1)S(1)}, bf16[3,3,3,128,128]{4,3,2,1,0:T(8,128)(2,1)}, u32[]{:S(2)}) copy-start(bf16[3,3,3,128,128]{4,3,2,1,0:T(8,128)(2,1)} %param.6) | copy-start | bytes 2654212
  0.7 17.9 %copy-start.1 = (bf16[2,16,32,128]{3,2,1,0:T(8,128)(2,1)S(1)}, bf16[2,16,32,128]{3,2,1,0:T(8,128)(2,1)}, u32[]{:S(2)}) copy-start(bf16[2,16,32,128]{3,2,1,0:T(8,128)(2,1)} %param.4) | copy-start | bytes 786436
  4.5 1.4 collective-permute-start
  7.8 10.1 %all-to-all-start = ((bf16[4,128,128]{2,1,0:T(8,128)(2,1)}), bf16[4,128,128]{2,1,0:T(8,128)(2,1)S(1)}, u32[]{:S(2)}, u32[]{:S(2)}) async-start(bf16[4,128,128]{2,1,0:T(8,128)(2,1)} %pad_maximum_fusion.3), calls=%async_computation | async-start | bytes 262144 | tf_op jit(solution)/shard_map/all_to_all | solution.py:125
  12.9 51.1 %copy-start.19 = (s32[128]{0:T(128)}, s32[128]{0:T(128)S(1)}, u32[]{:S(2)}) copy-start(s32[128]{0:T(128)S(1)} %and_select_fusion) | copy-start | bytes 1540
  18.2 15.9 %copy-start.11 = (f32[2,128]{1,0:T(2,128)}, f32[2,128]{1,0:T(2,128)S(1)}, u32[]{:S(2)}) copy-start(f32[2,128]{1,0:T(2,128)S(1)} %convolution_multiply_fusion.5) | copy-start | bytes 3076
  18.4 11.8 %copy-start.13 = (f32[2,128]{1,0:T(2,128)}, f32[2,128]{1,0:T(2,128)S(1)}, u32[]{:S(2)}) copy-start(f32[2,128]{1,0:T(2,128)S(1)} %fusion.18) | copy-start | bytes 3076
  19.0 10.2 %collective-permute-start.1 = (bf16[2,18,34,128]{3,2,0,1:T(8,128)(2,1)S(1)}, bf16[2,18,34,128]{3,2,0,1:T(8,128)(2,1)S(1)}, u32[]{:S(2)}, u32[]{:S(2)}) collective-permute-start(bf16[2,18,34,128]{3,2,0,1:T(8,128)(2,1)S(1)} %select_convert_fusion.2), channel_id=1, source_target_pairs={{0,8},{8,16},{16,24},{1,9},{9,17},{17,25},{2,10},{10,18},{18,26},{... | collective-permute-start | bytes 940040 | tf_op jit(solution)/shard_map/ppermute | solution.py:162
  34.5 1.6 %collective-permute-start.2 = (bf16[76,128]{1,0:T(8,128)(2,1)S(1)}, bf16[76,128]{1,0:T(8,128)(2,1)S(1)}, u32[]{:S(2)}, u32[]{:S(2)}) collective-permute-start(bf16[76,128]{1,0:T(8,128)(2,1)S(1)} %pad_maximum_fusion.11), channel_id=1, source_target_pairs={{0,4},{4,0},{1,5},{5,1},{2,6},{6,2},{3,7},{7,3},{8,12},{12,8},{9,1... | collective-permute-start | bytes 58376 | tf_op jit(solution)/shard_map/ppermute | solution.py:84
  34.8 14.5 %collective-permute-start.4 = (bf16[2,20,36,128]{3,2,1,0:T(8,128)(2,1)S(1)}, bf16[2,20,36,128]{3,2,1,0:T(8,128)(2,1)S(1)}, u32[]{:S(2)}, u32[]{:S(2)}) collective-permute-start(bf16[2,20,36,128]{3,2,1,0:T(8,128)(2,1)S(1)} %pad_maximum_fusion.2), channel_id=1, source_target_pairs={{8,0},{16,8},{24,16},{9,1},{17,9},{25,17},{10,2},{18,10},{26,18},{... | collective-permute-start | bytes 1105928 | tf_op jit(solution)/shard_map/ppermute | solution.py:162
  37.0 17.1 %all-to-all-start.1 = ((bf16[4,48,128]{2,1,0:T(8,128)(2,1)}), bf16[4,48,128]{2,1,0:T(8,128)(2,1)S(1)}, u32[]{:S(2)}, u32[]{:S(2)}) async-start(bf16[4,48,128]{2,1,0:T(8,128)(2,1)} %pad_maximum_fusion.5), calls=%async_computation.1 | async-start | bytes 98304 | tf_op jit(solution)/shard_map/all_to_all | solution.py:125
  56.0 8.0 %all-to-all-start.2 = ((f32[8,2,2,128]{3,2,1,0:T(2,128)}), f32[8,2,2,128]{3,2,1,0:T(2,128)S(1)}, u32[]{:S(2)}, u32[]{:S(2)}) async-start(f32[8,2,2,128]{3,2,1,0:T(2,128)} %broadcast_in_dim.185), calls=%async_computation.2 | async-start | bytes 32768 | tf_op jit(solution)/shard_map/all_to_all | solution.py:155
  65.8 7.1 %copy-start.9 = (bf16[1,4,18,34,128]{4,3,1,2,0:T(8,128)(2,1)S(1)}, bf16[1,4,18,34,128]{4,3,1,2,0:T(8,128)(2,1)}, u32[]{:S(2)}) copy-start(bf16[1,4,18,34,128]{4,3,1,2,0:T(8,128)(2,1)} %get-tuple-element.39) | copy-start | bytes 1880068
  81.5 2.5 %collective-permute-start.6 = (bf16[3456,128]{1,0:T(8,128)(2,1)S(1)}, bf16[3456,128]{1,0:T(8,128)(2,1)S(1)}, u32[]{:S(2)}, u32[]{:S(2)}) collective-permute-start(bf16[3456,128]{1,0:T(8,128)(2,1)S(1)} %bitcast.191), channel_id=1, source_target_pairs={{0,4},{4,0},{1,5},{5,1},{2,6},{6,2},{3,7},{7,3},{8,12},{12,8},{9,1... | collective-permute-start | bytes 2654216 | tf_op jit(solution)/shard_map/ppermute | solution.py:84
  84.2 20.5 %copy-start.8 = (bf16[2,18,34,128]{3,2,0,1:T(8,128)(2,1)S(1)}, bf16[2,18,34,128]{3,2,0,1:T(8,128)(2,1)}, u32[]{:S(2)}) copy-start(bf16[2,18,34,128]{3,2,0,1:T(8,128)(2,1)} %copy-done.7) | copy-start | bytes 940036
  99.8 17.5 %copy-start.6 = (bf16[2,18,34,128]{3,2,0,1:T(8,128)(2,1)S(1)}, bf16[2,18,34,128]{3,2,0,1:T(8,128)(2,1)}, u32[]{:S(2)}) copy-start(bf16[2,18,34,128]{3,2,0,1:T(8,128)(2,1)} %copy-done.5) | copy-start | bytes 940036
  100.6 12.5 %all-to-all-start.5 = ((bf16[4,216,128]{2,1,0:T(8,128)(2,1)}), bf16[4,216,128]{2,1,0:T(8,128)(2,1)S(1)}, u32[]{:S(2)}, u32[]{:S(2)}) async-start(bf16[4,216,128]{2,1,0:T(8,128)(2,1)} %bitcast.74), calls=%async_computation.5 | async-start | bytes 442368 | tf_op jit(solution)/shard_map/all_to_all | solution.py:175
  104.6 16.5 %collective-permute-start.5 = (bf16[2,18,34,128]{3,2,0,1:T(8,128)(2,1)S(1)}, bf16[2,18,34,128]{3,2,0,1:T(8,128)(2,1)S(1)}, u32[]{:S(2)}, u32[]{:S(2)}) collective-permute-start(bf16[2,18,34,128]{3,2,0,1:T(8,128)(2,1)S(1)} %copy-done.8), channel_id=1, source_target_pairs={{8,0},{16,8},{24,16},{9,1},{17,9},{25,17},{10,2},{18,10},{26,18},{... | collective-permute-start | bytes 940040 | tf_op jit(solution)/shard_map/ppermute | solution.py:162
  113.9 10.2 %all-to-all-start.6 = ((bf16[4,216,128]{2,1,0:T(8,128)(2,1)}), bf16[4,216,128]{2,1,0:T(8,128)(2,1)S(1)}, u32[]{:S(2)}, u32[]{:S(2)}) async-start(bf16[4,216,128]{2,1,0:T(8,128)(2,1)} %broadcast_in_dim.191), calls=%async_computation.6 | async-start | bytes 442368 | tf_op jit(solution)/shard_map/all_to_all | solution.py:181
  117.3 15.3 %collective-permute-start.3 = (bf16[2,18,34,128]{3,2,0,1:T(8,128)(2,1)S(1)}, bf16[2,18,34,128]{3,2,0,1:T(8,128)(2,1)S(1)}, u32[]{:S(2)}, u32[]{:S(2)}) collective-permute-start(bf16[2,18,34,128]{3,2,0,1:T(8,128)(2,1)S(1)} %copy-done.6), channel_id=1, source_target_pairs={{0,8},{8,16},{16,24},{1,9},{9,17},{17,25},{2,10},{10,18},{18,26},{... | collective-permute-start | bytes 940040 | tf_op jit(solution)/shard_map/ppermute | solution.py:162
  121.9 6.7 %copy-start.17 = (pred[8,5]{0,1:T(8,128)(4,1)S(1)}, pred[8,5]{0,1:T(8,128)(4,1)}, u32[]{:S(2)}) copy-start(pred[8,5]{0,1:T(8,128)(4,1)} %constant.122) | copy-start | bytes 124
  125.1 13.6 %all-to-all-start.7 = ((bf16[4,864,128]{2,1,0:T(8,128)(2,1)}), bf16[4,864,128]{2,1,0:T(8,128)(2,1)S(1)}, u32[]{:S(2)}, u32[]{:S(2)}) async-start(bf16[4,864,128]{2,1,0:T(8,128)(2,1)} %broadcast_in_dim.193), calls=%async_computation.7 | async-start | bytes 1769472 | tf_op jit(solution)/shard_map/all_to_all | solution.py:181
  139.3 8.7 %all-to-all-start.3 = ((f32[8,2,2,128]{3,2,1,0:T(2,128)}), f32[8,2,2,128]{3,2,1,0:T(2,128)}, u32[]{:S(2)}, u32[]{:S(2)}) async-start(f32[8,2,2,128]{3,2,1,0:T(2,128)} %broadcast_in_dim.187), calls=%async_computation.3 | async-start | bytes 32768 | tf_op jit(solution)/shard_map/all_to_all | solution.py:155
  143.3 8.9 %collective-permute-start.7 = (bf16[3456,128]{1,0:T(8,128)(2,1)S(1)}, bf16[3456,128]{1,0:T(8,128)(2,1)}, u32[]{:S(2)}, u32[]{:S(2)}) collective-permute-start(bf16[3456,128]{1,0:T(8,128)(2,1)S(1)} %bitcast.180), channel_id=1, source_target_pairs={{0,4},{4,0},{1,5},{5,1},{2,6},{6,2},{3,7},{7,3},{8,12},{12,8},{9,1... | collective-permute-start | bytes 2654216 | tf_op jit(solution)/shard_map/ppermute | solution.py:84
  (11 other events, 26.1 us)

commit v2 on v1

--- a/solution.py
+++ b/solution.py
@@ -167,24 +167,29 @@
     return act_grad * sigmoid_z * (1.0 + normed * (1.0 - sigmoid_z))
 
 
+def tiled(count, peers):
+    return -(-count // (16 * peers)) * 16
+
+
 def scatter_sum(values, axis):
     peers = lax.axis_size(axis)
-    share = -(-values.shape[0] // peers)
+    share = tiled(values.shape[0], peers)
     values = jnp.pad(values, ((0, share * peers - values.shape[0]), (0, 0)))
     slots = values.reshape(peers, share, values.shape[1]).astype(jnp.bfloat16)
     return lax.all_to_all(slots, axis, 0, 0).astype(jnp.float32).sum(0)
 
 
-def gather_shares(share, axis, rows):
+def gather_shares(share, axis):
     peers = lax.axis_size(axis)
     slots = jnp.broadcast_to(share[None], (peers,) + share.shape)
-    return lax.all_to_all(slots, axis, 0, 0).reshape(-1, share.shape[1])[:rows]
-
-
-def summed_kernels(first_term, second_term, factor):
+    return lax.all_to_all(slots, axis, 0, 0)
+
+
+def summed_kernels(first_term, second_term, sums, factor):
     shape = first_term.shape
     chans = shape[-1]
     first_term, second_term = first_term.reshape(-1, chans), second_term.reshape(-1, chans)
+    rows = first_term.shape[0]
     upper = lax.axis_index("row") == 0
     keep = jnp.where(upper, first_term, second_term)
     give = jnp.where(upper, second_term, first_term).astype(jnp.bfloat16)
@@ -192,12 +197,20 @@
     by_col = scatter_sum(keep, "col")
     by_tm = scatter_sum(by_col, "tm")
     done = (by_tm * factor).astype(jnp.bfloat16)
-    done = gather_shares(done, "tm", by_col.shape[0])
-    done = gather_shares(done, "col", keep.shape[0])
+    done = gather_shares(done, "tm").reshape(-1, chans)[: by_col.shape[0]]
+    parts = split3(sums + row_swap(sums)).reshape(-1, chans)
+    spare = -parts.shape[0] % 16
+    done = jnp.concatenate([done, jnp.pad(parts, ((0, spare), (0, 0)))], 0)
+    done = gather_shares(done, "col")
+    terms = done[:, by_col.shape[0] : done.shape[1] - spare].astype(jnp.float32)
+    total = terms.sum(0).reshape((3,) + sums.shape)
+    total = total[0] + (total[1] + total[2])
+    done = done[:, : by_col.shape[0]].reshape(-1, chans)[:rows]
     other = row_swap(done)
     return (
         jnp.where(upper, done, other).reshape(shape),
         jnp.where(upper, other, done).reshape(shape),
+        total,
     )
 
 
@@ -206,6 +219,7 @@
     cells = high * wide
     every = cells * frames * lax.axis_size("tm") * lax.axis_size("row") * lax.axis_size("col")
     factor = 1.0 / math.sqrt(every)
+    peers = lax.axis_size("row") * lax.axis_size("col")
 
     stats = local_stats(features.astype(jnp.float32))
     (wide_features, wide_grad), mean_first, std_first = exchange(
@@ -219,6 +233,7 @@
     grad_window = jnp.concatenate([wide_grad, later(wide_grad[:2], -1)], 0)
 
     hidden = conv_valid(pad_first, conv_first).astype(jnp.bfloat16)
+    hidden, grad_window = lax.optimization_barrier((hidden, grad_window))
     grad_act2 = conv_valid(grad_window, flipped(conv_second))
     stats = local_stats(hidden.astype(jnp.float32))
     (wide_hidden,), mean_second, std_second = exchange([hidden], [1], stats, cells)
@@ -233,11 +248,13 @@
     hidden_grad = std_second * (q - means[0] - normed * means[1])
     hidden_grad = jnp.where(rim_ok, hidden_grad, 0.0).astype(jnp.bfloat16)
 
+    pad_second = jnp.concatenate([later(act_second[-2:], 1), act_second], 0)
+    hidden_grad, pad_second = lax.optimization_barrier((hidden_grad, pad_second))
     hidden_window = jnp.concatenate([hidden_grad, later(hidden_grad[:2], -1)], 0)
-    pad_second = jnp.concatenate([later(act_second[-2:], 1), act_second], 0)
     first_term = weight_grad(pad_first, hidden_grad[core])
     second_term = jnp.flip(weight_grad(grad_window[core], act_second[core]), (0, 1, 2))
     second_term = jnp.swapaxes(second_term, 3, 4)
+    first_term, hidden_window = lax.optimization_barrier((first_term, hidden_window))
 
     branch = conv_valid(pad_second, conv_second)
     result = (features.astype(jnp.float32) + branch).astype(jnp.bfloat16)
@@ -245,12 +262,12 @@
     grad_act1 = conv_valid(hidden_window, flipped(conv_first))
     normed = (features.astype(jnp.float32) - mean_first) * std_first
     q = back_sums(grad_act1, normed)
-    means = frame_means(jnp.stack([q.sum((1, 2)), (q * normed).sum((1, 2))]), cells)
+    sums = jnp.stack([q.sum((1, 2)), (q * normed).sum((1, 2))])
+    first_grad, second_grad, total = summed_kernels(first_term, second_term, sums, factor)
+    means = group_total(total) / (cells * peers * (sums.shape[-1] // GROUPS))
     means = means[:, :, None, None, :]
     feature_grad = std_first * (q - means[0] - normed * means[1])
     feature_grad = (out_grad.astype(jnp.float32) + feature_grad).astype(jnp.bfloat16)
-
-    first_grad, second_grad = summed_kernels(first_term, second_term, factor)
     return (result, feature_grad, first_grad, second_grad)
 
 

time: 156 us -> 161 us (1.032)
  blocking collectives: 15.6 us -> 0 us
  waiting for transfers between devices: 40.7 us -> 48.9 us
  other arithmetic: 16.2 us -> 22.6 us
  local copies, waits for them, and re-layouts: 13 us -> 19 us
    all_to_all x1 -> x0, blocking collectives: 15.6 us -> none  [scatter_sum(): return lax.all_to_all(slots, axis, 0, 0).astype(jnp.float32).sum(0)]
    all_to_all x1 -> x2, waiting for transfers between devices: 7.16 us -> 14.4 us  [scatter_sum(): return lax.all_to_all(slots, axis, 0, 0).astype(jnp.float32).sum(0)]
    ppermute x4, waiting for transfers between devices: 15.6 us -> 9.77 us  [later(): return lax.ppermute(values, 'tm', pairs)]
    all_to_all x2, waiting for transfers between devices: 5.7 us -> 11.2 us  [gather_shares(): return lax.all_to_all(slots, axis, 0, 0)]
    all_to_all x2 -> x1, starting transfers between devices: 7.47 us -> 3.58 us  [frame_means(): total = lax.all_to_all(slots, ('row', 'col'), 0, 0).sum(0)]
    all_to_all x1 -> x2, starting transfers between devices: 4.01 us -> 7.52 us  [scatter_sum(): return lax.all_to_all(slots, axis, 0, 0).astype(jnp.float32).sum(0)]
    reshape x4, local copies, waits for them, and re-layouts: 0.03 us -> 2.64 us  [rows_of(): return jnp.concatenate([p.reshape(-1, p.shape[-1]) for p in pieces], 0)]
    concatenate x0 -> x3, other arithmetic: none -> 2.14 us  [the longest x1 1.18 us: on_device(): jnp.concatenate([hidden_grad, later(hidden_grad[:2], -1)], 0)]
  transfers between devices with their start and end apart: 15 -> 16, of which waited for: 10 -> 14; matrix products, arithmetic and copies ran while one was open for 15% -> 24% of each run, Pallas kernels for 0% -> 0%
where the time goes in v2:
time: 161 us; the launch traced here: 159 us
  waiting for transfers between devices  48.9 us (30%)
  starting transfers between devices  37.5 us (23%)
  matrix products  29.4 us (18%)
  other arithmetic  22.6 us (14%)
  local copies, waits for them, and re-layouts  19 us (12%)
  between operations  1.63 us (1%)
    transpose x2, matrix products, weight_grad(): return jnp.transpose(summed, (1, 2, 3, 4, 0))  15.8 us
    all_to_all x2, waiting for transfers between devices, scatter_sum(): return lax.all_to_all(slots, axis, 0, 0).astype(jnp.float32).sum(0)  14.4 us
    conv_general_dilated x4, matrix products, conv_valid(): lax.conv_general_dilated(window[None], kernel, (1, 1, 1), 'VALID', dimens...  12.4 us
    all_to_all x2, waiting for transfers between devices, gather_shares(): return lax.all_to_all(slots, axis, 0, 0)  11.2 us
    ppermute x4, starting transfers between devices, later(): return lax.ppermute(values, 'tm', pairs)  9.79 us
    ppermute x4, waiting for transfers between devices, later(): return lax.ppermute(values, 'tm', pairs)  9.77 us
    all_to_all x2, starting transfers between devices, exchange(): got = lax.all_to_all(slots, 'col', 0, 0)  8.95 us
    all_to_all x2, starting transfers between devices, scatter_sum(): return lax.all_to_all(slots, axis, 0, 0).astype(jnp.float32).sum(0)  7.52 us
  transfers between devices with their start and end apart: 16, of which 14 were waited for; matrix products, arithmetic and copies ran while one was open for 24% of the time, Pallas kernels for 0%

profile of v2, /device:TPU:0, one launch (start us, length us, event | category | flops | bytes accessed | tf_op | source)
XLA Modules:
  0.0 159.1 jit_solution(10225143390561364307)
XLA Ops:
  8.7 5.1 %all-to-all-start = ((bf16[4,128,128]{2,1,0:T(8,128)(2,1)}), bf16[4,128,128]{2,1,0:T(8,128)(2,1)S(1)}, u32[]{:S(2)}, u32[]{:S(2)}) async-start(bf16[4,128,128]{2,1,0:T(8,128)(2,1)} %pad_maximum_fusion.5), calls=%async_computation | async-start | bytes 262144 | tf_op jit(solution)/shard_map/all_to_all | solution.py:125
  13.8 5.0 %all-to-all-done = bf16[4,128,128]{2,1,0:T(8,128)(2,1)S(1)} async-done(((bf16[4,128,128]{2,1,0:T(8,128)(2,1)}), bf16[4,128,128]{2,1,0:T(8,128)(2,1)S(1)}, u32[]{:S(2)}, u32[]{:S(2)}) %all-to-all-start) | async-done | bytes 131104 | tf_op jit(solution)/shard_map/all_to_all | solution.py:125
  19.9 3.5 %collective-permute-start.1 = (bf16[2,18,34,128]{3,2,0,1:T(8,128)(2,1)S(1)}, bf16[2,18,34,128]{3,2,0,1:T(8,128)(2,1)S(1)}, u32[]{:S(2)}, u32[]{:S(2)}) collective-permute-start(bf16[2,18,34,128]{3,2,0,1:T(8,128)(2,1)S(1)} %select_convert_fusion.2), channel_id=1, source_target_pairs={{0,8},{8,16},{16,24},{1,9},{9,17},{17,25},{2,10},{10,18},{18,26},{... | collective-permute-start | bytes 940040 | tf_op jit(solution)/shard_map/ppermute | solution.py:162
  25.0 5.1 %collective-permute-done.1 = bf16[2,18,34,128]{3,2,0,1:T(8,128)(2,1)S(1)} collective-permute-done((bf16[2,18,34,128]{3,2,0,1:T(8,128)(2,1)S(1)}, bf16[2,18,34,128]{3,2,0,1:T(8,128)(2,1)S(1)}, u32[]{:S(2)}, u32[]{:S(2)}) %collective-permute-start.1) | collective-permute-done | bytes 313376 | tf_op jit(solution)/shard_map/ppermute | solution.py:162
  31.6 2.4 %fusion.10 = bf16[2,16,8,5,128]{4,2,3,1,0:T(8,128)(2,1)S(1)} fusion(bf16[3,3,3,128,128]{4,3,2,1,0:T(8,128)(2,1)S(1)} %copy-done.18, bf16[4,18,1,7,2,128]{5,3,4,1,0,2:T(8,128)(2,1)S(1)} %slice.281, bf16[4,18,1,8,5,128]{5,3,4,1,0,2:T(8,128)(2,1)S(1)} %copy.221, pred[8,5]{0,1:T(8,128)(4,1)S(1)} %copy-done.19), kind=kOutput, calls=%fused_computation.19 | convolution fusion | flops 1135886336 | bytes 2207784 | tf_op jit(solution)/shard_map/conv_general_dilated | solution.py:17
  46.9 3.9 %all-to-all-start.1 = ((bf16[4,48,128]{2,1,0:T(8,128)(2,1)}), bf16[4,48,128]{2,1,0:T(8,128)(2,1)}, u32[]{:S(2)}, u32[]{:S(2)}) async-start(bf16[4,48,128]{2,1,0:T(8,128)(2,1)} %pad_maximum_fusion.7), calls=%async_computation.1 | async-start | bytes 98304 | tf_op jit(solution)/shard_map/all_to_all | solution.py:125
  50.8 3.8 %convolution_select_fusion = f32[2,18,8,5,128]{4,2,3,1,0:T(8,128)S(1)} fusion(bf16[3,3,3,128,128]{4,3,2,1,0:T(8,128)(2,1)S(1)} %copy-done, bf16[4,20,1,7,2,128]{5,3,4,1,0,2:T(8,128)(2,1)} %slice.294, bf16[4,20,1,8,5,128]{5,3,4,1,0,2:T(8,128)(2,1)S(1)} %copy.229, pred[8,5]{0,1:T(8,128)(4,1)} %constant.130), kind=kOutput, calls=%fused_computation.15 | convolution fusion | flops 1277644800 | bytes 2727976 | tf_op jit(solution)/shard_map/conv_general_dilated | solution.py:17
  58.9 3.6 %all-to-all-start.2 = ((f32[8,2,2,128]{3,2,1,0:T(2,128)}), f32[8,2,2,128]{3,2,1,0:T(2,128)S(1)}, u32[]{:S(2)}, u32[]{:S(2)}) async-start(f32[8,2,2,128]{3,2,1,0:T(2,128)} %broadcast_in_dim.177), calls=%async_computation.2 | async-start | bytes 32768 | tf_op jit(solution)/shard_map/all_to_all | solution.py:155
  63.6 3.6 %all-to-all-done.2 = f32[8,2,2,128]{3,2,1,0:T(2,128)S(1)} async-done(((f32[8,2,2,128]{3,2,1,0:T(2,128)}), f32[8,2,2,128]{3,2,1,0:T(2,128)S(1)}, u32[]{:S(2)}, u32[]{:S(2)}) %all-to-all-start.2) | async-done | bytes 16416 | tf_op jit(solution)/shard_map/all_to_all | solution.py:155
  68.9 3.5 %collective-permute-start.4 = (bf16[2,18,34,128]{3,2,0,1:T(8,128)(2,1)S(1)}, bf16[2,18,34,128]{3,2,0,1:T(8,128)(2,1)S(1)}, u32[]{:S(2)}, u32[]{:S(2)}) collective-permute-start(bf16[2,18,34,128]{3,2,0,1:T(8,128)(2,1)S(1)} %get-tuple-element.49), channel_id=1, source_target_pairs={{0,8},{8,16},{16,24},{1,9},{9,17},{17,25},{2,10},{10,18},{18,26},{... | collective-permute-start | bytes 940040 | tf_op jit(solution)/shard_map/ppermute | solution.py:162
  72.4 8.2 %fusion.6 = f32[3,3,3,128,128]{3,4,2,1,0:T(8,128)} fusion(bf16[1,4,18,34,128]{4,3,2,1,0:T(8,128)(2,1)S(1)} %copy-done.8, bf16[2,16,32,1,128]{4,2,0,1,3:T(8,128)(2,1)S(1)} %slice_bitcast_fusion.3), kind=kOutput, calls=%fused_computation.11 | convolution fusion | flops 905969664 | bytes 2658304 | tf_op jit(solution)/shard_map/transpose | solution.py:40
  84.1 7.6 %fusion.8 = f32[3,3,3,128,128]{4,3,2,1,0:T(8,128)S(1)} fusion(bf16[1,4,18,34,128]{4,3,1,2,0:T(8,128)(2,1)S(1)} %get-tuple-element.47, bf16[2,16,32,1,128]{4,2,0,1,3:T(8,128)(2,1)S(1)} %slice_bitcast_fusion.4), kind=kOutput, calls=%fused_computation.13 | convolution fusion | flops 905969664 | bytes 2658304 | tf_op jit(solution)/shard_map/transpose | solution.py:40
  91.8 3.5 %collective-permute-done.5 = bf16[2,18,34,128]{3,2,0,1:T(8,128)(2,1)} collective-permute-done((bf16[2,18,34,128]{3,2,0,1:T(8,128)(2,1)}, bf16[2,18,34,128]{3,2,0,1:T(8,128)(2,1)}, u32[]{:S(2)}, u32[]{:S(2)}) %collective-permute-start.5) | collective-permute-done | bytes 313376 | tf_op jit(solution)/shard_map/ppermute | solution.py:162
  98.7 2.1 %collective-permute-done.6 = bf16[3456,128]{1,0:T(8,128)(2,1)S(1)} collective-permute-done((bf16[3456,128]{1,0:T(8,128)(2,1)S(1)}, bf16[3456,128]{1,0:T(8,128)(2,1)S(1)}, u32[]{:S(2)}, u32[]{:S(2)}) %collective-permute-start.6) | collective-permute-done | bytes 884768 | tf_op jit(solution)/shard_map/ppermute | solution.py:84
  101.9 3.5 %all-to-all-start.3 = ((bf16[4,864,128]{2,1,0:T(8,128)(2,1)}), bf16[4,864,128]{2,1,0:T(8,128)(2,1)S(1)}, u32[]{:S(2)}, u32[]{:S(2)}) async-start(bf16[4,864,128]{2,1,0:T(8,128)(2,1)} %bitcast.69), calls=%async_computation.3 | async-start | bytes 1769472 | tf_op jit(solution)/shard_map/all_to_all | solution.py:179
  106.1 11.7 %all-to-all-done.3 = bf16[4,864,128]{2,1,0:T(8,128)(2,1)S(1)} async-done(((bf16[4,864,128]{2,1,0:T(8,128)(2,1)}), bf16[4,864,128]{2,1,0:T(8,128)(2,1)S(1)}, u32[]{:S(2)}, u32[]{:S(2)}) %all-to-all-start.3) | async-done | bytes 884768 | tf_op jit(solution)/shard_map/all_to_all | solution.py:179
  118.7 4.0 %all-to-all-start.4 = ((bf16[4,224,128]{2,1,0:T(8,128)(2,1)}), bf16[4,224,128]{2,1,0:T(8,128)(2,1)S(1)}, u32[]{:S(2)}, u32[]{:S(2)}) async-start(bf16[4,224,128]{2,1,0:T(8,128)(2,1)} %bitcast.70), calls=%async_computation.4 | async-start | bytes 458752 | tf_op jit(solution)/shard_map/all_to_all | solution.py:179
  122.8 3.7 %convolution_select_fusion.1 = f32[2,16,8,5,128]{4,2,3,1,0:T(8,128)S(1)} fusion(bf16[3,3,3,128,128]{4,3,2,1,0:T(8,128)(2,1)} %param.5, bf16[4,18,1,7,2,128]{5,3,4,1,0,2:T(8,128)(2,1)S(1)} %slice.303, bf16[4,18,1,8,5,128]{5,3,4,1,0,2:T(8,128)(2,1)S(1)} %copy.246, pred[8,5]{0,1:T(8,128)(4,1)S(1)} %copy-done.20), kind=kOutput, calls=%fused_computation.16 | convolution fusion | flops 1135722496 | bytes 2535464 | tf_op jit(solution)/shard_map/conv_general_dilated | solution.py:17
  127.8 2.7 %all-to-all-done.4 = bf16[4,224,128]{2,1,0:T(8,128)(2,1)S(1)} async-done(((bf16[4,224,128]{2,1,0:T(8,128)(2,1)}), bf16[4,224,128]{2,1,0:T(8,128)(2,1)S(1)}, u32[]{:S(2)}, u32[]{:S(2)}) %all-to-all-start.4) | async-done | bytes 229408 | tf_op jit(solution)/shard_map/all_to_all | solution.py:179
  131.3 3.4 %all-to-all-start.5 = ((bf16[4,224,128]{2,1,0:T(8,128)(2,1)}), bf16[4,224,128]{2,1,0:T(8,128)(2,1)S(1)}, u32[]{:S(2)}, u32[]{:S(2)}) async-start(bf16[4,224,128]{2,1,0:T(8,128)(2,1)} %broadcast_in_dim.183), calls=%async_computation.5 | async-start | bytes 458752 | tf_op jit(solution)/shard_map/all_to_all | solution.py:185
  136.0 5.2 %all-to-all-done.5 = bf16[4,224,128]{2,1,0:T(8,128)(2,1)S(1)} async-done(((bf16[4,224,128]{2,1,0:T(8,128)(2,1)}), bf16[4,224,128]{2,1,0:T(8,128)(2,1)S(1)}, u32[]{:S(2)}, u32[]{:S(2)}) %all-to-all-start.5) | async-done | bytes 229408 | tf_op jit(solution)/shard_map/all_to_all | solution.py:185
  142.3 3.5 %all-to-all-start.6 = ((bf16[4,880,128]{2,1,0:T(8,128)(2,1)}), bf16[4,880,128]{2,1,0:T(8,128)(2,1)S(1)}, u32[]{:S(2)}, u32[]{:S(2)}) async-start(bf16[4,880,128]{2,1,0:T(8,128)(2,1)} %broadcast_in_dim.184), calls=%async_computation.6 | async-start | bytes 1802240 | tf_op jit(solution)/shard_map/all_to_all | solution.py:185
  146.5 2.5 %convolution_select_fusion.2 = f32[2,16,8,5,128]{4,2,3,1,0:T(8,128)S(1)} fusion(bf16[3,3,3,128,128]{4,3,2,1,0:T(8,128)(2,1)S(1)} %copy-done, bf16[4,18,1,7,2,128]{5,3,4,1,0,2:T(8,128)(2,1)S(1)} %slice.301, bf16[4,18,1,8,5,128]{5,3,4,1,0,2:T(8,128)(2,1)S(1)} %copy.237, pred[8,5]{0,1:T(8,128)(4,1)S(1)} %copy-done.20), kind=kOutput, calls=%fused_computation.17 | convolution fusion | flops 1135722496 | bytes 2535464 | tf_op jit(solution)/shard_map/conv_general_dilated | solution.py:17
  149.1 6.0 %all-to-all-done.6 = bf16[4,880,128]{2,1,0:T(8,128)(2,1)S(1)} async-done(((bf16[4,880,128]{2,1,0:T(8,128)(2,1)}), bf16[4,880,128]{2,1,0:T(8,128)(2,1)S(1)}, u32[]{:S(2)}, u32[]{:S(2)}) %all-to-all-start.6) | async-done | bytes 901152 | tf_op jit(solution)/shard_map/all_to_all | solution.py:185
  (212 shorter events, 50.4 us)
Async XLA Ops:
  0.6 50.2 %copy-start = (bf16[3,3,3,128,128]{4,3,2,1,0:T(8,128)(2,1)S(1)}, bf16[3,3,3,128,128]{4,3,2,1,0:T(8,128)(2,1)}, u32[]{:S(2)}) copy-start(bf16[3,3,3,128,128]{4,3,2,1,0:T(8,128)(2,1)} %param.6) | copy-start | bytes 2654212
  0.6 18.8 %copy-start.1 = (bf16[2,16,32,128]{3,2,1,0:T(8,128)(2,1)S(1)}, bf16[2,16,32,128]{3,2,1,0:T(8,128)(2,1)}, u32[]{:S(2)}) copy-start(bf16[2,16,32,128]{3,2,1,0:T(8,128)(2,1)} %param.4) | copy-start | bytes 786436
  2.9 20.5 %copy-start.4 = (bf16[2,16,32,128]{3,2,1,0:T(8,128)(2,1)S(1)}, bf16[2,16,32,128]{3,2,1,0:T(8,128)(2,1)}, u32[]{:S(2)}) copy-start(bf16[2,16,32,128]{3,2,1,0:T(8,128)(2,1)} %param.7) | copy-start | bytes 786436
  4.5 1.4 collective-permute-start
  5.1 18.5 %copy-start.9 = (pred[18,34]{1,0:T(8,128)(4,1)}, pred[18,34]{1,0:T(8,128)(4,1)S(1)}, u32[]{:S(2)}) copy-start(pred[18,34]{1,0:T(8,128)(4,1)S(1)} %broadcast_and_fusion) | copy-start | bytes 1840
  5.1 18.5 %copy-start.16 = (pred[4]{0:T(512)(128)(4,1)}, pred[4]{0:T(512)(128)(4,1)S(1)}, u32[]{:S(2)}) copy-start(pred[4]{0:T(512)(128)(4,1)S(1)} %get-tuple-element.96) | copy-start | bytes 16
  5.1 18.5 %copy-start.17 = (pred[4]{0:T(512)(128)(4,1)}, pred[4]{0:T(512)(128)(4,1)S(1)}, u32[]{:S(2)}) copy-start(pred[4]{0:T(512)(128)(4,1)S(1)} %get-tuple-element.97) | copy-start | bytes 16
  8.7 10.1 %all-to-all-start = ((bf16[4,128,128]{2,1,0:T(8,128)(2,1)}), bf16[4,128,128]{2,1,0:T(8,128)(2,1)S(1)}, u32[]{:S(2)}, u32[]{:S(2)}) async-start(bf16[4,128,128]{2,1,0:T(8,128)(2,1)} %pad_maximum_fusion.5), calls=%async_computation | async-start | bytes 262144 | tf_op jit(solution)/shard_map/all_to_all | solution.py:125
  13.8 11.2 %copy-start.21 = (s32[128]{0:T(128)}, s32[128]{0:T(128)S(1)}, u32[]{:S(2)}) copy-start(s32[128]{0:T(128)S(1)} %and_select_fusion) | copy-start | bytes 1540
  19.9 10.2 %collective-permute-start.1 = (bf16[2,18,34,128]{3,2,0,1:T(8,128)(2,1)S(1)}, bf16[2,18,34,128]{3,2,0,1:T(8,128)(2,1)S(1)}, u32[]{:S(2)}, u32[]{:S(2)}) collective-permute-start(bf16[2,18,34,128]{3,2,0,1:T(8,128)(2,1)S(1)} %select_convert_fusion.2), channel_id=1, source_target_pairs={{0,8},{8,16},{16,24},{1,9},{9,17},{17,25},{2,10},{10,18},{18,26},{... | collective-permute-start | bytes 940040 | tf_op jit(solution)/shard_map/ppermute | solution.py:162
  23.7 11.7 %collective-permute-start.2 = (bf16[2,20,36,128]{3,2,1,0:T(8,128)(2,1)S(1)}, bf16[2,20,36,128]{3,2,1,0:T(8,128)(2,1)S(1)}, u32[]{:S(2)}, u32[]{:S(2)}) collective-permute-start(bf16[2,20,36,128]{3,2,1,0:T(8,128)(2,1)S(1)} %pad_maximum_fusion.4), channel_id=1, source_target_pairs={{8,0},{16,8},{24,16},{9,1},{17,9},{25,17},{10,2},{18,10},{26,18},{... | collective-permute-start | bytes 1105928 | tf_op jit(solution)/shard_map/ppermute | solution.py:162
  35.9 1.7 %collective-permute-start.3 = (bf16[76,128]{1,0:T(8,128)(2,1)S(1)}, bf16[76,128]{1,0:T(8,128)(2,1)S(1)}, u32[]{:S(2)}, u32[]{:S(2)}) collective-permute-start(bf16[76,128]{1,0:T(8,128)(2,1)S(1)} %pad_maximum_fusion.13), channel_id=1, source_target_pairs={{0,4},{4,0},{1,5},{5,1},{2,6},{6,2},{3,7},{7,3},{8,12},{12,8},{9,1... | collective-permute-start | bytes 58376 | tf_op jit(solution)/shard_map/ppermute | solution.py:84
  46.9 8.8 %all-to-all-start.1 = ((bf16[4,48,128]{2,1,0:T(8,128)(2,1)}), bf16[4,48,128]{2,1,0:T(8,128)(2,1)}, u32[]{:S(2)}, u32[]{:S(2)}) async-start(bf16[4,48,128]{2,1,0:T(8,128)(2,1)} %pad_maximum_fusion.7), calls=%async_computation.1 | async-start | bytes 98304 | tf_op jit(solution)/shard_map/all_to_all | solution.py:125
  58.9 8.3 %all-to-all-start.2 = ((f32[8,2,2,128]{3,2,1,0:T(2,128)}), f32[8,2,2,128]{3,2,1,0:T(2,128)S(1)}, u32[]{:S(2)}, u32[]{:S(2)}) async-start(f32[8,2,2,128]{3,2,1,0:T(2,128)} %broadcast_in_dim.177), calls=%async_computation.2 | async-start | bytes 32768 | tf_op jit(solution)/shard_map/all_to_all | solution.py:155
  68.9 11.7 %collective-permute-start.4 = (bf16[2,18,34,128]{3,2,0,1:T(8,128)(2,1)S(1)}, bf16[2,18,34,128]{3,2,0,1:T(8,128)(2,1)S(1)}, u32[]{:S(2)}, u32[]{:S(2)}) collective-permute-start(bf16[2,18,34,128]{3,2,0,1:T(8,128)(2,1)S(1)} %get-tuple-element.49), channel_id=1, source_target_pairs={{0,8},{8,16},{16,24},{1,9},{9,17},{17,25},{2,10},{10,18},{18,26},{... | collective-permute-start | bytes 940040 | tf_op jit(solution)/shard_map/ppermute | solution.py:162
  82.6 12.7 %collective-permute-start.5 = (bf16[2,18,34,128]{3,2,0,1:T(8,128)(2,1)}, bf16[2,18,34,128]{3,2,0,1:T(8,128)(2,1)}, u32[]{:S(2)}, u32[]{:S(2)}) collective-permute-start(bf16[2,18,34,128]{3,2,0,1:T(8,128)(2,1)} %get-tuple-element.13), channel_id=1, source_target_pairs={{8,0},{16,8},{24,16},{9,1},{17,9},{25,17},{10,2},{18,10},{26,18},{... | collective-permute-start | bytes 940040 | tf_op jit(solution)/shard_map/ppermute | solution.py:162
  98.3 2.5 %collective-permute-start.6 = (bf16[3456,128]{1,0:T(8,128)(2,1)S(1)}, bf16[3456,128]{1,0:T(8,128)(2,1)S(1)}, u32[]{:S(2)}, u32[]{:S(2)}) collective-permute-start(bf16[3456,128]{1,0:T(8,128)(2,1)S(1)} %bitcast.194), channel_id=1, source_target_pairs={{0,4},{4,0},{1,5},{5,1},{2,6},{6,2},{3,7},{7,3},{8,12},{12,8},{9,1... | collective-permute-start | bytes 2654216 | tf_op jit(solution)/shard_map/ppermute | solution.py:84
  101.9 15.9 %all-to-all-start.3 = ((bf16[4,864,128]{2,1,0:T(8,128)(2,1)}), bf16[4,864,128]{2,1,0:T(8,128)(2,1)S(1)}, u32[]{:S(2)}, u32[]{:S(2)}) async-start(bf16[4,864,128]{2,1,0:T(8,128)(2,1)} %bitcast.69), calls=%async_computation.3 | async-start | bytes 1769472 | tf_op jit(solution)/shard_map/all_to_all | solution.py:179
  105.9 16.8 %copy-start.20 = (pred[8,5]{0,1:T(8,128)(4,1)S(1)}, pred[8,5]{0,1:T(8,128)(4,1)}, u32[]{:S(2)}) copy-start(pred[8,5]{0,1:T(8,128)(4,1)} %constant.128) | copy-start | bytes 124
  118.7 11.8 %all-to-all-start.4 = ((bf16[4,224,128]{2,1,0:T(8,128)(2,1)}), bf16[4,224,128]{2,1,0:T(8,128)(2,1)S(1)}, u32[]{:S(2)}, u32[]{:S(2)}) async-start(bf16[4,224,128]{2,1,0:T(8,128)(2,1)} %bitcast.70), calls=%async_computation.4 | async-start | bytes 458752 | tf_op jit(solution)/shard_map/all_to_all | solution.py:179
  131.3 9.9 %all-to-all-start.5 = ((bf16[4,224,128]{2,1,0:T(8,128)(2,1)}), bf16[4,224,128]{2,1,0:T(8,128)(2,1)S(1)}, u32[]{:S(2)}, u32[]{:S(2)}) async-start(bf16[4,224,128]{2,1,0:T(8,128)(2,1)} %broadcast_in_dim.183), calls=%async_computation.5 | async-start | bytes 458752 | tf_op jit(solution)/shard_map/all_to_all | solution.py:185
  134.7 1.2 collective-permute-start.7
  142.3 12.9 %all-to-all-start.6 = ((bf16[4,880,128]{2,1,0:T(8,128)(2,1)}), bf16[4,880,128]{2,1,0:T(8,128)(2,1)S(1)}, u32[]{:S(2)}, u32[]{:S(2)}) async-start(bf16[4,880,128]{2,1,0:T(8,128)(2,1)} %broadcast_in_dim.184), calls=%async_computation.6 | async-start | bytes 1802240 | tf_op jit(solution)/shard_map/all_to_all | solution.py:185
  155.2 2.5 %collective-permute-start.8 = (bf16[3456,128]{1,0:T(8,128)(2,1)S(1)}, bf16[3456,128]{1,0:T(8,128)(2,1)S(1)}, u32[]{:S(2)}, u32[]{:S(2)}) collective-permute-start(bf16[3456,128]{1,0:T(8,128)(2,1)S(1)} %bitcast.182), channel_id=1, source_target_pairs={{0,4},{4,0},{1,5},{5,1},{2,6},{6,2},{3,7},{7,3},{8,12},{12,8},{9,1... | collective-permute-start | bytes 2654216 | tf_op jit(solution)/shard_map/ppermute | solution.py:84
  (16 other events, 68.6 us)

commit v3 on v0

v3 whole, which is shorter than its diff:
```python
import functools
import math

import jax
import jax.numpy as jnp
from jax import lax
from jax.experimental import pallas as pl
from jax.experimental.pallas import tpu as pltpu
from jax.sharding import PartitionSpec as P

GROUPS = 32
EPSILON = 1e-06
F32 = jnp.float32
BF16 = jnp.bfloat16
LANES = 128
FRAMES = 2
STATS = 8
PARTS = 3 * STATS


def up(count, step):
    return -(-count // step) * step


class Sizes:
    def __init__(self, high, wide):
        self.high, self.wide = high, wide
        self.cells = high * wide

    def stride(self, rim):
        return up(self.high + 2 * rim, 8)

    def main(self, rim):
        return FRAMES * (self.high + 2 * rim) * self.wide

    def rows(self, rim):
        return up(self.main(rim) + 2 * rim * FRAMES * self.stride(rim), 16)

    def tall(self):
        return self.high + 2

    def broad(self):
        return up(self.wide + 2, 8)


def call(body, outs, args, scratch=(), smem=0, mib=16, flops=0):
    specs = [pl.BlockSpec(memory_space=pltpu.SMEM)] * smem
    specs += [pl.BlockSpec(memory_space=pltpu.VMEM)] * (len(args) - smem)
    shapes = [jax.ShapeDtypeStruct(shape, dtype) for shape, dtype in outs]
    moved = sum(math.prod(a.shape) * a.dtype.itemsize for a in [*args, *shapes])
    return pl.pallas_call(
        body,
        out_shape=shapes,
        in_specs=specs,
        out_specs=[pl.BlockSpec(memory_space=pltpu.VMEM)] * len(outs),
        scratch_shapes=[pltpu.VMEM(shape, dtype) for shape, dtype in scratch],
        cost_estimate=pl.CostEstimate(flops=flops, bytes_accessed=moved, transcendentals=0),
        compiler_params=pltpu.CompilerParams(vmem_limit_bytes=mib << 20),
    )(*args)


def lane_totals(stat):
    lane = lax.broadcasted_iota(jnp.int32, stat.shape, 1)
    step = 1
    while step < LANES // GROUPS:
        ahead = pltpu.roll(stat, LANES - step, 1)
        behind = pltpu.roll(stat, step, 1)
        stat = stat + jnp.where((lane // step) % 2 == 0, ahead, behind)
        step *= 2
    return stat


def split3(stat):
    high = stat.astype(BF16).astype(F32)
    rest = stat - high
    middle = rest.astype(BF16).astype(F32)
    return jnp.concatenate([high, middle, rest - middle], 0)


def join3(parts):
    parts = parts.astype(F32)
    return parts[:STATS] + (parts[STATS : 2 * STATS] + parts[2 * STATS : PARTS])


def stat_block(first, second):
    rest = jnp.zeros((STATS - 2 * FRAMES, LANES), F32)
    return jnp.concatenate([*first, *second, rest], 0)


def measured(frames):
    means, squares = [], []
    for frame in frames:
        mean = jnp.sum(frame, 0, keepdims=True) / frame.shape[0]
        centred = frame - mean
        means.append(mean)
        squares.append(jnp.sum(centred * centred, 0, keepdims=True))
    return stat_block(means, squares)


def merged(one, two, cells):
    delta = one - two
    extra = (0.5 * cells) * delta * delta
    mean = 0.5 * (one[:FRAMES] + two[:FRAMES])
    square = one[FRAMES : 2 * FRAMES] + two[FRAMES : 2 * FRAMES] + extra[:FRAMES]
    return jnp.concatenate([mean, square, jnp.zeros((STATS - 2 * FRAMES, LANES), F32)], 0)


def concluded(blocks, cells):
    per_group = LANES // GROUPS
    mean = sum(blocks[1:], blocks[0])[:FRAMES]
    mean = lane_totals(mean) / (len(blocks) * per_group)
    total = jnp.zeros((FRAMES, LANES), F32)
    for block in blocks:
        off = block[:FRAMES] - mean
        total = total + block[FRAMES : 2 * FRAMES] + cells * off * off
    spread = lane_totals(total) / (cells * len(blocks) * per_group)
    rest = jnp.zeros((STATS - 2 * FRAMES, LANES), F32)
    return jnp.concatenate([mean, lax.rsqrt(spread + EPSILON), rest], 0)


def rim_rows(place, got):
    upper = place[0] == 0
    nothing = jnp.zeros_like(got)
    return jnp.where(upper, nothing, got), jnp.where(upper, got, nothing)


def in_frame(shape, place, across, size, rim):
    row = lax.broadcasted_iota(jnp.int32, shape, 0)
    col = lax.broadcasted_iota(jnp.int32, shape, 1)
    top = jnp.where(place[0] == 0, rim, 0)
    bottom = jnp.where(place[0] == 0, size.high + 2 * rim, size.high + rim)
    left = jnp.where(place[1] == 0, rim, 0)
    right = jnp.where(place[1] == across - 1, size.wide + rim, size.wide + 2 * rim)
    return (row >= top) & (row < bottom) & (col >= left) & (col < right)


def start_body(size, place, features, out_grad, pay, stats):
    high, wide = size.high, size.wide
    upper = place[0] == 0
    at = 0
    for frame in range(FRAMES):
        pay[at : at + wide] = jnp.where(upper, features[frame, high - 1], features[frame, 0])
        at += wide
    for frame in range(FRAMES):
        for row in range(2):
            edge = jnp.where(upper, out_grad[frame, high - 2 + row], out_grad[frame, row])
            pay[at : at + wide] = edge
            at += wide
    found = measured([features[f].astype(F32).reshape(size.cells, LANES) for f in range(FRAMES)])
    stats[...] = found
    fill = jnp.zeros((pay.shape[0] - at - PARTS, LANES), F32)
    pay[at:] = jnp.concatenate([split3(found), fill], 0).astype(BF16)


def columns(own, top, bottom, col):
    return jnp.concatenate([*[r[col : col + 1] for r in top], own[:, col], *[r[col : col + 1] for r in bottom]], 0)


def slots_first_body(size, across, place, features, out_grad, got, stats, slots, flat):
    wide, high = size.wide, size.high
    edge = got.shape[0]
    flat[...] = jnp.zeros_like(flat)
    at = 0
    cols = {0: [], 1: []}
    for frame in range(FRAMES):
        rim = got[frame * wide : (frame + 1) * wide].astype(F32)
        top, bottom = rim_rows(place, rim)
        own = features[frame].astype(F32)
        for side, col in ((0, 0), (1, wide - 1)):
            flat[side, at : at + high + 2] = columns(own, [top], [bottom], col)
        at += size.stride(1)
    base = FRAMES * wide
    for j in range(2):
        for frame in range(FRAMES):
            tops, bottoms = [], []
            for row in range(2):
                first = base + (frame * 2 + row) * wide
                top, bottom = rim_rows(place, got[first : first + wide].astype(F32))
                tops.append(top)
                bottoms.append(bottom)
            own = out_grad[frame].astype(F32)
            for side, col in ((0, j), (1, wide - 2 + j)):
                flat[side, at : at + high + 4] = columns(own, tops, bottoms, col)
            at += size.stride(2)
    first = 3 * FRAMES * wide
    both = merged(stats[...], join3(got[first : first + PARTS]), size.cells)
    parts = split3(both)
    flat[0, at : at + PARTS] = parts
    flat[1, at : at + PARTS] = parts
    for peer in range(across):
        slots[peer] = jnp.where(peer > place[1], flat[1], flat[0]).astype(BF16)


def sides(place, across, got, first, count):
    left = got[jnp.maximum(place[1] - 1, 0), first : first + count].astype(F32)
    right = got[jnp.minimum(place[1] + 1, across - 1), first : first + count].astype(F32)
    nothing = jnp.zeros_like(left)
    left = jnp.where(place[1] > 0, left, nothing)
    right = jnp.where(place[1] < across - 1, right, nothing)
    return left, right


def padded_frame(size, own, top, bottom, left, right, frame):
    high, wide = size.high, size.wide
    frame[1 : high + 1, 1 : wide + 1] = own
    frame[0:1, 1 : wide + 1] = top[None]
    frame[high + 1 : high + 2, 1 : wide + 1] = bottom[None]
    tall = high + 2
    frame[:, 0:1] = left[:tall].reshape(tall, 1, LANES)
    frame[:, wide + 1 : wide + 2] = right[:tall].reshape(tall, 1, LANES)


def put_frame(size, frame, index, out):
    wide, tall, step = size.wide, size.tall(), size.stride(1)
    flat = frame[:, 1 : wide + 1].reshape(tall * wide, LANES)
    out[index * tall * wide : (index + 1) * tall * wide] = flat.astype(BF16)
    fill = jnp.zeros((step - tall, LANES), F32)
    left = frame[:, 0:1].reshape(tall, LANES)
    right = frame[:, wide + 1 : wide + 2].reshape(tall, LANES)
    return jnp.concatenate([left, fill], 0), jnp.concatenate([right, fill], 0)


def put_sides(out, first, blocks):
    fill = out.shape[0] - first - sum(b.shape[0] for b in blocks)
    if fill:
        blocks = [*blocks, jnp.zeros((fill, LANES), F32)]
    out[first:] = jnp.concatenate(blocks, 0).astype(BF16)


def act_first_body(
    size, across, place, features, out_grad, row_got, col_got, act, grad, norm, frame
):
    high, wide = size.high, size.wide
    at = FRAMES * size.stride(1) + 2 * FRAMES * size.stride(2)
    blocks = [join3(col_got[peer, at : at + PARTS]) for peer in range(across)]
    found = concluded(blocks, 2 * size.cells)
    norm[...] = found
    step = size.stride(1)
    left_all, right_all = sides(place, across, col_got, 0, FRAMES * step)
    ok = in_frame((size.tall(), size.broad(), LANES), place, across, size, 1)
    lefts, rights = [], []
    frame[...] = jnp.zeros_like(frame)
    for f in range(FRAMES):
        top, bottom = rim_rows(place, row_got[f * wide : (f + 1) * wide].astype(F32))
        padded_frame(
            size,
            features[f].astype(F32),
            top,
            bottom,
            left_all[f * step : (f + 1) * step],
            right_all[f * step : (f + 1) * step],
            frame,
        )
        normed = (frame[...] - found[f : f + 1][None]) * found[FRAMES + f : FRAMES + f + 1][None]
        frame[...] = jnp.where(ok, normed * jax.nn.sigmoid(normed), 0.0)
        left, right = put_frame(size, frame, f, act)
        lefts.append(left)
        rights.append(right)
    put_sides(act, size.main(1), lefts + rights)

    tall = high + 4
    for f in range(FRAMES):
        start = f * tall * wide
        for row in range(2):
            first = FRAMES * wide + (f * 2 + row) * wide
            top, bottom = rim_rows(place, row_got[first : first + wide])
            grad[start + row * wide : start + (row + 1) * wide] = top
            below = start + (high + 2 + row) * wide
            grad[below : below + wide] = bottom
        grad[start + 2 * wide : start + (high + 2) * wide] = out_grad[f].reshape(
            size.cells, LANES
        )
    left, right = sides(
        place, across, col_got, FRAMES * step, 2 * FRAMES * size.stride(2)
    )
    put_sides(grad, size.main(2), [left, right])


def spread_columns(size, rim, trim, wo, block, index, dst, at, frame):
    wide, high = size.wide, size.high
    tall, step = high + 2 * rim, size.stride(rim)
    main = block[index * tall * wide : (index + 1) * tall * wide].astype(F32)
    main = main.reshape(tall, wide, LANES)
    cut = rim - trim
    tall_out = tall - 2 * cut
    frame[:, trim : trim + wide] = main[cut : cut + tall_out]
    first = size.main(rim)
    edges = block[first:].astype(F32)
    for j in range(2 * rim):
        col = j - cut if j < rim else j - rim + trim + wide
        if j < cut or (j >= rim and j - rim >= trim):
            continue
        start = (j * FRAMES + index) * step
        edge = edges[start + cut : start + cut + tall_out]
        frame[:, col : col + 1] = edge.reshape(tall_out, 1, LANES)
    for c in range(3):
        dst[at, :, :, c * LANES : (c + 1) * LANES] = frame[:, c : c + wo].astype(BF16)


def spread_all(size, rim, trim, wo, near, far, dst, frame):
    filled = size.wide + 2 * trim
    if frame.shape[1] > filled:
        frame[:, filled:] = jnp.zeros((frame.shape[0], frame.shape[1] - filled, LANES), F32)
    for f in range(2 * FRAMES):
        block = near if f < FRAMES else far
        spread_columns(size, rim, trim, wo, block, f % FRAMES, dst, f, frame)


def convolved(x, kernel, turned):
    tall, wo = x.shape[1], x.shape[2]
    ho = tall - 2
    count = ho * wo
    span = 9 * LANES

    def cells(f):
        return jnp.concatenate(
            [x[f, b : b + ho].reshape(count, 3 * LANES) for b in range(3)], 1
        )

    def taps(a):
        if not turned:
            return kernel[a * span : (a + 1) * span]
        last = (3 - a) * 9 - 1
        return jnp.concatenate(
            [kernel[(last - k) * LANES : (last - k + 1) * LANES] for k in range(9)], 1
        )

    dims = (((1,), (1 if turned else 0,)), ((), ()))

    def dot(one, two):
        return lax.dot_general(one, two, dims, preferred_element_type=F32)

    def pair(one, two):
        return jnp.concatenate([one, two], 0 if turned else 1)

    both = dot(cells(1), pair(taps(1), taps(0))) + dot(cells(2), pair(taps(2), taps(1)))
    first = both[:, :LANES] + dot(cells(0), taps(0))
    second = both[:, LANES:] + dot(cells(3), taps(2))
    return first, second


def conv_scratch(size, trim, wo):
    tall = size.high + 2 * trim
    return [((2 * FRAMES, tall, wo, 3 * LANES), BF16), ((tall, up(wo + 2, 8), LANES), F32)]


def hidden_body(size, place, near, far, kernel, hidden, pay, stats, x, frame):
    high, wide = size.high, size.wide
    spread_all(size, 1, 1, wide, near, far, x, frame)
    sums = convolved(x, kernel, False)
    upper = place[0] == 0
    rounded = [s.astype(BF16) for s in sums]
    for f in range(FRAMES):
        hidden[f] = rounded[f].reshape(high, wide, LANES)
        edge = jnp.where(upper, rounded[f][size.cells - wide :], rounded[f][:wide])
        pay[f * wide : (f + 1) * wide] = edge
    found = measured([r.astype(F32) for r in rounded])
    stats[...] = found
    at = FRAMES * wide
    fill = jnp.zeros((pay.shape[0] - at - PARTS, LANES), F32)
    pay[at:] = jnp.concatenate([split3(found), fill], 0).astype(BF16)


def grad_act_body(size, near, far, kernel, out, x, frame):
    wo = x.shape[2]
    spread_all(size, 2, 2, wo, near, far, x, frame)
    sums = convolved(x, kernel, True)
    for f in range(FRAMES):
        out[f] = sums[f].reshape(size.tall(), wo, LANES)[:, : size.broad()]


def slots_second_body(size, across, place, hidden, got, stats, slots, flat):
    wide, high = size.wide, size.high
    flat[...] = jnp.zeros_like(flat)
    at = 0
    for frame in range(FRAMES):
        top, bottom = rim_rows(place, got[frame * wide : (frame + 1) * wide].astype(F32))
        own = hidden[frame].astype(F32)
        for side, col in ((0, 0), (1, wide - 1)):
            flat[side, at : at + high + 2] = columns(own, [top], [bottom], col)
        at += size.stride(1)
    first = FRAMES * wide
    parts = split3(merged(stats[...], join3(got[first : first + PARTS]), size.cells))
    flat[0, at : at + PARTS] = parts
    flat[1, at : at + PARTS] = parts
    for peer in range(across):
        slots[peer] = jnp.where(peer > place[1], flat[1], flat[0]).astype(BF16)


def act_second_body(
    size, across, place, hidden, row_got, col_got, grad_act, act, q, z, norm, slots, frame
):
    high, wide = size.high, size.wide
    step = size.stride(1)
    at = FRAMES * step
    found = concluded(
        [join3(col_got[peer, at : at + PARTS]) for peer in range(across)], 2 * size.cells
    )
    norm[...] = found
    left_all, right_all = sides(place, across, col_got, 0, FRAMES * step)
    ok = in_frame((size.tall(), size.broad(), LANES), place, across, size, 1)
    lefts, rights, firsts, seconds = [], [], [], []
    frame[...] = jnp.zeros_like(frame)
    for f in range(FRAMES):
        top, bottom = rim_rows(place, row_got[f * wide : (f + 1) * wide].astype(F32))
        padded_frame(
            size,
            hidden[f].astype(F32),
            top,
            bottom,
            left_all[f * step : (f + 1) * step],
            right_all[f * step : (f + 1) * step],
            frame,
        )
        normed = (frame[...] - found[f : f + 1][None]) * found[FRAMES + f : FRAMES + f + 1][None]
        sigmoid = jax.nn.sigmoid(normed)
        frame[...] = jnp.where(ok, normed * sigmoid, 0.0)
        left, right = put_frame(size, frame, f, act)
        lefts.append(left)
        rights.append(right)
        grad = grad_act[f] * sigmoid * (1.0 + normed * (1.0 - sigmoid))
        z[f] = normed
        q[f] = grad
        row = lax.broadcasted_iota(jnp.int32, grad.shape, 0)
        col = lax.broadcasted_iota(jnp.int32, grad.shape, 1)
        own = (row > 0) & (row <= high) & (col > 0) & (col <= wide)
        inner = jnp.where(own, grad, 0.0)
        firsts.append(jnp.sum(jnp.sum(inner, 0), 0, keepdims=True))
        seconds.append(jnp.sum(jnp.sum(inner * normed, 0), 0, keepdims=True))
    put_sides(act, size.main(1), lefts + rights)
    sums = stat_block(firsts, seconds)
    for peer in range(slots.shape[0]):
        slots[peer] = sums


def hidden_grad_body(size, across, place, q, z, got, norm, out, frame):
    peers = got.shape[0]
    total = got[0]
    for peer in range(1, peers):
        total = total + got[peer]
    means = lane_totals(total) / (size.cells * peers * (LANES // GROUPS))
    ok = in_frame((size.tall(), size.broad(), LANES), place, across, size, 1)
    lefts, rights = [], []
    for f in range(FRAMES):
        first, second = means[f : f + 1][None], means[FRAMES + f : FRAMES + f + 1][None]
        inv = norm[FRAMES + f : FRAMES + f + 1][None]
        frame[...] = jnp.where(ok, inv * (q[f] - first - z[f] * second), 0.0)
        left, right = put_frame(size, frame, f, out)
        lefts.append(left)
        rights.append(right)
    put_sides(out, size.main(1), lefts + rights)


def own_cells(size, block, f):
    start = (f * size.tall() + 1) * size.wide
    return block[start : start + size.cells]


def turned_cells(size, block, out):
    for f in range(FRAMES):
        cells = own_cells(size, block, f).astype(F32).T.astype(BF16)
        out[f * LANES : (f + 1) * LANES] = cells


def tap_sums(x, turned, b):
    ho, wo = x.shape[1] - 2, x.shape[2]

    def cells(f):
        return x[f, b : b + ho].reshape(ho * wo, 3 * LANES)

    def dot(one, two):
        return jnp.dot(one, two, preferred_element_type=F32)

    low = dot(turned[...], cells(1))
    high = dot(turned[...], cells(2))
    return (
        dot(turned[:LANES], cells(0)) + low[LANES:],
        low[:LANES] + high[LANES:],
        high[:LANES] + dot(turned[LANES:], cells(3)),
    )


def second_term_body(size, near, far, act, out, x, frame, turned):
    spread_all(size, 2, 1, size.wide, near, far, x, frame)
    turned_cells(size, act, turned)
    for b in range(3):
        for a, total in enumerate(tap_sums(x, turned, b)):
            for c in range(3):
                tap = ((2 - a) * 3 + 2 - b) * 3 + 2 - c
                out[tap * LANES : (tap + 1) * LANES] = total[:, c * LANES : (c + 1) * LANES]


def first_term_body(size, place, near, far, grad, second, keep, give, x, frame, turned, both):
    spread_all(size, 1, 1, size.wide, near, far, x, frame)
    turned_cells(size, grad, turned)
    for b in range(3):
        for a, total in enumerate(tap_sums(x, turned, b)):
            first = (a * 3 + b) * 3 * LANES
            both[first : first + 3 * LANES] = total.T
    upper = place[0] == 0
    keep[...] = jnp.where(upper, both[...], second[...])
    give[...] = jnp.where(upper, second[...], both[...]).astype(BF16)


def result_body(size, near, far, kernel, features, out, x, frame):
    spread_all(size, 1, 1, size.wide, near, far, x, frame)
    sums = convolved(x, kernel, False)
    for f in range(FRAMES):
        total = features[f].astype(F32) + sums[f].reshape(size.high, size.wide, LANES)
        out[f] = total.astype(BF16)


def back_first_body(size, near, far, kernel, features, norm, q, sums, x, frame):
    spread_all(size, 1, 1, size.wide, near, far, x, frame)
    grads = convolved(x, kernel, True)
    firsts, seconds = [], []
    for f in range(FRAMES):
        values = features[f].astype(F32).reshape(size.cells, LANES)
        normed = (values - norm[f : f + 1]) * norm[FRAMES + f : FRAMES + f + 1]
        sigmoid = jax.nn.sigmoid(normed)
        grad = grads[f] * sigmoid * (1.0 + normed * (1.0 - sigmoid))
        q[f] = grad
        firsts.append(jnp.sum(grad, 0, keepdims=True))
        seconds.append(jnp.sum(grad * normed, 0, keepdims=True))
    sums[...] = stat_block(firsts, seconds)


def feature_grad_body(size, peers, features, out_grad, norm, q, got, out):
    total = join3(got[0])
    for peer in range(1, got.shape[0]):
        total = total + join3(got[peer])
    means = lane_totals(total) / (size.cells * peers * (LANES // GROUPS))
    for f in range(FRAMES):
        values = features[f].astype(F32).reshape(size.cells, LANES)
        inv = norm[FRAMES + f : FRAMES + f + 1]
        normed = (values - norm[f : f + 1]) * inv
        grad = inv * (q[f] - means[f : f + 1] - normed * means[FRAMES + f : FRAMES + f + 1])
        grad = out_grad[f].astype(F32) + grad.reshape(size.high, size.wide, LANES)
        out[f] = grad.astype(BF16)


def row_swap(values):
    return lax.ppermute(values, "row", [(0, 1), (1, 0)])


def later(values, by):
    peers = lax.axis_size("tm")
    pairs = [(i, i + by) for i in range(peers) if 0 <= i + by < peers]
    return lax.ppermute(values, "tm", pairs)


def scatter_sum(values, axis):
    peers = lax.axis_size(axis)
    share = up(values.shape[0], 16 * peers) // peers
    values = jnp.pad(values, ((0, share * peers - values.shape[0]), (0, 0)))
    slots = values.reshape(peers, share, LANES).astype(BF16)
    return lax.all_to_all(slots, axis, 0, 0).astype(F32).sum(0)


def gather_shares(share, axis):
    peers = lax.axis_size(axis)
    slots = jnp.broadcast_to(share[None], (peers,) + share.shape)
    return lax.all_to_all(slots, axis, 0, 0)


def sum_parts(stat):
    high = lax.reduce_precision(stat, 8, 7)
    rest = stat - high
    middle = lax.reduce_precision(rest, 8, 7)
    return jnp.concatenate([high, middle, rest - middle], 0).astype(BF16)


def summed_kernels(keep, give, sums, factor):
    rows = keep.shape[0]
    upper = lax.axis_index("row") == 0
    keep = keep + row_swap(give).astype(F32)
    by_col = scatter_sum(keep, "col")
    by_tm = scatter_sum(by_col, "tm")
    done = (by_tm * factor).astype(BF16)
    done = gather_shares(done, "tm").reshape(-1, LANES)[: by_col.shape[0]]
    parts = sum_parts(sums + row_swap(sums))
    spare = -parts.shape[0] % 16
    done = jnp.concatenate([done, jnp.pad(parts, ((0, spare), (0, 0)))], 0)
    done = gather_shares(done, "col")
    terms = done[:, by_col.shape[0] :]
    done = done[:, : by_col.shape[0]].reshape(-1, LANES)[:rows]
    other = row_swap(done)
    return jnp.where(upper, done, other), jnp.where(upper, other, done), terms


def on_device(features, conv_first, conv_second, out_grad):
    frames, high, wide, chans = features.shape
    assert frames == FRAMES and chans == LANES and lax.axis_size("row") == 2
    size = Sizes(high, wide)
    across = lax.axis_size("col")
    peers = 2 * across
    factor = 1.0 / math.sqrt(size.cells * FRAMES * lax.axis_size("tm") * peers)
    place = jnp.stack([lax.axis_index("row"), lax.axis_index("col")]).astype(jnp.int32)
    taps = conv_first.shape
    first = conv_first.reshape(-1, LANES)
    second = conv_second.reshape(-1, LANES)
    work = 2 * first.size * size.cells * FRAMES
    part = functools.partial
    stat = ((STATS, LANES), F32)
    tall, broad = size.tall(), size.broad()
    frame = ((tall, broad, LANES), F32)

    edge = up(3 * FRAMES * wide + PARTS, 16)
    pay, stats = call(
        part(start_body, size), [((edge, LANES), BF16), stat], [place, features, out_grad], smem=1
    )
    row_got = row_swap(pay)
    lines = up(FRAMES * size.stride(1) + 2 * FRAMES * size.stride(2) + PARTS, 16)
    (slots,) = call(
        part(slots_first_body, size, across),
        [((across, lines, LANES), BF16)],
        [place, features, out_grad, row_got, stats],
        [((2, lines, LANES), F32)],
        smem=1,
    )
    col_got = lax.all_to_all(slots, "col", 0, 0)
    block = ((size.rows(1), LANES), BF16)
    act_first, grad, norm_first = call(
        part(act_first_body, size, across),
        [block, ((size.rows(2), LANES), BF16), stat],
        [place, features, out_grad, row_got, col_got],
        [frame],
        smem=1,
    )
    act_before = later(act_first, 1)
    grad_after = later(grad, -1)

    edge = up(FRAMES * wide + PARTS, 16)
    hidden, pay, stats = call(
        part(hidden_body, size),
        [(features.shape, BF16), ((edge, LANES), BF16), stat],
        [place, act_before, act_first, first],
        conv_scratch(size, 1, wide),
        smem=1,
        mib=24,
        flops=work,
    )
    pay, grad_after = lax.optimization_barrier((pay, grad_after))
    row_got = row_swap(pay)
    lines = up(FRAMES * size.stride(1) + PARTS, 16)
    (slots,) = call(
        part(slots_second_body, size, across),
        [((across, lines, LANES), BF16)],
        [place, hidden, row_got, stats],
        [((2, lines, LANES), F32)],
        smem=1,
    )
    col_got = lax.all_to_all(slots, "col", 0, 0)
    (grad_act,) = call(
        part(grad_act_body, size),
        [((FRAMES, tall, broad, LANES), F32)],
        [grad, grad_after, second],
        conv_scratch(size, 2, up(wide + 2, 16)),
        mib=32,
        flops=2 * work,
    )
    field = ((FRAMES, tall, broad, LANES), F32)
    act_second, q, z, norm_second, slots = call(
        part(act_second_body, size, across),
        [block, field, field, stat, ((peers, STATS, LANES), F32)],
        [place, hidden, row_got, col_got, grad_act],
        [frame],
        smem=1,
    )
    got = lax.all_to_all(slots, ("row", "col"), 0, 0)
    act_second_before = later(act_second, 1)
    turned = ((FRAMES * LANES, size.cells), BF16)
    (second_term,) = call(
        part(second_term_body, size),
        [(first.shape, F32)],
        [grad, grad_after, act_second],
        [*conv_scratch(size, 1, wide), turned],
        mib=24,
        flops=work,
    )
    (hidden_grad,) = call(
        part(hidden_grad_body, size, across),
        [block],
        [place, q, z, got, norm_second],
        [frame],
        smem=1,
    )
    hidden_grad, act_second_before = lax.optimization_barrier((hidden_grad, act_second_before))
    hidden_after = later(hidden_grad, -1)
    keep, give = call(
        part(first_term_body, size),
        [(first.shape, F32), (first.shape, BF16)],
        [place, act_before, act_first, hidden_grad, second_term],
        [*conv_scratch(size, 1, wide), turned, (first.shape, F32)],
        smem=1,
        mib=24,
        flops=work,
    )
    (result,) = call(
        part(result_body, size),
        [(features.shape, BF16)],
        [act_second_before, act_second, second, features],
        conv_scratch(size, 1, wide),
        mib=24,
        flops=work,
    )
    q, sums = call(
        part(back_first_body, size),
        [((FRAMES, size.cells, LANES), F32), stat],
        [hidden_grad, hidden_after, first, features, norm_first],
        conv_scratch(size, 1, wide),
        mib=24,
        flops=work,
    )
    first_grad, second_grad, terms = summed_kernels(keep, give, sums, factor)
    (feature_grad,) = call(
        part(feature_grad_body, size, peers),
        [(features.shape, BF16)],
        [features, out_grad, norm_first, q, terms],
    )
    return (result, feature_grad, first_grad.reshape(taps), second_grad.reshape(taps))


def solution(mesh):
    in_specs = (P("tm", "row", "col", None), P(), P(), P("tm", "row", "col", None))
    out_specs = (P("tm", "row", "col", None), P("tm", "row", "col", None), P(), P())
    return jax.shard_map(
        on_device, mesh=mesh, in_specs=in_specs, out_specs=out_specs, check_vma=False
    )
```

time: 335 us -> 129 us (0.39)
  waiting for transfers between devices: 117 us -> 23.7 us
  blocking collectives: 92 us -> 41.1 us
  starting transfers between devices: 53.2 us -> 24.2 us
  matrix products: 27.9 us -> 0 us
  Pallas kernels: 0 us -> 23.4 us
  other arithmetic: 18.4 us -> 3.29 us
  between operations: 14.9 us -> 0.89 us
    psum x1 -> x0, waiting for transfers between devices: 114 us -> none  [on_device(): lax.psum((first_term, second_term), ('tm', 'row', 'col'))]
    psum x6 -> x0, blocking collectives: 92 us -> none  [the longest x2 33.1 us: norm_act(): group_mean = lax.psum(group_sum(values), ('row', 'col')) / count]
    ppermute x20 -> x9, starting transfers between devices: 53.2 us -> 10.6 us  [the longest x4 9.56 us: later(): return lax.ppermute(values, 'tm', pairs)]
    all_to_all x0 -> x3, blocking collectives: none -> 41.1 us  [the longest x1 16.6 us: scatter_sum(): return lax.all_to_all(slots, axis, 0, 0).astype(F32).sum(0)]
    pallas_call x0 -> x13, Pallas kernels: none -> 23.4 us  [call(): pl.pallas_call(body, out_shape=shapes, in_specs=specs, out_specs=[pl.Bloc...]
    transpose x2 -> x0, matrix products: 18 us -> none  [weight_grad(): return jnp.transpose(summed, (1, 2, 3, 4, 0))]
    all_to_all x0 -> x4, starting transfers between devices: none -> 13.6 us  [the longest x1 3.57 us: gather_shares(): return lax.all_to_all(slots, axis, 0, 0)]
    ppermute x20 -> x9, waiting for transfers between devices: 3.41 us -> 14 us  [the longest x4 8.69 us: later(): return lax.ppermute(values, 'tm', pairs)]
  transfers between devices with their start and end apart: 21 -> 13, of which waited for: 5 -> 10; matrix products, arithmetic and copies ran while one was open for 12% -> 1% of each run, Pallas kernels for 0% -> 12%
where the time goes in v3:
time: 129 us; the launch traced here: 128 us
  blocking collectives  41.1 us (32%)
  starting transfers between devices  24.2 us (19%)
  waiting for transfers between devices  23.7 us (18%)
  Pallas kernels  23.4 us (18%)
  local copies, waits for them, and re-layouts  11 us (9%)
  other arithmetic  3.29 us (3%)
    pallas_call x13, Pallas kernels, call(): pl.pallas_call(body, out_shape=shapes, in_specs=specs, out_specs=[pl.Bloc...  23.4 us
    all_to_all x1, blocking collectives, scatter_sum(): return lax.all_to_all(slots, axis, 0, 0).astype(F32).sum(0)  16.6 us
    all_to_all x1, blocking collectives, gather_shares(): return lax.all_to_all(slots, axis, 0, 0)  14.1 us
    all_to_all x1, blocking collectives, on_device(): col_got = lax.all_to_all(slots, 'col', 0, 0)  10.4 us
    ppermute x4, starting transfers between devices, later(): return lax.ppermute(values, 'tm', pairs)  9.56 us
    ppermute x4, waiting for transfers between devices, later(): return lax.ppermute(values, 'tm', pairs)  8.69 us
    unnamed x36, local copies, waits for them, and re-layouts  8.49 us
    all_to_all x1, waiting for transfers between devices, scatter_sum(): return lax.all_to_all(slots, axis, 0, 0).astype(F32).sum(0)  6.82 us
  transfers between devices with their start and end apart: 13, of which 10 were waited for; matrix products, arithmetic and copies ran while one was open for 1% of the time, Pallas kernels for 12%

profile of v3, /device:TPU:0, one launch (start us, length us, event | category | flops | bytes accessed | tf_op | source)
XLA Modules:
  0.0 127.7 jit_solution(3195340881764574932)
XLA Ops:
  5.4 10.4 %all_to_all.35.col_got = bf16[4,176,128]{2,1,0:T(8,128)(2,1)S(1)} all-to-all(bf16[4,176,128]{2,1,0:T(8,128)(2,1)S(1)} %shard_map.76), channel_id=1, replica_groups=mesh['tm'=4,'row'=2,'col'=4] {'col'}, dimensions={0} | all-to-all | bytes 360448 | tf_op jit(solution)/shard_map/all_to_all | solution.py:621
  17.0 3.5 %collective-permute-start.1 = (bf16[1248,128]{1,0:T(8,128)(2,1)S(1)}, bf16[1248,128]{1,0:T(8,128)(2,1)S(1)}, u32[]{:S(2)}, u32[]{:S(2)}) collective-permute-start(bf16[1248,128]{1,0:T(8,128)(2,1)S(1)} %get-tuple-element.27.far), channel_id=1, source_target_pairs={{0,8},{8,16},{16,24},{1,9},{9,17},{17,25},{2,10},{10,18},{18,26},{... | collective-permute-start | bytes 958472 | tf_op jit(solution)/shard_map/ppermute | solution.py:549
  20.5 1.3 %collective-permute-start.2 = (bf16[1472,128]{1,0:T(8,128)(2,1)S(1)}, bf16[1472,128]{1,0:T(8,128)(2,1)S(1)}, u32[]{:S(2)}, u32[]{:S(2)}) collective-permute-start(bf16[1472,128]{1,0:T(8,128)(2,1)S(1)} %get-tuple-element.30.near), channel_id=1, source_target_pairs={{8,0},{16,8},{24,16},{9,1},{17,9},{25,17},{10,2},{18,10},{26,18},{... | collective-permute-start | bytes 1130504 | tf_op jit(solution)/shard_map/ppermute | solution.py:549
  21.8 4.4 %collective-permute-done.1.near = bf16[1248,128]{1,0:T(8,128)(2,1)S(1)} collective-permute-done((bf16[1248,128]{1,0:T(8,128)(2,1)S(1)}, bf16[1248,128]{1,0:T(8,128)(2,1)S(1)}, u32[]{:S(2)}, u32[]{:S(2)}) %collective-permute-start.1) | collective-permute-done | bytes 319520 | tf_op jit(solution)/shard_map/ppermute | solution.py:549
  26.2 2.4 %shard_map.78 = (bf16[2,16,32,128]{3,2,1,0:T(8,128)(2,1)S(1)}, bf16[96,128]{1,0:T(8,128)(2,1)S(1)}, f32[8,128]{1,0:T(8,128)S(1)}) custom-call(s32[2]{0:T(128)S(1)} %pad_add_fusion.place, bf16[1248,128]{1,0:T(8,128)(2,1)S(1)} %collective-permute-done.1.near, bf16[1248,128]{1,0:T(8,128)(2,1)S(1)} %get-tuple-element.27.far, bf16[3456,128]{1,0:T(8,128)(2,1)S(1)} %bitcast.12), custom_call_target="tpu_custom_call" | custom-call | flops 905969664 | bytes 1814536 | tf_op jit(solution)/shard_map/pallas_call | solution.py:51
  28.6 3.0 %collective-permute-done.2.far = bf16[1472,128]{1,0:T(8,128)(2,1)S(1)} collective-permute-done((bf16[1472,128]{1,0:T(8,128)(2,1)S(1)}, bf16[1472,128]{1,0:T(8,128)(2,1)S(1)}, u32[]{:S(2)}, u32[]{:S(2)}) %collective-permute-start.2) | collective-permute-done | bytes 376864 | tf_op jit(solution)/shard_map/ppermute | solution.py:549
  33.9 3.3 %all-to-all-start.1 = ((bf16[4,80,128]{2,1,0:T(8,128)(2,1)}), bf16[4,80,128]{2,1,0:T(8,128)(2,1)S(1)}, u32[]{:S(2)}, u32[]{:S(2)}) async-start(bf16[4,80,128]{2,1,0:T(8,128)(2,1)} %shard_map.79), calls=%async_computation.1 | async-start | bytes 163840 | tf_op jit(solution)/shard_map/all_to_all | solution.py:653
  38.3 2.7 %shard_map.80.grad_act = f32[2,18,40,128]{3,2,1,0:T(8,128)S(1)} custom-call(bf16[1472,128]{1,0:T(8,128)(2,1)S(1)} %get-tuple-element.30.near, bf16[1472,128]{1,0:T(8,128)(2,1)S(1)} %copy-done.10, bf16[3456,128]{1,0:T(8,128)(2,1)S(1)} %bitcast.14), custom_call_target="tpu_custom_call" | custom-call | flops 1811939328 | bytes 2375680 | tf_op jit(solution)/shard_map/pallas_call | solution.py:51
  42.1 2.3 %shard_map.81 = (bf16[1248,128]{1,0:T(8,128)(2,1)}, f32[2,18,40,128]{3,2,1,0:T(8,128)S(1)}, f32[2,18,40,128]{3,2,1,0:T(8,128)S(1)}, f32[8,128]{1,0:T(8,128)S(1)}, f32[8,8,128]{2,1,0:T(8,128)}) custom-call(s32[2]{0:T(128)S(1)} %pad_add_fusion.place, bf16[2,16,32,128]{3,2,1,0:T(8,128)(2,1)S(1)} %get-tuple-element.28.hidden, ...), custom_call_target="tpu_custom_call" | custom-call | bytes 2936840 | tf_op jit(solution)/shard_map/pallas_call | solution.py:51
  44.4 3.5 %collective-permute-start.4 = (bf16[1248,128]{1,0:T(8,128)(2,1)}, bf16[1248,128]{1,0:T(8,128)(2,1)S(1)}, u32[]{:S(2)}, u32[]{:S(2)}) collective-permute-start(bf16[1248,128]{1,0:T(8,128)(2,1)} %get-tuple-element.38.far.act), channel_id=1, source_target_pairs={{0,8},{8,16},{16,24},{1,9},{9,17},{17,25},{2,10},{10,18},{18,26},{... | collective-permute-start | bytes 958472 | tf_op jit(solution)/shard_map/ppermute | solution.py:549
  47.9 3.4 %all-to-all-start.2 = ((f32[8,8,128]{2,1,0:T(8,128)}), f32[8,8,128]{2,1,0:T(8,128)S(1)}, u32[]{:S(2)}, u32[]{:S(2)}) async-start(f32[8,8,128]{2,1,0:T(8,128)} %get-tuple-element.36), calls=%async_computation.2 | async-start | bytes 65536 | tf_op jit(solution)/shard_map/all_to_all | solution.py:670
  53.3 2.6 %shard_map.85.second = f32[3456,128]{1,0:T(8,128)S(1)} custom-call(bf16[1472,128]{1,0:T(8,128)(2,1)S(1)} %copy-done.8, bf16[1472,128]{1,0:T(8,128)(2,1)S(1)} %copy-done.11, bf16[1248,128]{1,0:T(8,128)(2,1)} %get-tuple-element.38.far.act), custom_call_target="tpu_custom_call" | custom-call | flops 905969664 | bytes 2842624 | tf_op jit(solution)/shard_map/pallas_call | solution.py:51
  60.5 2.3 %shard_map.86 = (f32[3456,128]{1,0:T(8,128)S(1)}, bf16[3456,128]{1,0:T(8,128)(2,1)S(1)}) custom-call(s32[2]{0:T(128)S(1)} %pad_add_fusion.place, bf16[1248,128]{1,0:T(8,128)(2,1)S(1)} %copy-done.15, bf16[1248,128]{1,0:T(8,128)(2,1)S(1)} %copy-done.13, bf16[1248,128]{1,0:T(8,128)(2,1)S(1)} %shard_map.82.near.grad, f32[3456,128]{1,0:T(8,128)S(1)} %copy-done.17), custom_call_target="tpu_custom_call" | custom-call | flops 905969664 | bytes 5382152 | tf_op jit(solution)/shard_map/pallas_call | solution.py:51
  63.3 2.1 %collective-permute-done.6 = bf16[3456,128]{1,0:T(8,128)(2,1)S(1)} collective-permute-done((bf16[3456,128]{1,0:T(8,128)(2,1)S(1)}, bf16[3456,128]{1,0:T(8,128)(2,1)S(1)}, u32[]{:S(2)}, u32[]{:S(2)}) %collective-permute-start.6) | collective-permute-done | bytes 884768 | tf_op jit(solution)/shard_map/ppermute | solution.py:543
  65.5 16.6 %all_to_all.36 = bf16[4,864,128]{2,1,0:T(8,128)(2,1)S(1)} all-to-all(bf16[4,864,128]{2,1,0:T(8,128)(2,1)S(1)} %bitcast.16), channel_id=1, replica_groups=mesh['tm'=4,'row'=2,'col'=4] {'col'}, dimensions={0} | all-to-all | bytes 1769472 | tf_op jit(solution)/shard_map/all_to_all | solution.py:557
  83.1 3.4 %all-to-all-start.4 = ((bf16[4,224,128]{2,1,0:T(8,128)(2,1)}), bf16[4,224,128]{2,1,0:T(8,128)(2,1)S(1)}, u32[]{:S(2)}, u32[]{:S(2)}) async-start(bf16[4,224,128]{2,1,0:T(8,128)(2,1)} %bitcast.5), calls=%async_computation.4 | async-start | bytes 458752 | tf_op jit(solution)/shard_map/all_to_all | solution.py:557
  87.8 6.8 %all-to-all-done.4 = bf16[4,224,128]{2,1,0:T(8,128)(2,1)S(1)} async-done(((bf16[4,224,128]{2,1,0:T(8,128)(2,1)}), bf16[4,224,128]{2,1,0:T(8,128)(2,1)S(1)}, u32[]{:S(2)}, u32[]{:S(2)}) %all-to-all-start.4) | async-done | bytes 229408 | tf_op jit(solution)/shard_map/all_to_all | solution.py:557
  95.3 3.6 %all-to-all-start.5 = ((bf16[4,224,128]{2,1,0:T(8,128)(2,1)}), bf16[4,224,128]{2,1,0:T(8,128)(2,1)S(1)}, u32[]{:S(2)}, u32[]{:S(2)}) async-start(bf16[4,224,128]{2,1,0:T(8,128)(2,1)} %broadcast_in_dim.4), calls=%async_computation.5 | async-start | bytes 458752 | tf_op jit(solution)/shard_map/all_to_all | solution.py:563
  98.9 1.4 %collective-permute-done.5.far = bf16[1248,128]{1,0:T(8,128)(2,1)S(1)} collective-permute-done((bf16[1248,128]{1,0:T(8,128)(2,1)S(1)}, bf16[1248,128]{1,0:T(8,128)(2,1)S(1)}, u32[]{:S(2)}, u32[]{:S(2)}) %collective-permute-start.5) | collective-permute-done | bytes 319520 | tf_op jit(solution)/shard_map/ppermute | solution.py:549
  100.3 1.8 %shard_map.84 = (f32[2,512,128]{2,1,0:T(8,128)S(1)}, f32[8,128]{1,0:T(8,128)S(1)}) custom-call(bf16[1248,128]{1,0:T(8,128)(2,1)S(1)} %shard_map.82.near.grad, bf16[1248,128]{1,0:T(8,128)(2,1)S(1)} %collective-permute-done.5.far, bf16[3456,128]{1,0:T(8,128)(2,1)S(1)} %bitcast.13, bf16[2,16,32,128]{3,2,1,0:T(8,128)(2,1)S(1)} %copy-done.1, ...), custom_call_target="tpu_custom_call" | custom-call | flops 905969664 | bytes 2318336 | tf_op jit(solution)/shard_map/pallas_call | solution.py:51
  103.4 1.8 %all-to-all-done.5 = bf16[4,224,128]{2,1,0:T(8,128)(2,1)S(1)} async-done(((bf16[4,224,128]{2,1,0:T(8,128)(2,1)}), bf16[4,224,128]{2,1,0:T(8,128)(2,1)S(1)}, u32[]{:S(2)}, u32[]{:S(2)}) %all-to-all-start.5) | async-done | bytes 229408 | tf_op jit(solution)/shard_map/all_to_all | solution.py:563
  105.4 14.1 %all_to_all.37 = bf16[4,896,128]{2,1,0:T(8,128)(2,1)S(1)} all-to-all(bf16[4,896,128]{2,1,0:T(8,128)(2,1)S(1)} %broadcast_in_dim.5), channel_id=1, replica_groups=mesh['tm'=4,'row'=2,'col'=4] {'col'}, dimensions={0} | all-to-all | bytes 1835008 | tf_op jit(solution)/shard_map/all_to_all | solution.py:563
  120.5 3.4 %shard_map.83 = bf16[2,16,32,128]{3,2,1,0:T(8,128)(2,1)} custom-call(bf16[1248,128]{1,0:T(8,128)(2,1)S(1)} %collective-permute-done.4.near, bf16[1248,128]{1,0:T(8,128)(2,1)} %get-tuple-element.38.far.act, bf16[3456,128]{1,0:T(8,128)(2,1)S(1)} %bitcast.15, bf16[2,16,32,128]{3,2,1,0:T(8,128)(2,1)S(1)} %copy-done.1), custom_call_target="tpu_custom_call" | custom-call | flops 905969664 | bytes 2048000 | tf_op jit(solution)/shard_map/pallas_call | solution.py:51
  124.9 2.8 %broadcast_select_fusion = (bf16[3456,128]{1,0:T(8,128)(2,1)}, bf16[3456,128]{1,0:T(8,128)(2,1)}) fusion(bf16[3456,128]{1,0:T(8,128)(2,1)} %collective-permute-done.8, pred[]{:T(512)S(6)} %eq.3, bf16[4,864,128]{2,1,0:T(8,128)(2,1)} %slice.14), kind=kLoop, calls=%fused_computation.1 | loop fusion | flops 884736 | bytes 3538945 | tf_op jit(solution)/shard_map/jit(_where)/select_n | solution.py:588
  (69 shorter events, 24.1 us)
Async XLA Ops:
  2.6 23.6 %copy-start.4 = (bf16[3,3,3,128,128]{4,3,2,1,0:T(8,128)(2,1)S(1)}, bf16[3,3,3,128,128]{4,3,2,1,0:T(8,128)(2,1)}, u32[]{:S(2)}) copy-start(bf16[3,3,3,128,128]{4,3,2,1,0:T(8,128)(2,1)} %param.5) | copy-start | bytes 2654212
  3.3 1.4 %collective-permute-start = (bf16[224,128]{1,0:T(8,128)(2,1)S(1)}, bf16[224,128]{1,0:T(8,128)(2,1)S(1)}, u32[]{:S(2)}, u32[]{:S(2)}) collective-permute-start(bf16[224,128]{1,0:T(8,128)(2,1)S(1)} %get-tuple-element.25), channel_id=1, source_target_pairs={{0,4},{4,0},{1,5},{5,1},{2,6},{6,2},{3,7},{7,3},{8,12},{12,8},{9,1... | collective-permute-start | bytes 172040 | tf_op jit(solution)/shard_map/ppermute | solution.py:543
  17.0 17.0 %copy-start.12 = (bf16[1248,128]{1,0:T(8,128)(2,1)}, bf16[1248,128]{1,0:T(8,128)(2,1)S(1)}, u32[]{:S(2)}) copy-start(bf16[1248,128]{1,0:T(8,128)(2,1)S(1)} %get-tuple-element.27.far) | copy-start | bytes 958468
  17.0 20.3 %copy-start.7 = (bf16[1472,128]{1,0:T(8,128)(2,1)}, bf16[1472,128]{1,0:T(8,128)(2,1)S(1)}, u32[]{:S(2)}) copy-start(bf16[1472,128]{1,0:T(8,128)(2,1)S(1)} %get-tuple-element.30.near) | copy-start | bytes 1130500
  17.0 9.2 %collective-permute-start.1 = (bf16[1248,128]{1,0:T(8,128)(2,1)S(1)}, bf16[1248,128]{1,0:T(8,128)(2,1)S(1)}, u32[]{:S(2)}, u32[]{:S(2)}) collective-permute-start(bf16[1248,128]{1,0:T(8,128)(2,1)S(1)} %get-tuple-element.27.far), channel_id=1, source_target_pairs={{0,8},{8,16},{16,24},{1,9},{9,17},{17,25},{2,10},{10,18},{18,26},{... | collective-permute-start | bytes 958472 | tf_op jit(solution)/shard_map/ppermute | solution.py:549
  20.5 11.0 %collective-permute-start.2 = (bf16[1472,128]{1,0:T(8,128)(2,1)S(1)}, bf16[1472,128]{1,0:T(8,128)(2,1)S(1)}, u32[]{:S(2)}, u32[]{:S(2)}) collective-permute-start(bf16[1472,128]{1,0:T(8,128)(2,1)S(1)} %get-tuple-element.30.near), channel_id=1, source_target_pairs={{8,0},{16,8},{24,16},{9,1},{17,9},{25,17},{10,2},{18,10},{26,18},{... | collective-permute-start | bytes 1130504 | tf_op jit(solution)/shard_map/ppermute | solution.py:549
  26.2 6.6 %copy-start.14 = (bf16[1248,128]{1,0:T(8,128)(2,1)}, bf16[1248,128]{1,0:T(8,128)(2,1)S(1)}, u32[]{:S(2)}) copy-start(bf16[1248,128]{1,0:T(8,128)(2,1)S(1)} %collective-permute-done.1.near) | copy-start | bytes 958468
  26.2 11.1 %copy-start.5 = (bf16[3,3,3,128,128]{4,3,2,1,0:T(8,128)(2,1)S(1)}, bf16[3,3,3,128,128]{4,3,2,1,0:T(8,128)(2,1)}, u32[]{:S(2)}) copy-start(bf16[3,3,3,128,128]{4,3,2,1,0:T(8,128)(2,1)} %param.6) | copy-start | bytes 2654212
  31.5 5.7 %copy-start.9 = (bf16[1472,128]{1,0:T(8,128)(2,1)}, bf16[1472,128]{1,0:T(8,128)(2,1)S(1)}, u32[]{:S(2)}) copy-start(bf16[1472,128]{1,0:T(8,128)(2,1)S(1)} %collective-permute-done.2.far) | copy-start | bytes 1130500
  31.5 1.2 collective-permute-start.3
  33.9 8.2 %all-to-all-start.1 = ((bf16[4,80,128]{2,1,0:T(8,128)(2,1)}), bf16[4,80,128]{2,1,0:T(8,128)(2,1)S(1)}, u32[]{:S(2)}, u32[]{:S(2)}) async-start(bf16[4,80,128]{2,1,0:T(8,128)(2,1)} %shard_map.79), calls=%async_computation.1 | async-start | bytes 163840 | tf_op jit(solution)/shard_map/all_to_all | solution.py:653
  44.4 13.7 %collective-permute-start.4 = (bf16[1248,128]{1,0:T(8,128)(2,1)}, bf16[1248,128]{1,0:T(8,128)(2,1)S(1)}, u32[]{:S(2)}, u32[]{:S(2)}) collective-permute-start(bf16[1248,128]{1,0:T(8,128)(2,1)} %get-tuple-element.38.far.act), channel_id=1, source_target_pairs={{0,8},{8,16},{16,24},{1,9},{9,17},{17,25},{2,10},{10,18},{18,26},{... | collective-permute-start | bytes 958472 | tf_op jit(solution)/shard_map/ppermute | solution.py:549
  47.9 9.2 %all-to-all-start.2 = ((f32[8,8,128]{2,1,0:T(8,128)}), f32[8,8,128]{2,1,0:T(8,128)S(1)}, u32[]{:S(2)}, u32[]{:S(2)}) async-start(f32[8,8,128]{2,1,0:T(8,128)} %get-tuple-element.36), calls=%async_computation.2 | async-start | bytes 65536 | tf_op jit(solution)/shard_map/all_to_all | solution.py:670
  55.8 1.2 copy-start.16
  57.1 1.5 %copy-start.17 = (f32[3456,128]{1,0:T(8,128)S(1)}, f32[3456,128]{1,0:T(8,128)}, u32[]{:S(2)}) copy-start(f32[3456,128]{1,0:T(8,128)} %copy-done.16) | copy-start | bytes 5308420
  62.8 2.5 %collective-permute-start.6 = (bf16[3456,128]{1,0:T(8,128)(2,1)S(1)}, bf16[3456,128]{1,0:T(8,128)(2,1)S(1)}, u32[]{:S(2)}, u32[]{:S(2)}) collective-permute-start(bf16[3456,128]{1,0:T(8,128)(2,1)S(1)} %get-tuple-element.44), channel_id=1, source_target_pairs={{0,4},{4,0},{1,5},{5,1},{2,6},{6,2},{3,7},{7,3},{8,12},{12,8},{9,1... | collective-permute-start | bytes 2654216 | tf_op jit(solution)/shard_map/ppermute | solution.py:543
  82.2 18.1 %copy-start.1 = (bf16[2,16,32,128]{3,2,1,0:T(8,128)(2,1)S(1)}, bf16[2,16,32,128]{3,2,1,0:T(8,128)(2,1)}, u32[]{:S(2)}) copy-start(bf16[2,16,32,128]{3,2,1,0:T(8,128)(2,1)} %features.11) | copy-start | bytes 786436
  83.1 11.5 %all-to-all-start.4 = ((bf16[4,224,128]{2,1,0:T(8,128)(2,1)}), bf16[4,224,128]{2,1,0:T(8,128)(2,1)S(1)}, u32[]{:S(2)}, u32[]{:S(2)}) async-start(bf16[4,224,128]{2,1,0:T(8,128)(2,1)} %bitcast.5), calls=%async_computation.4 | async-start | bytes 458752 | tf_op jit(solution)/shard_map/all_to_all | solution.py:557
  86.5 13.8 %collective-permute-start.5 = (bf16[1248,128]{1,0:T(8,128)(2,1)S(1)}, bf16[1248,128]{1,0:T(8,128)(2,1)S(1)}, u32[]{:S(2)}, u32[]{:S(2)}) collective-permute-start(bf16[1248,128]{1,0:T(8,128)(2,1)S(1)} %shard_map.82.near.grad), channel_id=1, source_target_pairs={{8,0},{16,8},{24,16},{9,1},{17,9},{25,17},{10,2},{18,10},{26,18},{... | collective-permute-start | bytes 958472 | tf_op jit(solution)/shard_map/ppermute | solution.py:549
  95.3 9.9 %all-to-all-start.5 = ((bf16[4,224,128]{2,1,0:T(8,128)(2,1)}), bf16[4,224,128]{2,1,0:T(8,128)(2,1)S(1)}, u32[]{:S(2)}, u32[]{:S(2)}) async-start(bf16[4,224,128]{2,1,0:T(8,128)(2,1)} %broadcast_in_dim.4), calls=%async_computation.5 | async-start | bytes 458752 | tf_op jit(solution)/shard_map/all_to_all | solution.py:563
  102.1 1.2 collective-permute-start.7
  105.4 15.1 %copy-start.6 = (bf16[3,3,3,128,128]{4,3,2,1,0:T(8,128)(2,1)S(1)}, bf16[3,3,3,128,128]{4,3,2,1,0:T(8,128)(2,1)}, u32[]{:S(2)}) copy-start(bf16[3,3,3,128,128]{4,3,2,1,0:T(8,128)(2,1)} %param.6) | copy-start | bytes 2654212
  120.5 3.4 %copy-start.3 = (bf16[2,16,32,128]{3,2,1,0:T(8,128)(2,1)S(1)}, bf16[2,16,32,128]{3,2,1,0:T(8,128)(2,1)}, u32[]{:S(2)}) copy-start(bf16[2,16,32,128]{3,2,1,0:T(8,128)(2,1)} %out_grad.7) | copy-start | bytes 786436
  120.5 4.5 %collective-permute-start.8 = (bf16[3456,128]{1,0:T(8,128)(2,1)}, bf16[3456,128]{1,0:T(8,128)(2,1)}, u32[]{:S(2)}, u32[]{:S(2)}) collective-permute-start(bf16[3456,128]{1,0:T(8,128)(2,1)} %bitcast.7), channel_id=1, source_target_pairs={{0,4},{4,0},{1,5},{5,1},{2,6},{6,2},{3,7},{7,3},{8,12},{12,8},{9,1... | collective-permute-start | bytes 2654216 | tf_op jit(solution)/shard_map/ppermute | solution.py:543
  (7 other events, 6.8 us)

commit v4 on v3

--- a/solution.py
+++ b/solution.py
@@ -43,7 +43,7 @@
         return up(self.wide + 2, 8)
 
 
-def call(body, outs, args, scratch=(), smem=0, mib=16, flops=0):
+def call(body, outs, args, scratch=(), smem=0, mib=8, flops=0):
     specs = [pl.BlockSpec(memory_space=pltpu.SMEM)] * smem
     specs += [pl.BlockSpec(memory_space=pltpu.VMEM)] * (len(args) - smem)
     shapes = [jax.ShapeDtypeStruct(shape, dtype) for shape, dtype in outs]
@@ -549,20 +549,6 @@
     return lax.ppermute(values, "tm", pairs)
 
 
-def scatter_sum(values, axis):
-    peers = lax.axis_size(axis)
-    share = up(values.shape[0], 16 * peers) // peers
-    values = jnp.pad(values, ((0, share * peers - values.shape[0]), (0, 0)))
-    slots = values.reshape(peers, share, LANES).astype(BF16)
-    return lax.all_to_all(slots, axis, 0, 0).astype(F32).sum(0)
-
-
-def gather_shares(share, axis):
-    peers = lax.axis_size(axis)
-    slots = jnp.broadcast_to(share[None], (peers,) + share.shape)
-    return lax.all_to_all(slots, axis, 0, 0)
-
-
 def sum_parts(stat):
     high = lax.reduce_precision(stat, 8, 7)
     rest = stat - high
@@ -570,22 +556,64 @@
     return jnp.concatenate([high, middle, rest - middle], 0).astype(BF16)
 
 
-def summed_kernels(keep, give, sums, factor):
-    rows = keep.shape[0]
-    upper = lax.axis_index("row") == 0
-    keep = keep + row_swap(give).astype(F32)
-    by_col = scatter_sum(keep, "col")
-    by_tm = scatter_sum(by_col, "tm")
-    done = (by_tm * factor).astype(BF16)
-    done = gather_shares(done, "tm").reshape(-1, LANES)[: by_col.shape[0]]
-    parts = sum_parts(sums + row_swap(sums))
-    spare = -parts.shape[0] % 16
-    done = jnp.concatenate([done, jnp.pad(parts, ((0, spare), (0, 0)))], 0)
-    done = gather_shares(done, "col")
-    terms = done[:, by_col.shape[0] :]
-    done = done[:, : by_col.shape[0]].reshape(-1, LANES)[:rows]
-    other = row_swap(done)
-    return jnp.where(upper, done, other), jnp.where(upper, other, done), terms
+def total_of(got):
+    total = got[0].astype(F32)
+    for peer in range(1, got.shape[0]):
+        total = total + got[peer].astype(F32)
+    return total
+
+
+def shared_body(got, out, flat):
+    rows, share = got.shape[1], out.shape[1]
+    if flat.shape[0] > rows:
+        flat[rows:] = jnp.zeros((flat.shape[0] - rows, LANES), F32)
+    flat[:rows] = total_of(got)
+    for peer in range(out.shape[0]):
+        out[peer] = flat[peer * share : (peer + 1) * share].astype(BF16)
+
+
+def finished_body(factor, got, out):
+    total = (total_of(got) * factor).astype(BF16)
+    for peer in range(out.shape[0]):
+        out[peer] = total
+
+
+def placed_body(rows, place, mine, theirs, first, second, sems):
+    def move(one, two):
+        copies = []
+        for peer in range(mine.shape[0]):
+            for k, (source, target) in enumerate(((mine, one), (theirs, two))):
+                copies.append(
+                    pltpu.make_async_copy(
+                        source.at[peer, pl.ds(0, rows)],
+                        target.at[pl.ds(peer * rows, rows)],
+                        sems.at[k, peer],
+                    )
+                )
+        for copy in copies:
+            copy.start()
+        for copy in copies:
+            copy.wait()
+
+    @pl.when(place[0] == 0)
+    def _():
+        move(first, second)
+
+    @pl.when(place[0] != 0)
+    def _():
+        move(second, first)
+
+
+def placed(place, mine, theirs, rows, count):
+    anywhere = pl.BlockSpec(memory_space=pl.ANY)
+    return pl.pallas_call(
+        functools.partial(placed_body, rows),
+        out_shape=[jax.ShapeDtypeStruct((count, LANES), BF16)] * 2,
+        in_specs=[pl.BlockSpec(memory_space=pltpu.SMEM), anywhere, anywhere],
+        out_specs=[anywhere, anywhere],
+        scratch_shapes=[pltpu.SemaphoreType.DMA((2, mine.shape[0]))],
+        compiler_params=pltpu.CompilerParams(vmem_limit_bytes=1 << 20),
+    )(place, mine, theirs)
 
 
 def on_device(features, conv_first, conv_second, out_grad):
@@ -637,10 +665,9 @@
         [place, act_before, act_first, first],
         conv_scratch(size, 1, wide),
         smem=1,
-        mib=24,
+        mib=14,
         flops=work,
     )
-    pay, grad_after = lax.optimization_barrier((pay, grad_after))
     row_got = row_swap(pay)
     lines = up(FRAMES * size.stride(1) + PARTS, 16)
     (slots,) = call(
@@ -650,13 +677,14 @@
         [((2, lines, LANES), F32)],
         smem=1,
     )
+    slots, grad_after = lax.optimization_barrier((slots, grad_after))
     col_got = lax.all_to_all(slots, "col", 0, 0)
     (grad_act,) = call(
         part(grad_act_body, size),
         [((FRAMES, tall, broad, LANES), F32)],
         [grad, grad_after, second],
         conv_scratch(size, 2, up(wide + 2, 16)),
-        mib=32,
+        mib=16,
         flops=2 * work,
     )
     field = ((FRAMES, tall, broad, LANES), F32)
@@ -668,14 +696,13 @@
         smem=1,
     )
     got = lax.all_to_all(slots, ("row", "col"), 0, 0)
-    act_second_before = later(act_second, 1)
     turned = ((FRAMES * LANES, size.cells), BF16)
     (second_term,) = call(
         part(second_term_body, size),
         [(first.shape, F32)],
         [grad, grad_after, act_second],
         [*conv_scratch(size, 1, wide), turned],
-        mib=24,
+        mib=14,
         flops=work,
     )
     (hidden_grad,) = call(
@@ -685,23 +712,39 @@
         [frame],
         smem=1,
     )
-    hidden_grad, act_second_before = lax.optimization_barrier((hidden_grad, act_second_before))
-    hidden_after = later(hidden_grad, -1)
     keep, give = call(
         part(first_term_body, size),
         [(first.shape, F32), (first.shape, BF16)],
         [place, act_before, act_first, hidden_grad, second_term],
         [*conv_scratch(size, 1, wide), turned, (first.shape, F32)],
         smem=1,
-        mib=24,
+        mib=20,
         flops=work,
     )
+    give, late_grad, late_act = lax.optimization_barrier((give, hidden_grad, act_second))
+    hidden_after = later(late_grad, -1)
+    act_before = later(late_act, 1)
+
+    along = lax.axis_size("tm")
+    rows = first.shape[0]
+    keep = keep + row_swap(give).astype(F32)
+    by_col = rows // across
+    slots = lax.all_to_all(keep.reshape(across, by_col, LANES).astype(BF16), "col", 0, 0)
+    share = up(by_col, 16 * along) // along
+    slots, hidden_after, act_before = lax.optimization_barrier((slots, hidden_after, act_before))
+    (slots,) = call(
+        shared_body,
+        [((along, share, LANES), BF16)],
+        [slots],
+        [((along * share, LANES), F32)],
+    )
+    got = lax.all_to_all(slots, "tm", 0, 0)
     (result,) = call(
         part(result_body, size),
         [(features.shape, BF16)],
-        [act_second_before, act_second, second, features],
+        [act_before, act_second, second, features],
         conv_scratch(size, 1, wide),
-        mib=24,
+        mib=14,
         flops=work,
     )
     q, sums = call(
@@ -709,14 +752,21 @@
         [((FRAMES, size.cells, LANES), F32), stat],
         [hidden_grad, hidden_after, first, features, norm_first],
         conv_scratch(size, 1, wide),
-        mib=24,
+        mib=14,
         flops=work,
     )
-    first_grad, second_grad, terms = summed_kernels(keep, give, sums, factor)
+    got, result = lax.optimization_barrier((got, result))
+    (slots,) = call(part(finished_body, factor), [((along, share, LANES), BF16)], [got])
+    done = lax.all_to_all(slots, "tm", 0, 0).reshape(-1, LANES)[:by_col]
+    parts = sum_parts(sums + row_swap(sums))
+    parts = jnp.pad(parts, ((0, -parts.shape[0] % 16), (0, 0)))
+    done = jnp.concatenate([done, parts], 0)
+    mine = lax.all_to_all(jnp.broadcast_to(done[None], (across, *done.shape)), "col", 0, 0)
+    first_grad, second_grad = placed(place, mine, row_swap(mine), by_col, rows)
     (feature_grad,) = call(
         part(feature_grad_body, size, peers),
         [(features.shape, BF16)],
-        [features, out_grad, norm_first, q, terms],
+        [features, out_grad, norm_first, q, mine[:, by_col:]],
     )
     return (result, feature_grad, first_grad.reshape(taps), second_grad.reshape(taps))
 

time: 129 us -> 122 us (0.946)
  blocking collectives: 41.1 us -> 24.5 us
  starting transfers between devices: 24.2 us -> 32 us
  waiting for transfers between devices: 23.7 us -> 26.1 us
  other arithmetic: 3.29 us -> 1.19 us
  Pallas kernels: 23.4 us -> 24.7 us
    all_to_all x2 -> x1, blocking collectives: 30.7 us -> 14.2 us  [on_device(): lax.all_to_all(jnp.broadcast_to(done[None], (across, *done.shape)), 'col'...]
    all_to_all x2 -> x3, starting transfers between devices: 6.95 us -> 13.5 us  [the longest x1 5.95 us: on_device(): got = lax.all_to_all(slots, 'tm', 0, 0)]
    all_to_all x2 -> x3, waiting for transfers between devices: 8.65 us -> 5.7 us  [the longest x1 3.28 us: on_device(): got = lax.all_to_all(slots, 'tm', 0, 0)]
    ppermute x4, waiting for transfers between devices: 8.69 us -> 11.6 us  [later(): return lax.ppermute(values, 'tm', pairs)]
    select_n x1 -> x0, other arithmetic: 2.75 us -> none  [summed_kernels(): return (jnp.where(upper, done, other), jnp.where(upper, other, done), terms)]
    unnamed x36 -> x48, local copies, waits for them, and re-layouts: 8.49 us -> 10.9 us
    pallas_call x0 -> x1, Pallas kernels: none -> 1.81 us  [placed(): pl.pallas_call(functools.partial(placed_body, rows), out_shape=[jax.Shape...]
    ppermute x5, waiting for transfers between devices: 5.29 us -> 6.72 us  [row_swap(): return lax.ppermute(values, 'row', [(0, 1), (1, 0)])]
  transfers between devices with their start and end apart: 13 -> 14, of which waited for: 10 -> 12; matrix products, arithmetic and copies ran while one was open for 1% -> 0% of each run, Pallas kernels for 12% -> 11%
where the time goes in v4:
time: 122 us; the launch traced here: 121 us
  starting transfers between devices  32 us (26%)
  waiting for transfers between devices  26.1 us (21%)
  Pallas kernels  24.7 us (20%)
  blocking collectives  24.5 us (20%)
  local copies, waits for them, and re-layouts  11 us (9%)
    pallas_call x15, Pallas kernels, call(): pl.pallas_call(body, out_shape=shapes, in_specs=specs, out_specs=[pl.Bloc...  22.9 us
    all_to_all x1, blocking collectives, on_device(): lax.all_to_all(jnp.broadcast_to(done[None], (across, *done.shape)), 'col'...  14.2 us
    ppermute x4, waiting for transfers between devices, later(): return lax.ppermute(values, 'tm', pairs)  11.6 us
    unnamed x48, local copies, waits for them, and re-layouts  10.9 us
    ppermute x4, starting transfers between devices, later(): return lax.ppermute(values, 'tm', pairs)  10.7 us
    all_to_all x1, blocking collectives, on_device(): col_got = lax.all_to_all(slots, 'col', 0, 0)  10.4 us
    ppermute x5, waiting for transfers between devices, row_swap(): return lax.ppermute(values, 'row', [(0, 1), (1, 0)])  6.72 us
    all_to_all x1, starting transfers between devices, on_device(): got = lax.all_to_all(slots, 'tm', 0, 0)  5.95 us
  transfers between devices with their start and end apart: 14, of which 12 were waited for; matrix products, arithmetic and copies ran while one was open for 0% of the time, Pallas kernels for 11%

profile of v4, /device:TPU:0, one launch (start us, length us, event | category | flops | bytes accessed | tf_op | source)
XLA Modules:
  0.0 120.7 jit_solution(5514490637112842713)
XLA Ops:
  5.4 10.4 %all_to_all.35.col_got = bf16[4,176,128]{2,1,0:T(8,128)(2,1)S(1)} all-to-all(bf16[4,176,128]{2,1,0:T(8,128)(2,1)S(1)} %shard_map.76), channel_id=1, replica_groups=mesh['tm'=4,'row'=2,'col'=4] {'col'}, dimensions={0} | all-to-all | bytes 360448 | tf_op jit(solution)/shard_map/all_to_all | solution.py:649
  17.0 3.5 %collective-permute-start.1 = (bf16[1248,128]{1,0:T(8,128)(2,1)S(1)}, bf16[1248,128]{1,0:T(8,128)(2,1)S(1)}, u32[]{:S(2)}, u32[]{:S(2)}) collective-permute-start(bf16[1248,128]{1,0:T(8,128)(2,1)S(1)} %get-tuple-element.35.far), channel_id=1, source_target_pairs={{0,8},{8,16},{16,24},{1,9},{9,17},{17,25},{2,10},{10,18},{18,26},{... | collective-permute-start | bytes 958472 | tf_op jit(solution)/shard_map/ppermute | solution.py:549
  21.8 4.4 %collective-permute-done.1.near = bf16[1248,128]{1,0:T(8,128)(2,1)S(1)} collective-permute-done((bf16[1248,128]{1,0:T(8,128)(2,1)S(1)}, bf16[1248,128]{1,0:T(8,128)(2,1)S(1)}, u32[]{:S(2)}, u32[]{:S(2)}) %collective-permute-start.1) | collective-permute-done | bytes 319520 | tf_op jit(solution)/shard_map/ppermute | solution.py:549
  26.2 2.4 %shard_map.78 = (bf16[2,16,32,128]{3,2,1,0:T(8,128)(2,1)S(1)}, bf16[96,128]{1,0:T(8,128)(2,1)S(1)}, f32[8,128]{1,0:T(8,128)S(1)}) custom-call(s32[2]{0:T(128)S(1)} %pad_add_fusion.place, bf16[1248,128]{1,0:T(8,128)(2,1)S(1)} %collective-permute-done.1.near, bf16[1248,128]{1,0:T(8,128)(2,1)S(1)} %get-tuple-element.35.far, bf16[3456,128]{1,0:T(8,128)(2,1)S(1)} %bitcast.10), custom_call_target="tpu_custom_call" | custom-call | flops 905969664 | bytes 1814536 | tf_op jit(solution)/shard_map/pallas_call | solution.py:51
  31.5 3.3 %all-to-all-start.1 = ((bf16[4,80,128]{2,1,0:T(8,128)(2,1)}), bf16[4,80,128]{2,1,0:T(8,128)(2,1)S(1)}, u32[]{:S(2)}, u32[]{:S(2)}) async-start(bf16[4,80,128]{2,1,0:T(8,128)(2,1)} %shard_map.79), calls=%async_computation.1 | async-start | bytes 163840 | tf_op jit(solution)/shard_map/all_to_all | solution.py:681
  34.8 2.8 %shard_map.80.grad_act = f32[2,18,40,128]{3,2,1,0:T(8,128)S(1)} custom-call(bf16[1472,128]{1,0:T(8,128)(2,1)S(1)} %get-tuple-element.39.near, bf16[1472,128]{1,0:T(8,128)(2,1)S(1)} %collective-permute-done.3.far, bf16[3456,128]{1,0:T(8,128)(2,1)S(1)} %bitcast.8), custom_call_target="tpu_custom_call" | custom-call | flops 1811939328 | bytes 2375680 | tf_op jit(solution)/shard_map/pallas_call | solution.py:51
  37.6 2.1 %all-to-all-done.1.col_got = bf16[4,80,128]{2,1,0:T(8,128)(2,1)S(1)} async-done(((bf16[4,80,128]{2,1,0:T(8,128)(2,1)}), bf16[4,80,128]{2,1,0:T(8,128)(2,1)S(1)}, u32[]{:S(2)}, u32[]{:S(2)}) %all-to-all-start.1) | async-done | bytes 81952 | tf_op jit(solution)/shard_map/all_to_all | solution.py:681
  39.7 2.2 %shard_map.81 = (bf16[1248,128]{1,0:T(8,128)(2,1)S(1)}, f32[2,18,40,128]{3,2,1,0:T(8,128)S(1)}, f32[2,18,40,128]{3,2,1,0:T(8,128)S(1)}, f32[8,128]{1,0:T(8,128)S(1)}, f32[8,8,128]{2,1,0:T(8,128)}) custom-call(s32[2]{0:T(128)S(1)} %pad_add_fusion.place, bf16[2,16,32,128]{3,2,1,0:T(8,128)(2,1)S(1)} %get-tuple-element.36.hidden, ...), custom_call_target="tpu_custom_call" | custom-call | bytes 2936840 | tf_op jit(solution)/shard_map/pallas_call | solution.py:51
  42.6 3.3 %all-to-all-start.2 = ((f32[8,8,128]{2,1,0:T(8,128)}), f32[8,8,128]{2,1,0:T(8,128)S(1)}, u32[]{:S(2)}, u32[]{:S(2)}) async-start(f32[8,8,128]{2,1,0:T(8,128)} %get-tuple-element.44), calls=%async_computation.2 | async-start | bytes 65536 | tf_op jit(solution)/shard_map/all_to_all | solution.py:698
  48.9 1.6 %shard_map.83.second = f32[3456,128]{1,0:T(8,128)S(1)} custom-call(bf16[1472,128]{1,0:T(8,128)(2,1)S(1)} %copy-done.8, bf16[1472,128]{1,0:T(8,128)(2,1)S(1)} %copy-done.10, bf16[1248,128]{1,0:T(8,128)(2,1)S(1)} %copy-done.14), custom_call_target="tpu_custom_call" | custom-call | flops 905969664 | bytes 2842624 | tf_op jit(solution)/shard_map/pallas_call | solution.py:51
  54.3 2.3 %shard_map.84 = (f32[3456,128]{1,0:T(8,128)S(1)}, bf16[3456,128]{1,0:T(8,128)(2,1)S(1)}) custom-call(s32[2]{0:T(128)S(1)} %pad_add_fusion.place, bf16[1248,128]{1,0:T(8,128)(2,1)S(1)} %copy-done.17, bf16[1248,128]{1,0:T(8,128)(2,1)S(1)} %copy-done.12, bf16[1248,128]{1,0:T(8,128)(2,1)S(1)} %shard_map.82.grad.near, f32[3456,128]{1,0:T(8,128)S(1)} %copy-done.23), custom_call_target="tpu_custom_call" | custom-call | flops 905969664 | bytes 5382152 | tf_op jit(solution)/shard_map/pallas_call | solution.py:51
  57.0 2.1 %collective-permute-done.4 = bf16[3456,128]{1,0:T(8,128)(2,1)S(1)} collective-permute-done((bf16[3456,128]{1,0:T(8,128)(2,1)S(1)}, bf16[3456,128]{1,0:T(8,128)(2,1)S(1)}, u32[]{:S(2)}, u32[]{:S(2)}) %collective-permute-start.4) | collective-permute-done | bytes 884768 | tf_op jit(solution)/shard_map/ppermute | solution.py:543
  60.2 4.2 %all-to-all-start.3 = ((bf16[4,864,128]{2,1,0:T(8,128)(2,1)}), bf16[4,864,128]{2,1,0:T(8,128)(2,1)S(1)}, u32[]{:S(2)}, u32[]{:S(2)}) async-start(bf16[4,864,128]{2,1,0:T(8,128)(2,1)} %bitcast.12), calls=%async_computation.3 | async-start | bytes 1769472 | tf_op jit(solution)/shard_map/all_to_all | solution.py:732
  65.7 4.6 %collective-permute-start.6 = (bf16[1248,128]{1,0:T(8,128)(2,1)S(1)}, bf16[1248,128]{1,0:T(8,128)(2,1)S(1)}, u32[]{:S(2)}, u32[]{:S(2)}) collective-permute-start(bf16[1248,128]{1,0:T(8,128)(2,1)S(1)} %copy-done.15), channel_id=1, source_target_pairs={{0,8},{8,16},{16,24},{1,9},{9,17},{17,25},{2,10},{10,18},{18,26},{... | collective-permute-start | bytes 958472 | tf_op jit(solution)/shard_map/ppermute | solution.py:549
  70.3 5.6 %collective-permute-done.5.far = bf16[1248,128]{1,0:T(8,128)(2,1)S(1)} collective-permute-done((bf16[1248,128]{1,0:T(8,128)(2,1)S(1)}, bf16[1248,128]{1,0:T(8,128)(2,1)S(1)}, u32[]{:S(2)}, u32[]{:S(2)}) %collective-permute-start.5) | collective-permute-done | bytes 319520 | tf_op jit(solution)/shard_map/ppermute | solution.py:549
  78.6 6.0 %all-to-all-start.4 = ((bf16[4,224,128]{2,1,0:T(8,128)(2,1)}), bf16[4,224,128]{2,1,0:T(8,128)(2,1)S(1)}, u32[]{:S(2)}, u32[]{:S(2)}) async-start(bf16[4,224,128]{2,1,0:T(8,128)(2,1)} %shard_map.85), calls=%async_computation.4 | async-start | bytes 458752 | tf_op jit(solution)/shard_map/all_to_all | solution.py:741
  85.5 2.5 %shard_map.86 = bf16[2,16,32,128]{3,2,1,0:T(8,128)(2,1)} custom-call(bf16[1248,128]{1,0:T(8,128)(2,1)S(1)} %copy-done.21, bf16[1248,128]{1,0:T(8,128)(2,1)S(1)} %copy-done.15, bf16[3456,128]{1,0:T(8,128)(2,1)S(1)} %bitcast.9, bf16[2,16,32,128]{3,2,1,0:T(8,128)(2,1)S(1)} %copy-done.1), custom_call_target="tpu_custom_call" | custom-call | flops 905969664 | bytes 2048000 | tf_op jit(solution)/shard_map/pallas_call | solution.py:51
  88.0 3.3 %all-to-all-done.4.got = bf16[4,224,128]{2,1,0:T(8,128)(2,1)S(1)} async-done(((bf16[4,224,128]{2,1,0:T(8,128)(2,1)}), bf16[4,224,128]{2,1,0:T(8,128)(2,1)S(1)}, u32[]{:S(2)}, u32[]{:S(2)}) %all-to-all-start.4) | async-done | bytes 229408 | tf_op jit(solution)/shard_map/all_to_all | solution.py:741
  92.0 3.4 %all-to-all-start.5 = ((bf16[4,224,128]{2,1,0:T(8,128)(2,1)}), bf16[4,224,128]{2,1,0:T(8,128)(2,1)S(1)}, u32[]{:S(2)}, u32[]{:S(2)}) async-start(bf16[4,224,128]{2,1,0:T(8,128)(2,1)} %shard_map.88), calls=%async_computation.5 | async-start | bytes 458752 | tf_op jit(solution)/shard_map/all_to_all | solution.py:760
  96.4 1.8 %shard_map.87 = (f32[2,512,128]{2,1,0:T(8,128)S(1)}, f32[8,128]{1,0:T(8,128)S(1)}) custom-call(bf16[1248,128]{1,0:T(8,128)(2,1)S(1)} %shard_map.82.grad.near, bf16[1248,128]{1,0:T(8,128)(2,1)S(1)} %copy-done.19, bf16[3456,128]{1,0:T(8,128)(2,1)S(1)} %bitcast.11, bf16[2,16,32,128]{3,2,1,0:T(8,128)(2,1)S(1)} %copy-done.1, f32[8,128]{1,0:T(8,128)S(1)} %get-tuple-element.55.norm), custom_call_target="tpu_custom_call" | custom-call | flops 905969664 | bytes 2318336 | tf_op jit(solution)/shard_map/pallas_call | solution.py:51
  99.4 2.4 %all-to-all-done.5 = bf16[4,224,128]{2,1,0:T(8,128)(2,1)S(1)} async-done(((bf16[4,224,128]{2,1,0:T(8,128)(2,1)}), bf16[4,224,128]{2,1,0:T(8,128)(2,1)S(1)}, u32[]{:S(2)}, u32[]{:S(2)}) %all-to-all-start.5) | async-done | bytes 229408 | tf_op jit(solution)/shard_map/all_to_all | solution.py:760
  102.0 14.2 %all_to_all.36.mine = bf16[4,896,128]{2,1,0:T(8,128)(2,1)S(1)} all-to-all(bf16[4,896,128]{2,1,0:T(8,128)(2,1)S(1)} %broadcast_in_dim.2), channel_id=1, replica_groups=mesh['tm'=4,'row'=2,'col'=4] {'col'}, dimensions={0} | all-to-all | bytes 1835008 | tf_op jit(solution)/shard_map/all_to_all | solution.py:764
  117.2 1.4 %collective-permute-done.8.theirs = bf16[4,896,128]{2,1,0:T(8,128)(2,1)S(1)} collective-permute-done((bf16[4,896,128]{2,1,0:T(8,128)(2,1)S(1)}, bf16[4,896,128]{2,1,0:T(8,128)(2,1)S(1)}, u32[]{:S(2)}, u32[]{:S(2)}) %collective-permute-start.8) | collective-permute-done | bytes 917536 | tf_op jit(solution)/shard_map/ppermute | solution.py:543
  118.7 1.8 %shard_map.90 = (bf16[3456,128]{1,0:T(8,128)(2,1)}, bf16[3456,128]{1,0:T(8,128)(2,1)}) custom-call(s32[2]{0:T(128)S(1)} %pad_add_fusion.place, bf16[4,896,128]{2,1,0:T(8,128)(2,1)S(1)} %all_to_all.36.mine, bf16[4,896,128]{2,1,0:T(8,128)(2,1)S(1)} %collective-permute-done.8.theirs), custom_call_target="tpu_custom_call" | custom-call | tf_op jit(solution)/shard_map/pallas_call | solution.py:609
  (78 shorter events, 28.2 us)
Async XLA Ops:
  2.6 23.6 %copy-start.5 = (bf16[3,3,3,128,128]{4,3,2,1,0:T(8,128)(2,1)S(1)}, bf16[3,3,3,128,128]{4,3,2,1,0:T(8,128)(2,1)}, u32[]{:S(2)}) copy-start(bf16[3,3,3,128,128]{4,3,2,1,0:T(8,128)(2,1)} %param.5) | copy-start | bytes 2654212
  3.3 1.4 %collective-permute-start = (bf16[224,128]{1,0:T(8,128)(2,1)S(1)}, bf16[224,128]{1,0:T(8,128)(2,1)S(1)}, u32[]{:S(2)}, u32[]{:S(2)}) collective-permute-start(bf16[224,128]{1,0:T(8,128)(2,1)S(1)} %get-tuple-element.33), channel_id=1, source_target_pairs={{0,4},{4,0},{1,5},{5,1},{2,6},{6,2},{3,7},{7,3},{8,12},{12,8},{9,1... | collective-permute-start | bytes 172040 | tf_op jit(solution)/shard_map/ppermute | solution.py:543
  17.0 14.1 %copy-start.11 = (bf16[1248,128]{1,0:T(8,128)(2,1)}, bf16[1248,128]{1,0:T(8,128)(2,1)S(1)}, u32[]{:S(2)}) copy-start(bf16[1248,128]{1,0:T(8,128)(2,1)S(1)} %get-tuple-element.35.far) | copy-start | bytes 958468
  17.0 17.9 %copy-start.7 = (bf16[1472,128]{1,0:T(8,128)(2,1)}, bf16[1472,128]{1,0:T(8,128)(2,1)S(1)}, u32[]{:S(2)}) copy-start(bf16[1472,128]{1,0:T(8,128)(2,1)S(1)} %get-tuple-element.39.near) | copy-start | bytes 1130500
  17.0 9.2 %collective-permute-start.1 = (bf16[1248,128]{1,0:T(8,128)(2,1)S(1)}, bf16[1248,128]{1,0:T(8,128)(2,1)S(1)}, u32[]{:S(2)}, u32[]{:S(2)}) collective-permute-start(bf16[1248,128]{1,0:T(8,128)(2,1)S(1)} %get-tuple-element.35.far), channel_id=1, source_target_pairs={{0,8},{8,16},{16,24},{1,9},{9,17},{17,25},{2,10},{10,18},{18,26},{... | collective-permute-start | bytes 958472 | tf_op jit(solution)/shard_map/ppermute | solution.py:549
  20.5 11.0 %collective-permute-start.3 = (bf16[1472,128]{1,0:T(8,128)(2,1)S(1)}, bf16[1472,128]{1,0:T(8,128)(2,1)S(1)}, u32[]{:S(2)}, u32[]{:S(2)}) collective-permute-start(bf16[1472,128]{1,0:T(8,128)(2,1)S(1)} %get-tuple-element.39.near), channel_id=1, source_target_pairs={{8,0},{16,8},{24,16},{9,1},{17,9},{25,17},{10,2},{18,10},{26,18},{... | collective-permute-start | bytes 1130504 | tf_op jit(solution)/shard_map/ppermute | solution.py:549
  26.2 4.9 %copy-start.16 = (bf16[1248,128]{1,0:T(8,128)(2,1)}, bf16[1248,128]{1,0:T(8,128)(2,1)S(1)}, u32[]{:S(2)}) copy-start(bf16[1248,128]{1,0:T(8,128)(2,1)S(1)} %collective-permute-done.1.near) | copy-start | bytes 958468
  26.2 8.7 %copy-start.4 = (bf16[3,3,3,128,128]{4,3,2,1,0:T(8,128)(2,1)S(1)}, bf16[3,3,3,128,128]{4,3,2,1,0:T(8,128)(2,1)}, u32[]{:S(2)}) copy-start(bf16[3,3,3,128,128]{4,3,2,1,0:T(8,128)(2,1)} %param.6) | copy-start | bytes 2654212
  28.6 1.3 %collective-permute-start.2 = (bf16[96,128]{1,0:T(8,128)(2,1)S(1)}, bf16[96,128]{1,0:T(8,128)(2,1)S(1)}, u32[]{:S(2)}, u32[]{:S(2)}) collective-permute-start(bf16[96,128]{1,0:T(8,128)(2,1)S(1)} %get-tuple-element.37), channel_id=1, source_target_pairs={{0,4},{4,0},{1,5},{5,1},{2,6},{6,2},{3,7},{7,3},{8,12},{12,8},{9,1... | collective-permute-start | bytes 73736 | tf_op jit(solution)/shard_map/ppermute | solution.py:543
  31.5 6.1 %copy-start.9 = (bf16[1472,128]{1,0:T(8,128)(2,1)}, bf16[1472,128]{1,0:T(8,128)(2,1)S(1)}, u32[]{:S(2)}) copy-start(bf16[1472,128]{1,0:T(8,128)(2,1)S(1)} %collective-permute-done.3.far) | copy-start | bytes 1130500
  31.5 8.2 %all-to-all-start.1 = ((bf16[4,80,128]{2,1,0:T(8,128)(2,1)}), bf16[4,80,128]{2,1,0:T(8,128)(2,1)S(1)}, u32[]{:S(2)}, u32[]{:S(2)}) async-start(bf16[4,80,128]{2,1,0:T(8,128)(2,1)} %shard_map.79), calls=%async_computation.1 | async-start | bytes 163840 | tf_op jit(solution)/shard_map/all_to_all | solution.py:681
  42.6 9.2 %all-to-all-start.2 = ((f32[8,8,128]{2,1,0:T(8,128)}), f32[8,8,128]{2,1,0:T(8,128)S(1)}, u32[]{:S(2)}, u32[]{:S(2)}) async-start(f32[8,8,128]{2,1,0:T(8,128)} %get-tuple-element.44), calls=%async_computation.2 | async-start | bytes 65536 | tf_op jit(solution)/shard_map/all_to_all | solution.py:698
  56.6 2.5 %collective-permute-start.4 = (bf16[3456,128]{1,0:T(8,128)(2,1)S(1)}, bf16[3456,128]{1,0:T(8,128)(2,1)S(1)}, u32[]{:S(2)}, u32[]{:S(2)}) collective-permute-start(bf16[3456,128]{1,0:T(8,128)(2,1)S(1)} %get-tuple-element.49), channel_id=1, source_target_pairs={{0,4},{4,0},{1,5},{5,1},{2,6},{6,2},{3,7},{7,3},{8,12},{12,8},{9,1... | collective-permute-start | bytes 2654216 | tf_op jit(solution)/shard_map/ppermute | solution.py:543
  60.2 5.5 %copy-start.15 = (bf16[1248,128]{1,0:T(8,128)(2,1)S(1)}, bf16[1248,128]{1,0:T(8,128)(2,1)}, u32[]{:S(2)}) copy-start(bf16[1248,128]{1,0:T(8,128)(2,1)} %copy-done.13) | copy-start | bytes 958468
  60.2 24.4 %copy-start.1 = (bf16[2,16,32,128]{3,2,1,0:T(8,128)(2,1)S(1)}, bf16[2,16,32,128]{3,2,1,0:T(8,128)(2,1)}, u32[]{:S(2)}) copy-start(bf16[2,16,32,128]{3,2,1,0:T(8,128)(2,1)} %features.11) | copy-start | bytes 786436
  60.2 17.6 %all-to-all-start.3 = ((bf16[4,864,128]{2,1,0:T(8,128)(2,1)}), bf16[4,864,128]{2,1,0:T(8,128)(2,1)S(1)}, u32[]{:S(2)}, u32[]{:S(2)}) async-start(bf16[4,864,128]{2,1,0:T(8,128)(2,1)} %bitcast.12), calls=%async_computation.3 | async-start | bytes 1769472 | tf_op jit(solution)/shard_map/all_to_all | solution.py:732
  64.4 11.5 %collective-permute-start.5 = (bf16[1248,128]{1,0:T(8,128)(2,1)S(1)}, bf16[1248,128]{1,0:T(8,128)(2,1)S(1)}, u32[]{:S(2)}, u32[]{:S(2)}) collective-permute-start(bf16[1248,128]{1,0:T(8,128)(2,1)S(1)} %shard_map.82.grad.near), channel_id=1, source_target_pairs={{8,0},{16,8},{24,16},{9,1},{17,9},{25,17},{10,2},{18,10},{26,18},{... | collective-permute-start | bytes 958472 | tf_op jit(solution)/shard_map/ppermute | solution.py:549
  65.7 11.4 %collective-permute-start.6 = (bf16[1248,128]{1,0:T(8,128)(2,1)S(1)}, bf16[1248,128]{1,0:T(8,128)(2,1)S(1)}, u32[]{:S(2)}, u32[]{:S(2)}) collective-permute-start(bf16[1248,128]{1,0:T(8,128)(2,1)S(1)} %copy-done.15), channel_id=1, source_target_pairs={{0,8},{8,16},{16,24},{1,9},{9,17},{17,25},{2,10},{10,18},{18,26},{... | collective-permute-start | bytes 958472 | tf_op jit(solution)/shard_map/ppermute | solution.py:549
  78.6 12.7 %all-to-all-start.4 = ((bf16[4,224,128]{2,1,0:T(8,128)(2,1)}), bf16[4,224,128]{2,1,0:T(8,128)(2,1)S(1)}, u32[]{:S(2)}, u32[]{:S(2)}) async-start(bf16[4,224,128]{2,1,0:T(8,128)(2,1)} %shard_map.85), calls=%async_computation.4 | async-start | bytes 458752 | tf_op jit(solution)/shard_map/all_to_all | solution.py:741
  85.5 9.9 %copy-start.6 = (bf16[3,3,3,128,128]{4,3,2,1,0:T(8,128)(2,1)S(1)}, bf16[3,3,3,128,128]{4,3,2,1,0:T(8,128)(2,1)}, u32[]{:S(2)}) copy-start(bf16[3,3,3,128,128]{4,3,2,1,0:T(8,128)(2,1)} %param.5) | copy-start | bytes 2654212
  92.0 9.9 %all-to-all-start.5 = ((bf16[4,224,128]{2,1,0:T(8,128)(2,1)}), bf16[4,224,128]{2,1,0:T(8,128)(2,1)S(1)}, u32[]{:S(2)}, u32[]{:S(2)}) async-start(bf16[4,224,128]{2,1,0:T(8,128)(2,1)} %shard_map.88), calls=%async_computation.5 | async-start | bytes 458752 | tf_op jit(solution)/shard_map/all_to_all | solution.py:760
  98.2 1.2 %collective-permute-start.7 = (f32[8,128]{1,0:T(8,128)S(1)}, f32[8,128]{1,0:T(8,128)S(1)}, u32[]{:S(2)}, u32[]{:S(2)}) collective-permute-start(f32[8,128]{1,0:T(8,128)S(1)} %get-tuple-element.59), channel_id=1, source_target_pairs={{0,4},{4,0},{1,5},{5,1},{2,6},{6,2},{3,7},{7,3},{8,12},{12,8},{9,1... | collective-permute-start | bytes 12296 | tf_op jit(solution)/shard_map/ppermute | solution.py:543
  101.9 14.3 %copy-start.3 = (bf16[2,16,32,128]{3,2,1,0:T(8,128)(2,1)S(1)}, bf16[2,16,32,128]{3,2,1,0:T(8,128)(2,1)}, u32[]{:S(2)}) copy-start(bf16[2,16,32,128]{3,2,1,0:T(8,128)(2,1)} %out_grad.7) | copy-start | bytes 786436
  116.2 2.5 %collective-permute-start.8 = (bf16[4,896,128]{2,1,0:T(8,128)(2,1)S(1)}, bf16[4,896,128]{2,1,0:T(8,128)(2,1)S(1)}, u32[]{:S(2)}, u32[]{:S(2)}) collective-permute-start(bf16[4,896,128]{2,1,0:T(8,128)(2,1)S(1)} %all_to_all.36.mine), channel_id=1, source_target_pairs={{0,4},{4,0},{1,5},{5,1},{2,6},{6,2},{3,7},{7,3},{8,12},{12,8},{9,1... | collective-permute-start | bytes 2752520 | tf_op jit(solution)/shard_map/ppermute | solution.py:543
  (14 other events, 18.6 us)

commit v5 on v4

--- a/solution.py
+++ b/solution.py
@@ -43,20 +43,33 @@
         return up(self.wide + 2, 8)
 
 
-def call(body, outs, args, scratch=(), smem=0, mib=8, flops=0):
+def call(body, outs, args, scratch=(), smem=0, far=0, sems=0, mib=8, flops=0, beside=False, out_far=0):
     specs = [pl.BlockSpec(memory_space=pltpu.SMEM)] * smem
-    specs += [pl.BlockSpec(memory_space=pltpu.VMEM)] * (len(args) - smem)
+    specs += [pl.BlockSpec(memory_space=pltpu.VMEM)] * (len(args) - smem - far)
+    specs += [pl.BlockSpec(memory_space=pltpu.HBM)] * far
+    near = len(args) - far
+    args = [*args[:near], *(pltpu.with_memory_space_constraint(a, pltpu.HBM) for a in args[near:])]
+    scratches = [pltpu.VMEM(shape, dtype) for shape, dtype in scratch]
+    if sems:
+        scratches.append(pltpu.SemaphoreType.DMA((sems,)))
     shapes = [jax.ShapeDtypeStruct(shape, dtype) for shape, dtype in outs]
+    kept = len(outs) - out_far
     moved = sum(math.prod(a.shape) * a.dtype.itemsize for a in [*args, *shapes])
+    moved = 0 if beside else moved
     return pl.pallas_call(
         body,
-        out_shape=shapes,
+        out_shape=shapes[:kept] + [pltpu.HBM(o.shape, o.dtype) for o in shapes[kept:]],
         in_specs=specs,
-        out_specs=[pl.BlockSpec(memory_space=pltpu.VMEM)] * len(outs),
-        scratch_shapes=[pltpu.VMEM(shape, dtype) for shape, dtype in scratch],
+        out_specs=[pl.BlockSpec(memory_space=pltpu.VMEM)] * kept
+        + [pl.BlockSpec(memory_space=pltpu.HBM)] * out_far,
+        scratch_shapes=scratches,
         cost_estimate=pl.CostEstimate(flops=flops, bytes_accessed=moved, transcendentals=0),
         compiler_params=pltpu.CompilerParams(vmem_limit_bytes=mib << 20),
     )(*args)
+
+
+def logistic(values):
+    return 0.5 * jnp.tanh(0.5 * values) + 0.5
 
 
 def lane_totals(stat):
@@ -134,61 +147,80 @@
     return (row >= top) & (row < bottom) & (col >= left) & (col < right)
 
 
-def start_body(size, place, features, out_grad, pay, stats):
+def take_columns(size, arrays, flat):
+    flat[...] = jnp.zeros_like(flat)
+    at = 0
+    for array, rim in arrays:
+        for j in range(rim):
+            for frame in range(FRAMES):
+                for side, col in ((0, j), (1, size.wide - rim + j)):
+                    rows = array[frame, :, col : col + 1].astype(F32)
+                    rows = rows.reshape(size.high, LANES)
+                    flat[side, at + rim : at + rim + size.high] = rows
+                at += size.stride(rim)
+
+
+def columns_body(size, hidden, flat):
+    take_columns(size, ((hidden, 1),), flat)
+
+
+def start_body(
+    size, place, features_far, grad_far, pay, stats, flat, features, out_grad, sems
+):
     high, wide = size.high, size.wide
     upper = place[0] == 0
+    copies = [
+        pltpu.make_async_copy(source.at[f], target.at[f], sems.at[FRAMES * k + f])
+        for k, (source, target) in enumerate(((features_far, features), (grad_far, out_grad)))
+        for f in range(FRAMES)
+    ]
+    for copy in copies:
+        copy.start()
+    for copy in copies[:FRAMES]:
+        copy.wait()
     at = 0
     for frame in range(FRAMES):
         pay[at : at + wide] = jnp.where(upper, features[frame, high - 1], features[frame, 0])
         at += wide
+    found = measured([features[f].astype(F32).reshape(size.cells, LANES) for f in range(FRAMES)])
+    stats[...] = found
+    for copy in copies[FRAMES:]:
+        copy.wait()
     for frame in range(FRAMES):
         for row in range(2):
             edge = jnp.where(upper, out_grad[frame, high - 2 + row], out_grad[frame, row])
             pay[at : at + wide] = edge
             at += wide
-    found = measured([features[f].astype(F32).reshape(size.cells, LANES) for f in range(FRAMES)])
-    stats[...] = found
     fill = jnp.zeros((pay.shape[0] - at - PARTS, LANES), F32)
     pay[at:] = jnp.concatenate([split3(found), fill], 0).astype(BF16)
-
-
-def columns(own, top, bottom, col):
-    return jnp.concatenate([*[r[col : col + 1] for r in top], own[:, col], *[r[col : col + 1] for r in bottom]], 0)
-
-
-def slots_first_body(size, across, place, features, out_grad, got, stats, slots, flat):
+    take_columns(size, ((features, 1), (out_grad, 2)), flat)
+
+
+def slots_body(size, rims, across, place, flat, got, stats, slots, work):
     wide, high = size.wide, size.high
-    edge = got.shape[0]
-    flat[...] = jnp.zeros_like(flat)
-    at = 0
-    cols = {0: [], 1: []}
-    for frame in range(FRAMES):
-        rim = got[frame * wide : (frame + 1) * wide].astype(F32)
-        top, bottom = rim_rows(place, rim)
-        own = features[frame].astype(F32)
-        for side, col in ((0, 0), (1, wide - 1)):
-            flat[side, at : at + high + 2] = columns(own, [top], [bottom], col)
-        at += size.stride(1)
-    base = FRAMES * wide
-    for j in range(2):
-        for frame in range(FRAMES):
-            tops, bottoms = [], []
-            for row in range(2):
-                first = base + (frame * 2 + row) * wide
-                top, bottom = rim_rows(place, got[first : first + wide].astype(F32))
-                tops.append(top)
-                bottoms.append(bottom)
-            own = out_grad[frame].astype(F32)
-            for side, col in ((0, j), (1, wide - 2 + j)):
-                flat[side, at : at + high + 4] = columns(own, tops, bottoms, col)
-            at += size.stride(2)
-    first = 3 * FRAMES * wide
-    both = merged(stats[...], join3(got[first : first + PARTS]), size.cells)
-    parts = split3(both)
-    flat[0, at : at + PARTS] = parts
-    flat[1, at : at + PARTS] = parts
+    upper = place[0] == 0
+    work[...] = flat[...]
+    at = base = 0
+    for rim in rims:
+        for j in range(rim):
+            for frame in range(FRAMES):
+                for row in range(rim):
+                    start = base + (frame * rim + row) * wide
+                    for side, col in ((0, j), (1, wide - rim + j)):
+                        cell = start - start % 16 + 16 * ((start % 16 + col) // 16)
+                        tile = got[cell : cell + 16].astype(F32)
+                        edge = tile[start + col - cell : start + col - cell + 1]
+                        nothing = jnp.zeros_like(edge)
+                        top, bottom = at + row, at + rim + high + row
+                        work[side, top : top + 1] = jnp.where(upper, nothing, edge)
+                        work[side, bottom : bottom + 1] = jnp.where(upper, edge, nothing)
+                at += size.stride(rim)
+        base += FRAMES * rim * wide
+    parts = split3(merged(stats[...], join3(got[base : base + PARTS]), size.cells))
+    work[0, at : at + PARTS] = parts
+    work[1, at : at + PARTS] = parts
     for peer in range(across):
-        slots[peer] = jnp.where(peer > place[1], flat[1], flat[0]).astype(BF16)
+        slots[peer] = jnp.where(peer > place[1], work[1], work[0]).astype(BF16)
 
 
 def sides(place, across, got, first, count):
@@ -252,7 +284,7 @@
             frame,
         )
         normed = (frame[...] - found[f : f + 1][None]) * found[FRAMES + f : FRAMES + f + 1][None]
-        frame[...] = jnp.where(ok, normed * jax.nn.sigmoid(normed), 0.0)
+        frame[...] = jnp.where(ok, normed * logistic(normed), 0.0)
         left, right = put_frame(size, frame, f, act)
         lefts.append(left)
         rights.append(right)
@@ -369,37 +401,36 @@
         out[f] = sums[f].reshape(size.tall(), wo, LANES)[:, : size.broad()]
 
 
-def slots_second_body(size, across, place, hidden, got, stats, slots, flat):
-    wide, high = size.wide, size.high
-    flat[...] = jnp.zeros_like(flat)
-    at = 0
-    for frame in range(FRAMES):
-        top, bottom = rim_rows(place, got[frame * wide : (frame + 1) * wide].astype(F32))
-        own = hidden[frame].astype(F32)
-        for side, col in ((0, 0), (1, wide - 1)):
-            flat[side, at : at + high + 2] = columns(own, [top], [bottom], col)
-        at += size.stride(1)
-    first = FRAMES * wide
-    parts = split3(merged(stats[...], join3(got[first : first + PARTS]), size.cells))
-    flat[0, at : at + PARTS] = parts
-    flat[1, at : at + PARTS] = parts
-    for peer in range(across):
-        slots[peer] = jnp.where(peer > place[1], flat[1], flat[0]).astype(BF16)
-
-
-def act_second_body(
-    size, across, place, hidden, row_got, col_got, grad_act, act, q, z, norm, slots, frame
-):
+def sums_second_body(size, across, hidden, col_got, grad_act, norm, slots):
     high, wide = size.high, size.wide
-    step = size.stride(1)
-    at = FRAMES * step
+    at = FRAMES * size.stride(1)
     found = concluded(
         [join3(col_got[peer, at : at + PARTS]) for peer in range(across)], 2 * size.cells
     )
     norm[...] = found
+    firsts, seconds = [], []
+    for f in range(FRAMES):
+        own = hidden[f].astype(F32)
+        normed = (own - found[f : f + 1][None]) * found[FRAMES + f : FRAMES + f + 1][None]
+        sigmoid = logistic(normed)
+        grad = grad_act[f, 1 : high + 1, 1 : wide + 1]
+        grad = grad * sigmoid * (1.0 + normed * (1.0 - sigmoid))
+        grad, normed = grad.reshape(size.cells, LANES), normed.reshape(size.cells, LANES)
+        firsts.append(jnp.sum(grad, 0, keepdims=True))
+        seconds.append(jnp.sum(grad * normed, 0, keepdims=True))
+    sums = stat_block(firsts, seconds)
+    for peer in range(slots.shape[0]):
+        slots[peer] = sums
+
+
+def act_second_body(
+    size, across, place, hidden, row_got, col_got, grad_act, norm, act, q_far, z_far, frame, q, z, sems
+):
+    wide = size.wide
+    step = size.stride(1)
     left_all, right_all = sides(place, across, col_got, 0, FRAMES * step)
     ok = in_frame((size.tall(), size.broad(), LANES), place, across, size, 1)
-    lefts, rights, firsts, seconds = [], [], [], []
+    lefts, rights, copies = [], [], []
     frame[...] = jnp.zeros_like(frame)
     for f in range(FRAMES):
         top, bottom = rim_rows(place, row_got[f * wide : (f + 1) * wide].astype(F32))
@@ -412,28 +443,24 @@
             right_all[f * step : (f + 1) * step],
             frame,
         )
-        normed = (frame[...] - found[f : f + 1][None]) * found[FRAMES + f : FRAMES + f + 1][None]
-        sigmoid = jax.nn.sigmoid(normed)
+        normed = (frame[...] - norm[f : f + 1][None]) * norm[FRAMES + f : FRAMES + f + 1][None]
+        sigmoid = logistic(normed)
         frame[...] = jnp.where(ok, normed * sigmoid, 0.0)
         left, right = put_frame(size, frame, f, act)
         lefts.append(left)
         rights.append(right)
-        grad = grad_act[f] * sigmoid * (1.0 + normed * (1.0 - sigmoid))
         z[f] = normed
-        q[f] = grad
-        row = lax.broadcasted_iota(jnp.int32, grad.shape, 0)
-        col = lax.broadcasted_iota(jnp.int32, grad.shape, 1)
-        own = (row > 0) & (row <= high) & (col > 0) & (col <= wide)
-        inner = jnp.where(own, grad, 0.0)
-        firsts.append(jnp.sum(jnp.sum(inner, 0), 0, keepdims=True))
-        seconds.append(jnp.sum(jnp.sum(inner * normed, 0), 0, keepdims=True))
+        q[f] = grad_act[f] * sigmoid * (1.0 + normed * (1.0 - sigmoid))
+        for k, (source, target) in enumerate(((q, q_far), (z, z_far))):
+            copy = pltpu.make_async_copy(source.at[f], target.at[f], sems.at[2 * f + k])
+            copy.start()
+            copies.append(copy)
     put_sides(act, size.main(1), lefts + rights)
-    sums = stat_block(firsts, seconds)
-    for peer in range(slots.shape[0]):
-        slots[peer] = sums
-
-
-def hidden_grad_body(size, across, place, q, z, got, norm, out, frame):
+    for copy in copies:
+        copy.wait()
+
+
+def hidden_grad(size, across, place, q, z, got, norm, out, frame, arrive):
     peers = got.shape[0]
     total = got[0]
     for peer in range(1, peers):
@@ -444,6 +471,7 @@
     for f in range(FRAMES):
         first, second = means[f : f + 1][None], means[FRAMES + f : FRAMES + f + 1][None]
         inv = norm[FRAMES + f : FRAMES + f + 1][None]
+        arrive(f)
         frame[...] = jnp.where(ok, inv * (q[f] - first - z[f] * second), 0.0)
         left, right = put_frame(size, frame, f, out)
         lefts.append(left)
@@ -480,23 +508,73 @@
     )
 
 
-def second_term_body(size, near, far, act, out, x, frame, turned):
+def second_term_body(size, near, far, act, out_far, x, frame, turned, out, sems):
     spread_all(size, 2, 1, size.wide, near, far, x, frame)
     turned_cells(size, act, turned)
+    span = 3 * LANES
+    copies = []
     for b in range(3):
         for a, total in enumerate(tap_sums(x, turned, b)):
             for c in range(3):
                 tap = ((2 - a) * 3 + 2 - b) * 3 + 2 - c
                 out[tap * LANES : (tap + 1) * LANES] = total[:, c * LANES : (c + 1) * LANES]
-
-
-def first_term_body(size, place, near, far, grad, second, keep, give, x, frame, turned, both):
+            rows = pl.ds(((2 - a) * 3 + 2 - b) * span, span)
+            copy = pltpu.make_async_copy(out.at[rows], out_far.at[rows], sems.at[3 * b + a])
+            copy.start()
+            copies.append(copy)
+    for copy in copies:
+        copy.wait()
+
+
+def first_term_body(
+    size,
+    across,
+    place,
+    got,
+    norm,
+    q_far,
+    z_far,
+    near_far,
+    far_far,
+    second_far,
+    grad,
+    keep,
+    give,
+    x,
+    frame,
+    turned,
+    both,
+    near,
+    far,
+    second,
+    q,
+    z,
+    sems,
+):
+    pairs = [(q_far.at[f], q.at[f]) for f in range(FRAMES)]
+    pairs += [(z_far.at[f], z.at[f]) for f in range(FRAMES)]
+    pairs += [(near_far, near), (far_far, far), (second_far, second)]
+    copies = [
+        pltpu.make_async_copy(source, target, sems.at[k])
+        for k, (source, target) in enumerate(pairs)
+    ]
+    for k in (0, FRAMES, 1, FRAMES + 1, 2 * FRAMES, 2 * FRAMES + 1, 2 * FRAMES + 2):
+        copies[k].start()
+
+    def arrive(f):
+        copies[f].wait()
+        copies[FRAMES + f].wait()
+
+    hidden_grad(size, across, place, q, z, got, norm, grad, frame, arrive)
+    turned_cells(size, grad, turned)
+    copies[2 * FRAMES].wait()
+    copies[2 * FRAMES + 1].wait()
     spread_all(size, 1, 1, size.wide, near, far, x, frame)
-    turned_cells(size, grad, turned)
     for b in range(3):
         for a, total in enumerate(tap_sums(x, turned, b)):
             first = (a * 3 + b) * 3 * LANES
             both[first : first + 3 * LANES] = total.T
+    copies[2 * FRAMES + 2].wait()
     upper = place[0] == 0
     keep[...] = jnp.where(upper, both[...], second[...])
     give[...] = jnp.where(upper, second[...], both[...]).astype(BF16)
@@ -517,7 +595,7 @@
     for f in range(FRAMES):
         values = features[f].astype(F32).reshape(size.cells, LANES)
         normed = (values - norm[f : f + 1]) * norm[FRAMES + f : FRAMES + f + 1]
-        sigmoid = jax.nn.sigmoid(normed)
+        sigmoid = logistic(normed)
         grad = grads[f] * sigmoid * (1.0 + normed * (1.0 - sigmoid))
         q[f] = grad
         firsts.append(jnp.sum(grad, 0, keepdims=True))
@@ -634,16 +712,22 @@
     frame = ((tall, broad, LANES), F32)
 
     edge = up(3 * FRAMES * wide + PARTS, 16)
-    pay, stats = call(
-        part(start_body, size), [((edge, LANES), BF16), stat], [place, features, out_grad], smem=1
+    lines = up(FRAMES * size.stride(1) + 2 * FRAMES * size.stride(2) + PARTS, 16)
+    flat = ((2, lines, LANES), F32)
+    pay, stats, cols, features_near, grad_near = call(
+        part(start_body, size),
+        [((edge, LANES), BF16), stat, flat, (features.shape, BF16), (features.shape, BF16)],
+        [place, features, out_grad],
+        smem=1,
+        far=2,
+        sems=2 * FRAMES,
     )
     row_got = row_swap(pay)
-    lines = up(FRAMES * size.stride(1) + 2 * FRAMES * size.stride(2) + PARTS, 16)
     (slots,) = call(
-        part(slots_first_body, size, across),
+        part(slots_body, size, (1, 2), across),
         [((across, lines, LANES), BF16)],
-        [place, features, out_grad, row_got, stats],
-        [((2, lines, LANES), F32)],
+        [place, cols, row_got, stats],
+        [flat],
         smem=1,
     )
     col_got = lax.all_to_all(slots, "col", 0, 0)
@@ -651,7 +735,7 @@
     act_first, grad, norm_first = call(
         part(act_first_body, size, across),
         [block, ((size.rows(2), LANES), BF16), stat],
-        [place, features, out_grad, row_got, col_got],
+        [place, features_near, grad_near, row_got, col_got],
         [frame],
         smem=1,
     )
@@ -670,11 +754,13 @@
     )
     row_got = row_swap(pay)
     lines = up(FRAMES * size.stride(1) + PARTS, 16)
+    flat = ((2, lines, LANES), F32)
+    (cols,) = call(part(columns_body, size), [flat], [hidden])
     (slots,) = call(
-        part(slots_second_body, size, across),
+        part(slots_body, size, (1,), across),
         [((across, lines, LANES), BF16)],
-        [place, hidden, row_got, stats],
-        [((2, lines, LANES), F32)],
+        [place, cols, row_got, stats],
+        [flat],
         smem=1,
     )
     slots, grad_after = lax.optimization_barrier((slots, grad_after))
@@ -688,42 +774,56 @@
         flops=2 * work,
     )
     field = ((FRAMES, tall, broad, LANES), F32)
-    act_second, q, z, norm_second, slots = call(
+    norm_second, slots = call(
+        part(sums_second_body, size, across),
+        [stat, ((peers, STATS, LANES), F32)],
+        [hidden, col_got, grad_act],
+    )
+    got = lax.all_to_all(slots, ("row", "col"), 0, 0)
+    act_second, q, z = call(
         part(act_second_body, size, across),
-        [block, field, field, stat, ((peers, STATS, LANES), F32)],
-        [place, hidden, row_got, col_got, grad_act],
-        [frame],
+        [block, field, field],
+        [place, hidden, row_got, col_got, grad_act, norm_second],
+        [frame, field, field],
         smem=1,
-    )
-    got = lax.all_to_all(slots, ("row", "col"), 0, 0)
+        sems=2 * FRAMES,
+        beside=True,
+        out_far=2,
+    )
     turned = ((FRAMES * LANES, size.cells), BF16)
     (second_term,) = call(
         part(second_term_body, size),
         [(first.shape, F32)],
         [grad, grad_after, act_second],
-        [*conv_scratch(size, 1, wide), turned],
-        mib=14,
-        flops=work,
-    )
-    (hidden_grad,) = call(
-        part(hidden_grad_body, size, across),
-        [block],
-        [place, q, z, got, norm_second],
-        [frame],
+        [*conv_scratch(size, 1, wide), turned, (first.shape, F32)],
+        sems=9,
+        mib=16,
+        beside=True,
+        out_far=1,
+    )
+    grad_second, keep, give = call(
+        part(first_term_body, size, across),
+        [block, (first.shape, F32), (first.shape, BF16)],
+        [place, got, norm_second, q, z, act_before, act_first, second_term],
+        [
+            *conv_scratch(size, 1, wide),
+            turned,
+            (first.shape, F32),
+            block,
+            block,
+            (first.shape, F32),
+            field,
+            field,
+        ],
         smem=1,
-    )
-    keep, give = call(
-        part(first_term_body, size),
-        [(first.shape, F32), (first.shape, BF16)],
-        [place, act_before, act_first, hidden_grad, second_term],
-        [*conv_scratch(size, 1, wide), turned, (first.shape, F32)],
-        smem=1,
+        far=5,
+        sems=2 * FRAMES + 3,
         mib=20,
         flops=work,
     )
-    give, late_grad, late_act = lax.optimization_barrier((give, hidden_grad, act_second))
-    hidden_after = later(late_grad, -1)
-    act_before = later(late_act, 1)
+    give, late_grad, late_act = lax.optimization_barrier((give, grad_second, act_second))
+    act_second_before = later(late_act, 1)
+    grad_second_after = later(late_grad, -1)
 
     along = lax.axis_size("tm")
     rows = first.shape[0]
@@ -731,7 +831,6 @@
     by_col = rows // across
     slots = lax.all_to_all(keep.reshape(across, by_col, LANES).astype(BF16), "col", 0, 0)
     share = up(by_col, 16 * along) // along
-    slots, hidden_after, act_before = lax.optimization_barrier((slots, hidden_after, act_before))
     (slots,) = call(
         shared_body,
         [((along, share, LANES), BF16)],
@@ -742,7 +841,7 @@
     (result,) = call(
         part(result_body, size),
         [(features.shape, BF16)],
-        [act_before, act_second, second, features],
+        [act_second_before, act_second, second, features],
         conv_scratch(size, 1, wide),
         mib=14,
         flops=work,
@@ -750,7 +849,7 @@
     q, sums = call(
         part(back_first_body, size),
         [((FRAMES, size.cells, LANES), F32), stat],
-        [hidden_grad, hidden_after, first, features, norm_first],
+        [grad_second, grad_second_after, first, features, norm_first],
         conv_scratch(size, 1, wide),
         mib=14,
         flops=work,

time: 122 us -> 119 us (0.975)
  local copies, waits for them, and re-layouts: 11 us -> 1.33 us
  Pallas kernels: 24.7 us -> 28.8 us
  waiting for transfers between devices: 26.1 us -> 28.8 us
    unnamed x48 -> x14, local copies, waits for them, and re-layouts: 10.9 us -> 1.2 us
    all_to_all x1, waiting for transfers between devices: 0.01 us -> 8.29 us  [on_device(): lax.all_to_all(keep.reshape(across, by_col, LANES).astype(BF16), 'col', 0...]
    ppermute x4, waiting for transfers between devices: 11.6 us -> 5.71 us  [later(): return lax.ppermute(values, 'tm', pairs)]
    pallas_call x15 -> x16, Pallas kernels: 22.9 us -> 27 us  [call(): pl.pallas_call(body, out_shape=shapes[:kept] + [pltpu.HBM(o.shape, o.dtyp...]
    all_to_all x1, waiting for transfers between devices: 3.28 us -> 4.71 us  [on_device(): got = lax.all_to_all(slots, 'tm', 0, 0)]
  transfers between devices with their start and end apart: 14 -> 14, of which waited for: 12 -> 12; matrix products, arithmetic and copies ran while one was open for 0% -> 0% of each run, Pallas kernels for 11% -> 15%
where the time goes in v5:
time: 119 us; the launch traced here: 117 us
  starting transfers between devices  30.8 us (26%)
  Pallas kernels  28.8 us (24%)
  waiting for transfers between devices  28.8 us (24%)
  blocking collectives  24.8 us (21%)
  local copies, waits for them, and re-layouts  1.33 us (1%)
  other arithmetic  1.25 us (1%)
    pallas_call x16, Pallas kernels, call(): pl.pallas_call(body, out_shape=shapes[:kept] + [pltpu.HBM(o.shape, o.dtyp...  27 us
    all_to_all x1, blocking collectives, on_device(): lax.all_to_all(jnp.broadcast_to(done[None], (across, *done.shape)), 'col'...  14.4 us
    all_to_all x1, blocking collectives, on_device(): col_got = lax.all_to_all(slots, 'col', 0, 0)  10.4 us
    ppermute x4, starting transfers between devices, later(): return lax.ppermute(values, 'tm', pairs)  10.2 us
    all_to_all x1, waiting for transfers between devices, on_device(): lax.all_to_all(keep.reshape(across, by_col, LANES).astype(BF16), 'col', 0...  8.29 us
    ppermute x5, waiting for transfers between devices, row_swap(): return lax.ppermute(values, 'row', [(0, 1), (1, 0)])  6.65 us
    ppermute x4, waiting for transfers between devices, later(): return lax.ppermute(values, 'tm', pairs)  5.71 us
    all_to_all x1, starting transfers between devices, on_device(): got = lax.all_to_all(slots, 'tm', 0, 0)  5.29 us
  transfers between devices with their start and end apart: 14, of which 12 were waited for; matrix products, arithmetic and copies ran while one was open for 0% of the time, Pallas kernels for 15%

profile of v5, /device:TPU:0, one launch (start us, length us, event | category | flops | bytes accessed | tf_op | source)
XLA Modules:
  0.0 116.8 jit_solution(340420014223920377)
XLA Ops:
  0.7 1.8 %shard_map.75 = (bf16[224,128]{1,0:T(8,128)(2,1)S(1)}, f32[8,128]{1,0:T(8,128)S(1)}, f32[2,176,128]{2,1,0:T(8,128)S(1)}, bf16[2,16,32,128]{3,2,1,0:T(8,128)(2,1)S(1)}, bf16[2,16,32,128]{3,2,1,0:T(8,128)(2,1)S(1)}) custom-call(s32[2]{0:T(128)S(1)} %pad_add_fusion.place, bf16[2,16,32,128]{3,2,1,0:T(8,128)(2,1)} %features.5, bf16[2,16,32,128]{3,2,1,0:T(8,128)(2,1)} %out_grad.1), custom_call_target="tpu_custom_call" | custom-call | bytes 1290248 | tf_op jit(solution)/shard_map/pallas_call | solution.py:59
  4.5 10.4 %all_to_all.35.col_got = bf16[4,176,128]{2,1,0:T(8,128)(2,1)S(1)} all-to-all(bf16[4,176,128]{2,1,0:T(8,128)(2,1)S(1)} %shard_map.76), channel_id=1, replica_groups=mesh['tm'=4,'row'=2,'col'=4] {'col'}, dimensions={0} | all-to-all | bytes 360448 | tf_op jit(solution)/shard_map/all_to_all | solution.py:733
  16.2 3.5 %collective-permute-start.1 = (bf16[1248,128]{1,0:T(8,128)(2,1)S(1)}, bf16[1248,128]{1,0:T(8,128)(2,1)S(1)}, u32[]{:S(2)}, u32[]{:S(2)}) collective-permute-start(bf16[1248,128]{1,0:T(8,128)(2,1)S(1)} %get-tuple-element.39.far.far_far), channel_id=1, source_target_pairs={{0,8},{8,16},{16,24},{1,9},{9,17},{17,25},{2,10},{10,18},{18,26},{... | collective-permute-start | bytes 958472 | tf_op jit(solution)/shard_map/ppermute | solution.py:627
  21.0 4.4 %collective-permute-done.1.near.near_far = bf16[1248,128]{1,0:T(8,128)(2,1)S(1)} collective-permute-done((bf16[1248,128]{1,0:T(8,128)(2,1)S(1)}, bf16[1248,128]{1,0:T(8,128)(2,1)S(1)}, u32[]{:S(2)}, u32[]{:S(2)}) %collective-permute-start.1) | collective-permute-done | bytes 319520 | tf_op jit(solution)/shard_map/ppermute | solution.py:627
  25.3 2.4 %shard_map.78 = (bf16[2,16,32,128]{3,2,1,0:T(8,128)(2,1)S(1)}, bf16[96,128]{1,0:T(8,128)(2,1)S(1)}, f32[8,128]{1,0:T(8,128)S(1)}) custom-call(s32[2]{0:T(128)S(1)} %pad_add_fusion.place, bf16[1248,128]{1,0:T(8,128)(2,1)S(1)} %collective-permute-done.1.near.near_far, bf16[1248,128]{1,0:T(8,128)(2,1)S(1)} %get-tuple-element.39.far.far_far, ...), custom_call_target="tpu_custom_call" | custom-call | flops 905969664 | bytes 1814536 | tf_op jit(solution)/shard_map/pallas_call | solution.py:59
  30.7 3.3 %all-to-all-start.1 = ((bf16[4,80,128]{2,1,0:T(8,128)(2,1)}), bf16[4,80,128]{2,1,0:T(8,128)(2,1)S(1)}, u32[]{:S(2)}, u32[]{:S(2)}) async-start(bf16[4,80,128]{2,1,0:T(8,128)(2,1)} %shard_map.80), calls=%async_computation.1 | async-start | bytes 163840 | tf_op jit(solution)/shard_map/all_to_all | solution.py:767
  34.0 2.8 %shard_map.81.grad_act = f32[2,18,40,128]{3,2,1,0:T(8,128)S(1)} custom-call(bf16[1472,128]{1,0:T(8,128)(2,1)S(1)} %get-tuple-element.43.near, bf16[1472,128]{1,0:T(8,128)(2,1)S(1)} %collective-permute-done.3.far, bf16[3456,128]{1,0:T(8,128)(2,1)S(1)} %bitcast.8), custom_call_target="tpu_custom_call" | custom-call | flops 1811939328 | bytes 2375680 | tf_op jit(solution)/shard_map/pallas_call | solution.py:59
  36.8 2.0 %all-to-all-done.1.col_got = bf16[4,80,128]{2,1,0:T(8,128)(2,1)S(1)} async-done(((bf16[4,80,128]{2,1,0:T(8,128)(2,1)}), bf16[4,80,128]{2,1,0:T(8,128)(2,1)S(1)}, u32[]{:S(2)}, u32[]{:S(2)}) %all-to-all-start.1) | async-done | bytes 81952 | tf_op jit(solution)/shard_map/all_to_all | solution.py:767
  40.1 3.3 %all-to-all-start.2 = ((f32[8,8,128]{2,1,0:T(8,128)}), f32[8,8,128]{2,1,0:T(8,128)S(1)}, u32[]{:S(2)}, u32[]{:S(2)}) async-start(f32[8,8,128]{2,1,0:T(8,128)} %get-tuple-element.46), calls=%async_computation.2 | async-start | bytes 65536 | tf_op jit(solution)/shard_map/all_to_all | solution.py:782
  43.4 2.2 %shard_map.83 = (bf16[1248,128]{1,0:T(8,128)(2,1)S(1)}, f32[2,18,40,128]{3,2,1,0:T(8,128)}, f32[2,18,40,128]{3,2,1,0:T(8,128)}) custom-call(s32[2]{0:T(128)S(1)} %pad_add_fusion.place, bf16[2,16,32,128]{3,2,1,0:T(8,128)(2,1)S(1)} %get-tuple-element.40.hidden, bf16[96,128]{1,0:T(8,128)(2,1)S(1)} %collective-permute-done.2.got.row_got, ...), custom_call_target="tpu_custom_call" | custom-call | tf_op jit(solution)/shard_map/pallas_call | solution.py:59
  45.6 2.5 %shard_map.84.second_far = f32[3456,128]{1,0:T(8,128)} custom-call(bf16[1472,128]{1,0:T(8,128)(2,1)S(1)} %get-tuple-element.43.near, bf16[1472,128]{1,0:T(8,128)(2,1)S(1)} %collective-permute-done.3.far, bf16[1248,128]{1,0:T(8,128)(2,1)S(1)} %get-tuple-element.55.act.far), custom_call_target="tpu_custom_call" | custom-call | tf_op jit(solution)/shard_map/pallas_call | solution.py:59
  48.2 4.1 %shard_map.85 = (bf16[1248,128]{1,0:T(8,128)(2,1)S(1)}, f32[3456,128]{1,0:T(8,128)S(1)}, bf16[3456,128]{1,0:T(8,128)(2,1)S(1)}) custom-call(s32[2]{0:T(128)S(1)} %pad_add_fusion.place, f32[8,8,128]{2,1,0:T(8,128)S(1)} %all-to-all-done.2.got, f32[8,128]{1,0:T(8,128)S(1)} %get-tuple-element.47.norm, f32[2,18,40,128]{3,2,1,0:T(8,128)} %get-tuple-element.48.q_far, ...), custom_call_target="tpu_custom_call" | custom-call | flops 905969664 | bytes 6893576 | tf_op jit(solution)/shard_map/pallas_call | solution.py:59
  52.8 2.1 %collective-permute-done.4 = bf16[3456,128]{1,0:T(8,128)(2,1)S(1)} collective-permute-done((bf16[3456,128]{1,0:T(8,128)(2,1)S(1)}, bf16[3456,128]{1,0:T(8,128)(2,1)S(1)}, u32[]{:S(2)}, u32[]{:S(2)}) %collective-permute-start.4) | collective-permute-done | bytes 884768 | tf_op jit(solution)/shard_map/ppermute | solution.py:621
  56.0 4.2 %all-to-all-start.3 = ((bf16[4,864,128]{2,1,0:T(8,128)(2,1)}), bf16[4,864,128]{2,1,0:T(8,128)(2,1)S(1)}, u32[]{:S(2)}, u32[]{:S(2)}) async-start(bf16[4,864,128]{2,1,0:T(8,128)(2,1)} %bitcast.12), calls=%async_computation.3 | async-start | bytes 1769472 | tf_op jit(solution)/shard_map/all_to_all | solution.py:832
  60.2 3.9 %collective-permute-start.5 = (bf16[1248,128]{1,0:T(8,128)(2,1)S(1)}, bf16[1248,128]{1,0:T(8,128)(2,1)S(1)}, u32[]{:S(2)}, u32[]{:S(2)}) collective-permute-start(bf16[1248,128]{1,0:T(8,128)(2,1)S(1)} %get-tuple-element.55.act.far), channel_id=1, source_target_pairs={{0,8},{8,16},{16,24},{1,9},{9,17},{17,25},{2,10},{10,18},{18,26},{... | collective-permute-start | bytes 958472 | tf_op jit(solution)/shard_map/ppermute | solution.py:627
  64.1 8.3 %all-to-all-done.3.got = bf16[4,864,128]{2,1,0:T(8,128)(2,1)S(1)} async-done(((bf16[4,864,128]{2,1,0:T(8,128)(2,1)}), bf16[4,864,128]{2,1,0:T(8,128)(2,1)S(1)}, u32[]{:S(2)}, u32[]{:S(2)}) %all-to-all-start.3) | async-done | bytes 884768 | tf_op jit(solution)/shard_map/all_to_all | solution.py:832
  73.2 5.3 %all-to-all-start.4 = ((bf16[4,224,128]{2,1,0:T(8,128)(2,1)}), bf16[4,224,128]{2,1,0:T(8,128)(2,1)S(1)}, u32[]{:S(2)}, u32[]{:S(2)}) async-start(bf16[4,224,128]{2,1,0:T(8,128)(2,1)} %shard_map.86), calls=%async_computation.4 | async-start | bytes 458752 | tf_op jit(solution)/shard_map/all_to_all | solution.py:840
  78.4 1.5 %collective-permute-start.6 = (bf16[1248,128]{1,0:T(8,128)(2,1)S(1)}, bf16[1248,128]{1,0:T(8,128)(2,1)S(1)}, u32[]{:S(2)}, u32[]{:S(2)}) collective-permute-start(bf16[1248,128]{1,0:T(8,128)(2,1)S(1)} %get-tuple-element.58.near), channel_id=1, source_target_pairs={{8,0},{16,8},{24,16},{9,1},{17,9},{25,17},{10,2},{18,10},{26,18},{... | collective-permute-start | bytes 958472 | tf_op jit(solution)/shard_map/ppermute | solution.py:627
  79.9 2.5 %shard_map.87 = bf16[2,16,32,128]{3,2,1,0:T(8,128)(2,1)} custom-call(bf16[1248,128]{1,0:T(8,128)(2,1)S(1)} %collective-permute-done.5.near, bf16[1248,128]{1,0:T(8,128)(2,1)S(1)} %get-tuple-element.55.act.far, bf16[3456,128]{1,0:T(8,128)(2,1)S(1)} %bitcast.9, bf16[2,16,32,128]{3,2,1,0:T(8,128)(2,1)S(1)} %copy-done), custom_call_target="tpu_custom_call" | custom-call | flops 905969664 | bytes 2048000 | tf_op jit(solution)/shard_map/pallas_call | solution.py:59
  82.4 4.7 %all-to-all-done.4.got = bf16[4,224,128]{2,1,0:T(8,128)(2,1)S(1)} async-done(((bf16[4,224,128]{2,1,0:T(8,128)(2,1)}), bf16[4,224,128]{2,1,0:T(8,128)(2,1)S(1)}, u32[]{:S(2)}, u32[]{:S(2)}) %all-to-all-start.4) | async-done | bytes 229408 | tf_op jit(solution)/shard_map/all_to_all | solution.py:840
  87.8 3.4 %all-to-all-start.5 = ((bf16[4,224,128]{2,1,0:T(8,128)(2,1)}), bf16[4,224,128]{2,1,0:T(8,128)(2,1)S(1)}, u32[]{:S(2)}, u32[]{:S(2)}) async-start(bf16[4,224,128]{2,1,0:T(8,128)(2,1)} %shard_map.89), calls=%async_computation.5 | async-start | bytes 458752 | tf_op jit(solution)/shard_map/all_to_all | solution.py:859
  93.2 1.9 %shard_map.88 = (f32[2,512,128]{2,1,0:T(8,128)S(1)}, f32[8,128]{1,0:T(8,128)S(1)}) custom-call(bf16[1248,128]{1,0:T(8,128)(2,1)S(1)} %get-tuple-element.58.near, bf16[1248,128]{1,0:T(8,128)(2,1)S(1)} %collective-permute-done.6.far, bf16[3456,128]{1,0:T(8,128)(2,1)S(1)} %bitcast.11, bf16[2,16,32,128]{3,2,1,0:T(8,128)(2,1)S(1)} %copy-done, ...), custom_call_target="tpu_custom_call" | custom-call | flops 905969664 | bytes 2318336 | tf_op jit(solution)/shard_map/pallas_call | solution.py:59
  97.9 14.4 %all_to_all.36.mine = bf16[4,896,128]{2,1,0:T(8,128)(2,1)S(1)} all-to-all(bf16[4,896,128]{2,1,0:T(8,128)(2,1)S(1)} %broadcast_in_dim.2), channel_id=1, replica_groups=mesh['tm'=4,'row'=2,'col'=4] {'col'}, dimensions={0} | all-to-all | bytes 1835008 | tf_op jit(solution)/shard_map/all_to_all | solution.py:863
  114.8 1.8 %shard_map.91 = (bf16[3456,128]{1,0:T(8,128)(2,1)}, bf16[3456,128]{1,0:T(8,128)(2,1)}) custom-call(s32[2]{0:T(128)S(1)} %pad_add_fusion.place, bf16[4,896,128]{2,1,0:T(8,128)(2,1)S(1)} %all_to_all.36.mine, bf16[4,896,128]{2,1,0:T(8,128)(2,1)S(1)} %collective-permute-done.8.theirs), custom_call_target="tpu_custom_call" | custom-call | tf_op jit(solution)/shard_map/pallas_call | solution.py:687
  (45 shorter events, 19.2 us)
Async XLA Ops:
  0.6 24.7 %copy-start.5 = (bf16[3,3,3,128,128]{4,3,2,1,0:T(8,128)(2,1)S(1)}, bf16[3,3,3,128,128]{4,3,2,1,0:T(8,128)(2,1)}, u32[]{:S(2)}) copy-start(bf16[3,3,3,128,128]{4,3,2,1,0:T(8,128)(2,1)} %param.5) | copy-start | bytes 2654212
  2.5 1.4 %collective-permute-start = (bf16[224,128]{1,0:T(8,128)(2,1)S(1)}, bf16[224,128]{1,0:T(8,128)(2,1)S(1)}, u32[]{:S(2)}, u32[]{:S(2)}) collective-permute-start(bf16[224,128]{1,0:T(8,128)(2,1)S(1)} %get-tuple-element.36), channel_id=1, source_target_pairs={{0,4},{4,0},{1,5},{5,1},{2,6},{6,2},{3,7},{7,3},{8,12},{12,8},{9,1... | collective-permute-start | bytes 172040 | tf_op jit(solution)/shard_map/ppermute | solution.py:621
  16.2 11.7 %copy-start.2 = (bf16[1248,128]{1,0:T(8,128)(2,1)}, bf16[1248,128]{1,0:T(8,128)(2,1)S(1)}, u32[]{:S(2)}) copy-start(bf16[1248,128]{1,0:T(8,128)(2,1)S(1)} %get-tuple-element.39.far.far_far) | copy-start | bytes 958468
  16.2 9.2 %collective-permute-start.1 = (bf16[1248,128]{1,0:T(8,128)(2,1)S(1)}, bf16[1248,128]{1,0:T(8,128)(2,1)S(1)}, u32[]{:S(2)}, u32[]{:S(2)}) collective-permute-start(bf16[1248,128]{1,0:T(8,128)(2,1)S(1)} %get-tuple-element.39.far.far_far), channel_id=1, source_target_pairs={{0,8},{8,16},{16,24},{1,9},{9,17},{17,25},{2,10},{10,18},{18,26},{... | collective-permute-start | bytes 958472 | tf_op jit(solution)/shard_map/ppermute | solution.py:627
  19.7 11.0 %collective-permute-start.3 = (bf16[1472,128]{1,0:T(8,128)(2,1)S(1)}, bf16[1472,128]{1,0:T(8,128)(2,1)S(1)}, u32[]{:S(2)}, u32[]{:S(2)}) collective-permute-start(bf16[1472,128]{1,0:T(8,128)(2,1)S(1)} %get-tuple-element.43.near), channel_id=1, source_target_pairs={{8,0},{16,8},{24,16},{9,1},{17,9},{25,17},{10,2},{18,10},{26,18},{... | collective-permute-start | bytes 1130504 | tf_op jit(solution)/shard_map/ppermute | solution.py:627
  25.3 2.5 %copy-start.3 = (bf16[1248,128]{1,0:T(8,128)(2,1)}, bf16[1248,128]{1,0:T(8,128)(2,1)S(1)}, u32[]{:S(2)}) copy-start(bf16[1248,128]{1,0:T(8,128)(2,1)S(1)} %collective-permute-done.1.near.near_far) | copy-start | bytes 958468
  25.3 8.7 %copy-start.4 = (bf16[3,3,3,128,128]{4,3,2,1,0:T(8,128)(2,1)S(1)}, bf16[3,3,3,128,128]{4,3,2,1,0:T(8,128)(2,1)}, u32[]{:S(2)}) copy-start(bf16[3,3,3,128,128]{4,3,2,1,0:T(8,128)(2,1)} %param.6) | copy-start | bytes 2654212
  27.7 1.3 %collective-permute-start.2 = (bf16[96,128]{1,0:T(8,128)(2,1)S(1)}, bf16[96,128]{1,0:T(8,128)(2,1)S(1)}, u32[]{:S(2)}, u32[]{:S(2)}) collective-permute-start(bf16[96,128]{1,0:T(8,128)(2,1)S(1)} %get-tuple-element.41), channel_id=1, source_target_pairs={{0,4},{4,0},{1,5},{5,1},{2,6},{6,2},{3,7},{7,3},{8,12},{12,8},{9,1... | collective-permute-start | bytes 73736 | tf_op jit(solution)/shard_map/ppermute | solution.py:621
  30.7 8.2 %all-to-all-start.1 = ((bf16[4,80,128]{2,1,0:T(8,128)(2,1)}), bf16[4,80,128]{2,1,0:T(8,128)(2,1)S(1)}, u32[]{:S(2)}, u32[]{:S(2)}) async-start(bf16[4,80,128]{2,1,0:T(8,128)(2,1)} %shard_map.80), calls=%async_computation.1 | async-start | bytes 163840 | tf_op jit(solution)/shard_map/all_to_all | solution.py:767
  40.1 8.1 %all-to-all-start.2 = ((f32[8,8,128]{2,1,0:T(8,128)}), f32[8,8,128]{2,1,0:T(8,128)S(1)}, u32[]{:S(2)}, u32[]{:S(2)}) async-start(f32[8,8,128]{2,1,0:T(8,128)} %get-tuple-element.46), calls=%async_computation.2 | async-start | bytes 65536 | tf_op jit(solution)/shard_map/all_to_all | solution.py:782
  52.3 2.5 %collective-permute-start.4 = (bf16[3456,128]{1,0:T(8,128)(2,1)S(1)}, bf16[3456,128]{1,0:T(8,128)(2,1)S(1)}, u32[]{:S(2)}, u32[]{:S(2)}) collective-permute-start(bf16[3456,128]{1,0:T(8,128)(2,1)S(1)} %get-tuple-element.54), channel_id=1, source_target_pairs={{0,4},{4,0},{1,5},{5,1},{2,6},{6,2},{3,7},{7,3},{8,12},{12,8},{9,1... | collective-permute-start | bytes 2654216 | tf_op jit(solution)/shard_map/ppermute | solution.py:621
  56.0 23.9 %copy-start = (bf16[2,16,32,128]{3,2,1,0:T(8,128)(2,1)S(1)}, bf16[2,16,32,128]{3,2,1,0:T(8,128)(2,1)}, u32[]{:S(2)}) copy-start(bf16[2,16,32,128]{3,2,1,0:T(8,128)(2,1)} %features.5) | copy-start | bytes 786436
  56.0 16.4 %all-to-all-start.3 = ((bf16[4,864,128]{2,1,0:T(8,128)(2,1)}), bf16[4,864,128]{2,1,0:T(8,128)(2,1)S(1)}, u32[]{:S(2)}, u32[]{:S(2)}) async-start(bf16[4,864,128]{2,1,0:T(8,128)(2,1)} %bitcast.12), calls=%async_computation.3 | async-start | bytes 1769472 | tf_op jit(solution)/shard_map/all_to_all | solution.py:832
  60.2 19.8 %collective-permute-start.5 = (bf16[1248,128]{1,0:T(8,128)(2,1)S(1)}, bf16[1248,128]{1,0:T(8,128)(2,1)S(1)}, u32[]{:S(2)}, u32[]{:S(2)}) collective-permute-start(bf16[1248,128]{1,0:T(8,128)(2,1)S(1)} %get-tuple-element.55.act.far), channel_id=1, source_target_pairs={{0,8},{8,16},{16,24},{1,9},{9,17},{17,25},{2,10},{10,18},{18,26},{... | collective-permute-start | bytes 958472 | tf_op jit(solution)/shard_map/ppermute | solution.py:627
  73.2 13.9 %all-to-all-start.4 = ((bf16[4,224,128]{2,1,0:T(8,128)(2,1)}), bf16[4,224,128]{2,1,0:T(8,128)(2,1)S(1)}, u32[]{:S(2)}, u32[]{:S(2)}) async-start(bf16[4,224,128]{2,1,0:T(8,128)(2,1)} %shard_map.86), calls=%async_computation.4 | async-start | bytes 458752 | tf_op jit(solution)/shard_map/all_to_all | solution.py:840
  78.4 13.6 %collective-permute-start.6 = (bf16[1248,128]{1,0:T(8,128)(2,1)S(1)}, bf16[1248,128]{1,0:T(8,128)(2,1)S(1)}, u32[]{:S(2)}, u32[]{:S(2)}) collective-permute-start(bf16[1248,128]{1,0:T(8,128)(2,1)S(1)} %get-tuple-element.58.near), channel_id=1, source_target_pairs={{8,0},{16,8},{24,16},{9,1},{17,9},{25,17},{10,2},{18,10},{26,18},{... | collective-permute-start | bytes 958472 | tf_op jit(solution)/shard_map/ppermute | solution.py:627
  87.8 9.9 %all-to-all-start.5 = ((bf16[4,224,128]{2,1,0:T(8,128)(2,1)}), bf16[4,224,128]{2,1,0:T(8,128)(2,1)S(1)}, u32[]{:S(2)}, u32[]{:S(2)}) async-start(bf16[4,224,128]{2,1,0:T(8,128)(2,1)} %shard_map.89), calls=%async_computation.5 | async-start | bytes 458752 | tf_op jit(solution)/shard_map/all_to_all | solution.py:859
  92.1 1.2 %copy-start.6 = (bf16[3,3,3,128,128]{4,3,2,1,0:T(8,128)(2,1)S(1)}, bf16[3,3,3,128,128]{4,3,2,1,0:T(8,128)(2,1)}, u32[]{:S(2)}) copy-start(bf16[3,3,3,128,128]{4,3,2,1,0:T(8,128)(2,1)} %param.5) | copy-start | bytes 2654212
  95.1 1.2 %collective-permute-start.7 = (f32[8,128]{1,0:T(8,128)S(1)}, f32[8,128]{1,0:T(8,128)S(1)}, u32[]{:S(2)}, u32[]{:S(2)}) collective-permute-start(f32[8,128]{1,0:T(8,128)S(1)} %get-tuple-element.61), channel_id=1, source_target_pairs={{0,4},{4,0},{1,5},{5,1},{2,6},{6,2},{3,7},{7,3},{8,12},{12,8},{9,1... | collective-permute-start | bytes 12296 | tf_op jit(solution)/shard_map/ppermute | solution.py:621
  97.7 14.6 %copy-start.1 = (bf16[2,16,32,128]{3,2,1,0:T(8,128)(2,1)S(1)}, bf16[2,16,32,128]{3,2,1,0:T(8,128)(2,1)}, u32[]{:S(2)}) copy-start(bf16[2,16,32,128]{3,2,1,0:T(8,128)(2,1)} %out_grad.1) | copy-start | bytes 786436
  112.3 2.5 %collective-permute-start.8 = (bf16[4,896,128]{2,1,0:T(8,128)(2,1)S(1)}, bf16[4,896,128]{2,1,0:T(8,128)(2,1)S(1)}, u32[]{:S(2)}, u32[]{:S(2)}) collective-permute-start(bf16[4,896,128]{2,1,0:T(8,128)(2,1)S(1)} %all_to_all.36.mine), channel_id=1, source_target_pairs={{0,4},{4,0},{1,5},{5,1},{2,6},{6,2},{3,7},{7,3},{8,12},{12,8},{9,1... | collective-permute-start | bytes 2752520 | tf_op jit(solution)/shard_map/ppermute | solution.py:621

commit v6 on v5

--- a/solution.py
+++ b/solution.py
@@ -333,14 +333,13 @@
     filled = size.wide + 2 * trim
     if frame.shape[1] > filled:
         frame[:, filled:] = jnp.zeros((frame.shape[0], frame.shape[1] - filled, LANES), F32)
-    for f in range(2 * FRAMES):
+    for f in range(dst.shape[0]):
         block = near if f < FRAMES else far
         spread_columns(size, rim, trim, wo, block, f % FRAMES, dst, f, frame)
 
 
-def convolved(x, kernel, turned):
-    tall, wo = x.shape[1], x.shape[2]
-    ho = tall - 2
+def tap_dot(x, kernel, turned):
+    ho, wo = x.shape[1] - 2, x.shape[2]
     count = ho * wo
     span = 9 * LANES
 
@@ -359,27 +358,47 @@
 
     dims = (((1,), (1 if turned else 0,)), ((), ()))
 
-    def dot(one, two):
-        return lax.dot_general(one, two, dims, preferred_element_type=F32)
-
-    def pair(one, two):
-        return jnp.concatenate([one, two], 0 if turned else 1)
-
-    both = dot(cells(1), pair(taps(1), taps(0))) + dot(cells(2), pair(taps(2), taps(1)))
-    first = both[:, :LANES] + dot(cells(0), taps(0))
-    second = both[:, LANES:] + dot(cells(3), taps(2))
-    return first, second
-
-
-def conv_scratch(size, trim, wo):
+    def dot(f, *times):
+        weights = [taps(a) for a in times]
+        if len(weights) > 1:
+            weights = [jnp.concatenate(weights, 0 if turned else 1)]
+        return lax.dot_general(cells(f), weights[0], dims, preferred_element_type=F32)
+
+    return dot
+
+
+def convolved(x, kernel, turned):
+    dot = tap_dot(x, kernel, turned)
+    both = dot(1, 1, 0) + dot(2, 2, 1)
+    return both[:, :LANES] + dot(0, 0), both[:, LANES:] + dot(3, 2)
+
+
+def conv_scratch(size, trim, wo, frames=2 * FRAMES):
     tall = size.high + 2 * trim
-    return [((2 * FRAMES, tall, wo, 3 * LANES), BF16), ((tall, up(wo + 2, 8), LANES), F32)]
-
-
-def hidden_body(size, place, near, far, kernel, hidden, pay, stats, x, frame):
+    return [((frames, tall, wo, 3 * LANES), BF16), ((tall, up(wo + 2, 8), LANES), F32)]
+
+
+def hidden_own_body(size, own, kernel, sums, x_far, x, frame, sems):
+    spread_all(size, 1, 1, size.wide, own, None, x, frame)
+    copy = pltpu.make_async_copy(x, x_far, sems.at[0])
+    copy.start()
+    dot = tap_dot(x, kernel, False)
+    both = dot(0, 2, 1)
+    sums[0] = both[:, :LANES]
+    sums[1] = both[:, LANES:] + dot(1, 2)
+    copy.wait()
+
+
+def hidden_body(
+    size, place, before, sums, kernel, hidden, pay, stats, x_far, x, frame, sems
+):
     high, wide = size.high, size.wide
-    spread_all(size, 1, 1, wide, near, far, x, frame)
-    sums = convolved(x, kernel, False)
+    spread_all(size, 1, 1, wide, before, None, x, frame)
+    copy = pltpu.make_async_copy(x, x_far, sems.at[0])
+    copy.start()
+    dot = tap_dot(x, kernel, False)
+    both = dot(1, 1, 0)
+    sums = (sums[0] + both[:, :LANES] + dot(0, 0), sums[1] + both[:, LANES:])
     upper = place[0] == 0
     rounded = [s.astype(BF16) for s in sums]
     for f in range(FRAMES):
@@ -391,6 +410,7 @@
     at = FRAMES * wide
     fill = jnp.zeros((pay.shape[0] - at - PARTS, LANES), F32)
     pay[at:] = jnp.concatenate([split3(found), fill], 0).astype(BF16)
+    copy.wait()
 
 
 def grad_act_body(size, near, far, kernel, out, x, frame):
@@ -535,7 +555,7 @@
     q_far,
     z_far,
     near_far,
-    far_far,
+    own_far,
     second_far,
     grad,
     keep,
@@ -543,9 +563,6 @@
     x,
     frame,
     turned,
-    both,
-    near,
-    far,
     second,
     q,
     z,
@@ -553,7 +570,8 @@
 ):
     pairs = [(q_far.at[f], q.at[f]) for f in range(FRAMES)]
     pairs += [(z_far.at[f], z.at[f]) for f in range(FRAMES)]
-    pairs += [(near_far, near), (far_far, far), (second_far, second)]
+    pairs += [(near_far, x.at[pl.ds(0, FRAMES)]), (own_far, x.at[pl.ds(FRAMES, FRAMES)])]
+    pairs += [(second_far, second)]
     copies = [
         pltpu.make_async_copy(source, target, sems.at[k])
         for k, (source, target) in enumerate(pairs)
@@ -567,17 +585,15 @@
 
     hidden_grad(size, across, place, q, z, got, norm, grad, frame, arrive)
     turned_cells(size, grad, turned)
-    copies[2 * FRAMES].wait()
-    copies[2 * FRAMES + 1].wait()
-    spread_all(size, 1, 1, size.wide, near, far, x, frame)
+    for copy in copies[2 * FRAMES :]:
+        copy.wait()
+    upper = place[0] == 0
     for b in range(3):
         for a, total in enumerate(tap_sums(x, turned, b)):
-            first = (a * 3 + b) * 3 * LANES
-            both[first : first + 3 * LANES] = total.T
-    copies[2 * FRAMES + 2].wait()
-    upper = place[0] == 0
-    keep[...] = jnp.where(upper, both[...], second[...])
-    give[...] = jnp.where(upper, second[...], both[...]).astype(BF16)
+            rows = slice((a * 3 + b) * 3 * LANES, (a * 3 + b + 1) * 3 * LANES)
+            one, two = total.T, second[rows]
+            keep[rows] = jnp.where(upper, one, two)
+            give[rows] = jnp.where(upper, two, one).astype(BF16)
 
 
 def result_body(size, near, far, kernel, features, out, x, frame):
@@ -641,6 +657,13 @@
     return total
 
 
+def joined_body(keep, got, out):
+    share = out.shape[1]
+    for peer in range(out.shape[0]):
+        rows = slice(peer * share, (peer + 1) * share)
+        out[peer] = (keep[rows] + got[rows].astype(F32)).astype(BF16)
+
+
 def shared_body(got, out, flat):
     rows, share = got.shape[1], out.shape[1]
     if flat.shape[0] > rows:
@@ -656,42 +679,42 @@
         out[peer] = total
 
 
-def placed_body(rows, place, mine, theirs, first, second, sems):
-    def move(one, two):
-        copies = []
-        for peer in range(mine.shape[0]):
-            for k, (source, target) in enumerate(((mine, one), (theirs, two))):
-                copies.append(
-                    pltpu.make_async_copy(
-                        source.at[peer, pl.ds(0, rows)],
-                        target.at[pl.ds(peer * rows, rows)],
-                        sems.at[k, peer],
-                    )
-                )
+def placed_body(rows, swapped, *refs):
+    place, block, first, second, sems = refs[0], refs[1], *refs[-3:]
+
+    def move(target):
+        copies = [
+            pltpu.make_async_copy(
+                block.at[peer, pl.ds(0, rows)], target.at[pl.ds(peer * rows, rows)], sems.at[peer]
+            )
+            for peer in range(block.shape[0])
+        ]
         for copy in copies:
             copy.start()
         for copy in copies:
             copy.wait()
 
-    @pl.when(place[0] == 0)
+    @pl.when(place[0] == swapped)
     def _():
-        move(first, second)
-
-    @pl.when(place[0] != 0)
+        move(first)
+
+    @pl.when(place[0] != swapped)
     def _():
-        move(second, first)
-
-
-def placed(place, mine, theirs, rows, count):
+        move(second)
+
+
+def placed(place, block, swapped, rows, so_far):
     anywhere = pl.BlockSpec(memory_space=pl.ANY)
+    shape = (rows * block.shape[0], LANES)
     return pl.pallas_call(
-        functools.partial(placed_body, rows),
-        out_shape=[jax.ShapeDtypeStruct((count, LANES), BF16)] * 2,
-        in_specs=[pl.BlockSpec(memory_space=pltpu.SMEM), anywhere, anywhere],
+        functools.partial(placed_body, rows, swapped),
+        out_shape=[jax.ShapeDtypeStruct(shape, BF16)] * 2,
+        in_specs=[pl.BlockSpec(memory_space=pltpu.SMEM)] + [anywhere] * (1 + len(so_far)),
         out_specs=[anywhere, anywhere],
-        scratch_shapes=[pltpu.SemaphoreType.DMA((2, mine.shape[0]))],
+        input_output_aliases={2 + k: k for k in range(len(so_far))},
+        scratch_shapes=[pltpu.SemaphoreType.DMA((block.shape[0],))],
         compiler_params=pltpu.CompilerParams(vmem_limit_bytes=1 << 20),
-    )(place, mine, theirs)
+    )(place, block, *so_far)
 
 
 def on_device(features, conv_first, conv_second, out_grad):
@@ -743,14 +766,27 @@
     grad_after = later(grad, -1)
 
     edge = up(FRAMES * wide + PARTS, 16)
-    hidden, pay, stats = call(
+    halves = ((FRAMES, tall, wide, 3 * LANES), BF16)
+    sums, x_own = call(
+        part(hidden_own_body, size),
+        [((FRAMES, size.cells, LANES), F32), halves],
+        [act_first, first],
+        conv_scratch(size, 1, wide, FRAMES),
+        sems=1,
+        mib=12,
+        flops=work // 2,
+        out_far=1,
+    )
+    hidden, pay, stats, x_before = call(
         part(hidden_body, size),
-        [(features.shape, BF16), ((edge, LANES), BF16), stat],
-        [place, act_before, act_first, first],
-        conv_scratch(size, 1, wide),
+        [(features.shape, BF16), ((edge, LANES), BF16), stat, halves],
+        [place, act_before, sums, first],
+        conv_scratch(size, 1, wide, FRAMES),
         smem=1,
-        mib=14,
-        flops=work,
+        sems=1,
+        mib=12,
+        flops=work // 2,
+        out_far=1,
     )
     row_got = row_swap(pay)
     lines = up(FRAMES * size.stride(1) + PARTS, 16)
@@ -804,17 +840,8 @@
     grad_second, keep, give = call(
         part(first_term_body, size, across),
         [block, (first.shape, F32), (first.shape, BF16)],
-        [place, got, norm_second, q, z, act_before, act_first, second_term],
-        [
-            *conv_scratch(size, 1, wide),
-            turned,
-            (first.shape, F32),
-            block,
-            block,
-            (first.shape, F32),
-            field,
-            field,
-        ],
+        [place, got, norm_second, q, z, x_before, x_own, second_term],
+        [*conv_scratch(size, 1, wide), turned, (first.shape, F32), field, field],
         smem=1,
         far=5,
         sems=2 * FRAMES + 3,
@@ -827,9 +854,10 @@
 
     along = lax.axis_size("tm")
     rows = first.shape[0]
-    keep = keep + row_swap(give).astype(F32)
     by_col = rows // across
-    slots = lax.all_to_all(keep.reshape(across, by_col, LANES).astype(BF16), "col", 0, 0)
+    (slots,) = call(joined_body, [((across, by_col, LANES), BF16)], [keep, row_swap(give)])
+    slots = lax.all_to_all(slots, "col", 0, 0)
+    slots, grad_second_after = lax.optimization_barrier((slots, grad_second_after))
     share = up(by_col, 16 * along) // along
     (slots,) = call(
         shared_body,
@@ -861,7 +889,9 @@
     parts = jnp.pad(parts, ((0, -parts.shape[0] % 16), (0, 0)))
     done = jnp.concatenate([done, parts], 0)
     mine = lax.all_to_all(jnp.broadcast_to(done[None], (across, *done.shape)), "col", 0, 0)
-    first_grad, second_grad = placed(place, mine, row_swap(mine), by_col, rows)
+    theirs = row_swap(mine)
+    so_far = placed(place, mine, 0, by_col, [])
+    first_grad, second_grad = placed(place, theirs, 1, by_col, so_far)
     (feature_grad,) = call(
         part(feature_grad_body, size, peers),
         [(features.shape, BF16)],

time: 119 us -> 115 us (0.966)
  waiting for transfers between devices: 28.8 us -> 23.4 us
  Pallas kernels: 28.8 us -> 32.8 us
  blocking collectives: 24.8 us -> 22.7 us
    all_to_all x1, waiting for transfers between devices: 8.29 us -> 0.78 us  [on_device(): slots = lax.all_to_all(slots, 'col', 0, 0)]
    ppermute x4, waiting for transfers between devices: 5.71 us -> 8.87 us  [later(): return lax.ppermute(values, 'tm', pairs)]
    pallas_call x16 -> x18, Pallas kernels: 27 us -> 29.8 us  [call(): pl.pallas_call(body, out_shape=shapes[:kept] + [pltpu.HBM(o.shape, o.dtyp...]
    all_to_all x1, waiting for transfers between devices: 1.35 us -> 3.4 us  [on_device(): done = lax.all_to_all(slots, 'tm', 0, 0).reshape(-1, LANES)[:by_col]]
    all_to_all x1, blocking collectives: 14.4 us -> 12.4 us  [on_device(): lax.all_to_all(jnp.broadcast_to(done[None], (across, *done.shape)), 'col'...]
    ppermute x5, waiting for transfers between devices: 6.65 us -> 5.24 us  [row_swap(): return lax.ppermute(values, 'row', [(0, 1), (1, 0)])]
    pallas_call x1 -> x2, Pallas kernels: 1.81 us -> 2.98 us  [placed(): pl.pallas_call(functools.partial(placed_body, rows, swapped), out_shape=[...]
  transfers between devices with their start and end apart: 14 -> 14, of which waited for: 12 -> 11; matrix products, arithmetic and copies ran while one was open for 0% -> 0% of each run, Pallas kernels for 15% -> 18%
where the time goes in v6:
time: 115 us; the launch traced here: 114 us
  Pallas kernels  32.8 us (29%)
  starting transfers between devices  31.2 us (27%)
  waiting for transfers between devices  23.4 us (20%)
  blocking collectives  22.7 us (20%)
  local copies, waits for them, and re-layouts  2.48 us (2%)
    pallas_call x18, Pallas kernels, call(): pl.pallas_call(body, out_shape=shapes[:kept] + [pltpu.HBM(o.shape, o.dtyp...  29.8 us
    all_to_all x1, blocking collectives, on_device(): lax.all_to_all(jnp.broadcast_to(done[None], (across, *done.shape)), 'col'...  12.4 us
    ppermute x4, starting transfers between devices, later(): return lax.ppermute(values, 'tm', pairs)  10.6 us
    all_to_all x1, blocking collectives, on_device(): col_got = lax.all_to_all(slots, 'col', 0, 0)  10.4 us
    ppermute x4, waiting for transfers between devices, later(): return lax.ppermute(values, 'tm', pairs)  8.87 us
    all_to_all x1, starting transfers between devices, on_device(): got = lax.all_to_all(slots, 'tm', 0, 0)  5.25 us
    ppermute x5, waiting for transfers between devices, row_swap(): return lax.ppermute(values, 'row', [(0, 1), (1, 0)])  5.24 us
    all_to_all x1, starting transfers between devices, on_device(): slots = lax.all_to_all(slots, 'col', 0, 0)  4.19 us
  transfers between devices with their start and end apart: 14, of which 11 were waited for; matrix products, arithmetic and copies ran while one was open for 0% of the time, Pallas kernels for 18%

profile of v6, /device:TPU:0, one launch (start us, length us, event | category | flops | bytes accessed | tf_op | source)
XLA Modules:
  0.0 113.8 jit_solution(16076553661015450643)
XLA Ops:
  0.7 1.8 %shard_map.75 = (bf16[224,128]{1,0:T(8,128)(2,1)S(1)}, f32[8,128]{1,0:T(8,128)S(1)}, f32[2,176,128]{2,1,0:T(8,128)S(1)}, bf16[2,16,32,128]{3,2,1,0:T(8,128)(2,1)S(1)}, bf16[2,16,32,128]{3,2,1,0:T(8,128)(2,1)S(1)}) custom-call(s32[2]{0:T(128)S(1)} %pad_add_fusion.place.refs_0_, bf16[2,16,32,128]{3,2,1,0:T(8,128)(2,1)} %features.5, ...), custom_call_target="tpu_custom_call" | custom-call | bytes 1290248 | tf_op jit(solution)/shard_map/pallas_call | solution.py:59
  4.5 10.4 %all_to_all.35.col_got = bf16[4,176,128]{2,1,0:T(8,128)(2,1)S(1)} all-to-all(bf16[4,176,128]{2,1,0:T(8,128)(2,1)S(1)} %shard_map.76), channel_id=1, replica_groups=mesh['tm'=4,'row'=2,'col'=4] {'col'}, dimensions={0} | all-to-all | bytes 360448 | tf_op jit(solution)/shard_map/all_to_all | solution.py:756
  16.1 3.5 %collective-permute-start.1 = (bf16[1248,128]{1,0:T(8,128)(2,1)S(1)}, bf16[1248,128]{1,0:T(8,128)(2,1)S(1)}, u32[]{:S(2)}, u32[]{:S(2)}) collective-permute-start(bf16[1248,128]{1,0:T(8,128)(2,1)S(1)} %get-tuple-element.46.own), channel_id=1, source_target_pairs={{0,8},{8,16},{16,24},{1,9},{9,17},{17,25},{2,10},{10,18},{18,26},{... | collective-permute-start | bytes 958472 | tf_op jit(solution)/shard_map/ppermute | solution.py:643
  21.0 1.6 %shard_map.78 = (f32[2,512,128]{2,1,0:T(8,128)S(1)}, bf16[2,18,32,384]{3,2,1,0:T(8,128)(2,1)}) custom-call(bf16[1248,128]{1,0:T(8,128)(2,1)S(1)} %get-tuple-element.46.own, bf16[3456,128]{1,0:T(8,128)(2,1)S(1)} %bitcast.7), custom_call_target="tpu_custom_call" | custom-call | flops 452984832 | bytes 2613248 | tf_op jit(solution)/shard_map/pallas_call | solution.py:59
  22.5 2.8 %collective-permute-done.1.before = bf16[1248,128]{1,0:T(8,128)(2,1)S(1)} collective-permute-done((bf16[1248,128]{1,0:T(8,128)(2,1)S(1)}, bf16[1248,128]{1,0:T(8,128)(2,1)S(1)}, u32[]{:S(2)}, u32[]{:S(2)}) %collective-permute-start.1) | collective-permute-done | bytes 319520 | tf_op jit(solution)/shard_map/ppermute | solution.py:643
  25.3 2.4 %shard_map.79 = (bf16[2,16,32,128]{3,2,1,0:T(8,128)(2,1)S(1)}, bf16[96,128]{1,0:T(8,128)(2,1)S(1)}, f32[8,128]{1,0:T(8,128)S(1)}, bf16[2,18,32,384]{3,2,1,0:T(8,128)(2,1)}) custom-call(s32[2]{0:T(128)S(1)} %pad_add_fusion.place.refs_0_, bf16[1248,128]{1,0:T(8,128)(2,1)S(1)} %collective-permute-done.1.before, f32[2,512,128]{2,1,0:T(8,128)S(1)} %get-tuple-element.47.sums, ...), custom_call_target="tpu_custom_call" | custom-call | flops 452984832 | bytes 2904072 | tf_op jit(solution)/shard_map/pallas_call | solution.py:59
  30.7 3.3 %all-to-all-start.1 = ((bf16[4,80,128]{2,1,0:T(8,128)(2,1)}), bf16[4,80,128]{2,1,0:T(8,128)(2,1)S(1)}, u32[]{:S(2)}, u32[]{:S(2)}) async-start(bf16[4,80,128]{2,1,0:T(8,128)(2,1)} %shard_map.81), calls=%async_computation.1 | async-start | bytes 163840 | tf_op jit(solution)/shard_map/all_to_all | solution.py:803
  35.2 2.7 %shard_map.82.grad_act = f32[2,18,40,128]{3,2,1,0:T(8,128)S(1)} custom-call(bf16[1472,128]{1,0:T(8,128)(2,1)S(1)} %get-tuple-element.51.near, bf16[1472,128]{1,0:T(8,128)(2,1)S(1)} %collective-permute-done.3.far, bf16[3456,128]{1,0:T(8,128)(2,1)S(1)} %bitcast.10), custom_call_target="tpu_custom_call" | custom-call | flops 1811939328 | bytes 2375680 | tf_op jit(solution)/shard_map/pallas_call | solution.py:59
  40.0 3.3 %all-to-all-start.2 = ((f32[8,8,128]{2,1,0:T(8,128)}), f32[8,8,128]{2,1,0:T(8,128)S(1)}, u32[]{:S(2)}, u32[]{:S(2)}) async-start(f32[8,8,128]{2,1,0:T(8,128)} %get-tuple-element.54), calls=%async_computation.2 | async-start | bytes 65536 | tf_op jit(solution)/shard_map/all_to_all | solution.py:818
  43.4 2.2 %shard_map.84 = (bf16[1248,128]{1,0:T(8,128)(2,1)S(1)}, f32[2,18,40,128]{3,2,1,0:T(8,128)}, f32[2,18,40,128]{3,2,1,0:T(8,128)}) custom-call(s32[2]{0:T(128)S(1)} %pad_add_fusion.place.refs_0_, bf16[2,16,32,128]{3,2,1,0:T(8,128)(2,1)S(1)} %get-tuple-element.48.hidden, bf16[96,128]{1,0:T(8,128)(2,1)S(1)} %collective-permute-done.2.got.row_got, ...), custom_call_target="tpu_custom_call" | custom-call | tf_op jit(solution)/shard_map/pallas_call | solution.py:59
  45.6 2.5 %shard_map.85.second_far = f32[3456,128]{1,0:T(8,128)} custom-call(bf16[1472,128]{1,0:T(8,128)(2,1)S(1)} %get-tuple-element.51.near, bf16[1472,128]{1,0:T(8,128)(2,1)S(1)} %collective-permute-done.3.far, bf16[1248,128]{1,0:T(8,128)(2,1)S(1)} %get-tuple-element.67.act.far), custom_call_target="tpu_custom_call" | custom-call | tf_op jit(solution)/shard_map/pallas_call | solution.py:59
  48.1 4.6 %shard_map.86 = (bf16[1248,128]{1,0:T(8,128)(2,1)S(1)}, f32[3456,128]{1,0:T(8,128)S(1)}, bf16[3456,128]{1,0:T(8,128)(2,1)S(1)}) custom-call(s32[2]{0:T(128)S(1)} %pad_add_fusion.place.refs_0_, f32[8,8,128]{2,1,0:T(8,128)S(1)} %all-to-all-done.2.got, f32[8,128]{1,0:T(8,128)S(1)} %get-tuple-element.55.norm, f32[2,18,40,128]{3,2,1,0:T(8,128)} %get-tuple-element.56.q_far, ...), custom_call_target="tpu_custom_call" | custom-call | flops 905969664 | bytes 8024072 | tf_op jit(solution)/shard_map/pallas_call | solution.py:59
  53.2 2.1 %collective-permute-done.4.got = bf16[3456,128]{1,0:T(8,128)(2,1)S(1)} collective-permute-done((bf16[3456,128]{1,0:T(8,128)(2,1)S(1)}, bf16[3456,128]{1,0:T(8,128)(2,1)S(1)}, u32[]{:S(2)}, u32[]{:S(2)}) %collective-permute-start.4) | collective-permute-done | bytes 884768 | tf_op jit(solution)/shard_map/ppermute | solution.py:637
  56.3 4.2 %all-to-all-start.3 = ((bf16[4,864,128]{2,1,0:T(8,128)(2,1)}), bf16[4,864,128]{2,1,0:T(8,128)(2,1)S(1)}, u32[]{:S(2)}, u32[]{:S(2)}) async-start(bf16[4,864,128]{2,1,0:T(8,128)(2,1)} %shard_map.87), calls=%async_computation.3 | async-start | bytes 1769472 | tf_op jit(solution)/shard_map/all_to_all | solution.py:859
  61.8 4.6 %collective-permute-start.6 = (bf16[1248,128]{1,0:T(8,128)(2,1)S(1)}, bf16[1248,128]{1,0:T(8,128)(2,1)S(1)}, u32[]{:S(2)}, u32[]{:S(2)}) collective-permute-start(bf16[1248,128]{1,0:T(8,128)(2,1)S(1)} %get-tuple-element.67.act.far), channel_id=1, source_target_pairs={{0,8},{8,16},{16,24},{1,9},{9,17},{17,25},{2,10},{10,18},{18,26},{... | collective-permute-start | bytes 958472 | tf_op jit(solution)/shard_map/ppermute | solution.py:643
  66.3 5.6 %collective-permute-done.5.far = bf16[1248,128]{1,0:T(8,128)(2,1)S(1)} collective-permute-done((bf16[1248,128]{1,0:T(8,128)(2,1)S(1)}, bf16[1248,128]{1,0:T(8,128)(2,1)S(1)}, u32[]{:S(2)}, u32[]{:S(2)}) %collective-permute-start.5) | collective-permute-done | bytes 319520 | tf_op jit(solution)/shard_map/ppermute | solution.py:643
  73.5 5.2 %all-to-all-start.4 = ((bf16[4,224,128]{2,1,0:T(8,128)(2,1)}), bf16[4,224,128]{2,1,0:T(8,128)(2,1)S(1)}, u32[]{:S(2)}, u32[]{:S(2)}) async-start(bf16[4,224,128]{2,1,0:T(8,128)(2,1)} %shard_map.88), calls=%async_computation.4 | async-start | bytes 458752 | tf_op jit(solution)/shard_map/all_to_all | solution.py:868
  79.9 2.4 %shard_map.89 = bf16[2,16,32,128]{3,2,1,0:T(8,128)(2,1)} custom-call(bf16[1248,128]{1,0:T(8,128)(2,1)S(1)} %collective-permute-done.6.near, bf16[1248,128]{1,0:T(8,128)(2,1)S(1)} %get-tuple-element.67.act.far, bf16[3456,128]{1,0:T(8,128)(2,1)S(1)} %bitcast.11, bf16[2,16,32,128]{3,2,1,0:T(8,128)(2,1)S(1)} %copy-done), custom_call_target="tpu_custom_call" | custom-call | flops 905969664 | bytes 2048000 | tf_op jit(solution)/shard_map/pallas_call | solution.py:59
  82.3 4.1 %all-to-all-done.4.got = bf16[4,224,128]{2,1,0:T(8,128)(2,1)S(1)} async-done(((bf16[4,224,128]{2,1,0:T(8,128)(2,1)}), bf16[4,224,128]{2,1,0:T(8,128)(2,1)S(1)}, u32[]{:S(2)}, u32[]{:S(2)}) %all-to-all-start.4) | async-done | bytes 229408 | tf_op jit(solution)/shard_map/all_to_all | solution.py:868
  87.1 3.4 %all-to-all-start.5 = ((bf16[4,224,128]{2,1,0:T(8,128)(2,1)}), bf16[4,224,128]{2,1,0:T(8,128)(2,1)S(1)}, u32[]{:S(2)}, u32[]{:S(2)}) async-start(bf16[4,224,128]{2,1,0:T(8,128)(2,1)} %shard_map.91), calls=%async_computation.5 | async-start | bytes 458752 | tf_op jit(solution)/shard_map/all_to_all | solution.py:887
  90.5 1.8 %shard_map.90 = (f32[2,512,128]{2,1,0:T(8,128)S(1)}, f32[8,128]{1,0:T(8,128)S(1)}) custom-call(bf16[1248,128]{1,0:T(8,128)(2,1)S(1)} %get-tuple-element.65.near, bf16[1248,128]{1,0:T(8,128)(2,1)S(1)} %collective-permute-done.5.far, bf16[3456,128]{1,0:T(8,128)(2,1)S(1)} %bitcast.9, bf16[2,16,32,128]{3,2,1,0:T(8,128)(2,1)S(1)} %copy-done, ...), custom_call_target="tpu_custom_call" | custom-call | flops 905969664 | bytes 2318336 | tf_op jit(solution)/shard_map/pallas_call | solution.py:59
  93.6 3.4 %all-to-all-done.5 = bf16[4,224,128]{2,1,0:T(8,128)(2,1)S(1)} async-done(((bf16[4,224,128]{2,1,0:T(8,128)(2,1)}), bf16[4,224,128]{2,1,0:T(8,128)(2,1)S(1)}, u32[]{:S(2)}, u32[]{:S(2)}) %all-to-all-start.5) | async-done | bytes 229408 | tf_op jit(solution)/shard_map/all_to_all | solution.py:887
  97.2 12.4 %all_to_all.36.refs_1_ = bf16[4,896,128]{2,1,0:T(8,128)(2,1)S(1)} all-to-all(bf16[4,896,128]{2,1,0:T(8,128)(2,1)S(1)} %broadcast_in_dim.2), channel_id=1, replica_groups=mesh['tm'=4,'row'=2,'col'=4] {'col'}, dimensions={0} | all-to-all | bytes 1835008 | tf_op jit(solution)/shard_map/all_to_all | solution.py:891
  112.1 1.5 %shard_map.94 = (bf16[3456,128]{1,0:T(8,128)(2,1)}, bf16[3456,128]{1,0:T(8,128)(2,1)}) custom-call(s32[2]{0:T(128)S(1)} %pad_add_fusion.place.refs_0_, bf16[4,896,128]{2,1,0:T(8,128)(2,1)S(1)} %collective-permute-done.8.refs_1_, bf16[3456,128]{1,0:T(8,128)(2,1)} %get-tuple-element.74.refs_2_, ...), custom_call_target="tpu_custom_call", output_to_operand_aliasing={{0}: (2, {}), {1}: (3, {})} | custom-call | tf_op jit(solution)/shard_map/pallas_call | solution.py:709
  (43 shorter events, 21.1 us)
Async XLA Ops:
  0.6 20.3 %copy-start.2 = (bf16[3,3,3,128,128]{4,3,2,1,0:T(8,128)(2,1)S(1)}, bf16[3,3,3,128,128]{4,3,2,1,0:T(8,128)(2,1)}, u32[]{:S(2)}) copy-start(bf16[3,3,3,128,128]{4,3,2,1,0:T(8,128)(2,1)} %param.5) | copy-start | bytes 2654212
  2.5 1.4 %collective-permute-start = (bf16[224,128]{1,0:T(8,128)(2,1)S(1)}, bf16[224,128]{1,0:T(8,128)(2,1)S(1)}, u32[]{:S(2)}, u32[]{:S(2)}) collective-permute-start(bf16[224,128]{1,0:T(8,128)(2,1)S(1)} %get-tuple-element.43), channel_id=1, source_target_pairs={{0,4},{4,0},{1,5},{5,1},{2,6},{6,2},{3,7},{7,3},{8,12},{12,8},{9,1... | collective-permute-start | bytes 172040 | tf_op jit(solution)/shard_map/ppermute | solution.py:637
  16.1 9.2 %collective-permute-start.1 = (bf16[1248,128]{1,0:T(8,128)(2,1)S(1)}, bf16[1248,128]{1,0:T(8,128)(2,1)S(1)}, u32[]{:S(2)}, u32[]{:S(2)}) collective-permute-start(bf16[1248,128]{1,0:T(8,128)(2,1)S(1)} %get-tuple-element.46.own), channel_id=1, source_target_pairs={{0,8},{8,16},{16,24},{1,9},{9,17},{17,25},{2,10},{10,18},{18,26},{... | collective-permute-start | bytes 958472 | tf_op jit(solution)/shard_map/ppermute | solution.py:643
  19.7 11.0 %collective-permute-start.3 = (bf16[1472,128]{1,0:T(8,128)(2,1)S(1)}, bf16[1472,128]{1,0:T(8,128)(2,1)S(1)}, u32[]{:S(2)}, u32[]{:S(2)}) collective-permute-start(bf16[1472,128]{1,0:T(8,128)(2,1)S(1)} %get-tuple-element.51.near), channel_id=1, source_target_pairs={{8,0},{16,8},{24,16},{9,1},{17,9},{25,17},{10,2},{18,10},{26,18},{... | collective-permute-start | bytes 1130504 | tf_op jit(solution)/shard_map/ppermute | solution.py:643
  27.7 1.3 %collective-permute-start.2 = (bf16[96,128]{1,0:T(8,128)(2,1)S(1)}, bf16[96,128]{1,0:T(8,128)(2,1)S(1)}, u32[]{:S(2)}, u32[]{:S(2)}) collective-permute-start(bf16[96,128]{1,0:T(8,128)(2,1)S(1)} %get-tuple-element.49), channel_id=1, source_target_pairs={{0,4},{4,0},{1,5},{5,1},{2,6},{6,2},{3,7},{7,3},{8,12},{12,8},{9,1... | collective-permute-start | bytes 73736 | tf_op jit(solution)/shard_map/ppermute | solution.py:637
  30.7 8.2 %all-to-all-start.1 = ((bf16[4,80,128]{2,1,0:T(8,128)(2,1)}), bf16[4,80,128]{2,1,0:T(8,128)(2,1)S(1)}, u32[]{:S(2)}, u32[]{:S(2)}) async-start(bf16[4,80,128]{2,1,0:T(8,128)(2,1)} %shard_map.81), calls=%async_computation.1 | async-start | bytes 163840 | tf_op jit(solution)/shard_map/all_to_all | solution.py:803
  34.0 1.2 %copy-start.3 = (bf16[3,3,3,128,128]{4,3,2,1,0:T(8,128)(2,1)S(1)}, bf16[3,3,3,128,128]{4,3,2,1,0:T(8,128)(2,1)}, u32[]{:S(2)}) copy-start(bf16[3,3,3,128,128]{4,3,2,1,0:T(8,128)(2,1)} %param.6) | copy-start | bytes 2654212
  40.0 8.1 %all-to-all-start.2 = ((f32[8,8,128]{2,1,0:T(8,128)}), f32[8,8,128]{2,1,0:T(8,128)S(1)}, u32[]{:S(2)}, u32[]{:S(2)}) async-start(f32[8,8,128]{2,1,0:T(8,128)} %get-tuple-element.54), calls=%async_computation.2 | async-start | bytes 65536 | tf_op jit(solution)/shard_map/all_to_all | solution.py:818
  52.7 2.5 %collective-permute-start.4 = (bf16[3456,128]{1,0:T(8,128)(2,1)S(1)}, bf16[3456,128]{1,0:T(8,128)(2,1)S(1)}, u32[]{:S(2)}, u32[]{:S(2)}) collective-permute-start(bf16[3456,128]{1,0:T(8,128)(2,1)S(1)} %get-tuple-element.64), channel_id=1, source_target_pairs={{0,4},{4,0},{1,5},{5,1},{2,6},{6,2},{3,7},{7,3},{8,12},{12,8},{9,1... | collective-permute-start | bytes 2654216 | tf_op jit(solution)/shard_map/ppermute | solution.py:637
  56.3 22.4 %copy-start = (bf16[2,16,32,128]{3,2,1,0:T(8,128)(2,1)S(1)}, bf16[2,16,32,128]{3,2,1,0:T(8,128)(2,1)}, u32[]{:S(2)}) copy-start(bf16[2,16,32,128]{3,2,1,0:T(8,128)(2,1)} %features.5) | copy-start | bytes 786436
  56.3 16.4 %all-to-all-start.3 = ((bf16[4,864,128]{2,1,0:T(8,128)(2,1)}), bf16[4,864,128]{2,1,0:T(8,128)(2,1)S(1)}, u32[]{:S(2)}, u32[]{:S(2)}) async-start(bf16[4,864,128]{2,1,0:T(8,128)(2,1)} %shard_map.87), calls=%async_computation.3 | async-start | bytes 1769472 | tf_op jit(solution)/shard_map/all_to_all | solution.py:859
  60.5 11.4 %collective-permute-start.5 = (bf16[1248,128]{1,0:T(8,128)(2,1)S(1)}, bf16[1248,128]{1,0:T(8,128)(2,1)S(1)}, u32[]{:S(2)}, u32[]{:S(2)}) collective-permute-start(bf16[1248,128]{1,0:T(8,128)(2,1)S(1)} %get-tuple-element.65.near), channel_id=1, source_target_pairs={{8,0},{16,8},{24,16},{9,1},{17,9},{25,17},{10,2},{18,10},{26,18},{... | collective-permute-start | bytes 958472 | tf_op jit(solution)/shard_map/ppermute | solution.py:643
  61.8 17.0 %collective-permute-start.6 = (bf16[1248,128]{1,0:T(8,128)(2,1)S(1)}, bf16[1248,128]{1,0:T(8,128)(2,1)S(1)}, u32[]{:S(2)}, u32[]{:S(2)}) collective-permute-start(bf16[1248,128]{1,0:T(8,128)(2,1)S(1)} %get-tuple-element.67.act.far), channel_id=1, source_target_pairs={{0,8},{8,16},{16,24},{1,9},{9,17},{17,25},{2,10},{10,18},{18,26},{... | collective-permute-start | bytes 958472 | tf_op jit(solution)/shard_map/ppermute | solution.py:643
  73.5 12.9 %all-to-all-start.4 = ((bf16[4,224,128]{2,1,0:T(8,128)(2,1)}), bf16[4,224,128]{2,1,0:T(8,128)(2,1)S(1)}, u32[]{:S(2)}, u32[]{:S(2)}) async-start(bf16[4,224,128]{2,1,0:T(8,128)(2,1)} %shard_map.88), calls=%async_computation.4 | async-start | bytes 458752 | tf_op jit(solution)/shard_map/all_to_all | solution.py:868
  78.7 1.2 %copy-start.4 = (bf16[3,3,3,128,128]{4,3,2,1,0:T(8,128)(2,1)S(1)}, bf16[3,3,3,128,128]{4,3,2,1,0:T(8,128)(2,1)}, u32[]{:S(2)}) copy-start(bf16[3,3,3,128,128]{4,3,2,1,0:T(8,128)(2,1)} %param.6) | copy-start | bytes 2654212
  87.1 9.9 %all-to-all-start.5 = ((bf16[4,224,128]{2,1,0:T(8,128)(2,1)}), bf16[4,224,128]{2,1,0:T(8,128)(2,1)S(1)}, u32[]{:S(2)}, u32[]{:S(2)}) async-start(bf16[4,224,128]{2,1,0:T(8,128)(2,1)} %shard_map.91), calls=%async_computation.5 | async-start | bytes 458752 | tf_op jit(solution)/shard_map/all_to_all | solution.py:887
  92.4 1.2 %collective-permute-start.7 = (f32[8,128]{1,0:T(8,128)S(1)}, f32[8,128]{1,0:T(8,128)S(1)}, u32[]{:S(2)}, u32[]{:S(2)}) collective-permute-start(f32[8,128]{1,0:T(8,128)S(1)} %get-tuple-element.73), channel_id=1, source_target_pairs={{0,4},{4,0},{1,5},{5,1},{2,6},{6,2},{3,7},{7,3},{8,12},{12,8},{9,1... | collective-permute-start | bytes 12296 | tf_op jit(solution)/shard_map/ppermute | solution.py:637
  97.0 12.6 %copy-start.1 = (bf16[2,16,32,128]{3,2,1,0:T(8,128)(2,1)S(1)}, bf16[2,16,32,128]{3,2,1,0:T(8,128)(2,1)}, u32[]{:S(2)}) copy-start(bf16[2,16,32,128]{3,2,1,0:T(8,128)(2,1)} %out_grad.1) | copy-start | bytes 786436
  109.6 2.5 %collective-permute-start.8 = (bf16[4,896,128]{2,1,0:T(8,128)(2,1)S(1)}, bf16[4,896,128]{2,1,0:T(8,128)(2,1)S(1)}, u32[]{:S(2)}, u32[]{:S(2)}) collective-permute-start(bf16[4,896,128]{2,1,0:T(8,128)(2,1)S(1)} %all_to_all.36.refs_1_), channel_id=1, source_target_pairs={{0,4},{4,0},{1,5},{5,1},{2,6},{6,2},{3,7},{7,3},{8,12},{12,8},{9,1... | collective-permute-start | bytes 2752520 | tf_op jit(solution)/shard_map/ppermute | solution.py:637

commit v7 on v6

--- a/solution.py
+++ b/solution.py
@@ -158,10 +158,6 @@
                     rows = rows.reshape(size.high, LANES)
                     flat[side, at + rim : at + rim + size.high] = rows
                 at += size.stride(rim)
-
-
-def columns_body(size, hidden, flat):
-    take_columns(size, ((hidden, 1),), flat)
 
 
 def start_body(
@@ -378,39 +374,36 @@
     return [((frames, tall, wo, 3 * LANES), BF16), ((tall, up(wo + 2, 8), LANES), F32)]
 
 
-def hidden_own_body(size, own, kernel, sums, x_far, x, frame, sems):
+def hidden_own_body(size, own, kernel, sums, x, frame):
     spread_all(size, 1, 1, size.wide, own, None, x, frame)
-    copy = pltpu.make_async_copy(x, x_far, sems.at[0])
-    copy.start()
     dot = tap_dot(x, kernel, False)
     both = dot(0, 2, 1)
     sums[0] = both[:, :LANES]
     sums[1] = both[:, LANES:] + dot(1, 2)
-    copy.wait()
-
-
-def hidden_body(
-    size, place, before, sums, kernel, hidden, pay, stats, x_far, x, frame, sems
-):
+
+
+def hidden_body(size, across, place, before, sums, kernel, hidden, slots, x, frame, flat):
     high, wide = size.high, size.wide
     spread_all(size, 1, 1, wide, before, None, x, frame)
-    copy = pltpu.make_async_copy(x, x_far, sems.at[0])
-    copy.start()
     dot = tap_dot(x, kernel, False)
     both = dot(1, 1, 0)
     sums = (sums[0] + both[:, :LANES] + dot(0, 0), sums[1] + both[:, LANES:])
+    rounded = [s.astype(BF16) for s in sums]
+    for f in range(FRAMES):
+        hidden[f] = rounded[f].reshape(high, wide, LANES)
+    span = span_second(size)
+    found = split3(measured([r.astype(F32) for r in rounded]))
+    take_columns(size, ((hidden, 1),), flat)
     upper = place[0] == 0
-    rounded = [s.astype(BF16) for s in sums]
-    for f in range(FRAMES):
-        hidden[f] = rounded[f].reshape(high, wide, LANES)
-        edge = jnp.where(upper, rounded[f][size.cells - wide :], rounded[f][:wide])
-        pay[f * wide : (f + 1) * wide] = edge
-    found = measured([r.astype(F32) for r in rounded])
-    stats[...] = found
-    at = FRAMES * wide
-    fill = jnp.zeros((pay.shape[0] - at - PARTS, LANES), F32)
-    pay[at:] = jnp.concatenate([split3(found), fill], 0).astype(BF16)
-    copy.wait()
+    edges = [jnp.where(upper, r[size.cells - wide :], r[:wide]).astype(F32) for r in rounded]
+    fill = jnp.zeros((span - FRAMES * wide, LANES), F32)
+    edges = jnp.concatenate([*edges, fill] if fill.shape[0] else edges, 0)
+    rest = jnp.zeros((slots.shape[1] - span - PARTS, LANES), F32)
+    for peer in range(slots.shape[0]):
+        col = peer % across
+        side = jnp.where(col > place[1], flat[1], flat[0])
+        content = jnp.where(col == place[1], edges, side)
+        slots[peer] = jnp.concatenate([content, found, rest], 0).astype(BF16)
 
 
 def grad_act_body(size, near, far, kernel, out, x, frame):
@@ -421,12 +414,36 @@
         out[f] = sums[f].reshape(size.tall(), wo, LANES)[:, : size.broad()]
 
 
-def sums_second_body(size, across, hidden, col_got, grad_act, norm, slots):
+def crossed_sides(size, place, across, got):
+    step, high = size.stride(1), size.high
+    count = FRAMES * step
+    upper = place[0] == 0
+    row = lax.broadcasted_iota(jnp.int32, (count, LANES), 0)
+    found = []
+    for at, there in (
+        (jnp.maximum(place[1] - 1, 0), place[1] > 0),
+        (jnp.minimum(place[1] + 1, across - 1), place[1] < across - 1),
+    ):
+        block = got[place[0] * across + at, 0:count].astype(F32)
+        cross = got[(1 - place[0]) * across + at, 0:count].astype(F32)
+        for f in range(FRAMES):
+            above = jnp.where(upper, 0.0, cross[f * step + high : f * step + high + 1])
+            below = jnp.where(upper, cross[f * step + 1 : f * step + 2], 0.0)
+            block = jnp.where(row == f * step, above, block)
+            block = jnp.where(row == f * step + high + 1, below, block)
+        found.append(jnp.where(there, block, 0.0))
+    return found
+
+
+def span_second(size):
+    return up(max(FRAMES * size.wide, FRAMES * size.stride(1)), 16)
+
+
+def sums_second_body(size, across, hidden, got, grad_act, norm, slots):
     high, wide = size.high, size.wide
-    at = FRAMES * size.stride(1)
-    found = concluded(
-        [join3(col_got[peer, at : at + PARTS]) for peer in range(across)], 2 * size.cells
-    )
+    at = span_second(size)
+    blocks = [join3(got[peer, at : at + PARTS]) for peer in range(got.shape[0])]
+    found = concluded(blocks, size.cells)
     norm[...] = found
     firsts, seconds = [], []
     for f in range(FRAMES):
@@ -444,16 +461,17 @@
 
 
 def act_second_body(
-    size, across, place, hidden, row_got, col_got, grad_act, norm, act, q_far, z_far, frame, q, z, sems
+    size, across, place, hidden, got, grad_act, norm, act, q_far, z_far, frame, q, z, sems
 ):
     wide = size.wide
     step = size.stride(1)
-    left_all, right_all = sides(place, across, col_got, 0, FRAMES * step)
+    left_all, right_all = crossed_sides(size, place, across, got)
     ok = in_frame((size.tall(), size.broad(), LANES), place, across, size, 1)
     lefts, rights, copies = [], [], []
     frame[...] = jnp.zeros_like(frame)
-    for f in range(FRAMES):
-        top, bottom = rim_rows(place, row_got[f * wide : (f + 1) * wide].astype(F32))
+    facing = (1 - place[0]) * across + place[1]
+    for f in range(FRAMES):
+        top, bottom = rim_rows(place, got[facing, f * wide : (f + 1) * wide].astype(F32))
         padded_frame(
             size,
             hidden[f].astype(F32),
@@ -528,7 +546,7 @@
     )
 
 
-def second_term_body(size, near, far, act, out_far, x, frame, turned, out, sems):
+def second_term_body(size, near, far, act, out_far, short_far, x, frame, turned, out, short, sems):
     spread_all(size, 2, 1, size.wide, near, far, x, frame)
     turned_cells(size, act, turned)
     span = 3 * LANES
@@ -537,11 +555,16 @@
         for a, total in enumerate(tap_sums(x, turned, b)):
             for c in range(3):
                 tap = ((2 - a) * 3 + 2 - b) * 3 + 2 - c
-                out[tap * LANES : (tap + 1) * LANES] = total[:, c * LANES : (c + 1) * LANES]
+                rows = slice(tap * LANES, (tap + 1) * LANES)
+                piece = total[:, c * LANES : (c + 1) * LANES]
+                out[rows] = piece
+                short[rows] = piece.astype(BF16)
             rows = pl.ds(((2 - a) * 3 + 2 - b) * span, span)
-            copy = pltpu.make_async_copy(out.at[rows], out_far.at[rows], sems.at[3 * b + a])
-            copy.start()
-            copies.append(copy)
+            for k, (source, target) in enumerate(((out, out_far), (short, short_far))):
+                sem = sems.at[2 * (3 * b + a) + k]
+                copy = pltpu.make_async_copy(source.at[rows], target.at[rows], sem)
+                copy.start()
+                copies.append(copy)
     for copy in copies:
         copy.wait()
 
@@ -556,22 +579,24 @@
     z_far,
     near_far,
     own_far,
-    second_far,
-    grad,
-    keep,
+    short_far,
+    out,
     give,
+    grad_far,
     x,
     frame,
     turned,
-    second,
+    grad,
+    near,
+    own,
+    short,
     q,
     z,
     sems,
 ):
     pairs = [(q_far.at[f], q.at[f]) for f in range(FRAMES)]
     pairs += [(z_far.at[f], z.at[f]) for f in range(FRAMES)]
-    pairs += [(near_far, x.at[pl.ds(0, FRAMES)]), (own_far, x.at[pl.ds(FRAMES, FRAMES)])]
-    pairs += [(second_far, second)]
+    pairs += [(near_far, near), (own_far, own), (short_far, short)]
     copies = [
         pltpu.make_async_copy(source, target, sems.at[k])
         for k, (source, target) in enumerate(pairs)
@@ -584,16 +609,20 @@
         copies[FRAMES + f].wait()
 
     hidden_grad(size, across, place, q, z, got, norm, grad, frame, arrive)
+    sent = pltpu.make_async_copy(grad, grad_far, sems.at[len(pairs)])
+    sent.start()
     turned_cells(size, grad, turned)
     for copy in copies[2 * FRAMES :]:
         copy.wait()
+    spread_all(size, 1, 1, size.wide, near, own, x, frame)
     upper = place[0] == 0
     for b in range(3):
         for a, total in enumerate(tap_sums(x, turned, b)):
             rows = slice((a * 3 + b) * 3 * LANES, (a * 3 + b + 1) * 3 * LANES)
-            one, two = total.T, second[rows]
-            keep[rows] = jnp.where(upper, one, two)
-            give[rows] = jnp.where(upper, two, one).astype(BF16)
+            piece = total.T
+            out[rows] = piece
+            give[rows] = jnp.where(upper, short[rows], piece.astype(BF16))
+    sent.wait()
 
 
 def result_body(size, near, far, kernel, features, out, x, frame):
@@ -657,11 +686,13 @@
     return total
 
 
-def joined_body(keep, got, out):
+def joined_body(place, first, second, got, out):
     share = out.shape[1]
+    upper = place[0] == 0
     for peer in range(out.shape[0]):
         rows = slice(peer * share, (peer + 1) * share)
-        out[peer] = (keep[rows] + got[rows].astype(F32)).astype(BF16)
+        keep = jnp.where(upper, first[rows], second[rows])
+        out[peer] = (keep + got[rows].astype(F32)).astype(BF16)
 
 
 def shared_body(got, out, flat):
@@ -762,45 +793,29 @@
         [frame],
         smem=1,
     )
+    grad_after = later(grad, -1)
     act_before = later(act_first, 1)
-    grad_after = later(grad, -1)
 
     edge = up(FRAMES * wide + PARTS, 16)
-    halves = ((FRAMES, tall, wide, 3 * LANES), BF16)
-    sums, x_own = call(
+    (sums,) = call(
         part(hidden_own_body, size),
-        [((FRAMES, size.cells, LANES), F32), halves],
+        [((FRAMES, size.cells, LANES), F32)],
         [act_first, first],
         conv_scratch(size, 1, wide, FRAMES),
-        sems=1,
         mib=12,
         flops=work // 2,
-        out_far=1,
-    )
-    hidden, pay, stats, x_before = call(
-        part(hidden_body, size),
-        [(features.shape, BF16), ((edge, LANES), BF16), stat, halves],
+    )
+    span = span_second(size)
+    hidden, slots = call(
+        part(hidden_body, size, across),
+        [(features.shape, BF16), ((peers, up(span + PARTS, 16), LANES), BF16)],
         [place, act_before, sums, first],
-        conv_scratch(size, 1, wide, FRAMES),
+        [*conv_scratch(size, 1, wide, FRAMES), ((2, span, LANES), F32)],
         smem=1,
-        sems=1,
         mib=12,
         flops=work // 2,
-        out_far=1,
-    )
-    row_got = row_swap(pay)
-    lines = up(FRAMES * size.stride(1) + PARTS, 16)
-    flat = ((2, lines, LANES), F32)
-    (cols,) = call(part(columns_body, size), [flat], [hidden])
-    (slots,) = call(
-        part(slots_body, size, (1,), across),
-        [((across, lines, LANES), BF16)],
-        [place, cols, row_got, stats],
-        [flat],
-        smem=1,
-    )
-    slots, grad_after = lax.optimization_barrier((slots, grad_after))
-    col_got = lax.all_to_all(slots, "col", 0, 0)
+    )
+    got = lax.all_to_all(slots, ("row", "col"), 0, 0)
     (grad_act,) = call(
         part(grad_act_body, size),
         [((FRAMES, tall, broad, LANES), F32)],
@@ -813,40 +828,41 @@
     norm_second, slots = call(
         part(sums_second_body, size, across),
         [stat, ((peers, STATS, LANES), F32)],
-        [hidden, col_got, grad_act],
-    )
-    got = lax.all_to_all(slots, ("row", "col"), 0, 0)
+        [hidden, got, grad_act],
+    )
     act_second, q, z = call(
         part(act_second_body, size, across),
         [block, field, field],
-        [place, hidden, row_got, col_got, grad_act, norm_second],
+        [place, hidden, got, grad_act, norm_second],
         [frame, field, field],
         smem=1,
         sems=2 * FRAMES,
         beside=True,
         out_far=2,
     )
+    got = lax.all_to_all(slots, ("row", "col"), 0, 0)
     turned = ((FRAMES * LANES, size.cells), BF16)
-    (second_term,) = call(
+    second_term, second_short = call(
         part(second_term_body, size),
-        [(first.shape, F32)],
+        [(first.shape, F32), (first.shape, BF16)],
         [grad, grad_after, act_second],
-        [*conv_scratch(size, 1, wide), turned, (first.shape, F32)],
-        sems=9,
+        [*conv_scratch(size, 1, wide), turned, (first.shape, F32), (first.shape, BF16)],
+        sems=18,
         mib=16,
         beside=True,
-        out_far=1,
-    )
-    grad_second, keep, give = call(
+        out_far=2,
+    )
+    first_term, give, grad_second = call(
         part(first_term_body, size, across),
-        [block, (first.shape, F32), (first.shape, BF16)],
-        [place, got, norm_second, q, z, x_before, x_own, second_term],
-        [*conv_scratch(size, 1, wide), turned, (first.shape, F32), field, field],
+        [(first.shape, F32), (first.shape, BF16), block],
+        [place, got, norm_second, q, z, act_before, act_first, second_short],
+        [*conv_scratch(size, 1, wide), turned, *[block] * 3, (first.shape, BF16), field, field],
         smem=1,
         far=5,
-        sems=2 * FRAMES + 3,
+        sems=2 * FRAMES + 4,
         mib=20,
         flops=work,
+        out_far=1,
     )
     give, late_grad, late_act = lax.optimization_barrier((give, grad_second, act_second))
     act_second_before = later(late_act, 1)
@@ -855,7 +871,12 @@
     along = lax.axis_size("tm")
     rows = first.shape[0]
     by_col = rows // across
-    (slots,) = call(joined_body, [((across, by_col, LANES), BF16)], [keep, row_swap(give)])
+    (slots,) = call(
+        joined_body,
+        [((across, by_col, LANES), BF16)],
+        [place, first_term, second_term, row_swap(give)],
+        smem=1,
+    )
     slots = lax.all_to_all(slots, "col", 0, 0)
     slots, grad_second_after = lax.optimization_barrier((slots, grad_second_after))
     share = up(by_col, 16 * along) // along

time: 115 us -> 116 us (level)
  starting transfers between devices: 31.2 us -> 33.4 us
  Pallas kernels: 32.8 us -> 31.2 us
    all_to_all x1 -> x2, starting transfers between devices: 3.34 us -> 6.73 us  [on_device(): got = lax.all_to_all(slots, ('row', 'col'), 0, 0)]
    all_to_all x1 -> x0, starting transfers between devices: 3.3 us -> none  [on_device(): col_got = lax.all_to_all(slots, 'col', 0, 0)]
    all_to_all x1 -> x2, waiting for transfers between devices: 0.01 us -> 1.97 us  [on_device(): got = lax.all_to_all(slots, ('row', 'col'), 0, 0)]
    pallas_call x18 -> x16, Pallas kernels: 29.8 us -> 28.2 us  [call(): pl.pallas_call(body, out_shape=shapes[:kept] + [pltpu.HBM(o.shape, o.dtyp...]
    ppermute x4, starting transfers between devices: 10.6 us -> 12.2 us  [later(): return lax.ppermute(values, 'tm', pairs)]
    ppermute x4, waiting for transfers between devices: 8.87 us -> 10.1 us  [later(): return lax.ppermute(values, 'tm', pairs)]
    ppermute x5 -> x4, waiting for transfers between devices: 5.24 us -> 4.1 us  [row_swap(): return lax.ppermute(values, 'row', [(0, 1), (1, 0)])]
    unnamed x10 -> x18, local copies, waits for them, and re-layouts: 2.34 us -> 2.36 us
  transfers between devices with their start and end apart: 14 -> 13, of which waited for: 11 -> 9; matrix products, arithmetic and copies ran while one was open for 0% -> 0% of each run, Pallas kernels for 18% -> 16%
where the time goes in v7:
time: 116 us; the launch traced here: 115 us
  starting transfers between devices  33.4 us (29%)
  Pallas kernels  31.2 us (27%)
  waiting for transfers between devices  24 us (21%)
  blocking collectives  22.7 us (20%)
  local copies, waits for them, and re-layouts  2.49 us (2%)
    pallas_call x16, Pallas kernels, call(): pl.pallas_call(body, out_shape=shapes[:kept] + [pltpu.HBM(o.shape, o.dtyp...  28.2 us
    all_to_all x1, blocking collectives, on_device(): lax.all_to_all(jnp.broadcast_to(done[None], (across, *done.shape)), 'col'...  12.4 us
    ppermute x4, starting transfers between devices, later(): return lax.ppermute(values, 'tm', pairs)  12.2 us
    all_to_all x1, blocking collectives, on_device(): col_got = lax.all_to_all(slots, 'col', 0, 0)  10.4 us
    ppermute x4, waiting for transfers between devices, later(): return lax.ppermute(values, 'tm', pairs)  10.1 us
    all_to_all x2, starting transfers between devices, on_device(): got = lax.all_to_all(slots, ('row', 'col'), 0, 0)  6.73 us
    all_to_all x1, starting transfers between devices, on_device(): got = lax.all_to_all(slots, 'tm', 0, 0)  5.8 us
    all_to_all x1, starting transfers between devices, on_device(): slots = lax.all_to_all(slots, 'col', 0, 0)  4.18 us
  transfers between devices with their start and end apart: 13, of which 9 were waited for; matrix products, arithmetic and copies ran while one was open for 0% of the time, Pallas kernels for 16%

profile of v7, /device:TPU:0, one launch (start us, length us, event | category | flops | bytes accessed | tf_op | source)
XLA Modules:
  0.0 114.9 jit_solution(15213765290217372282)
XLA Ops:
  0.7 1.8 %shard_map.75 = (bf16[224,128]{1,0:T(8,128)(2,1)S(1)}, f32[8,128]{1,0:T(8,128)S(1)}, f32[2,176,128]{2,1,0:T(8,128)S(1)}, bf16[2,16,32,128]{3,2,1,0:T(8,128)(2,1)S(1)}, bf16[2,16,32,128]{3,2,1,0:T(8,128)(2,1)S(1)}) custom-call(s32[2]{0:T(128)S(1)} %pad_add_fusion.place.refs_0_, bf16[2,16,32,128]{3,2,1,0:T(8,128)(2,1)} %features.5, ...), custom_call_target="tpu_custom_call" | custom-call | bytes 1290248 | tf_op jit(solution)/shard_map/pallas_call | solution.py:59
  4.5 10.4 %all_to_all.35.col_got = bf16[4,176,128]{2,1,0:T(8,128)(2,1)S(1)} all-to-all(bf16[4,176,128]{2,1,0:T(8,128)(2,1)S(1)} %shard_map.76), channel_id=1, replica_groups=mesh['tm'=4,'row'=2,'col'=4] {'col'}, dimensions={0} | all-to-all | bytes 360448 | tf_op jit(solution)/shard_map/all_to_all | solution.py:787
  17.5 4.6 %collective-permute-start.1 = (bf16[1248,128]{1,0:T(8,128)(2,1)S(1)}, bf16[1248,128]{1,0:T(8,128)(2,1)S(1)}, u32[]{:S(2)}, u32[]{:S(2)}) collective-permute-start(bf16[1248,128]{1,0:T(8,128)(2,1)S(1)} %get-tuple-element.42.own.own_far), channel_id=1, source_target_pairs={{0,8},{8,16},{16,24},{1,9},{9,17},{17,25},{2,10},{10,18},{18,26},{... | collective-permute-start | bytes 958472 | tf_op jit(solution)/shard_map/ppermute | solution.py:672
  22.9 4.5 %collective-permute-done.1.before.near_far = bf16[1248,128]{1,0:T(8,128)(2,1)S(1)} collective-permute-done((bf16[1248,128]{1,0:T(8,128)(2,1)S(1)}, bf16[1248,128]{1,0:T(8,128)(2,1)S(1)}, u32[]{:S(2)}, u32[]{:S(2)}) %collective-permute-start.1) | collective-permute-done | bytes 319520 | tf_op jit(solution)/shard_map/ppermute | solution.py:672
  27.4 2.3 %shard_map.79 = (bf16[2,16,32,128]{3,2,1,0:T(8,128)(2,1)S(1)}, bf16[8,96,128]{2,1,0:T(8,128)(2,1)}) custom-call(s32[2]{0:T(128)S(1)} %pad_add_fusion.place.refs_0_, bf16[1248,128]{1,0:T(8,128)(2,1)S(1)} %collective-permute-done.1.before.near_far, f32[2,512,128]{2,1,0:T(8,128)S(1)} %shard_map.78.sums, bf16[3456,128]{1,0:T(8,128)(2,1)S(1)} %bitcast.8), custom_call_target="tpu_custom_call" | custom-call | flops 452984832 | bytes 2187272 | tf_op jit(solution)/shard_map/pallas_call | solution.py:59
  29.7 3.4 %all-to-all-start.1 = ((bf16[8,96,128]{2,1,0:T(8,128)(2,1)}), bf16[8,96,128]{2,1,0:T(8,128)(2,1)S(1)}, u32[]{:S(2)}, u32[]{:S(2)}) async-start(bf16[8,96,128]{2,1,0:T(8,128)(2,1)} %get-tuple-element.44), calls=%async_computation.1 | async-start | bytes 393216 | tf_op jit(solution)/shard_map/all_to_all | solution.py:818
  34.3 2.7 %shard_map.80.grad_act = f32[2,18,40,128]{3,2,1,0:T(8,128)S(1)} custom-call(bf16[1472,128]{1,0:T(8,128)(2,1)S(1)} %get-tuple-element.45.near, bf16[1472,128]{1,0:T(8,128)(2,1)S(1)} %collective-permute-done.2.far, bf16[3456,128]{1,0:T(8,128)(2,1)S(1)} %bitcast.10), custom_call_target="tpu_custom_call" | custom-call | flops 1811939328 | bytes 2375680 | tf_op jit(solution)/shard_map/pallas_call | solution.py:59
  37.0 2.0 %all-to-all-done.1.got = bf16[8,96,128]{2,1,0:T(8,128)(2,1)S(1)} async-done(((bf16[8,96,128]{2,1,0:T(8,128)(2,1)}), bf16[8,96,128]{2,1,0:T(8,128)(2,1)S(1)}, u32[]{:S(2)}, u32[]{:S(2)}) %all-to-all-start.1) | async-done | bytes 196640 | tf_op jit(solution)/shard_map/all_to_all | solution.py:818
  40.2 3.3 %all-to-all-start.2 = ((f32[8,8,128]{2,1,0:T(8,128)}), f32[8,8,128]{2,1,0:T(8,128)S(1)}, u32[]{:S(2)}, u32[]{:S(2)}) async-start(f32[8,8,128]{2,1,0:T(8,128)} %get-tuple-element.46), calls=%async_computation.2 | async-start | bytes 65536 | tf_op jit(solution)/shard_map/all_to_all | solution.py:843
  43.5 2.2 %shard_map.82 = (bf16[1248,128]{1,0:T(8,128)(2,1)S(1)}, f32[2,18,40,128]{3,2,1,0:T(8,128)}, f32[2,18,40,128]{3,2,1,0:T(8,128)}) custom-call(s32[2]{0:T(128)S(1)} %pad_add_fusion.place.refs_0_, bf16[2,16,32,128]{3,2,1,0:T(8,128)(2,1)S(1)} %get-tuple-element.43.hidden, bf16[8,96,128]{2,1,0:T(8,128)(2,1)S(1)} %all-to-all-done.1.got, ...), custom_call_target="tpu_custom_call" | custom-call | tf_op jit(solution)/shard_map/pallas_call | solution.py:59
  45.8 2.7 %shard_map.83 = (f32[3456,128]{1,0:T(8,128)}, bf16[3456,128]{1,0:T(8,128)(2,1)}) custom-call(bf16[1472,128]{1,0:T(8,128)(2,1)S(1)} %get-tuple-element.45.near, bf16[1472,128]{1,0:T(8,128)(2,1)S(1)} %collective-permute-done.2.far, bf16[1248,128]{1,0:T(8,128)(2,1)S(1)} %get-tuple-element.59.act.far), custom_call_target="tpu_custom_call" | custom-call | tf_op jit(solution)/shard_map/pallas_call | solution.py:59
  48.4 4.1 %shard_map.84 = (f32[3456,128]{1,0:T(8,128)S(1)}, bf16[3456,128]{1,0:T(8,128)(2,1)S(1)}, bf16[1248,128]{1,0:T(8,128)(2,1)}) custom-call(s32[2]{0:T(128)S(1)} %pad_add_fusion.place.refs_0_, f32[8,8,128]{2,1,0:T(8,128)S(1)} %all-to-all-done.2.got, f32[8,128]{1,0:T(8,128)S(1)} %get-tuple-element.47.norm, f32[2,18,40,128]{3,2,1,0:T(8,128)} %get-tuple-element.48.q_far, ...), custom_call_target="tpu_custom_call" | custom-call | flops 905969664 | bytes 6008840 | tf_op jit(solution)/shard_map/pallas_call | solution.py:59
  53.0 2.1 %collective-permute-done.3.got = bf16[3456,128]{1,0:T(8,128)(2,1)S(1)} collective-permute-done((bf16[3456,128]{1,0:T(8,128)(2,1)S(1)}, bf16[3456,128]{1,0:T(8,128)(2,1)S(1)}, u32[]{:S(2)}, u32[]{:S(2)}) %collective-permute-start.3) | collective-permute-done | bytes 884768 | tf_op jit(solution)/shard_map/ppermute | solution.py:666
  55.1 1.8 %shard_map.85 = bf16[4,864,128]{2,1,0:T(8,128)(2,1)} custom-call(s32[2]{0:T(128)S(1)} %pad_add_fusion.place.refs_0_, f32[3456,128]{1,0:T(8,128)S(1)} %get-tuple-element.52.first, f32[3456,128]{1,0:T(8,128)S(1)} %copy-done.1, bf16[3456,128]{1,0:T(8,128)(2,1)S(1)} %collective-permute-done.3.got), custom_call_target="tpu_custom_call" | custom-call | bytes 5308424 | tf_op jit(solution)/shard_map/pallas_call | solution.py:59
  56.9 4.2 %all-to-all-start.3 = ((bf16[4,864,128]{2,1,0:T(8,128)(2,1)}), bf16[4,864,128]{2,1,0:T(8,128)(2,1)S(1)}, u32[]{:S(2)}, u32[]{:S(2)}) async-start(bf16[4,864,128]{2,1,0:T(8,128)(2,1)} %shard_map.85), calls=%async_computation.3 | async-start | bytes 1769472 | tf_op jit(solution)/shard_map/all_to_all | solution.py:880
  62.4 5.0 %collective-permute-start.5 = (bf16[1248,128]{1,0:T(8,128)(2,1)S(1)}, bf16[1248,128]{1,0:T(8,128)(2,1)S(1)}, u32[]{:S(2)}, u32[]{:S(2)}) collective-permute-start(bf16[1248,128]{1,0:T(8,128)(2,1)S(1)} %get-tuple-element.59.act.far), channel_id=1, source_target_pairs={{0,8},{8,16},{16,24},{1,9},{9,17},{17,25},{2,10},{10,18},{18,26},{... | collective-permute-start | bytes 958472 | tf_op jit(solution)/shard_map/ppermute | solution.py:672
  67.4 5.6 %collective-permute-done.4.far = bf16[1248,128]{1,0:T(8,128)(2,1)S(1)} collective-permute-done((bf16[1248,128]{1,0:T(8,128)(2,1)S(1)}, bf16[1248,128]{1,0:T(8,128)(2,1)S(1)}, u32[]{:S(2)}, u32[]{:S(2)}) %collective-permute-start.4) | collective-permute-done | bytes 319520 | tf_op jit(solution)/shard_map/ppermute | solution.py:672
  74.1 5.8 %all-to-all-start.4 = ((bf16[4,224,128]{2,1,0:T(8,128)(2,1)}), bf16[4,224,128]{2,1,0:T(8,128)(2,1)S(1)}, u32[]{:S(2)}, u32[]{:S(2)}) async-start(bf16[4,224,128]{2,1,0:T(8,128)(2,1)} %shard_map.86), calls=%async_computation.4 | async-start | bytes 458752 | tf_op jit(solution)/shard_map/all_to_all | solution.py:889
  81.0 2.4 %shard_map.87 = bf16[2,16,32,128]{3,2,1,0:T(8,128)(2,1)} custom-call(bf16[1248,128]{1,0:T(8,128)(2,1)S(1)} %collective-permute-done.5.near, bf16[1248,128]{1,0:T(8,128)(2,1)S(1)} %get-tuple-element.59.act.far, bf16[3456,128]{1,0:T(8,128)(2,1)S(1)} %bitcast.11, bf16[2,16,32,128]{3,2,1,0:T(8,128)(2,1)S(1)} %copy-done.2), custom_call_target="tpu_custom_call" | custom-call | flops 905969664 | bytes 2048000 | tf_op jit(solution)/shard_map/pallas_call | solution.py:59
  83.5 4.1 %all-to-all-done.4.got = bf16[4,224,128]{2,1,0:T(8,128)(2,1)S(1)} async-done(((bf16[4,224,128]{2,1,0:T(8,128)(2,1)}), bf16[4,224,128]{2,1,0:T(8,128)(2,1)S(1)}, u32[]{:S(2)}, u32[]{:S(2)}) %all-to-all-start.4) | async-done | bytes 229408 | tf_op jit(solution)/shard_map/all_to_all | solution.py:889
  88.3 3.4 %all-to-all-start.5 = ((bf16[4,224,128]{2,1,0:T(8,128)(2,1)}), bf16[4,224,128]{2,1,0:T(8,128)(2,1)S(1)}, u32[]{:S(2)}, u32[]{:S(2)}) async-start(bf16[4,224,128]{2,1,0:T(8,128)(2,1)} %shard_map.89), calls=%async_computation.5 | async-start | bytes 458752 | tf_op jit(solution)/shard_map/all_to_all | solution.py:908
  91.7 1.8 %shard_map.88 = (f32[2,512,128]{2,1,0:T(8,128)S(1)}, f32[8,128]{1,0:T(8,128)S(1)}) custom-call(bf16[1248,128]{1,0:T(8,128)(2,1)S(1)} %copy-done.8, bf16[1248,128]{1,0:T(8,128)(2,1)S(1)} %collective-permute-done.4.far, bf16[3456,128]{1,0:T(8,128)(2,1)S(1)} %bitcast.9, bf16[2,16,32,128]{3,2,1,0:T(8,128)(2,1)S(1)} %copy-done.2, f32[8,128]{1,0:T(8,128)S(1)} %get-tuple-element.61.norm), custom_call_target="tpu_custom_call" | custom-call | flops 905969664 | bytes 2318336 | tf_op jit(solution)/shard_map/pallas_call | solution.py:59
  94.7 3.4 %all-to-all-done.5 = bf16[4,224,128]{2,1,0:T(8,128)(2,1)S(1)} async-done(((bf16[4,224,128]{2,1,0:T(8,128)(2,1)}), bf16[4,224,128]{2,1,0:T(8,128)(2,1)S(1)}, u32[]{:S(2)}, u32[]{:S(2)}) %all-to-all-start.5) | async-done | bytes 229408 | tf_op jit(solution)/shard_map/all_to_all | solution.py:908
  98.3 12.4 %all_to_all.36.refs_1_ = bf16[4,896,128]{2,1,0:T(8,128)(2,1)S(1)} all-to-all(bf16[4,896,128]{2,1,0:T(8,128)(2,1)S(1)} %broadcast_in_dim.2), channel_id=1, replica_groups=mesh['tm'=4,'row'=2,'col'=4] {'col'}, dimensions={0} | all-to-all | bytes 1835008 | tf_op jit(solution)/shard_map/all_to_all | solution.py:912
  (47 shorter events, 18.0 us)
Async XLA Ops:
  0.6 21.4 %copy-start = (bf16[3,3,3,128,128]{4,3,2,1,0:T(8,128)(2,1)S(1)}, bf16[3,3,3,128,128]{4,3,2,1,0:T(8,128)(2,1)}, u32[]{:S(2)}) copy-start(bf16[3,3,3,128,128]{4,3,2,1,0:T(8,128)(2,1)} %param.5) | copy-start | bytes 2654212
  2.5 1.4 %collective-permute-start = (bf16[224,128]{1,0:T(8,128)(2,1)S(1)}, bf16[224,128]{1,0:T(8,128)(2,1)S(1)}, u32[]{:S(2)}, u32[]{:S(2)}) collective-permute-start(bf16[224,128]{1,0:T(8,128)(2,1)S(1)} %get-tuple-element.39), channel_id=1, source_target_pairs={{0,4},{4,0},{1,5},{5,1},{2,6},{6,2},{3,7},{7,3},{8,12},{12,8},{9,1... | collective-permute-start | bytes 172040 | tf_op jit(solution)/shard_map/ppermute | solution.py:666
  16.1 13.5 %copy-start.4 = (bf16[1248,128]{1,0:T(8,128)(2,1)}, bf16[1248,128]{1,0:T(8,128)(2,1)S(1)}, u32[]{:S(2)}) copy-start(bf16[1248,128]{1,0:T(8,128)(2,1)S(1)} %get-tuple-element.42.own.own_far) | copy-start | bytes 958468
  16.2 16.9 %collective-permute-start.2 = (bf16[1472,128]{1,0:T(8,128)(2,1)S(1)}, bf16[1472,128]{1,0:T(8,128)(2,1)S(1)}, u32[]{:S(2)}, u32[]{:S(2)}) collective-permute-start(bf16[1472,128]{1,0:T(8,128)(2,1)S(1)} %get-tuple-element.45.near), channel_id=1, source_target_pairs={{8,0},{16,8},{24,16},{9,1},{17,9},{25,17},{10,2},{18,10},{26,18},{... | collective-permute-start | bytes 1130504 | tf_op jit(solution)/shard_map/ppermute | solution.py:672
  17.5 10.0 %collective-permute-start.1 = (bf16[1248,128]{1,0:T(8,128)(2,1)S(1)}, bf16[1248,128]{1,0:T(8,128)(2,1)S(1)}, u32[]{:S(2)}, u32[]{:S(2)}) collective-permute-start(bf16[1248,128]{1,0:T(8,128)(2,1)S(1)} %get-tuple-element.42.own.own_far), channel_id=1, source_target_pairs={{0,8},{8,16},{16,24},{1,9},{9,17},{17,25},{2,10},{10,18},{18,26},{... | collective-permute-start | bytes 958472 | tf_op jit(solution)/shard_map/ppermute | solution.py:672
  27.4 9.6 %copy-start.5 = (bf16[1248,128]{1,0:T(8,128)(2,1)}, bf16[1248,128]{1,0:T(8,128)(2,1)S(1)}, u32[]{:S(2)}) copy-start(bf16[1248,128]{1,0:T(8,128)(2,1)S(1)} %collective-permute-done.1.before.near_far) | copy-start | bytes 958468
  29.7 9.3 %all-to-all-start.1 = ((bf16[8,96,128]{2,1,0:T(8,128)(2,1)}), bf16[8,96,128]{2,1,0:T(8,128)(2,1)S(1)}, u32[]{:S(2)}, u32[]{:S(2)}) async-start(bf16[8,96,128]{2,1,0:T(8,128)(2,1)} %get-tuple-element.44), calls=%async_computation.1 | async-start | bytes 393216 | tf_op jit(solution)/shard_map/all_to_all | solution.py:818
  33.1 1.2 %copy-start.6 = (bf16[3,3,3,128,128]{4,3,2,1,0:T(8,128)(2,1)S(1)}, bf16[3,3,3,128,128]{4,3,2,1,0:T(8,128)(2,1)}, u32[]{:S(2)}) copy-start(bf16[3,3,3,128,128]{4,3,2,1,0:T(8,128)(2,1)} %param.6) | copy-start | bytes 2654212
  40.2 8.3 %all-to-all-start.2 = ((f32[8,8,128]{2,1,0:T(8,128)}), f32[8,8,128]{2,1,0:T(8,128)S(1)}, u32[]{:S(2)}, u32[]{:S(2)}) async-start(f32[8,8,128]{2,1,0:T(8,128)} %get-tuple-element.46), calls=%async_computation.2 | async-start | bytes 65536 | tf_op jit(solution)/shard_map/all_to_all | solution.py:843
  48.4 6.7 %copy-start.1 = (f32[3456,128]{1,0:T(8,128)S(1)}, f32[3456,128]{1,0:T(8,128)}, u32[]{:S(2)}) copy-start(f32[3456,128]{1,0:T(8,128)} %get-tuple-element.53.second) | copy-start | bytes 5308420
  52.5 2.5 %collective-permute-start.3 = (bf16[3456,128]{1,0:T(8,128)(2,1)S(1)}, bf16[3456,128]{1,0:T(8,128)(2,1)S(1)}, u32[]{:S(2)}, u32[]{:S(2)}) collective-permute-start(bf16[3456,128]{1,0:T(8,128)(2,1)S(1)} %get-tuple-element.56), channel_id=1, source_target_pairs={{0,4},{4,0},{1,5},{5,1},{2,6},{6,2},{3,7},{7,3},{8,12},{12,8},{9,1... | collective-permute-start | bytes 2654216 | tf_op jit(solution)/shard_map/ppermute | solution.py:666
  56.9 4.2 %copy-start.8 = (bf16[1248,128]{1,0:T(8,128)(2,1)S(1)}, bf16[1248,128]{1,0:T(8,128)(2,1)}, u32[]{:S(2)}) copy-start(bf16[1248,128]{1,0:T(8,128)(2,1)} %get-tuple-element.57.near) | copy-start | bytes 958468
  56.9 23.0 %copy-start.2 = (bf16[2,16,32,128]{3,2,1,0:T(8,128)(2,1)S(1)}, bf16[2,16,32,128]{3,2,1,0:T(8,128)(2,1)}, u32[]{:S(2)}) copy-start(bf16[2,16,32,128]{3,2,1,0:T(8,128)(2,1)} %features.5) | copy-start | bytes 786436
  56.9 16.4 %all-to-all-start.3 = ((bf16[4,864,128]{2,1,0:T(8,128)(2,1)}), bf16[4,864,128]{2,1,0:T(8,128)(2,1)S(1)}, u32[]{:S(2)}, u32[]{:S(2)}) async-start(bf16[4,864,128]{2,1,0:T(8,128)(2,1)} %shard_map.85), calls=%async_computation.3 | async-start | bytes 1769472 | tf_op jit(solution)/shard_map/all_to_all | solution.py:880
  61.1 11.9 %collective-permute-start.4 = (bf16[1248,128]{1,0:T(8,128)(2,1)S(1)}, bf16[1248,128]{1,0:T(8,128)(2,1)S(1)}, u32[]{:S(2)}, u32[]{:S(2)}) collective-permute-start(bf16[1248,128]{1,0:T(8,128)(2,1)S(1)} %copy-done.8), channel_id=1, source_target_pairs={{8,0},{16,8},{24,16},{9,1},{17,9},{25,17},{10,2},{18,10},{26,18},{... | collective-permute-start | bytes 958472 | tf_op jit(solution)/shard_map/ppermute | solution.py:672
  62.4 17.5 %collective-permute-start.5 = (bf16[1248,128]{1,0:T(8,128)(2,1)S(1)}, bf16[1248,128]{1,0:T(8,128)(2,1)S(1)}, u32[]{:S(2)}, u32[]{:S(2)}) collective-permute-start(bf16[1248,128]{1,0:T(8,128)(2,1)S(1)} %get-tuple-element.59.act.far), channel_id=1, source_target_pairs={{0,8},{8,16},{16,24},{1,9},{9,17},{17,25},{2,10},{10,18},{18,26},{... | collective-permute-start | bytes 958472 | tf_op jit(solution)/shard_map/ppermute | solution.py:672
  74.1 13.5 %all-to-all-start.4 = ((bf16[4,224,128]{2,1,0:T(8,128)(2,1)}), bf16[4,224,128]{2,1,0:T(8,128)(2,1)S(1)}, u32[]{:S(2)}, u32[]{:S(2)}) async-start(bf16[4,224,128]{2,1,0:T(8,128)(2,1)} %shard_map.86), calls=%async_computation.4 | async-start | bytes 458752 | tf_op jit(solution)/shard_map/all_to_all | solution.py:889
  79.9 1.2 %copy-start.7 = (bf16[3,3,3,128,128]{4,3,2,1,0:T(8,128)(2,1)S(1)}, bf16[3,3,3,128,128]{4,3,2,1,0:T(8,128)(2,1)}, u32[]{:S(2)}) copy-start(bf16[3,3,3,128,128]{4,3,2,1,0:T(8,128)(2,1)} %param.6) | copy-start | bytes 2654212
  88.3 9.9 %all-to-all-start.5 = ((bf16[4,224,128]{2,1,0:T(8,128)(2,1)}), bf16[4,224,128]{2,1,0:T(8,128)(2,1)S(1)}, u32[]{:S(2)}, u32[]{:S(2)}) async-start(bf16[4,224,128]{2,1,0:T(8,128)(2,1)} %shard_map.89), calls=%async_computation.5 | async-start | bytes 458752 | tf_op jit(solution)/shard_map/all_to_all | solution.py:908
  93.5 1.2 %collective-permute-start.6 = (f32[8,128]{1,0:T(8,128)S(1)}, f32[8,128]{1,0:T(8,128)S(1)}, u32[]{:S(2)}, u32[]{:S(2)}) collective-permute-start(f32[8,128]{1,0:T(8,128)S(1)} %get-tuple-element.65), channel_id=1, source_target_pairs={{0,4},{4,0},{1,5},{5,1},{2,6},{6,2},{3,7},{7,3},{8,12},{12,8},{9,1... | collective-permute-start | bytes 12296 | tf_op jit(solution)/shard_map/ppermute | solution.py:666
  98.2 12.5 %copy-start.3 = (bf16[2,16,32,128]{3,2,1,0:T(8,128)(2,1)S(1)}, bf16[2,16,32,128]{3,2,1,0:T(8,128)(2,1)}, u32[]{:S(2)}) copy-start(bf16[2,16,32,128]{3,2,1,0:T(8,128)(2,1)} %out_grad.1) | copy-start | bytes 786436
  110.7 2.5 %collective-permute-start.7 = (bf16[4,896,128]{2,1,0:T(8,128)(2,1)S(1)}, bf16[4,896,128]{2,1,0:T(8,128)(2,1)S(1)}, u32[]{:S(2)}, u32[]{:S(2)}) collective-permute-start(bf16[4,896,128]{2,1,0:T(8,128)(2,1)S(1)} %all_to_all.36.refs_1_), channel_id=1, source_target_pairs={{0,4},{4,0},{1,5},{5,1},{2,6},{6,2},{3,7},{7,3},{8,12},{12,8},{9,1... | collective-permute-start | bytes 2752520 | tf_op jit(solution)/shard_map/ppermute | solution.py:666

commit v8 on v7

--- a/solution.py
+++ b/solution.py
@@ -406,9 +406,12 @@
         slots[peer] = jnp.concatenate([content, found, rest], 0).astype(BF16)
 
 
-def grad_act_body(size, near, far, kernel, out, x, frame):
+def grad_act_body(size, near, far, kernel_far, out, x, frame, kernel, sems):
     wo = x.shape[2]
+    copy = pltpu.make_async_copy(kernel_far, kernel, sems.at[0])
+    copy.start()
     spread_all(size, 2, 2, wo, near, far, x, frame)
+    copy.wait()
     sums = convolved(x, kernel, True)
     for f in range(FRAMES):
         out[f] = sums[f].reshape(size.tall(), wo, LANES)[:, : size.broad()]
@@ -589,20 +592,25 @@
     grad,
     near,
     own,
-    short,
     q,
     z,
     sems,
 ):
     pairs = [(q_far.at[f], q.at[f]) for f in range(FRAMES)]
     pairs += [(z_far.at[f], z.at[f]) for f in range(FRAMES)]
-    pairs += [(near_far, near), (own_far, own), (short_far, short)]
+    pairs += [(near_far, near), (own_far, own)]
     copies = [
         pltpu.make_async_copy(source, target, sems.at[k])
         for k, (source, target) in enumerate(pairs)
     ]
-    for k in (0, FRAMES, 1, FRAMES + 1, 2 * FRAMES, 2 * FRAMES + 1, 2 * FRAMES + 2):
+    for k in (0, FRAMES, 1, FRAMES + 1, 2 * FRAMES, 2 * FRAMES + 1):
         copies[k].start()
+    upper = place[0] == 0
+    given = pltpu.make_async_copy(short_far, give, sems.at[len(pairs) + 1])
+
+    @pl.when(upper)
+    def _():
+        given.start()
 
     def arrive(f):
         copies[f].wait()
@@ -615,13 +623,19 @@
     for copy in copies[2 * FRAMES :]:
         copy.wait()
     spread_all(size, 1, 1, size.wide, near, own, x, frame)
-    upper = place[0] == 0
     for b in range(3):
         for a, total in enumerate(tap_sums(x, turned, b)):
             rows = slice((a * 3 + b) * 3 * LANES, (a * 3 + b + 1) * 3 * LANES)
-            piece = total.T
-            out[rows] = piece
-            give[rows] = jnp.where(upper, short[rows], piece.astype(BF16))
+            out[rows] = total.T
+
+    @pl.when(jnp.logical_not(upper))
+    def _():
+        give[...] = out[...].astype(BF16)
+
+    @pl.when(upper)
+    def _():
+        given.wait()
+
     sent.wait()
 
 
@@ -688,11 +702,19 @@
 
 def joined_body(place, first, second, got, out):
     share = out.shape[1]
-    upper = place[0] == 0
-    for peer in range(out.shape[0]):
-        rows = slice(peer * share, (peer + 1) * share)
-        keep = jnp.where(upper, first[rows], second[rows])
-        out[peer] = (keep + got[rows].astype(F32)).astype(BF16)
+
+    def add(keep):
+        for peer in range(out.shape[0]):
+            rows = slice(peer * share, (peer + 1) * share)
+            out[peer] = (keep[rows] + got[rows].astype(F32)).astype(BF16)
+
+    @pl.when(place[0] == 0)
+    def _():
+        add(first)
+
+    @pl.when(place[0] != 0)
+    def _():
+        add(second)
 
 
 def shared_body(got, out, flat):
@@ -820,8 +842,10 @@
         part(grad_act_body, size),
         [((FRAMES, tall, broad, LANES), F32)],
         [grad, grad_after, second],
-        conv_scratch(size, 2, up(wide + 2, 16)),
-        mib=16,
+        [*conv_scratch(size, 2, up(wide + 2, 16)), (second.shape, BF16)],
+        far=1,
+        sems=1,
+        mib=18,
         flops=2 * work,
     )
     field = ((FRAMES, tall, broad, LANES), F32)
@@ -856,7 +880,7 @@
         part(first_term_body, size, across),
         [(first.shape, F32), (first.shape, BF16), block],
         [place, got, norm_second, q, z, act_before, act_first, second_short],
-        [*conv_scratch(size, 1, wide), turned, *[block] * 3, (first.shape, BF16), field, field],
+        [*conv_scratch(size, 1, wide), turned, *[block] * 3, field, field],
         smem=1,
         far=5,
         sems=2 * FRAMES + 4,

time: 116 us -> 115 us (level)
  local copies, waits for them, and re-layouts: 2.49 us -> 1.33 us
    unnamed x18 -> x16, local copies, waits for them, and re-layouts: 2.36 us -> 1.19 us
  transfers between devices with their start and end apart: 13 -> 13, of which waited for: 9 -> 9; matrix products, arithmetic and copies ran while one was open for 0% -> 0% of each run, Pallas kernels for 16% -> 17%
where the time goes in v8:
time: 115 us
  starting transfers between devices  33.4 us (29%)
  Pallas kernels  31.5 us (27%)
  waiting for transfers between devices  24.5 us (21%)
  blocking collectives  22.7 us (20%)
  local copies, waits for them, and re-layouts  1.33 us (1%)
    pallas_call x16, Pallas kernels, call(): pl.pallas_call(body, out_shape=shapes[:kept] + [pltpu.HBM(o.shape, o.dtyp...  28.6 us
    all_to_all x1, blocking collectives, on_device(): lax.all_to_all(jnp.broadcast_to(done[None], (across, *done.shape)), 'col'...  12.4 us
    ppermute x4, starting transfers between devices, later(): return lax.ppermute(values, 'tm', pairs)  12.2 us
    all_to_all x1, blocking collectives, on_device(): col_got = lax.all_to_all(slots, 'col', 0, 0)  10.4 us
    ppermute x4, waiting for transfers between devices, later(): return lax.ppermute(values, 'tm', pairs)  10.2 us
    all_to_all x2, starting transfers between devices, on_device(): got = lax.all_to_all(slots, ('row', 'col'), 0, 0)  6.73 us
    all_to_all x1, starting transfers between devices, on_device(): got = lax.all_to_all(slots, 'tm', 0, 0)  5.8 us
    all_to_all x1, starting transfers between devices, on_device(): slots = lax.all_to_all(slots, 'col', 0, 0)  4.15 us
  transfers between devices with their start and end apart: 13, of which 9 were waited for; matrix products, arithmetic and copies ran while one was open for 0% of the time, Pallas kernels for 17%

profile of v8, /device:TPU:0, one launch (start us, length us, event | category | flops | bytes accessed | tf_op | source)
XLA Modules:
  0.0 114.6 jit_solution(565231198734936990)
XLA Ops:
  0.7 1.8 %shard_map.75 = (bf16[224,128]{1,0:T(8,128)(2,1)S(1)}, f32[8,128]{1,0:T(8,128)S(1)}, f32[2,176,128]{2,1,0:T(8,128)S(1)}, bf16[2,16,32,128]{3,2,1,0:T(8,128)(2,1)S(1)}, bf16[2,16,32,128]{3,2,1,0:T(8,128)(2,1)S(1)}) custom-call(s32[2]{0:T(128)S(1)} %pad_add_fusion.place.refs_0_, bf16[2,16,32,128]{3,2,1,0:T(8,128)(2,1)} %features.5, ...), custom_call_target="tpu_custom_call" | custom-call | bytes 1290248 | tf_op jit(solution)/shard_map/pallas_call | solution.py:59
  4.5 10.4 %all_to_all.35.col_got = bf16[4,176,128]{2,1,0:T(8,128)(2,1)S(1)} all-to-all(bf16[4,176,128]{2,1,0:T(8,128)(2,1)S(1)} %shard_map.76), channel_id=1, replica_groups=mesh['tm'=4,'row'=2,'col'=4] {'col'}, dimensions={0} | all-to-all | bytes 360448 | tf_op jit(solution)/shard_map/all_to_all | solution.py:809
  17.5 4.6 %collective-permute-start.1 = (bf16[1248,128]{1,0:T(8,128)(2,1)S(1)}, bf16[1248,128]{1,0:T(8,128)(2,1)S(1)}, u32[]{:S(2)}, u32[]{:S(2)}) collective-permute-start(bf16[1248,128]{1,0:T(8,128)(2,1)S(1)} %get-tuple-element.42.own.own_far), channel_id=1, source_target_pairs={{0,8},{8,16},{16,24},{1,9},{9,17},{17,25},{2,10},{10,18},{18,26},{... | collective-permute-start | bytes 958472 | tf_op jit(solution)/shard_map/ppermute | solution.py:686
  22.9 4.5 %collective-permute-done.1.before.near_far = bf16[1248,128]{1,0:T(8,128)(2,1)S(1)} collective-permute-done((bf16[1248,128]{1,0:T(8,128)(2,1)S(1)}, bf16[1248,128]{1,0:T(8,128)(2,1)S(1)}, u32[]{:S(2)}, u32[]{:S(2)}) %collective-permute-start.1) | collective-permute-done | bytes 319520 | tf_op jit(solution)/shard_map/ppermute | solution.py:686
  27.4 2.3 %shard_map.79 = (bf16[2,16,32,128]{3,2,1,0:T(8,128)(2,1)S(1)}, bf16[8,96,128]{2,1,0:T(8,128)(2,1)}) custom-call(s32[2]{0:T(128)S(1)} %pad_add_fusion.place.refs_0_, bf16[1248,128]{1,0:T(8,128)(2,1)S(1)} %collective-permute-done.1.before.near_far, f32[2,512,128]{2,1,0:T(8,128)S(1)} %shard_map.78.sums, bf16[3456,128]{1,0:T(8,128)(2,1)S(1)} %bitcast.8), custom_call_target="tpu_custom_call" | custom-call | flops 452984832 | bytes 2187272 | tf_op jit(solution)/shard_map/pallas_call | solution.py:59
  29.7 3.4 %all-to-all-start.1 = ((bf16[8,96,128]{2,1,0:T(8,128)(2,1)}), bf16[8,96,128]{2,1,0:T(8,128)(2,1)S(1)}, u32[]{:S(2)}, u32[]{:S(2)}) async-start(bf16[8,96,128]{2,1,0:T(8,128)(2,1)} %get-tuple-element.44), calls=%async_computation.1 | async-start | bytes 393216 | tf_op jit(solution)/shard_map/all_to_all | solution.py:840
  33.1 3.5 %shard_map.80.grad_act = f32[2,18,40,128]{3,2,1,0:T(8,128)S(1)} custom-call(bf16[1472,128]{1,0:T(8,128)(2,1)S(1)} %get-tuple-element.45.near, bf16[1472,128]{1,0:T(8,128)(2,1)S(1)} %collective-permute-done.2.far, bf16[3456,128]{1,0:T(8,128)(2,1)} %bitcast.10), custom_call_target="tpu_custom_call" | custom-call | flops 1811939328 | bytes 2375680 | tf_op jit(solution)/shard_map/pallas_call | solution.py:59
  36.6 2.3 %all-to-all-done.1.got = bf16[8,96,128]{2,1,0:T(8,128)(2,1)S(1)} async-done(((bf16[8,96,128]{2,1,0:T(8,128)(2,1)}), bf16[8,96,128]{2,1,0:T(8,128)(2,1)S(1)}, u32[]{:S(2)}, u32[]{:S(2)}) %all-to-all-start.1) | async-done | bytes 196640 | tf_op jit(solution)/shard_map/all_to_all | solution.py:840
  40.2 3.3 %all-to-all-start.2 = ((f32[8,8,128]{2,1,0:T(8,128)}), f32[8,8,128]{2,1,0:T(8,128)S(1)}, u32[]{:S(2)}, u32[]{:S(2)}) async-start(f32[8,8,128]{2,1,0:T(8,128)} %get-tuple-element.46), calls=%async_computation.2 | async-start | bytes 65536 | tf_op jit(solution)/shard_map/all_to_all | solution.py:867
  43.5 2.2 %shard_map.82 = (bf16[1248,128]{1,0:T(8,128)(2,1)S(1)}, f32[2,18,40,128]{3,2,1,0:T(8,128)}, f32[2,18,40,128]{3,2,1,0:T(8,128)}) custom-call(s32[2]{0:T(128)S(1)} %pad_add_fusion.place.refs_0_, bf16[2,16,32,128]{3,2,1,0:T(8,128)(2,1)S(1)} %get-tuple-element.43.hidden, bf16[8,96,128]{2,1,0:T(8,128)(2,1)S(1)} %all-to-all-done.1.got, ...), custom_call_target="tpu_custom_call" | custom-call | tf_op jit(solution)/shard_map/pallas_call | solution.py:59
  45.8 2.7 %shard_map.83 = (f32[3456,128]{1,0:T(8,128)}, bf16[3456,128]{1,0:T(8,128)(2,1)}) custom-call(bf16[1472,128]{1,0:T(8,128)(2,1)S(1)} %get-tuple-element.45.near, bf16[1472,128]{1,0:T(8,128)(2,1)S(1)} %collective-permute-done.2.far, bf16[1248,128]{1,0:T(8,128)(2,1)S(1)} %get-tuple-element.59.act.far), custom_call_target="tpu_custom_call" | custom-call | tf_op jit(solution)/shard_map/pallas_call | solution.py:59
  48.4 3.8 %shard_map.84 = (f32[3456,128]{1,0:T(8,128)S(1)}, bf16[3456,128]{1,0:T(8,128)(2,1)S(1)}, bf16[1248,128]{1,0:T(8,128)(2,1)}) custom-call(s32[2]{0:T(128)S(1)} %pad_add_fusion.place.refs_0_, f32[8,8,128]{2,1,0:T(8,128)S(1)} %all-to-all-done.2.got, f32[8,128]{1,0:T(8,128)S(1)} %get-tuple-element.47.norm, f32[2,18,40,128]{3,2,1,0:T(8,128)} %get-tuple-element.48.q_far, ...), custom_call_target="tpu_custom_call" | custom-call | flops 905969664 | bytes 6008840 | tf_op jit(solution)/shard_map/pallas_call | solution.py:59
  52.8 2.1 %collective-permute-done.3.got = bf16[3456,128]{1,0:T(8,128)(2,1)S(1)} collective-permute-done((bf16[3456,128]{1,0:T(8,128)(2,1)S(1)}, bf16[3456,128]{1,0:T(8,128)(2,1)S(1)}, u32[]{:S(2)}, u32[]{:S(2)}) %collective-permute-start.3) | collective-permute-done | bytes 884768 | tf_op jit(solution)/shard_map/ppermute | solution.py:680
  54.8 1.6 %shard_map.85 = bf16[4,864,128]{2,1,0:T(8,128)(2,1)} custom-call(s32[2]{0:T(128)S(1)} %pad_add_fusion.place.refs_0_, f32[3456,128]{1,0:T(8,128)S(1)} %get-tuple-element.52.first, f32[3456,128]{1,0:T(8,128)S(1)} %copy-done.1, bf16[3456,128]{1,0:T(8,128)(2,1)S(1)} %collective-permute-done.3.got), custom_call_target="tpu_custom_call" | custom-call | bytes 5308424 | tf_op jit(solution)/shard_map/pallas_call | solution.py:59
  56.5 4.2 %all-to-all-start.3 = ((bf16[4,864,128]{2,1,0:T(8,128)(2,1)}), bf16[4,864,128]{2,1,0:T(8,128)(2,1)S(1)}, u32[]{:S(2)}, u32[]{:S(2)}) async-start(bf16[4,864,128]{2,1,0:T(8,128)(2,1)} %shard_map.85), calls=%async_computation.3 | async-start | bytes 1769472 | tf_op jit(solution)/shard_map/all_to_all | solution.py:904
  61.9 5.0 %collective-permute-start.5 = (bf16[1248,128]{1,0:T(8,128)(2,1)S(1)}, bf16[1248,128]{1,0:T(8,128)(2,1)S(1)}, u32[]{:S(2)}, u32[]{:S(2)}) collective-permute-start(bf16[1248,128]{1,0:T(8,128)(2,1)S(1)} %get-tuple-element.59.act.far), channel_id=1, source_target_pairs={{0,8},{8,16},{16,24},{1,9},{9,17},{17,25},{2,10},{10,18},{18,26},{... | collective-permute-start | bytes 958472 | tf_op jit(solution)/shard_map/ppermute | solution.py:686
  67.0 5.7 %collective-permute-done.4.far = bf16[1248,128]{1,0:T(8,128)(2,1)S(1)} collective-permute-done((bf16[1248,128]{1,0:T(8,128)(2,1)S(1)}, bf16[1248,128]{1,0:T(8,128)(2,1)S(1)}, u32[]{:S(2)}, u32[]{:S(2)}) %collective-permute-start.4) | collective-permute-done | bytes 319520 | tf_op jit(solution)/shard_map/ppermute | solution.py:686
  73.7 5.8 %all-to-all-start.4 = ((bf16[4,224,128]{2,1,0:T(8,128)(2,1)}), bf16[4,224,128]{2,1,0:T(8,128)(2,1)S(1)}, u32[]{:S(2)}, u32[]{:S(2)}) async-start(bf16[4,224,128]{2,1,0:T(8,128)(2,1)} %shard_map.86), calls=%async_computation.4 | async-start | bytes 458752 | tf_op jit(solution)/shard_map/all_to_all | solution.py:913
  80.7 2.4 %shard_map.87 = bf16[2,16,32,128]{3,2,1,0:T(8,128)(2,1)} custom-call(bf16[1248,128]{1,0:T(8,128)(2,1)S(1)} %collective-permute-done.5.near, bf16[1248,128]{1,0:T(8,128)(2,1)S(1)} %get-tuple-element.59.act.far, bf16[3456,128]{1,0:T(8,128)(2,1)S(1)} %bitcast.11, bf16[2,16,32,128]{3,2,1,0:T(8,128)(2,1)S(1)} %copy-done.2), custom_call_target="tpu_custom_call" | custom-call | flops 905969664 | bytes 2048000 | tf_op jit(solution)/shard_map/pallas_call | solution.py:59
  83.1 4.2 %all-to-all-done.4.got = bf16[4,224,128]{2,1,0:T(8,128)(2,1)S(1)} async-done(((bf16[4,224,128]{2,1,0:T(8,128)(2,1)}), bf16[4,224,128]{2,1,0:T(8,128)(2,1)S(1)}, u32[]{:S(2)}, u32[]{:S(2)}) %all-to-all-start.4) | async-done | bytes 229408 | tf_op jit(solution)/shard_map/all_to_all | solution.py:913
  88.0 3.4 %all-to-all-start.5 = ((bf16[4,224,128]{2,1,0:T(8,128)(2,1)}), bf16[4,224,128]{2,1,0:T(8,128)(2,1)S(1)}, u32[]{:S(2)}, u32[]{:S(2)}) async-start(bf16[4,224,128]{2,1,0:T(8,128)(2,1)} %shard_map.89), calls=%async_computation.5 | async-start | bytes 458752 | tf_op jit(solution)/shard_map/all_to_all | solution.py:932
  91.4 1.8 %shard_map.88 = (f32[2,512,128]{2,1,0:T(8,128)S(1)}, f32[8,128]{1,0:T(8,128)S(1)}) custom-call(bf16[1248,128]{1,0:T(8,128)(2,1)S(1)} %copy-done.7, bf16[1248,128]{1,0:T(8,128)(2,1)S(1)} %collective-permute-done.4.far, bf16[3456,128]{1,0:T(8,128)(2,1)S(1)} %bitcast.9, bf16[2,16,32,128]{3,2,1,0:T(8,128)(2,1)S(1)} %copy-done.2, f32[8,128]{1,0:T(8,128)S(1)} %get-tuple-element.61.norm), custom_call_target="tpu_custom_call" | custom-call | flops 905969664 | bytes 2318336 | tf_op jit(solution)/shard_map/pallas_call | solution.py:59
  94.4 3.4 %all-to-all-done.5 = bf16[4,224,128]{2,1,0:T(8,128)(2,1)S(1)} async-done(((bf16[4,224,128]{2,1,0:T(8,128)(2,1)}), bf16[4,224,128]{2,1,0:T(8,128)(2,1)S(1)}, u32[]{:S(2)}, u32[]{:S(2)}) %all-to-all-start.5) | async-done | bytes 229408 | tf_op jit(solution)/shard_map/all_to_all | solution.py:932
  98.0 12.4 %all_to_all.36.refs_1_ = bf16[4,896,128]{2,1,0:T(8,128)(2,1)S(1)} all-to-all(bf16[4,896,128]{2,1,0:T(8,128)(2,1)S(1)} %broadcast_in_dim.2), channel_id=1, replica_groups=mesh['tm'=4,'row'=2,'col'=4] {'col'}, dimensions={0} | all-to-all | bytes 1835008 | tf_op jit(solution)/shard_map/all_to_all | solution.py:936
  (45 shorter events, 16.9 us)
Async XLA Ops:
  0.6 21.4 %copy-start = (bf16[3,3,3,128,128]{4,3,2,1,0:T(8,128)(2,1)S(1)}, bf16[3,3,3,128,128]{4,3,2,1,0:T(8,128)(2,1)}, u32[]{:S(2)}) copy-start(bf16[3,3,3,128,128]{4,3,2,1,0:T(8,128)(2,1)} %param.5) | copy-start | bytes 2654212
  2.5 1.4 %collective-permute-start = (bf16[224,128]{1,0:T(8,128)(2,1)S(1)}, bf16[224,128]{1,0:T(8,128)(2,1)S(1)}, u32[]{:S(2)}, u32[]{:S(2)}) collective-permute-start(bf16[224,128]{1,0:T(8,128)(2,1)S(1)} %get-tuple-element.39), channel_id=1, source_target_pairs={{0,4},{4,0},{1,5},{5,1},{2,6},{6,2},{3,7},{7,3},{8,12},{12,8},{9,1... | collective-permute-start | bytes 172040 | tf_op jit(solution)/shard_map/ppermute | solution.py:680
  16.1 13.5 %copy-start.4 = (bf16[1248,128]{1,0:T(8,128)(2,1)}, bf16[1248,128]{1,0:T(8,128)(2,1)S(1)}, u32[]{:S(2)}) copy-start(bf16[1248,128]{1,0:T(8,128)(2,1)S(1)} %get-tuple-element.42.own.own_far) | copy-start | bytes 958468
  16.2 16.9 %collective-permute-start.2 = (bf16[1472,128]{1,0:T(8,128)(2,1)S(1)}, bf16[1472,128]{1,0:T(8,128)(2,1)S(1)}, u32[]{:S(2)}, u32[]{:S(2)}) collective-permute-start(bf16[1472,128]{1,0:T(8,128)(2,1)S(1)} %get-tuple-element.45.near), channel_id=1, source_target_pairs={{8,0},{16,8},{24,16},{9,1},{17,9},{25,17},{10,2},{18,10},{26,18},{... | collective-permute-start | bytes 1130504 | tf_op jit(solution)/shard_map/ppermute | solution.py:686
  17.5 10.0 %collective-permute-start.1 = (bf16[1248,128]{1,0:T(8,128)(2,1)S(1)}, bf16[1248,128]{1,0:T(8,128)(2,1)S(1)}, u32[]{:S(2)}, u32[]{:S(2)}) collective-permute-start(bf16[1248,128]{1,0:T(8,128)(2,1)S(1)} %get-tuple-element.42.own.own_far), channel_id=1, source_target_pairs={{0,8},{8,16},{16,24},{1,9},{9,17},{17,25},{2,10},{10,18},{18,26},{... | collective-permute-start | bytes 958472 | tf_op jit(solution)/shard_map/ppermute | solution.py:686
  27.4 9.2 %copy-start.5 = (bf16[1248,128]{1,0:T(8,128)(2,1)}, bf16[1248,128]{1,0:T(8,128)(2,1)S(1)}, u32[]{:S(2)}) copy-start(bf16[1248,128]{1,0:T(8,128)(2,1)S(1)} %collective-permute-done.1.before.near_far) | copy-start | bytes 958468
  29.7 9.3 %all-to-all-start.1 = ((bf16[8,96,128]{2,1,0:T(8,128)(2,1)}), bf16[8,96,128]{2,1,0:T(8,128)(2,1)S(1)}, u32[]{:S(2)}, u32[]{:S(2)}) async-start(bf16[8,96,128]{2,1,0:T(8,128)(2,1)} %get-tuple-element.44), calls=%async_computation.1 | async-start | bytes 393216 | tf_op jit(solution)/shard_map/all_to_all | solution.py:840
  40.2 8.3 %all-to-all-start.2 = ((f32[8,8,128]{2,1,0:T(8,128)}), f32[8,8,128]{2,1,0:T(8,128)S(1)}, u32[]{:S(2)}, u32[]{:S(2)}) async-start(f32[8,8,128]{2,1,0:T(8,128)} %get-tuple-element.46), calls=%async_computation.2 | async-start | bytes 65536 | tf_op jit(solution)/shard_map/all_to_all | solution.py:867
  48.4 6.4 %copy-start.1 = (f32[3456,128]{1,0:T(8,128)S(1)}, f32[3456,128]{1,0:T(8,128)}, u32[]{:S(2)}) copy-start(f32[3456,128]{1,0:T(8,128)} %get-tuple-element.53.second) | copy-start | bytes 5308420
  52.3 2.6 %collective-permute-start.3 = (bf16[3456,128]{1,0:T(8,128)(2,1)S(1)}, bf16[3456,128]{1,0:T(8,128)(2,1)S(1)}, u32[]{:S(2)}, u32[]{:S(2)}) collective-permute-start(bf16[3456,128]{1,0:T(8,128)(2,1)S(1)} %get-tuple-element.56), channel_id=1, source_target_pairs={{0,4},{4,0},{1,5},{5,1},{2,6},{6,2},{3,7},{7,3},{8,12},{12,8},{9,1... | collective-permute-start | bytes 2654216 | tf_op jit(solution)/shard_map/ppermute | solution.py:680
  56.5 4.2 %copy-start.7 = (bf16[1248,128]{1,0:T(8,128)(2,1)S(1)}, bf16[1248,128]{1,0:T(8,128)(2,1)}, u32[]{:S(2)}) copy-start(bf16[1248,128]{1,0:T(8,128)(2,1)} %get-tuple-element.57.near) | copy-start | bytes 958468
  56.5 23.1 %copy-start.2 = (bf16[2,16,32,128]{3,2,1,0:T(8,128)(2,1)S(1)}, bf16[2,16,32,128]{3,2,1,0:T(8,128)(2,1)}, u32[]{:S(2)}) copy-start(bf16[2,16,32,128]{3,2,1,0:T(8,128)(2,1)} %features.5) | copy-start | bytes 786436
  56.5 16.5 %all-to-all-start.3 = ((bf16[4,864,128]{2,1,0:T(8,128)(2,1)}), bf16[4,864,128]{2,1,0:T(8,128)(2,1)S(1)}, u32[]{:S(2)}, u32[]{:S(2)}) async-start(bf16[4,864,128]{2,1,0:T(8,128)(2,1)} %shard_map.85), calls=%async_computation.3 | async-start | bytes 1769472 | tf_op jit(solution)/shard_map/all_to_all | solution.py:904
  60.6 12.1 %collective-permute-start.4 = (bf16[1248,128]{1,0:T(8,128)(2,1)S(1)}, bf16[1248,128]{1,0:T(8,128)(2,1)S(1)}, u32[]{:S(2)}, u32[]{:S(2)}) collective-permute-start(bf16[1248,128]{1,0:T(8,128)(2,1)S(1)} %copy-done.7), channel_id=1, source_target_pairs={{8,0},{16,8},{24,16},{9,1},{17,9},{25,17},{10,2},{18,10},{26,18},{... | collective-permute-start | bytes 958472 | tf_op jit(solution)/shard_map/ppermute | solution.py:686
  61.9 17.6 %collective-permute-start.5 = (bf16[1248,128]{1,0:T(8,128)(2,1)S(1)}, bf16[1248,128]{1,0:T(8,128)(2,1)S(1)}, u32[]{:S(2)}, u32[]{:S(2)}) collective-permute-start(bf16[1248,128]{1,0:T(8,128)(2,1)S(1)} %get-tuple-element.59.act.far), channel_id=1, source_target_pairs={{0,8},{8,16},{16,24},{1,9},{9,17},{17,25},{2,10},{10,18},{18,26},{... | collective-permute-start | bytes 958472 | tf_op jit(solution)/shard_map/ppermute | solution.py:686
  73.7 13.5 %all-to-all-start.4 = ((bf16[4,224,128]{2,1,0:T(8,128)(2,1)}), bf16[4,224,128]{2,1,0:T(8,128)(2,1)S(1)}, u32[]{:S(2)}, u32[]{:S(2)}) async-start(bf16[4,224,128]{2,1,0:T(8,128)(2,1)} %shard_map.86), calls=%async_computation.4 | async-start | bytes 458752 | tf_op jit(solution)/shard_map/all_to_all | solution.py:913
  79.5 1.2 %copy-start.6 = (bf16[3,3,3,128,128]{4,3,2,1,0:T(8,128)(2,1)S(1)}, bf16[3,3,3,128,128]{4,3,2,1,0:T(8,128)(2,1)}, u32[]{:S(2)}) copy-start(bf16[3,3,3,128,128]{4,3,2,1,0:T(8,128)(2,1)} %param.6) | copy-start | bytes 2654212
  88.0 9.9 %all-to-all-start.5 = ((bf16[4,224,128]{2,1,0:T(8,128)(2,1)}), bf16[4,224,128]{2,1,0:T(8,128)(2,1)S(1)}, u32[]{:S(2)}, u32[]{:S(2)}) async-start(bf16[4,224,128]{2,1,0:T(8,128)(2,1)} %shard_map.89), calls=%async_computation.5 | async-start | bytes 458752 | tf_op jit(solution)/shard_map/all_to_all | solution.py:932
  93.2 1.2 %collective-permute-start.6 = (f32[8,128]{1,0:T(8,128)S(1)}, f32[8,128]{1,0:T(8,128)S(1)}, u32[]{:S(2)}, u32[]{:S(2)}) collective-permute-start(f32[8,128]{1,0:T(8,128)S(1)} %get-tuple-element.65), channel_id=1, source_target_pairs={{0,4},{4,0},{1,5},{5,1},{2,6},{6,2},{3,7},{7,3},{8,12},{12,8},{9,1... | collective-permute-start | bytes 12296 | tf_op jit(solution)/shard_map/ppermute | solution.py:680
  97.9 12.5 %copy-start.3 = (bf16[2,16,32,128]{3,2,1,0:T(8,128)(2,1)S(1)}, bf16[2,16,32,128]{3,2,1,0:T(8,128)(2,1)}, u32[]{:S(2)}) copy-start(bf16[2,16,32,128]{3,2,1,0:T(8,128)(2,1)} %out_grad.1) | copy-start | bytes 786436
  110.4 2.5 %collective-permute-start.7 = (bf16[4,896,128]{2,1,0:T(8,128)(2,1)S(1)}, bf16[4,896,128]{2,1,0:T(8,128)(2,1)S(1)}, u32[]{:S(2)}, u32[]{:S(2)}) collective-permute-start(bf16[4,896,128]{2,1,0:T(8,128)(2,1)S(1)} %all_to_all.36.refs_1_), channel_id=1, source_target_pairs={{0,4},{4,0},{1,5},{5,1},{2,6},{6,2},{3,7},{7,3},{8,12},{12,8},{9,1... | collective-permute-start | bytes 2752520 | tf_op jit(solution)/shard_map/ppermute | solution.py:680

commit v9 on v8

--- a/solution.py
+++ b/solution.py
@@ -583,7 +583,8 @@
     near_far,
     own_far,
     short_far,
-    out,
+    second_far,
+    keep,
     give,
     grad_far,
     x,
@@ -607,10 +608,15 @@
         copies[k].start()
     upper = place[0] == 0
     given = pltpu.make_async_copy(short_far, give, sems.at[len(pairs) + 1])
+    kept = pltpu.make_async_copy(second_far, keep, sems.at[len(pairs) + 2])
 
     @pl.when(upper)
     def _():
         given.start()
+
+    @pl.when(jnp.logical_not(upper))
+    def _():
+        kept.start()
 
     def arrive(f):
         copies[f].wait()
@@ -623,18 +629,28 @@
     for copy in copies[2 * FRAMES :]:
         copy.wait()
     spread_all(size, 1, 1, size.wide, near, own, x, frame)
+
+    def put(rows, piece):
+        @pl.when(upper)
+        def _():
+            keep[rows] = piece
+
+        @pl.when(jnp.logical_not(upper))
+        def _():
+            give[rows] = piece.astype(BF16)
+
     for b in range(3):
         for a, total in enumerate(tap_sums(x, turned, b)):
             rows = slice((a * 3 + b) * 3 * LANES, (a * 3 + b + 1) * 3 * LANES)
-            out[rows] = total.T
-
-    @pl.when(jnp.logical_not(upper))
-    def _():
-        give[...] = out[...].astype(BF16)
+            put(rows, total.T)
 
     @pl.when(upper)
     def _():
         given.wait()
+
+    @pl.when(jnp.logical_not(upper))
+    def _():
+        kept.wait()
 
     sent.wait()
 
@@ -700,21 +716,11 @@
     return total
 
 
-def joined_body(place, first, second, got, out):
+def joined_body(keep, got, out):
     share = out.shape[1]
-
-    def add(keep):
-        for peer in range(out.shape[0]):
-            rows = slice(peer * share, (peer + 1) * share)
-            out[peer] = (keep[rows] + got[rows].astype(F32)).astype(BF16)
-
-    @pl.when(place[0] == 0)
-    def _():
-        add(first)
-
-    @pl.when(place[0] != 0)
-    def _():
-        add(second)
+    for peer in range(out.shape[0]):
+        rows = slice(peer * share, (peer + 1) * share)
+        out[peer] = (keep[rows] + got[rows].astype(F32)).astype(BF16)
 
 
 def shared_body(got, out, flat):
@@ -835,7 +841,7 @@
         [*conv_scratch(size, 1, wide, FRAMES), ((2, span, LANES), F32)],
         smem=1,
         mib=12,
-        flops=work // 2,
+        flops=2 * work,
     )
     got = lax.all_to_all(slots, ("row", "col"), 0, 0)
     (grad_act,) = call(
@@ -876,14 +882,14 @@
         beside=True,
         out_far=2,
     )
-    first_term, give, grad_second = call(
+    keep, give, grad_second = call(
         part(first_term_body, size, across),
         [(first.shape, F32), (first.shape, BF16), block],
-        [place, got, norm_second, q, z, act_before, act_first, second_short],
+        [place, got, norm_second, q, z, act_before, act_first, second_short, second_term],
         [*conv_scratch(size, 1, wide), turned, *[block] * 3, field, field],
         smem=1,
-        far=5,
-        sems=2 * FRAMES + 4,
+        far=6,
+        sems=2 * FRAMES + 5,
         mib=20,
         flops=work,
         out_far=1,
@@ -895,12 +901,7 @@
     along = lax.axis_size("tm")
     rows = first.shape[0]
     by_col = rows // across
-    (slots,) = call(
-        joined_body,
-        [((across, by_col, LANES), BF16)],
-        [place, first_term, second_term, row_swap(give)],
-        smem=1,
-    )
+    (slots,) = call(joined_body, [((across, by_col, LANES), BF16)], [keep, row_swap(give)])
     slots = lax.all_to_all(slots, "col", 0, 0)
     slots, grad_second_after = lax.optimization_barrier((slots, grad_second_after))
     share = up(by_col, 16 * along) // along

time: 115 us -> 114 us (level)
  waiting for transfers between devices: 24.5 us -> 23.2 us
    ppermute x4, waiting for transfers between devices: 10.2 us -> 8.99 us  [later(): return lax.ppermute(values, 'tm', pairs)]
where the time goes in v9:
time: 114 us; the launch traced here: 113 us
  starting transfers between devices  32.4 us (28%)
  Pallas kernels  32.3 us (28%)
  waiting for transfers between devices  23.2 us (20%)
  blocking collectives  22.8 us (20%)
  local copies, waits for them, and re-layouts  1.33 us (1%)
    pallas_call x16, Pallas kernels, call(): pl.pallas_call(body, out_shape=shapes[:kept] + [pltpu.HBM(o.shape, o.dtyp...  29.4 us
    all_to_all x1, blocking collectives, on_device(): lax.all_to_all(jnp.broadcast_to(done[None], (across, *done.shape)), 'col'...  12.4 us
    ppermute x4, starting transfers between devices, later(): return lax.ppermute(values, 'tm', pairs)  11.3 us
    all_to_all x1, blocking collectives, on_device(): col_got = lax.all_to_all(slots, 'col', 0, 0)  10.4 us
    ppermute x4, waiting for transfers between devices, later(): return lax.ppermute(values, 'tm', pairs)  8.99 us
    all_to_all x2, starting transfers between devices, on_device(): got = lax.all_to_all(slots, ('row', 'col'), 0, 0)  6.73 us
    all_to_all x1, starting transfers between devices, on_device(): got = lax.all_to_all(slots, 'tm', 0, 0)  5.77 us
    all_to_all x1, waiting for transfers between devices, on_device(): got = lax.all_to_all(slots, 'tm', 0, 0)  4.12 us
  transfers between devices with their start and end apart: 13, of which 9 were waited for; matrix products, arithmetic and copies ran while one was open for 0% of the time, Pallas kernels for 17%

profile of v9, /device:TPU:0, one launch (start us, length us, event | category | flops | bytes accessed | tf_op | source)
XLA Modules:
  0.0 113.2 jit_solution(8719930776063825338)
XLA Ops:
  0.7 1.8 %shard_map.75 = (bf16[224,128]{1,0:T(8,128)(2,1)S(1)}, f32[8,128]{1,0:T(8,128)S(1)}, f32[2,176,128]{2,1,0:T(8,128)S(1)}, bf16[2,16,32,128]{3,2,1,0:T(8,128)(2,1)S(1)}, bf16[2,16,32,128]{3,2,1,0:T(8,128)(2,1)S(1)}) custom-call(s32[2]{0:T(128)S(1)} %pad_add_fusion.place.refs_0_, bf16[2,16,32,128]{3,2,1,0:T(8,128)(2,1)} %features.5, ...), custom_call_target="tpu_custom_call" | custom-call | bytes 1290248 | tf_op jit(solution)/shard_map/pallas_call | solution.py:59
  4.5 10.4 %all_to_all.35.col_got = bf16[4,176,128]{2,1,0:T(8,128)(2,1)S(1)} all-to-all(bf16[4,176,128]{2,1,0:T(8,128)(2,1)S(1)} %shard_map.76), channel_id=1, replica_groups=mesh['tm'=4,'row'=2,'col'=4] {'col'}, dimensions={0} | all-to-all | bytes 360448 | tf_op jit(solution)/shard_map/all_to_all | solution.py:815
  16.2 3.5 %collective-permute-start.1 = (bf16[1248,128]{1,0:T(8,128)(2,1)S(1)}, bf16[1248,128]{1,0:T(8,128)(2,1)S(1)}, u32[]{:S(2)}, u32[]{:S(2)}) collective-permute-start(bf16[1248,128]{1,0:T(8,128)(2,1)S(1)} %get-tuple-element.42.own.own_far), channel_id=1, source_target_pairs={{0,8},{8,16},{16,24},{1,9},{9,17},{17,25},{2,10},{10,18},{18,26},{... | collective-permute-start | bytes 958472 | tf_op jit(solution)/shard_map/ppermute | solution.py:702
  21.8 3.5 %collective-permute-done.1.before.near_far = bf16[1248,128]{1,0:T(8,128)(2,1)S(1)} collective-permute-done((bf16[1248,128]{1,0:T(8,128)(2,1)S(1)}, bf16[1248,128]{1,0:T(8,128)(2,1)S(1)}, u32[]{:S(2)}, u32[]{:S(2)}) %collective-permute-start.1) | collective-permute-done | bytes 319520 | tf_op jit(solution)/shard_map/ppermute | solution.py:702
  25.3 2.3 %shard_map.79 = (bf16[2,16,32,128]{3,2,1,0:T(8,128)(2,1)S(1)}, bf16[8,96,128]{2,1,0:T(8,128)(2,1)}) custom-call(s32[2]{0:T(128)S(1)} %pad_add_fusion.place.refs_0_, bf16[1248,128]{1,0:T(8,128)(2,1)S(1)} %collective-permute-done.1.before.near_far, f32[2,512,128]{2,1,0:T(8,128)S(1)} %shard_map.78.sums, bf16[3456,128]{1,0:T(8,128)(2,1)S(1)} %bitcast.8), custom_call_target="tpu_custom_call" | custom-call | flops 1811939328 | bytes 2187272 | tf_op jit(solution)/shard_map/pallas_call | solution.py:59
  27.6 3.4 %all-to-all-start.1 = ((bf16[8,96,128]{2,1,0:T(8,128)(2,1)}), bf16[8,96,128]{2,1,0:T(8,128)(2,1)S(1)}, u32[]{:S(2)}, u32[]{:S(2)}) async-start(bf16[8,96,128]{2,1,0:T(8,128)(2,1)} %get-tuple-element.44), calls=%async_computation.1 | async-start | bytes 393216 | tf_op jit(solution)/shard_map/all_to_all | solution.py:846
  31.0 3.5 %shard_map.80.grad_act = f32[2,18,40,128]{3,2,1,0:T(8,128)S(1)} custom-call(bf16[1472,128]{1,0:T(8,128)(2,1)S(1)} %get-tuple-element.45.near, bf16[1472,128]{1,0:T(8,128)(2,1)S(1)} %collective-permute-done.2.far, bf16[3456,128]{1,0:T(8,128)(2,1)} %bitcast.10), custom_call_target="tpu_custom_call" | custom-call | flops 1811939328 | bytes 2375680 | tf_op jit(solution)/shard_map/pallas_call | solution.py:59
  34.6 2.3 %all-to-all-done.1.got = bf16[8,96,128]{2,1,0:T(8,128)(2,1)S(1)} async-done(((bf16[8,96,128]{2,1,0:T(8,128)(2,1)}), bf16[8,96,128]{2,1,0:T(8,128)(2,1)S(1)}, u32[]{:S(2)}, u32[]{:S(2)}) %all-to-all-start.1) | async-done | bytes 196640 | tf_op jit(solution)/shard_map/all_to_all | solution.py:846
  38.1 3.3 %all-to-all-start.2 = ((f32[8,8,128]{2,1,0:T(8,128)}), f32[8,8,128]{2,1,0:T(8,128)S(1)}, u32[]{:S(2)}, u32[]{:S(2)}) async-start(f32[8,8,128]{2,1,0:T(8,128)} %get-tuple-element.46), calls=%async_computation.2 | async-start | bytes 65536 | tf_op jit(solution)/shard_map/all_to_all | solution.py:873
  41.5 2.2 %shard_map.82 = (bf16[1248,128]{1,0:T(8,128)(2,1)S(1)}, f32[2,18,40,128]{3,2,1,0:T(8,128)}, f32[2,18,40,128]{3,2,1,0:T(8,128)}) custom-call(s32[2]{0:T(128)S(1)} %pad_add_fusion.place.refs_0_, bf16[2,16,32,128]{3,2,1,0:T(8,128)(2,1)S(1)} %get-tuple-element.43.hidden, bf16[8,96,128]{2,1,0:T(8,128)(2,1)S(1)} %all-to-all-done.1.got, ...), custom_call_target="tpu_custom_call" | custom-call | tf_op jit(solution)/shard_map/pallas_call | solution.py:59
  43.7 2.7 %shard_map.83 = (f32[3456,128]{1,0:T(8,128)}, bf16[3456,128]{1,0:T(8,128)(2,1)}) custom-call(bf16[1472,128]{1,0:T(8,128)(2,1)S(1)} %get-tuple-element.45.near, bf16[1472,128]{1,0:T(8,128)(2,1)S(1)} %collective-permute-done.2.far, bf16[1248,128]{1,0:T(8,128)(2,1)S(1)} %get-tuple-element.59.act.far), custom_call_target="tpu_custom_call" | custom-call | tf_op jit(solution)/shard_map/pallas_call | solution.py:59
  46.4 5.0 %shard_map.84 = (f32[3456,128]{1,0:T(8,128)S(1)}, bf16[3456,128]{1,0:T(8,128)(2,1)S(1)}, bf16[1248,128]{1,0:T(8,128)(2,1)}) custom-call(s32[2]{0:T(128)S(1)} %pad_add_fusion.place.refs_0_, f32[8,8,128]{2,1,0:T(8,128)S(1)} %all-to-all-done.2.got, f32[8,128]{1,0:T(8,128)S(1)} %get-tuple-element.47.norm, f32[2,18,40,128]{3,2,1,0:T(8,128)} %get-tuple-element.48.q_far, ...), custom_call_target="tpu_custom_call" | custom-call | flops 905969664 | bytes 7778312 | tf_op jit(solution)/shard_map/pallas_call | solution.py:59
  52.0 2.1 %collective-permute-done.3.got = bf16[3456,128]{1,0:T(8,128)(2,1)S(1)} collective-permute-done((bf16[3456,128]{1,0:T(8,128)(2,1)S(1)}, bf16[3456,128]{1,0:T(8,128)(2,1)S(1)}, u32[]{:S(2)}, u32[]{:S(2)}) %collective-permute-start.3) | collective-permute-done | bytes 884768 | tf_op jit(solution)/shard_map/ppermute | solution.py:696
  55.1 4.1 %all-to-all-start.3 = ((bf16[4,864,128]{2,1,0:T(8,128)(2,1)}), bf16[4,864,128]{2,1,0:T(8,128)(2,1)S(1)}, u32[]{:S(2)}, u32[]{:S(2)}) async-start(bf16[4,864,128]{2,1,0:T(8,128)(2,1)} %shard_map.85), calls=%async_computation.3 | async-start | bytes 1769472 | tf_op jit(solution)/shard_map/all_to_all | solution.py:905
  60.5 5.2 %collective-permute-start.5 = (bf16[1248,128]{1,0:T(8,128)(2,1)S(1)}, bf16[1248,128]{1,0:T(8,128)(2,1)S(1)}, u32[]{:S(2)}, u32[]{:S(2)}) collective-permute-start(bf16[1248,128]{1,0:T(8,128)(2,1)S(1)} %get-tuple-element.59.act.far), channel_id=1, source_target_pairs={{0,8},{8,16},{16,24},{1,9},{9,17},{17,25},{2,10},{10,18},{18,26},{... | collective-permute-start | bytes 958472 | tf_op jit(solution)/shard_map/ppermute | solution.py:702
  65.8 5.5 %collective-permute-done.4.far = bf16[1248,128]{1,0:T(8,128)(2,1)S(1)} collective-permute-done((bf16[1248,128]{1,0:T(8,128)(2,1)S(1)}, bf16[1248,128]{1,0:T(8,128)(2,1)S(1)}, u32[]{:S(2)}, u32[]{:S(2)}) %collective-permute-start.4) | collective-permute-done | bytes 319520 | tf_op jit(solution)/shard_map/ppermute | solution.py:702
  72.3 5.8 %all-to-all-start.4 = ((bf16[4,224,128]{2,1,0:T(8,128)(2,1)}), bf16[4,224,128]{2,1,0:T(8,128)(2,1)S(1)}, u32[]{:S(2)}, u32[]{:S(2)}) async-start(bf16[4,224,128]{2,1,0:T(8,128)(2,1)} %shard_map.86), calls=%async_computation.4 | async-start | bytes 458752 | tf_op jit(solution)/shard_map/all_to_all | solution.py:914
  79.3 2.4 %shard_map.87 = bf16[2,16,32,128]{3,2,1,0:T(8,128)(2,1)} custom-call(bf16[1248,128]{1,0:T(8,128)(2,1)S(1)} %collective-permute-done.5.near, bf16[1248,128]{1,0:T(8,128)(2,1)S(1)} %get-tuple-element.59.act.far, bf16[3456,128]{1,0:T(8,128)(2,1)S(1)} %bitcast.11, bf16[2,16,32,128]{3,2,1,0:T(8,128)(2,1)S(1)} %copy-done.1), custom_call_target="tpu_custom_call" | custom-call | flops 905969664 | bytes 2048000 | tf_op jit(solution)/shard_map/pallas_call | solution.py:59
  81.7 4.1 %all-to-all-done.4.got = bf16[4,224,128]{2,1,0:T(8,128)(2,1)S(1)} async-done(((bf16[4,224,128]{2,1,0:T(8,128)(2,1)}), bf16[4,224,128]{2,1,0:T(8,128)(2,1)S(1)}, u32[]{:S(2)}, u32[]{:S(2)}) %all-to-all-start.4) | async-done | bytes 229408 | tf_op jit(solution)/shard_map/all_to_all | solution.py:914
  86.5 3.4 %all-to-all-start.5 = ((bf16[4,224,128]{2,1,0:T(8,128)(2,1)}), bf16[4,224,128]{2,1,0:T(8,128)(2,1)S(1)}, u32[]{:S(2)}, u32[]{:S(2)}) async-start(bf16[4,224,128]{2,1,0:T(8,128)(2,1)} %shard_map.89), calls=%async_computation.5 | async-start | bytes 458752 | tf_op jit(solution)/shard_map/all_to_all | solution.py:933
  89.9 1.9 %shard_map.88 = (f32[2,512,128]{2,1,0:T(8,128)S(1)}, f32[8,128]{1,0:T(8,128)S(1)}) custom-call(bf16[1248,128]{1,0:T(8,128)(2,1)S(1)} %copy-done.6, bf16[1248,128]{1,0:T(8,128)(2,1)S(1)} %collective-permute-done.4.far, bf16[3456,128]{1,0:T(8,128)(2,1)S(1)} %bitcast.9, bf16[2,16,32,128]{3,2,1,0:T(8,128)(2,1)S(1)} %copy-done.1, f32[8,128]{1,0:T(8,128)S(1)} %get-tuple-element.61.norm), custom_call_target="tpu_custom_call" | custom-call | flops 905969664 | bytes 2318336 | tf_op jit(solution)/shard_map/pallas_call | solution.py:59
  93.0 3.4 %all-to-all-done.5 = bf16[4,224,128]{2,1,0:T(8,128)(2,1)S(1)} async-done(((bf16[4,224,128]{2,1,0:T(8,128)(2,1)}), bf16[4,224,128]{2,1,0:T(8,128)(2,1)S(1)}, u32[]{:S(2)}, u32[]{:S(2)}) %all-to-all-start.5) | async-done | bytes 229408 | tf_op jit(solution)/shard_map/all_to_all | solution.py:933
  96.6 12.4 %all_to_all.36.refs_1_ = bf16[4,896,128]{2,1,0:T(8,128)(2,1)S(1)} all-to-all(bf16[4,896,128]{2,1,0:T(8,128)(2,1)S(1)} %broadcast_in_dim.2), channel_id=1, replica_groups=mesh['tm'=4,'row'=2,'col'=4] {'col'}, dimensions={0} | all-to-all | bytes 1835008 | tf_op jit(solution)/shard_map/all_to_all | solution.py:937
  111.5 1.5 %shard_map.92 = (bf16[3456,128]{1,0:T(8,128)(2,1)}, bf16[3456,128]{1,0:T(8,128)(2,1)}) custom-call(s32[2]{0:T(128)S(1)} %pad_add_fusion.place.refs_0_, bf16[4,896,128]{2,1,0:T(8,128)(2,1)S(1)} %collective-permute-done.7.refs_1_, bf16[3456,128]{1,0:T(8,128)(2,1)} %get-tuple-element.66.refs_2_, ...), custom_call_target="tpu_custom_call", output_to_operand_aliasing={{0}: (2, {}), {1}: (3, {})} | custom-call | tf_op jit(solution)/shard_map/pallas_call | solution.py:768
  (43 shorter events, 16.5 us)
Async XLA Ops:
  0.6 20.3 %copy-start.3 = (bf16[3,3,3,128,128]{4,3,2,1,0:T(8,128)(2,1)S(1)}, bf16[3,3,3,128,128]{4,3,2,1,0:T(8,128)(2,1)}, u32[]{:S(2)}) copy-start(bf16[3,3,3,128,128]{4,3,2,1,0:T(8,128)(2,1)} %param.5) | copy-start | bytes 2654212
  2.5 1.4 %collective-permute-start = (bf16[224,128]{1,0:T(8,128)(2,1)S(1)}, bf16[224,128]{1,0:T(8,128)(2,1)S(1)}, u32[]{:S(2)}, u32[]{:S(2)}) collective-permute-start(bf16[224,128]{1,0:T(8,128)(2,1)S(1)} %get-tuple-element.39), channel_id=1, source_target_pairs={{0,4},{4,0},{1,5},{5,1},{2,6},{6,2},{3,7},{7,3},{8,12},{12,8},{9,1... | collective-permute-start | bytes 172040 | tf_op jit(solution)/shard_map/ppermute | solution.py:696
  16.2 11.5 %copy-start = (bf16[1248,128]{1,0:T(8,128)(2,1)}, bf16[1248,128]{1,0:T(8,128)(2,1)S(1)}, u32[]{:S(2)}) copy-start(bf16[1248,128]{1,0:T(8,128)(2,1)S(1)} %get-tuple-element.42.own.own_far) | copy-start | bytes 958468
  16.2 9.2 %collective-permute-start.1 = (bf16[1248,128]{1,0:T(8,128)(2,1)S(1)}, bf16[1248,128]{1,0:T(8,128)(2,1)S(1)}, u32[]{:S(2)}, u32[]{:S(2)}) collective-permute-start(bf16[1248,128]{1,0:T(8,128)(2,1)S(1)} %get-tuple-element.42.own.own_far), channel_id=1, source_target_pairs={{0,8},{8,16},{16,24},{1,9},{9,17},{17,25},{2,10},{10,18},{18,26},{... | collective-permute-start | bytes 958472 | tf_op jit(solution)/shard_map/ppermute | solution.py:702
  19.7 11.4 %collective-permute-start.2 = (bf16[1472,128]{1,0:T(8,128)(2,1)S(1)}, bf16[1472,128]{1,0:T(8,128)(2,1)S(1)}, u32[]{:S(2)}, u32[]{:S(2)}) collective-permute-start(bf16[1472,128]{1,0:T(8,128)(2,1)S(1)} %get-tuple-element.45.near), channel_id=1, source_target_pairs={{8,0},{16,8},{24,16},{9,1},{17,9},{25,17},{10,2},{18,10},{26,18},{... | collective-permute-start | bytes 1130504 | tf_op jit(solution)/shard_map/ppermute | solution.py:702
  25.3 2.3 %copy-start.4 = (bf16[1248,128]{1,0:T(8,128)(2,1)}, bf16[1248,128]{1,0:T(8,128)(2,1)S(1)}, u32[]{:S(2)}) copy-start(bf16[1248,128]{1,0:T(8,128)(2,1)S(1)} %collective-permute-done.1.before.near_far) | copy-start | bytes 958468
  27.6 9.3 %all-to-all-start.1 = ((bf16[8,96,128]{2,1,0:T(8,128)(2,1)}), bf16[8,96,128]{2,1,0:T(8,128)(2,1)S(1)}, u32[]{:S(2)}, u32[]{:S(2)}) async-start(bf16[8,96,128]{2,1,0:T(8,128)(2,1)} %get-tuple-element.44), calls=%async_computation.1 | async-start | bytes 393216 | tf_op jit(solution)/shard_map/all_to_all | solution.py:846
  38.1 8.3 %all-to-all-start.2 = ((f32[8,8,128]{2,1,0:T(8,128)}), f32[8,8,128]{2,1,0:T(8,128)S(1)}, u32[]{:S(2)}, u32[]{:S(2)}) async-start(f32[8,8,128]{2,1,0:T(8,128)} %get-tuple-element.46), calls=%async_computation.2 | async-start | bytes 65536 | tf_op jit(solution)/shard_map/all_to_all | solution.py:873
  51.4 2.6 %collective-permute-start.3 = (bf16[3456,128]{1,0:T(8,128)(2,1)S(1)}, bf16[3456,128]{1,0:T(8,128)(2,1)S(1)}, u32[]{:S(2)}, u32[]{:S(2)}) collective-permute-start(bf16[3456,128]{1,0:T(8,128)(2,1)S(1)} %get-tuple-element.56), channel_id=1, source_target_pairs={{0,4},{4,0},{1,5},{5,1},{2,6},{6,2},{3,7},{7,3},{8,12},{12,8},{9,1... | collective-permute-start | bytes 2654216 | tf_op jit(solution)/shard_map/ppermute | solution.py:696
  54.0 5.2 %copy-start.6 = (bf16[1248,128]{1,0:T(8,128)(2,1)S(1)}, bf16[1248,128]{1,0:T(8,128)(2,1)}, u32[]{:S(2)}) copy-start(bf16[1248,128]{1,0:T(8,128)(2,1)} %get-tuple-element.57.near) | copy-start | bytes 958468
  55.1 23.0 %copy-start.1 = (bf16[2,16,32,128]{3,2,1,0:T(8,128)(2,1)S(1)}, bf16[2,16,32,128]{3,2,1,0:T(8,128)(2,1)}, u32[]{:S(2)}) copy-start(bf16[2,16,32,128]{3,2,1,0:T(8,128)(2,1)} %features.5) | copy-start | bytes 786436
  55.1 16.4 %all-to-all-start.3 = ((bf16[4,864,128]{2,1,0:T(8,128)(2,1)}), bf16[4,864,128]{2,1,0:T(8,128)(2,1)S(1)}, u32[]{:S(2)}, u32[]{:S(2)}) async-start(bf16[4,864,128]{2,1,0:T(8,128)(2,1)} %shard_map.85), calls=%async_computation.3 | async-start | bytes 1769472 | tf_op jit(solution)/shard_map/all_to_all | solution.py:905
  59.2 12.0 %collective-permute-start.4 = (bf16[1248,128]{1,0:T(8,128)(2,1)S(1)}, bf16[1248,128]{1,0:T(8,128)(2,1)S(1)}, u32[]{:S(2)}, u32[]{:S(2)}) collective-permute-start(bf16[1248,128]{1,0:T(8,128)(2,1)S(1)} %copy-done.6), channel_id=1, source_target_pairs={{8,0},{16,8},{24,16},{9,1},{17,9},{25,17},{10,2},{18,10},{26,18},{... | collective-permute-start | bytes 958472 | tf_op jit(solution)/shard_map/ppermute | solution.py:702
  60.5 17.5 %collective-permute-start.5 = (bf16[1248,128]{1,0:T(8,128)(2,1)S(1)}, bf16[1248,128]{1,0:T(8,128)(2,1)S(1)}, u32[]{:S(2)}, u32[]{:S(2)}) collective-permute-start(bf16[1248,128]{1,0:T(8,128)(2,1)S(1)} %get-tuple-element.59.act.far), channel_id=1, source_target_pairs={{0,8},{8,16},{16,24},{1,9},{9,17},{17,25},{2,10},{10,18},{18,26},{... | collective-permute-start | bytes 958472 | tf_op jit(solution)/shard_map/ppermute | solution.py:702
  72.3 13.5 %all-to-all-start.4 = ((bf16[4,224,128]{2,1,0:T(8,128)(2,1)}), bf16[4,224,128]{2,1,0:T(8,128)(2,1)S(1)}, u32[]{:S(2)}, u32[]{:S(2)}) async-start(bf16[4,224,128]{2,1,0:T(8,128)(2,1)} %shard_map.86), calls=%async_computation.4 | async-start | bytes 458752 | tf_op jit(solution)/shard_map/all_to_all | solution.py:914
  78.1 1.2 %copy-start.5 = (bf16[3,3,3,128,128]{4,3,2,1,0:T(8,128)(2,1)S(1)}, bf16[3,3,3,128,128]{4,3,2,1,0:T(8,128)(2,1)}, u32[]{:S(2)}) copy-start(bf16[3,3,3,128,128]{4,3,2,1,0:T(8,128)(2,1)} %param.6) | copy-start | bytes 2654212
  86.5 9.9 %all-to-all-start.5 = ((bf16[4,224,128]{2,1,0:T(8,128)(2,1)}), bf16[4,224,128]{2,1,0:T(8,128)(2,1)S(1)}, u32[]{:S(2)}, u32[]{:S(2)}) async-start(bf16[4,224,128]{2,1,0:T(8,128)(2,1)} %shard_map.89), calls=%async_computation.5 | async-start | bytes 458752 | tf_op jit(solution)/shard_map/all_to_all | solution.py:933
  91.8 1.2 %collective-permute-start.6 = (f32[8,128]{1,0:T(8,128)S(1)}, f32[8,128]{1,0:T(8,128)S(1)}, u32[]{:S(2)}, u32[]{:S(2)}) collective-permute-start(f32[8,128]{1,0:T(8,128)S(1)} %get-tuple-element.65), channel_id=1, source_target_pairs={{0,4},{4,0},{1,5},{5,1},{2,6},{6,2},{3,7},{7,3},{8,12},{12,8},{9,1... | collective-permute-start | bytes 12296 | tf_op jit(solution)/shard_map/ppermute | solution.py:696
  96.4 12.6 %copy-start.2 = (bf16[2,16,32,128]{3,2,1,0:T(8,128)(2,1)S(1)}, bf16[2,16,32,128]{3,2,1,0:T(8,128)(2,1)}, u32[]{:S(2)}) copy-start(bf16[2,16,32,128]{3,2,1,0:T(8,128)(2,1)} %out_grad.1) | copy-start | bytes 786436
  109.0 2.5 %collective-permute-start.7 = (bf16[4,896,128]{2,1,0:T(8,128)(2,1)S(1)}, bf16[4,896,128]{2,1,0:T(8,128)(2,1)S(1)}, u32[]{:S(2)}, u32[]{:S(2)}) collective-permute-start(bf16[4,896,128]{2,1,0:T(8,128)(2,1)S(1)} %all_to_all.36.refs_1_), channel_id=1, source_target_pairs={{0,4},{4,0},{1,5},{5,1},{2,6},{6,2},{3,7},{7,3},{8,12},{12,8},{9,1... | collective-permute-start | bytes 2752520 | tf_op jit(solution)/shard_map/ppermute | solution.py:696

commit v10 on v8

--- a/solution.py
+++ b/solution.py
@@ -583,8 +583,10 @@
     near_far,
     own_far,
     short_far,
+    second_far,
     out,
     give,
+    second,
     grad_far,
     x,
     frame,
@@ -607,10 +609,13 @@
         copies[k].start()
     upper = place[0] == 0
     given = pltpu.make_async_copy(short_far, give, sems.at[len(pairs) + 1])
+    fetched = pltpu.make_async_copy(second_far, second, sems.at[len(pairs) + 2])
 
     @pl.when(upper)
     def _():
         given.start()
+
+    fetched.start()
 
     def arrive(f):
         copies[f].wait()
@@ -623,6 +628,7 @@
     for copy in copies[2 * FRAMES :]:
         copy.wait()
     spread_all(size, 1, 1, size.wide, near, own, x, frame)
+
     for b in range(3):
         for a, total in enumerate(tap_sums(x, turned, b)):
             rows = slice((a * 3 + b) * 3 * LANES, (a * 3 + b + 1) * 3 * LANES)
@@ -636,6 +642,7 @@
     def _():
         given.wait()
 
+    fetched.wait()
     sent.wait()
 
 
@@ -835,7 +842,7 @@
         [*conv_scratch(size, 1, wide, FRAMES), ((2, span, LANES), F32)],
         smem=1,
         mib=12,
-        flops=work // 2,
+        flops=2 * work,
     )
     got = lax.all_to_all(slots, ("row", "col"), 0, 0)
     (grad_act,) = call(
@@ -876,14 +883,14 @@
         beside=True,
         out_far=2,
     )
-    first_term, give, grad_second = call(
+    first_term, give, second_near, grad_second = call(
         part(first_term_body, size, across),
-        [(first.shape, F32), (first.shape, BF16), block],
-        [place, got, norm_second, q, z, act_before, act_first, second_short],
+        [(first.shape, F32), (first.shape, BF16), (first.shape, F32), block],
+        [place, got, norm_second, q, z, act_before, act_first, second_short, second_term],
         [*conv_scratch(size, 1, wide), turned, *[block] * 3, field, field],
         smem=1,
-        far=5,
-        sems=2 * FRAMES + 4,
+        far=6,
+        sems=2 * FRAMES + 5,
         mib=20,
         flops=work,
         out_far=1,
@@ -898,7 +905,7 @@
     (slots,) = call(
         joined_body,
         [((across, by_col, LANES), BF16)],
-        [place, first_term, second_term, row_swap(give)],
+        [place, first_term, second_near, row_swap(give)],
         smem=1,
     )
     slots = lax.all_to_all(slots, "col", 0, 0)

time: 115 us -> 113 us (0.983)
  waiting for transfers between devices: 24.5 us -> 23.3 us
where the time goes in v10:
time: 113 us; the launch traced here: 112 us
  starting transfers between devices  32.3 us (29%)
  Pallas kernels  31.7 us (28%)
  waiting for transfers between devices  23.3 us (21%)
  blocking collectives  22.8 us (20%)
  local copies, waits for them, and re-layouts  1.33 us (1%)
    pallas_call x16, Pallas kernels, call(): pl.pallas_call(body, out_shape=shapes[:kept] + [pltpu.HBM(o.shape, o.dtyp...  28.7 us
    all_to_all x1, blocking collectives, on_device(): lax.all_to_all(jnp.broadcast_to(done[None], (across, *done.shape)), 'col'...  12.4 us
    ppermute x4, starting transfers between devices, later(): return lax.ppermute(values, 'tm', pairs)  11.1 us
    all_to_all x1, blocking collectives, on_device(): col_got = lax.all_to_all(slots, 'col', 0, 0)  10.4 us
    ppermute x4, waiting for transfers between devices, later(): return lax.ppermute(values, 'tm', pairs)  9.13 us
    all_to_all x2, starting transfers between devices, on_device(): got = lax.all_to_all(slots, ('row', 'col'), 0, 0)  6.73 us
    all_to_all x1, starting transfers between devices, on_device(): got = lax.all_to_all(slots, 'tm', 0, 0)  5.78 us
    all_to_all x1, starting transfers between devices, on_device(): slots = lax.all_to_all(slots, 'col', 0, 0)  4.15 us
  transfers between devices with their start and end apart: 13, of which 9 were waited for; matrix products, arithmetic and copies ran while one was open for 0% of the time, Pallas kernels for 17%

profile of v10, /device:TPU:0, one launch (start us, length us, event | category | flops | bytes accessed | tf_op | source)
XLA Modules:
  0.0 112.4 jit_solution(11280222172661299373)
XLA Ops:
  0.7 1.8 %shard_map.75 = (bf16[224,128]{1,0:T(8,128)(2,1)S(1)}, f32[8,128]{1,0:T(8,128)S(1)}, f32[2,176,128]{2,1,0:T(8,128)S(1)}, bf16[2,16,32,128]{3,2,1,0:T(8,128)(2,1)S(1)}, bf16[2,16,32,128]{3,2,1,0:T(8,128)(2,1)S(1)}) custom-call(s32[2]{0:T(128)S(1)} %pad_add_fusion.place.refs_0_, bf16[2,16,32,128]{3,2,1,0:T(8,128)(2,1)} %features.5, ...), custom_call_target="tpu_custom_call" | custom-call | bytes 1290248 | tf_op jit(solution)/shard_map/pallas_call | solution.py:59
  4.5 10.4 %all_to_all.35.col_got = bf16[4,176,128]{2,1,0:T(8,128)(2,1)S(1)} all-to-all(bf16[4,176,128]{2,1,0:T(8,128)(2,1)S(1)} %shard_map.76), channel_id=1, replica_groups=mesh['tm'=4,'row'=2,'col'=4] {'col'}, dimensions={0} | all-to-all | bytes 360448 | tf_op jit(solution)/shard_map/all_to_all | solution.py:816
  16.2 3.5 %collective-permute-start.1 = (bf16[1248,128]{1,0:T(8,128)(2,1)S(1)}, bf16[1248,128]{1,0:T(8,128)(2,1)S(1)}, u32[]{:S(2)}, u32[]{:S(2)}) collective-permute-start(bf16[1248,128]{1,0:T(8,128)(2,1)S(1)} %get-tuple-element.43.own.own_far), channel_id=1, source_target_pairs={{0,8},{8,16},{16,24},{1,9},{9,17},{17,25},{2,10},{10,18},{18,26},{... | collective-permute-start | bytes 958472 | tf_op jit(solution)/shard_map/ppermute | solution.py:693
  21.8 3.5 %collective-permute-done.1.before.near_far = bf16[1248,128]{1,0:T(8,128)(2,1)S(1)} collective-permute-done((bf16[1248,128]{1,0:T(8,128)(2,1)S(1)}, bf16[1248,128]{1,0:T(8,128)(2,1)S(1)}, u32[]{:S(2)}, u32[]{:S(2)}) %collective-permute-start.1) | collective-permute-done | bytes 319520 | tf_op jit(solution)/shard_map/ppermute | solution.py:693
  25.3 2.3 %shard_map.79 = (bf16[2,16,32,128]{3,2,1,0:T(8,128)(2,1)S(1)}, bf16[8,96,128]{2,1,0:T(8,128)(2,1)}) custom-call(s32[2]{0:T(128)S(1)} %pad_add_fusion.place.refs_0_, bf16[1248,128]{1,0:T(8,128)(2,1)S(1)} %collective-permute-done.1.before.near_far, f32[2,512,128]{2,1,0:T(8,128)S(1)} %shard_map.78.sums, bf16[3456,128]{1,0:T(8,128)(2,1)S(1)} %bitcast.8), custom_call_target="tpu_custom_call" | custom-call | flops 1811939328 | bytes 2187272 | tf_op jit(solution)/shard_map/pallas_call | solution.py:59
  27.6 3.4 %all-to-all-start.1 = ((bf16[8,96,128]{2,1,0:T(8,128)(2,1)}), bf16[8,96,128]{2,1,0:T(8,128)(2,1)S(1)}, u32[]{:S(2)}, u32[]{:S(2)}) async-start(bf16[8,96,128]{2,1,0:T(8,128)(2,1)} %get-tuple-element.45), calls=%async_computation.1 | async-start | bytes 393216 | tf_op jit(solution)/shard_map/all_to_all | solution.py:847
  31.0 3.5 %shard_map.80.grad_act = f32[2,18,40,128]{3,2,1,0:T(8,128)S(1)} custom-call(bf16[1472,128]{1,0:T(8,128)(2,1)S(1)} %get-tuple-element.46.near, bf16[1472,128]{1,0:T(8,128)(2,1)S(1)} %collective-permute-done.2.far, bf16[3456,128]{1,0:T(8,128)(2,1)} %bitcast.10), custom_call_target="tpu_custom_call" | custom-call | flops 1811939328 | bytes 2375680 | tf_op jit(solution)/shard_map/pallas_call | solution.py:59
  34.6 2.3 %all-to-all-done.1.got = bf16[8,96,128]{2,1,0:T(8,128)(2,1)S(1)} async-done(((bf16[8,96,128]{2,1,0:T(8,128)(2,1)}), bf16[8,96,128]{2,1,0:T(8,128)(2,1)S(1)}, u32[]{:S(2)}, u32[]{:S(2)}) %all-to-all-start.1) | async-done | bytes 196640 | tf_op jit(solution)/shard_map/all_to_all | solution.py:847
  38.1 3.3 %all-to-all-start.2 = ((f32[8,8,128]{2,1,0:T(8,128)}), f32[8,8,128]{2,1,0:T(8,128)S(1)}, u32[]{:S(2)}, u32[]{:S(2)}) async-start(f32[8,8,128]{2,1,0:T(8,128)} %get-tuple-element.47), calls=%async_computation.2 | async-start | bytes 65536 | tf_op jit(solution)/shard_map/all_to_all | solution.py:874
  41.5 2.2 %shard_map.82 = (bf16[1248,128]{1,0:T(8,128)(2,1)S(1)}, f32[2,18,40,128]{3,2,1,0:T(8,128)}, f32[2,18,40,128]{3,2,1,0:T(8,128)}) custom-call(s32[2]{0:T(128)S(1)} %pad_add_fusion.place.refs_0_, bf16[2,16,32,128]{3,2,1,0:T(8,128)(2,1)S(1)} %get-tuple-element.44.hidden, bf16[8,96,128]{2,1,0:T(8,128)(2,1)S(1)} %all-to-all-done.1.got, ...), custom_call_target="tpu_custom_call" | custom-call | tf_op jit(solution)/shard_map/pallas_call | solution.py:59
  43.7 2.7 %shard_map.83 = (f32[3456,128]{1,0:T(8,128)}, bf16[3456,128]{1,0:T(8,128)(2,1)}) custom-call(bf16[1472,128]{1,0:T(8,128)(2,1)S(1)} %get-tuple-element.46.near, bf16[1472,128]{1,0:T(8,128)(2,1)S(1)} %collective-permute-done.2.far, bf16[1248,128]{1,0:T(8,128)(2,1)S(1)} %get-tuple-element.61.act.far), custom_call_target="tpu_custom_call" | custom-call | tf_op jit(solution)/shard_map/pallas_call | solution.py:59
  46.4 3.8 %shard_map.84 = (f32[3456,128]{1,0:T(8,128)S(1)}, bf16[3456,128]{1,0:T(8,128)(2,1)S(1)}, f32[3456,128]{1,0:T(8,128)S(1)}, bf16[1248,128]{1,0:T(8,128)(2,1)}) custom-call(s32[2]{0:T(128)S(1)} %pad_add_fusion.place.refs_0_, f32[8,8,128]{2,1,0:T(8,128)S(1)} %all-to-all-done.2.got, f32[8,128]{1,0:T(8,128)S(1)} %get-tuple-element.48.norm, ...), custom_call_target="tpu_custom_call" | custom-call | flops 905969664 | bytes 9547784 | tf_op jit(solution)/shard_map/pallas_call | solution.py:59
  50.7 2.1 %collective-permute-done.3.got = bf16[3456,128]{1,0:T(8,128)(2,1)S(1)} collective-permute-done((bf16[3456,128]{1,0:T(8,128)(2,1)S(1)}, bf16[3456,128]{1,0:T(8,128)(2,1)S(1)}, u32[]{:S(2)}, u32[]{:S(2)}) %collective-permute-start.3) | collective-permute-done | bytes 884768 | tf_op jit(solution)/shard_map/ppermute | solution.py:687
  52.8 1.6 %shard_map.85 = bf16[4,864,128]{2,1,0:T(8,128)(2,1)} custom-call(s32[2]{0:T(128)S(1)} %pad_add_fusion.place.refs_0_, f32[3456,128]{1,0:T(8,128)S(1)} %get-tuple-element.54.first, f32[3456,128]{1,0:T(8,128)S(1)} %get-tuple-element.55.second, bf16[3456,128]{1,0:T(8,128)(2,1)S(1)} %collective-permute-done.3.got), custom_call_target="tpu_custom_call" | custom-call | bytes 5308424 | tf_op jit(solution)/shard_map/pallas_call | solution.py:59
  54.4 4.2 %all-to-all-start.3 = ((bf16[4,864,128]{2,1,0:T(8,128)(2,1)}), bf16[4,864,128]{2,1,0:T(8,128)(2,1)S(1)}, u32[]{:S(2)}, u32[]{:S(2)}) async-start(bf16[4,864,128]{2,1,0:T(8,128)(2,1)} %shard_map.85), calls=%async_computation.3 | async-start | bytes 1769472 | tf_op jit(solution)/shard_map/all_to_all | solution.py:911
  59.9 5.0 %collective-permute-start.5 = (bf16[1248,128]{1,0:T(8,128)(2,1)S(1)}, bf16[1248,128]{1,0:T(8,128)(2,1)S(1)}, u32[]{:S(2)}, u32[]{:S(2)}) collective-permute-start(bf16[1248,128]{1,0:T(8,128)(2,1)S(1)} %get-tuple-element.61.act.far), channel_id=1, source_target_pairs={{0,8},{8,16},{16,24},{1,9},{9,17},{17,25},{2,10},{10,18},{18,26},{... | collective-permute-start | bytes 958472 | tf_op jit(solution)/shard_map/ppermute | solution.py:693
  64.9 5.6 %collective-permute-done.4.far = bf16[1248,128]{1,0:T(8,128)(2,1)S(1)} collective-permute-done((bf16[1248,128]{1,0:T(8,128)(2,1)S(1)}, bf16[1248,128]{1,0:T(8,128)(2,1)S(1)}, u32[]{:S(2)}, u32[]{:S(2)}) %collective-permute-start.4) | collective-permute-done | bytes 319520 | tf_op jit(solution)/shard_map/ppermute | solution.py:693
  71.6 5.8 %all-to-all-start.4 = ((bf16[4,224,128]{2,1,0:T(8,128)(2,1)}), bf16[4,224,128]{2,1,0:T(8,128)(2,1)S(1)}, u32[]{:S(2)}, u32[]{:S(2)}) async-start(bf16[4,224,128]{2,1,0:T(8,128)(2,1)} %shard_map.86), calls=%async_computation.4 | async-start | bytes 458752 | tf_op jit(solution)/shard_map/all_to_all | solution.py:920
  78.5 2.4 %shard_map.87 = bf16[2,16,32,128]{3,2,1,0:T(8,128)(2,1)} custom-call(bf16[1248,128]{1,0:T(8,128)(2,1)S(1)} %collective-permute-done.5.near, bf16[1248,128]{1,0:T(8,128)(2,1)S(1)} %get-tuple-element.61.act.far, bf16[3456,128]{1,0:T(8,128)(2,1)S(1)} %bitcast.11, bf16[2,16,32,128]{3,2,1,0:T(8,128)(2,1)S(1)} %copy-done.1), custom_call_target="tpu_custom_call" | custom-call | flops 905969664 | bytes 2048000 | tf_op jit(solution)/shard_map/pallas_call | solution.py:59
  81.0 4.1 %all-to-all-done.4.got = bf16[4,224,128]{2,1,0:T(8,128)(2,1)S(1)} async-done(((bf16[4,224,128]{2,1,0:T(8,128)(2,1)}), bf16[4,224,128]{2,1,0:T(8,128)(2,1)S(1)}, u32[]{:S(2)}, u32[]{:S(2)}) %all-to-all-start.4) | async-done | bytes 229408 | tf_op jit(solution)/shard_map/all_to_all | solution.py:920
  85.8 3.4 %all-to-all-start.5 = ((bf16[4,224,128]{2,1,0:T(8,128)(2,1)}), bf16[4,224,128]{2,1,0:T(8,128)(2,1)S(1)}, u32[]{:S(2)}, u32[]{:S(2)}) async-start(bf16[4,224,128]{2,1,0:T(8,128)(2,1)} %shard_map.89), calls=%async_computation.5 | async-start | bytes 458752 | tf_op jit(solution)/shard_map/all_to_all | solution.py:939
  89.2 1.9 %shard_map.88 = (f32[2,512,128]{2,1,0:T(8,128)S(1)}, f32[8,128]{1,0:T(8,128)S(1)}) custom-call(bf16[1248,128]{1,0:T(8,128)(2,1)S(1)} %copy-done.6, bf16[1248,128]{1,0:T(8,128)(2,1)S(1)} %collective-permute-done.4.far, bf16[3456,128]{1,0:T(8,128)(2,1)S(1)} %bitcast.9, bf16[2,16,32,128]{3,2,1,0:T(8,128)(2,1)S(1)} %copy-done.1, f32[8,128]{1,0:T(8,128)S(1)} %get-tuple-element.63.norm), custom_call_target="tpu_custom_call" | custom-call | flops 905969664 | bytes 2318336 | tf_op jit(solution)/shard_map/pallas_call | solution.py:59
  92.3 3.4 %all-to-all-done.5 = bf16[4,224,128]{2,1,0:T(8,128)(2,1)S(1)} async-done(((bf16[4,224,128]{2,1,0:T(8,128)(2,1)}), bf16[4,224,128]{2,1,0:T(8,128)(2,1)S(1)}, u32[]{:S(2)}, u32[]{:S(2)}) %all-to-all-start.5) | async-done | bytes 229408 | tf_op jit(solution)/shard_map/all_to_all | solution.py:939
  95.8 12.4 %all_to_all.36.refs_1_ = bf16[4,896,128]{2,1,0:T(8,128)(2,1)S(1)} all-to-all(bf16[4,896,128]{2,1,0:T(8,128)(2,1)S(1)} %broadcast_in_dim.2), channel_id=1, replica_groups=mesh['tm'=4,'row'=2,'col'=4] {'col'}, dimensions={0} | all-to-all | bytes 1835008 | tf_op jit(solution)/shard_map/all_to_all | solution.py:943
  (43 shorter events, 16.9 us)
Async XLA Ops:
  0.6 20.3 %copy-start.3 = (bf16[3,3,3,128,128]{4,3,2,1,0:T(8,128)(2,1)S(1)}, bf16[3,3,3,128,128]{4,3,2,1,0:T(8,128)(2,1)}, u32[]{:S(2)}) copy-start(bf16[3,3,3,128,128]{4,3,2,1,0:T(8,128)(2,1)} %param.5) | copy-start | bytes 2654212
  2.5 1.4 %collective-permute-start = (bf16[224,128]{1,0:T(8,128)(2,1)S(1)}, bf16[224,128]{1,0:T(8,128)(2,1)S(1)}, u32[]{:S(2)}, u32[]{:S(2)}) collective-permute-start(bf16[224,128]{1,0:T(8,128)(2,1)S(1)} %get-tuple-element.40), channel_id=1, source_target_pairs={{0,4},{4,0},{1,5},{5,1},{2,6},{6,2},{3,7},{7,3},{8,12},{12,8},{9,1... | collective-permute-start | bytes 172040 | tf_op jit(solution)/shard_map/ppermute | solution.py:687
  16.2 11.5 %copy-start = (bf16[1248,128]{1,0:T(8,128)(2,1)}, bf16[1248,128]{1,0:T(8,128)(2,1)S(1)}, u32[]{:S(2)}) copy-start(bf16[1248,128]{1,0:T(8,128)(2,1)S(1)} %get-tuple-element.43.own.own_far) | copy-start | bytes 958468
  16.2 9.2 %collective-permute-start.1 = (bf16[1248,128]{1,0:T(8,128)(2,1)S(1)}, bf16[1248,128]{1,0:T(8,128)(2,1)S(1)}, u32[]{:S(2)}, u32[]{:S(2)}) collective-permute-start(bf16[1248,128]{1,0:T(8,128)(2,1)S(1)} %get-tuple-element.43.own.own_far), channel_id=1, source_target_pairs={{0,8},{8,16},{16,24},{1,9},{9,17},{17,25},{2,10},{10,18},{18,26},{... | collective-permute-start | bytes 958472 | tf_op jit(solution)/shard_map/ppermute | solution.py:693
  19.7 11.4 %collective-permute-start.2 = (bf16[1472,128]{1,0:T(8,128)(2,1)S(1)}, bf16[1472,128]{1,0:T(8,128)(2,1)S(1)}, u32[]{:S(2)}, u32[]{:S(2)}) collective-permute-start(bf16[1472,128]{1,0:T(8,128)(2,1)S(1)} %get-tuple-element.46.near), channel_id=1, source_target_pairs={{8,0},{16,8},{24,16},{9,1},{17,9},{25,17},{10,2},{18,10},{26,18},{... | collective-permute-start | bytes 1130504 | tf_op jit(solution)/shard_map/ppermute | solution.py:693
  25.3 2.3 %copy-start.4 = (bf16[1248,128]{1,0:T(8,128)(2,1)}, bf16[1248,128]{1,0:T(8,128)(2,1)S(1)}, u32[]{:S(2)}) copy-start(bf16[1248,128]{1,0:T(8,128)(2,1)S(1)} %collective-permute-done.1.before.near_far) | copy-start | bytes 958468
  27.6 9.3 %all-to-all-start.1 = ((bf16[8,96,128]{2,1,0:T(8,128)(2,1)}), bf16[8,96,128]{2,1,0:T(8,128)(2,1)S(1)}, u32[]{:S(2)}, u32[]{:S(2)}) async-start(bf16[8,96,128]{2,1,0:T(8,128)(2,1)} %get-tuple-element.45), calls=%async_computation.1 | async-start | bytes 393216 | tf_op jit(solution)/shard_map/all_to_all | solution.py:847
  38.1 8.3 %all-to-all-start.2 = ((f32[8,8,128]{2,1,0:T(8,128)}), f32[8,8,128]{2,1,0:T(8,128)S(1)}, u32[]{:S(2)}, u32[]{:S(2)}) async-start(f32[8,8,128]{2,1,0:T(8,128)} %get-tuple-element.47), calls=%async_computation.2 | async-start | bytes 65536 | tf_op jit(solution)/shard_map/all_to_all | solution.py:874
  50.2 2.6 %collective-permute-start.3 = (bf16[3456,128]{1,0:T(8,128)(2,1)S(1)}, bf16[3456,128]{1,0:T(8,128)(2,1)S(1)}, u32[]{:S(2)}, u32[]{:S(2)}) collective-permute-start(bf16[3456,128]{1,0:T(8,128)(2,1)S(1)} %get-tuple-element.58), channel_id=1, source_target_pairs={{0,4},{4,0},{1,5},{5,1},{2,6},{6,2},{3,7},{7,3},{8,12},{12,8},{9,1... | collective-permute-start | bytes 2654216 | tf_op jit(solution)/shard_map/ppermute | solution.py:687
  54.4 4.2 %copy-start.6 = (bf16[1248,128]{1,0:T(8,128)(2,1)S(1)}, bf16[1248,128]{1,0:T(8,128)(2,1)}, u32[]{:S(2)}) copy-start(bf16[1248,128]{1,0:T(8,128)(2,1)} %get-tuple-element.59.near) | copy-start | bytes 958468
  54.4 23.0 %copy-start.1 = (bf16[2,16,32,128]{3,2,1,0:T(8,128)(2,1)S(1)}, bf16[2,16,32,128]{3,2,1,0:T(8,128)(2,1)}, u32[]{:S(2)}) copy-start(bf16[2,16,32,128]{3,2,1,0:T(8,128)(2,1)} %features.5) | copy-start | bytes 786436
  54.4 16.4 %all-to-all-start.3 = ((bf16[4,864,128]{2,1,0:T(8,128)(2,1)}), bf16[4,864,128]{2,1,0:T(8,128)(2,1)S(1)}, u32[]{:S(2)}, u32[]{:S(2)}) async-start(bf16[4,864,128]{2,1,0:T(8,128)(2,1)} %shard_map.85), calls=%async_computation.3 | async-start | bytes 1769472 | tf_op jit(solution)/shard_map/all_to_all | solution.py:911
  58.6 12.0 %collective-permute-start.4 = (bf16[1248,128]{1,0:T(8,128)(2,1)S(1)}, bf16[1248,128]{1,0:T(8,128)(2,1)S(1)}, u32[]{:S(2)}, u32[]{:S(2)}) collective-permute-start(bf16[1248,128]{1,0:T(8,128)(2,1)S(1)} %copy-done.6), channel_id=1, source_target_pairs={{8,0},{16,8},{24,16},{9,1},{17,9},{25,17},{10,2},{18,10},{26,18},{... | collective-permute-start | bytes 958472 | tf_op jit(solution)/shard_map/ppermute | solution.py:693
  59.9 17.5 %collective-permute-start.5 = (bf16[1248,128]{1,0:T(8,128)(2,1)S(1)}, bf16[1248,128]{1,0:T(8,128)(2,1)S(1)}, u32[]{:S(2)}, u32[]{:S(2)}) collective-permute-start(bf16[1248,128]{1,0:T(8,128)(2,1)S(1)} %get-tuple-element.61.act.far), channel_id=1, source_target_pairs={{0,8},{8,16},{16,24},{1,9},{9,17},{17,25},{2,10},{10,18},{18,26},{... | collective-permute-start | bytes 958472 | tf_op jit(solution)/shard_map/ppermute | solution.py:693
  71.6 13.5 %all-to-all-start.4 = ((bf16[4,224,128]{2,1,0:T(8,128)(2,1)}), bf16[4,224,128]{2,1,0:T(8,128)(2,1)S(1)}, u32[]{:S(2)}, u32[]{:S(2)}) async-start(bf16[4,224,128]{2,1,0:T(8,128)(2,1)} %shard_map.86), calls=%async_computation.4 | async-start | bytes 458752 | tf_op jit(solution)/shard_map/all_to_all | solution.py:920
  77.4 1.2 %copy-start.5 = (bf16[3,3,3,128,128]{4,3,2,1,0:T(8,128)(2,1)S(1)}, bf16[3,3,3,128,128]{4,3,2,1,0:T(8,128)(2,1)}, u32[]{:S(2)}) copy-start(bf16[3,3,3,128,128]{4,3,2,1,0:T(8,128)(2,1)} %param.6) | copy-start | bytes 2654212
  85.8 9.9 %all-to-all-start.5 = ((bf16[4,224,128]{2,1,0:T(8,128)(2,1)}), bf16[4,224,128]{2,1,0:T(8,128)(2,1)S(1)}, u32[]{:S(2)}, u32[]{:S(2)}) async-start(bf16[4,224,128]{2,1,0:T(8,128)(2,1)} %shard_map.89), calls=%async_computation.5 | async-start | bytes 458752 | tf_op jit(solution)/shard_map/all_to_all | solution.py:939
  91.0 1.2 %collective-permute-start.6 = (f32[8,128]{1,0:T(8,128)S(1)}, f32[8,128]{1,0:T(8,128)S(1)}, u32[]{:S(2)}, u32[]{:S(2)}) collective-permute-start(f32[8,128]{1,0:T(8,128)S(1)} %get-tuple-element.67), channel_id=1, source_target_pairs={{0,4},{4,0},{1,5},{5,1},{2,6},{6,2},{3,7},{7,3},{8,12},{12,8},{9,1... | collective-permute-start | bytes 12296 | tf_op jit(solution)/shard_map/ppermute | solution.py:687
  95.7 12.6 %copy-start.2 = (bf16[2,16,32,128]{3,2,1,0:T(8,128)(2,1)S(1)}, bf16[2,16,32,128]{3,2,1,0:T(8,128)(2,1)}, u32[]{:S(2)}) copy-start(bf16[2,16,32,128]{3,2,1,0:T(8,128)(2,1)} %out_grad.1) | copy-start | bytes 786436
  108.3 2.5 %collective-permute-start.7 = (bf16[4,896,128]{2,1,0:T(8,128)(2,1)S(1)}, bf16[4,896,128]{2,1,0:T(8,128)(2,1)S(1)}, u32[]{:S(2)}, u32[]{:S(2)}) collective-permute-start(bf16[4,896,128]{2,1,0:T(8,128)(2,1)S(1)} %all_to_all.36.refs_1_), channel_id=1, source_target_pairs={{0,4},{4,0},{1,5},{5,1},{2,6},{6,2},{3,7},{7,3},{8,12},{12,8},{9,1... | collective-permute-start | bytes 2752520 | tf_op jit(solution)/shard_map/ppermute | solution.py:687

commit v11 on v8

--- a/solution.py
+++ b/solution.py
@@ -549,7 +549,7 @@
     )
 
 
-def second_term_body(size, near, far, act, out_far, short_far, x, frame, turned, out, short, sems):
+def second_term_body(size, near, far, act, out_far, x, frame, turned, out, sems):
     spread_all(size, 2, 1, size.wide, near, far, x, frame)
     turned_cells(size, act, turned)
     span = 3 * LANES
@@ -559,15 +559,11 @@
             for c in range(3):
                 tap = ((2 - a) * 3 + 2 - b) * 3 + 2 - c
                 rows = slice(tap * LANES, (tap + 1) * LANES)
-                piece = total[:, c * LANES : (c + 1) * LANES]
-                out[rows] = piece
-                short[rows] = piece.astype(BF16)
+                out[rows] = total[:, c * LANES : (c + 1) * LANES]
             rows = pl.ds(((2 - a) * 3 + 2 - b) * span, span)
-            for k, (source, target) in enumerate(((out, out_far), (short, short_far))):
-                sem = sems.at[2 * (3 * b + a) + k]
-                copy = pltpu.make_async_copy(source.at[rows], target.at[rows], sem)
-                copy.start()
-                copies.append(copy)
+            copy = pltpu.make_async_copy(out.at[rows], out_far.at[rows], sems.at[3 * b + a])
+            copy.start()
+            copies.append(copy)
     for copy in copies:
         copy.wait()
 
@@ -582,8 +578,8 @@
     z_far,
     near_far,
     own_far,
-    short_far,
-    out,
+    second_far,
+    both,
     give,
     grad_far,
     x,
@@ -606,11 +602,8 @@
     for k in (0, FRAMES, 1, FRAMES + 1, 2 * FRAMES, 2 * FRAMES + 1):
         copies[k].start()
     upper = place[0] == 0
-    given = pltpu.make_async_copy(short_far, give, sems.at[len(pairs) + 1])
-
-    @pl.when(upper)
-    def _():
-        given.start()
+    fetched = pltpu.make_async_copy(second_far, both.at[1], sems.at[len(pairs) + 1])
+    fetched.start()
 
     def arrive(f):
         copies[f].wait()
@@ -623,18 +616,20 @@
     for copy in copies[2 * FRAMES :]:
         copy.wait()
     spread_all(size, 1, 1, size.wide, near, own, x, frame)
+    fetched.wait()
+
+    @pl.when(upper)
+    def _():
+        give[...] = both[1].astype(BF16)
+
     for b in range(3):
         for a, total in enumerate(tap_sums(x, turned, b)):
             rows = slice((a * 3 + b) * 3 * LANES, (a * 3 + b + 1) * 3 * LANES)
-            out[rows] = total.T
+            both[0, rows] = total.T
 
     @pl.when(jnp.logical_not(upper))
     def _():
-        give[...] = out[...].astype(BF16)
-
-    @pl.when(upper)
-    def _():
-        given.wait()
+        give[...] = both[0].astype(BF16)
 
     sent.wait()
 
@@ -700,21 +695,11 @@
     return total
 
 
-def joined_body(place, first, second, got, out):
+def joined_body(place, both, got, out):
     share = out.shape[1]
-
-    def add(keep):
-        for peer in range(out.shape[0]):
-            rows = slice(peer * share, (peer + 1) * share)
-            out[peer] = (keep[rows] + got[rows].astype(F32)).astype(BF16)
-
-    @pl.when(place[0] == 0)
-    def _():
-        add(first)
-
-    @pl.when(place[0] != 0)
-    def _():
-        add(second)
+    for peer in range(out.shape[0]):
+        rows = slice(peer * share, (peer + 1) * share)
+        out[peer] = (both[place[0], rows] + got[rows].astype(F32)).astype(BF16)
 
 
 def shared_body(got, out, flat):
@@ -835,7 +820,7 @@
         [*conv_scratch(size, 1, wide, FRAMES), ((2, span, LANES), F32)],
         smem=1,
         mib=12,
-        flops=work // 2,
+        flops=2 * work,
     )
     got = lax.all_to_all(slots, ("row", "col"), 0, 0)
     (grad_act,) = call(
@@ -866,20 +851,20 @@
     )
     got = lax.all_to_all(slots, ("row", "col"), 0, 0)
     turned = ((FRAMES * LANES, size.cells), BF16)
-    second_term, second_short = call(
+    (second_term,) = call(
         part(second_term_body, size),
-        [(first.shape, F32), (first.shape, BF16)],
+        [(first.shape, F32)],
         [grad, grad_after, act_second],
-        [*conv_scratch(size, 1, wide), turned, (first.shape, F32), (first.shape, BF16)],
-        sems=18,
+        [*conv_scratch(size, 1, wide), turned, (first.shape, F32)],
+        sems=9,
         mib=16,
         beside=True,
-        out_far=2,
-    )
-    first_term, give, grad_second = call(
+        out_far=1,
+    )
+    both, give, grad_second = call(
         part(first_term_body, size, across),
-        [(first.shape, F32), (first.shape, BF16), block],
-        [place, got, norm_second, q, z, act_before, act_first, second_short],
+        [((2, *first.shape), F32), (first.shape, BF16), block],
+        [place, got, norm_second, q, z, act_before, act_first, second_term],
         [*conv_scratch(size, 1, wide), turned, *[block] * 3, field, field],
         smem=1,
         far=5,
@@ -898,7 +883,7 @@
     (slots,) = call(
         joined_body,
         [((across, by_col, LANES), BF16)],
-        [place, first_term, second_term, row_swap(give)],
+        [place, both, row_swap(give)],
         smem=1,
     )
     slots = lax.all_to_all(slots, "col", 0, 0)

time: 115 us -> 113 us (0.983)
  waiting for transfers between devices: 24.5 us -> 22.1 us
  starting transfers between devices: 33.4 us -> 32.1 us
  local copies, waits for them, and re-layouts: 1.33 us -> 2.49 us
    ppermute x4, waiting for transfers between devices: 10.2 us -> 7.95 us  [later(): return lax.ppermute(values, 'tm', pairs)]
    unnamed x16, local copies, waits for them, and re-layouts: 1.19 us -> 2.35 us
where the time goes in v11:
time: 113 us
  starting transfers between devices  32.1 us (28%)
  Pallas kernels  32 us (28%)
  blocking collectives  22.8 us (20%)
  waiting for transfers between devices  22.1 us (20%)
  local copies, waits for them, and re-layouts  2.49 us (2%)
    pallas_call x16, Pallas kernels, call(): pl.pallas_call(body, out_shape=shapes[:kept] + [pltpu.HBM(o.shape, o.dtyp...  29 us
    all_to_all x1, blocking collectives, on_device(): lax.all_to_all(jnp.broadcast_to(done[None], (across, *done.shape)), 'col'...  12.4 us
    ppermute x4, starting transfers between devices, later(): return lax.ppermute(values, 'tm', pairs)  11.1 us
    all_to_all x1, blocking collectives, on_device(): col_got = lax.all_to_all(slots, 'col', 0, 0)  10.4 us
    ppermute x4, waiting for transfers between devices, later(): return lax.ppermute(values, 'tm', pairs)  7.95 us
    all_to_all x2, starting transfers between devices, on_device(): got = lax.all_to_all(slots, ('row', 'col'), 0, 0)  6.73 us
    all_to_all x1, starting transfers between devices, on_device(): got = lax.all_to_all(slots, 'tm', 0, 0)  5.78 us
    ppermute x4, waiting for transfers between devices, row_swap(): return lax.ppermute(values, 'row', [(0, 1), (1, 0)])  4.11 us
  transfers between devices with their start and end apart: 13, of which 9 were waited for; matrix products, arithmetic and copies ran while one was open for 0% of the time, Pallas kernels for 17%

profile of v11, /device:TPU:0, one launch (start us, length us, event | category | flops | bytes accessed | tf_op | source)
XLA Modules:
  0.0 112.6 jit_solution(15317599651958308870)
XLA Ops:
  0.7 1.8 %shard_map.75 = (bf16[224,128]{1,0:T(8,128)(2,1)S(1)}, f32[8,128]{1,0:T(8,128)S(1)}, f32[2,176,128]{2,1,0:T(8,128)S(1)}, bf16[2,16,32,128]{3,2,1,0:T(8,128)(2,1)S(1)}, bf16[2,16,32,128]{3,2,1,0:T(8,128)(2,1)S(1)}) custom-call(s32[2]{0:T(128)S(1)} %pad_add_fusion.place.refs_0_, bf16[2,16,32,128]{3,2,1,0:T(8,128)(2,1)} %features.5, ...), custom_call_target="tpu_custom_call" | custom-call | bytes 1290248 | tf_op jit(solution)/shard_map/pallas_call | solution.py:59
  4.5 10.4 %all_to_all.35.col_got = bf16[4,176,128]{2,1,0:T(8,128)(2,1)S(1)} all-to-all(bf16[4,176,128]{2,1,0:T(8,128)(2,1)S(1)} %shard_map.76), channel_id=1, replica_groups=mesh['tm'=4,'row'=2,'col'=4] {'col'}, dimensions={0} | all-to-all | bytes 360448 | tf_op jit(solution)/shard_map/all_to_all | solution.py:794
  16.2 3.5 %collective-permute-start.1 = (bf16[1248,128]{1,0:T(8,128)(2,1)S(1)}, bf16[1248,128]{1,0:T(8,128)(2,1)S(1)}, u32[]{:S(2)}, u32[]{:S(2)}) collective-permute-start(bf16[1248,128]{1,0:T(8,128)(2,1)S(1)} %get-tuple-element.40.own.own_far), channel_id=1, source_target_pairs={{0,8},{8,16},{16,24},{1,9},{9,17},{17,25},{2,10},{10,18},{18,26},{... | collective-permute-start | bytes 958472 | tf_op jit(solution)/shard_map/ppermute | solution.py:681
  23.0 2.3 %collective-permute-done.1.before.near_far = bf16[1248,128]{1,0:T(8,128)(2,1)S(1)} collective-permute-done((bf16[1248,128]{1,0:T(8,128)(2,1)S(1)}, bf16[1248,128]{1,0:T(8,128)(2,1)S(1)}, u32[]{:S(2)}, u32[]{:S(2)}) %collective-permute-start.1) | collective-permute-done | bytes 319520 | tf_op jit(solution)/shard_map/ppermute | solution.py:681
  25.3 2.3 %shard_map.79 = (bf16[2,16,32,128]{3,2,1,0:T(8,128)(2,1)S(1)}, bf16[8,96,128]{2,1,0:T(8,128)(2,1)}) custom-call(s32[2]{0:T(128)S(1)} %pad_add_fusion.place.refs_0_, bf16[1248,128]{1,0:T(8,128)(2,1)S(1)} %collective-permute-done.1.before.near_far, f32[2,512,128]{2,1,0:T(8,128)S(1)} %shard_map.78.sums, bf16[3456,128]{1,0:T(8,128)(2,1)S(1)} %bitcast.8), custom_call_target="tpu_custom_call" | custom-call | flops 1811939328 | bytes 2187272 | tf_op jit(solution)/shard_map/pallas_call | solution.py:59
  27.6 3.4 %all-to-all-start.1 = ((bf16[8,96,128]{2,1,0:T(8,128)(2,1)}), bf16[8,96,128]{2,1,0:T(8,128)(2,1)S(1)}, u32[]{:S(2)}, u32[]{:S(2)}) async-start(bf16[8,96,128]{2,1,0:T(8,128)(2,1)} %get-tuple-element.42), calls=%async_computation.1 | async-start | bytes 393216 | tf_op jit(solution)/shard_map/all_to_all | solution.py:825
  31.0 3.5 %shard_map.80.grad_act = f32[2,18,40,128]{3,2,1,0:T(8,128)S(1)} custom-call(bf16[1472,128]{1,0:T(8,128)(2,1)S(1)} %get-tuple-element.43.near, bf16[1472,128]{1,0:T(8,128)(2,1)S(1)} %collective-permute-done.2.far, bf16[3456,128]{1,0:T(8,128)(2,1)} %bitcast.10), custom_call_target="tpu_custom_call" | custom-call | flops 1811939328 | bytes 2375680 | tf_op jit(solution)/shard_map/pallas_call | solution.py:59
  34.6 2.3 %all-to-all-done.1.got = bf16[8,96,128]{2,1,0:T(8,128)(2,1)S(1)} async-done(((bf16[8,96,128]{2,1,0:T(8,128)(2,1)}), bf16[8,96,128]{2,1,0:T(8,128)(2,1)S(1)}, u32[]{:S(2)}, u32[]{:S(2)}) %all-to-all-start.1) | async-done | bytes 196640 | tf_op jit(solution)/shard_map/all_to_all | solution.py:825
  38.1 3.3 %all-to-all-start.2 = ((f32[8,8,128]{2,1,0:T(8,128)}), f32[8,8,128]{2,1,0:T(8,128)S(1)}, u32[]{:S(2)}, u32[]{:S(2)}) async-start(f32[8,8,128]{2,1,0:T(8,128)} %get-tuple-element.44), calls=%async_computation.2 | async-start | bytes 65536 | tf_op jit(solution)/shard_map/all_to_all | solution.py:852
  41.5 2.2 %shard_map.82 = (bf16[1248,128]{1,0:T(8,128)(2,1)S(1)}, f32[2,18,40,128]{3,2,1,0:T(8,128)}, f32[2,18,40,128]{3,2,1,0:T(8,128)}) custom-call(s32[2]{0:T(128)S(1)} %pad_add_fusion.place.refs_0_, bf16[2,16,32,128]{3,2,1,0:T(8,128)(2,1)S(1)} %get-tuple-element.41.hidden, bf16[8,96,128]{2,1,0:T(8,128)(2,1)S(1)} %all-to-all-done.1.got, ...), custom_call_target="tpu_custom_call" | custom-call | tf_op jit(solution)/shard_map/pallas_call | solution.py:59
  43.7 2.5 %shard_map.83.second_far = f32[3456,128]{1,0:T(8,128)} custom-call(bf16[1472,128]{1,0:T(8,128)(2,1)S(1)} %get-tuple-element.43.near, bf16[1472,128]{1,0:T(8,128)(2,1)S(1)} %collective-permute-done.2.far, bf16[1248,128]{1,0:T(8,128)(2,1)S(1)} %get-tuple-element.55.act.far), custom_call_target="tpu_custom_call" | custom-call | tf_op jit(solution)/shard_map/pallas_call | solution.py:59
  46.2 4.3 %shard_map.84 = (f32[2,3456,128]{2,1,0:T(8,128)S(1)}, bf16[3456,128]{1,0:T(8,128)(2,1)S(1)}, bf16[1248,128]{1,0:T(8,128)(2,1)}) custom-call(s32[2]{0:T(128)S(1)} %pad_add_fusion.place.refs_0_, f32[8,8,128]{2,1,0:T(8,128)S(1)} %all-to-all-done.2.got, f32[8,128]{1,0:T(8,128)S(1)} %get-tuple-element.45.norm, f32[2,18,40,128]{3,2,1,0:T(8,128)} %get-tuple-element.46.q_far, ...), custom_call_target="tpu_custom_call" | custom-call | flops 905969664 | bytes 8663048 | tf_op jit(solution)/shard_map/pallas_call | solution.py:59
  51.0 2.1 %collective-permute-done.3.got = bf16[3456,128]{1,0:T(8,128)(2,1)S(1)} collective-permute-done((bf16[3456,128]{1,0:T(8,128)(2,1)S(1)}, bf16[3456,128]{1,0:T(8,128)(2,1)S(1)}, u32[]{:S(2)}, u32[]{:S(2)}) %collective-permute-start.3) | collective-permute-done | bytes 884768 | tf_op jit(solution)/shard_map/ppermute | solution.py:675
  53.0 1.7 %shard_map.85 = bf16[4,864,128]{2,1,0:T(8,128)(2,1)} custom-call(s32[2]{0:T(128)S(1)} %pad_add_fusion.place.refs_0_, f32[2,3456,128]{2,1,0:T(8,128)S(1)} %get-tuple-element.49.both, bf16[3456,128]{1,0:T(8,128)(2,1)S(1)} %collective-permute-done.3.got), custom_call_target="tpu_custom_call" | custom-call | bytes 5308424 | tf_op jit(solution)/shard_map/pallas_call | solution.py:59
  54.7 4.1 %all-to-all-start.3 = ((bf16[4,864,128]{2,1,0:T(8,128)(2,1)}), bf16[4,864,128]{2,1,0:T(8,128)(2,1)S(1)}, u32[]{:S(2)}, u32[]{:S(2)}) async-start(bf16[4,864,128]{2,1,0:T(8,128)(2,1)} %shard_map.85), calls=%async_computation.3 | async-start | bytes 1769472 | tf_op jit(solution)/shard_map/all_to_all | solution.py:889
  60.1 5.0 %collective-permute-start.5 = (bf16[1248,128]{1,0:T(8,128)(2,1)S(1)}, bf16[1248,128]{1,0:T(8,128)(2,1)S(1)}, u32[]{:S(2)}, u32[]{:S(2)}) collective-permute-start(bf16[1248,128]{1,0:T(8,128)(2,1)S(1)} %get-tuple-element.55.act.far), channel_id=1, source_target_pairs={{0,8},{8,16},{16,24},{1,9},{9,17},{17,25},{2,10},{10,18},{18,26},{... | collective-permute-start | bytes 958472 | tf_op jit(solution)/shard_map/ppermute | solution.py:681
  65.1 5.6 %collective-permute-done.4.far = bf16[1248,128]{1,0:T(8,128)(2,1)S(1)} collective-permute-done((bf16[1248,128]{1,0:T(8,128)(2,1)S(1)}, bf16[1248,128]{1,0:T(8,128)(2,1)S(1)}, u32[]{:S(2)}, u32[]{:S(2)}) %collective-permute-start.4) | collective-permute-done | bytes 319520 | tf_op jit(solution)/shard_map/ppermute | solution.py:681
  71.8 5.8 %all-to-all-start.4 = ((bf16[4,224,128]{2,1,0:T(8,128)(2,1)}), bf16[4,224,128]{2,1,0:T(8,128)(2,1)S(1)}, u32[]{:S(2)}, u32[]{:S(2)}) async-start(bf16[4,224,128]{2,1,0:T(8,128)(2,1)} %shard_map.86), calls=%async_computation.4 | async-start | bytes 458752 | tf_op jit(solution)/shard_map/all_to_all | solution.py:898
  78.7 2.4 %shard_map.87 = bf16[2,16,32,128]{3,2,1,0:T(8,128)(2,1)} custom-call(bf16[1248,128]{1,0:T(8,128)(2,1)S(1)} %collective-permute-done.5.near, bf16[1248,128]{1,0:T(8,128)(2,1)S(1)} %get-tuple-element.55.act.far, bf16[3456,128]{1,0:T(8,128)(2,1)S(1)} %bitcast.11, bf16[2,16,32,128]{3,2,1,0:T(8,128)(2,1)S(1)} %copy-done.1), custom_call_target="tpu_custom_call" | custom-call | flops 905969664 | bytes 2048000 | tf_op jit(solution)/shard_map/pallas_call | solution.py:59
  81.2 4.1 %all-to-all-done.4.got = bf16[4,224,128]{2,1,0:T(8,128)(2,1)S(1)} async-done(((bf16[4,224,128]{2,1,0:T(8,128)(2,1)}), bf16[4,224,128]{2,1,0:T(8,128)(2,1)S(1)}, u32[]{:S(2)}, u32[]{:S(2)}) %all-to-all-start.4) | async-done | bytes 229408 | tf_op jit(solution)/shard_map/all_to_all | solution.py:898
  86.0 3.4 %all-to-all-start.5 = ((bf16[4,224,128]{2,1,0:T(8,128)(2,1)}), bf16[4,224,128]{2,1,0:T(8,128)(2,1)S(1)}, u32[]{:S(2)}, u32[]{:S(2)}) async-start(bf16[4,224,128]{2,1,0:T(8,128)(2,1)} %shard_map.89), calls=%async_computation.5 | async-start | bytes 458752 | tf_op jit(solution)/shard_map/all_to_all | solution.py:917
  89.4 1.9 %shard_map.88 = (f32[2,512,128]{2,1,0:T(8,128)S(1)}, f32[8,128]{1,0:T(8,128)S(1)}) custom-call(bf16[1248,128]{1,0:T(8,128)(2,1)S(1)} %copy-done.7, bf16[1248,128]{1,0:T(8,128)(2,1)S(1)} %collective-permute-done.4.far, bf16[3456,128]{1,0:T(8,128)(2,1)S(1)} %bitcast.9, bf16[2,16,32,128]{3,2,1,0:T(8,128)(2,1)S(1)} %copy-done.1, f32[8,128]{1,0:T(8,128)S(1)} %get-tuple-element.57.norm), custom_call_target="tpu_custom_call" | custom-call | flops 905969664 | bytes 2318336 | tf_op jit(solution)/shard_map/pallas_call | solution.py:59
  92.5 3.4 %all-to-all-done.5 = bf16[4,224,128]{2,1,0:T(8,128)(2,1)S(1)} async-done(((bf16[4,224,128]{2,1,0:T(8,128)(2,1)}), bf16[4,224,128]{2,1,0:T(8,128)(2,1)S(1)}, u32[]{:S(2)}, u32[]{:S(2)}) %all-to-all-start.5) | async-done | bytes 229408 | tf_op jit(solution)/shard_map/all_to_all | solution.py:917
  96.0 12.4 %all_to_all.36.refs_1_ = bf16[4,896,128]{2,1,0:T(8,128)(2,1)S(1)} all-to-all(bf16[4,896,128]{2,1,0:T(8,128)(2,1)S(1)} %broadcast_in_dim.2), channel_id=1, replica_groups=mesh['tm'=4,'row'=2,'col'=4] {'col'}, dimensions={0} | all-to-all | bytes 1835008 | tf_op jit(solution)/shard_map/all_to_all | solution.py:921
  (45 shorter events, 17.9 us)
Async XLA Ops:
  0.6 24.7 %copy-start.4 = (bf16[3,3,3,128,128]{4,3,2,1,0:T(8,128)(2,1)S(1)}, bf16[3,3,3,128,128]{4,3,2,1,0:T(8,128)(2,1)}, u32[]{:S(2)}) copy-start(bf16[3,3,3,128,128]{4,3,2,1,0:T(8,128)(2,1)} %param.5) | copy-start | bytes 2654212
  2.5 1.4 %collective-permute-start = (bf16[224,128]{1,0:T(8,128)(2,1)S(1)}, bf16[224,128]{1,0:T(8,128)(2,1)S(1)}, u32[]{:S(2)}, u32[]{:S(2)}) collective-permute-start(bf16[224,128]{1,0:T(8,128)(2,1)S(1)} %get-tuple-element.37), channel_id=1, source_target_pairs={{0,4},{4,0},{1,5},{5,1},{2,6},{6,2},{3,7},{7,3},{8,12},{12,8},{9,1... | collective-permute-start | bytes 172040 | tf_op jit(solution)/shard_map/ppermute | solution.py:675
  16.2 11.5 %copy-start = (bf16[1248,128]{1,0:T(8,128)(2,1)}, bf16[1248,128]{1,0:T(8,128)(2,1)S(1)}, u32[]{:S(2)}) copy-start(bf16[1248,128]{1,0:T(8,128)(2,1)S(1)} %get-tuple-element.40.own.own_far) | copy-start | bytes 958468
  16.2 9.2 %collective-permute-start.1 = (bf16[1248,128]{1,0:T(8,128)(2,1)S(1)}, bf16[1248,128]{1,0:T(8,128)(2,1)S(1)}, u32[]{:S(2)}, u32[]{:S(2)}) collective-permute-start(bf16[1248,128]{1,0:T(8,128)(2,1)S(1)} %get-tuple-element.40.own.own_far), channel_id=1, source_target_pairs={{0,8},{8,16},{16,24},{1,9},{9,17},{17,25},{2,10},{10,18},{18,26},{... | collective-permute-start | bytes 958472 | tf_op jit(solution)/shard_map/ppermute | solution.py:681
  19.7 11.4 %collective-permute-start.2 = (bf16[1472,128]{1,0:T(8,128)(2,1)S(1)}, bf16[1472,128]{1,0:T(8,128)(2,1)S(1)}, u32[]{:S(2)}, u32[]{:S(2)}) collective-permute-start(bf16[1472,128]{1,0:T(8,128)(2,1)S(1)} %get-tuple-element.43.near), channel_id=1, source_target_pairs={{8,0},{16,8},{24,16},{9,1},{17,9},{25,17},{10,2},{18,10},{26,18},{... | collective-permute-start | bytes 1130504 | tf_op jit(solution)/shard_map/ppermute | solution.py:681
  21.0 1.2 %copy-start.3 = (bf16[3,3,3,128,128]{4,3,2,1,0:T(8,128)(2,1)S(1)}, bf16[3,3,3,128,128]{4,3,2,1,0:T(8,128)(2,1)}, u32[]{:S(2)}) copy-start(bf16[3,3,3,128,128]{4,3,2,1,0:T(8,128)(2,1)} %param.5) | copy-start | bytes 2654212
  25.3 2.3 %copy-start.5 = (bf16[1248,128]{1,0:T(8,128)(2,1)}, bf16[1248,128]{1,0:T(8,128)(2,1)S(1)}, u32[]{:S(2)}) copy-start(bf16[1248,128]{1,0:T(8,128)(2,1)S(1)} %collective-permute-done.1.before.near_far) | copy-start | bytes 958468
  27.6 9.3 %all-to-all-start.1 = ((bf16[8,96,128]{2,1,0:T(8,128)(2,1)}), bf16[8,96,128]{2,1,0:T(8,128)(2,1)S(1)}, u32[]{:S(2)}, u32[]{:S(2)}) async-start(bf16[8,96,128]{2,1,0:T(8,128)(2,1)} %get-tuple-element.42), calls=%async_computation.1 | async-start | bytes 393216 | tf_op jit(solution)/shard_map/all_to_all | solution.py:825
  38.1 8.1 %all-to-all-start.2 = ((f32[8,8,128]{2,1,0:T(8,128)}), f32[8,8,128]{2,1,0:T(8,128)S(1)}, u32[]{:S(2)}, u32[]{:S(2)}) async-start(f32[8,8,128]{2,1,0:T(8,128)} %get-tuple-element.44), calls=%async_computation.2 | async-start | bytes 65536 | tf_op jit(solution)/shard_map/all_to_all | solution.py:852
  50.5 2.5 %collective-permute-start.3 = (bf16[3456,128]{1,0:T(8,128)(2,1)S(1)}, bf16[3456,128]{1,0:T(8,128)(2,1)S(1)}, u32[]{:S(2)}, u32[]{:S(2)}) collective-permute-start(bf16[3456,128]{1,0:T(8,128)(2,1)S(1)} %get-tuple-element.52), channel_id=1, source_target_pairs={{0,4},{4,0},{1,5},{5,1},{2,6},{6,2},{3,7},{7,3},{8,12},{12,8},{9,1... | collective-permute-start | bytes 2654216 | tf_op jit(solution)/shard_map/ppermute | solution.py:675
  53.0 5.8 %copy-start.7 = (bf16[1248,128]{1,0:T(8,128)(2,1)S(1)}, bf16[1248,128]{1,0:T(8,128)(2,1)}, u32[]{:S(2)}) copy-start(bf16[1248,128]{1,0:T(8,128)(2,1)} %get-tuple-element.53.near) | copy-start | bytes 958468
  53.0 24.5 %copy-start.1 = (bf16[2,16,32,128]{3,2,1,0:T(8,128)(2,1)S(1)}, bf16[2,16,32,128]{3,2,1,0:T(8,128)(2,1)}, u32[]{:S(2)}) copy-start(bf16[2,16,32,128]{3,2,1,0:T(8,128)(2,1)} %features.5) | copy-start | bytes 786436
  54.7 16.3 %all-to-all-start.3 = ((bf16[4,864,128]{2,1,0:T(8,128)(2,1)}), bf16[4,864,128]{2,1,0:T(8,128)(2,1)S(1)}, u32[]{:S(2)}, u32[]{:S(2)}) async-start(bf16[4,864,128]{2,1,0:T(8,128)(2,1)} %shard_map.85), calls=%async_computation.3 | async-start | bytes 1769472 | tf_op jit(solution)/shard_map/all_to_all | solution.py:889
  58.8 11.9 %collective-permute-start.4 = (bf16[1248,128]{1,0:T(8,128)(2,1)S(1)}, bf16[1248,128]{1,0:T(8,128)(2,1)S(1)}, u32[]{:S(2)}, u32[]{:S(2)}) collective-permute-start(bf16[1248,128]{1,0:T(8,128)(2,1)S(1)} %copy-done.7), channel_id=1, source_target_pairs={{8,0},{16,8},{24,16},{9,1},{17,9},{25,17},{10,2},{18,10},{26,18},{... | collective-permute-start | bytes 958472 | tf_op jit(solution)/shard_map/ppermute | solution.py:681
  60.1 17.5 %collective-permute-start.5 = (bf16[1248,128]{1,0:T(8,128)(2,1)S(1)}, bf16[1248,128]{1,0:T(8,128)(2,1)S(1)}, u32[]{:S(2)}, u32[]{:S(2)}) collective-permute-start(bf16[1248,128]{1,0:T(8,128)(2,1)S(1)} %get-tuple-element.55.act.far), channel_id=1, source_target_pairs={{0,8},{8,16},{16,24},{1,9},{9,17},{17,25},{2,10},{10,18},{18,26},{... | collective-permute-start | bytes 958472 | tf_op jit(solution)/shard_map/ppermute | solution.py:681
  71.8 13.5 %all-to-all-start.4 = ((bf16[4,224,128]{2,1,0:T(8,128)(2,1)}), bf16[4,224,128]{2,1,0:T(8,128)(2,1)S(1)}, u32[]{:S(2)}, u32[]{:S(2)}) async-start(bf16[4,224,128]{2,1,0:T(8,128)(2,1)} %shard_map.86), calls=%async_computation.4 | async-start | bytes 458752 | tf_op jit(solution)/shard_map/all_to_all | solution.py:898
  77.6 1.2 %copy-start.6 = (bf16[3,3,3,128,128]{4,3,2,1,0:T(8,128)(2,1)S(1)}, bf16[3,3,3,128,128]{4,3,2,1,0:T(8,128)(2,1)}, u32[]{:S(2)}) copy-start(bf16[3,3,3,128,128]{4,3,2,1,0:T(8,128)(2,1)} %param.6) | copy-start | bytes 2654212
  86.0 9.9 %all-to-all-start.5 = ((bf16[4,224,128]{2,1,0:T(8,128)(2,1)}), bf16[4,224,128]{2,1,0:T(8,128)(2,1)S(1)}, u32[]{:S(2)}, u32[]{:S(2)}) async-start(bf16[4,224,128]{2,1,0:T(8,128)(2,1)} %shard_map.89), calls=%async_computation.5 | async-start | bytes 458752 | tf_op jit(solution)/shard_map/all_to_all | solution.py:917
  89.4 19.1 %copy-start.2 = (bf16[2,16,32,128]{3,2,1,0:T(8,128)(2,1)S(1)}, bf16[2,16,32,128]{3,2,1,0:T(8,128)(2,1)}, u32[]{:S(2)}) copy-start(bf16[2,16,32,128]{3,2,1,0:T(8,128)(2,1)} %out_grad.1) | copy-start | bytes 786436
  91.2 1.2 %collective-permute-start.6 = (f32[8,128]{1,0:T(8,128)S(1)}, f32[8,128]{1,0:T(8,128)S(1)}, u32[]{:S(2)}, u32[]{:S(2)}) collective-permute-start(f32[8,128]{1,0:T(8,128)S(1)} %get-tuple-element.61), channel_id=1, source_target_pairs={{0,4},{4,0},{1,5},{5,1},{2,6},{6,2},{3,7},{7,3},{8,12},{12,8},{9,1... | collective-permute-start | bytes 12296 | tf_op jit(solution)/shard_map/ppermute | solution.py:675
  108.4 2.5 %collective-permute-start.7 = (bf16[4,896,128]{2,1,0:T(8,128)(2,1)S(1)}, bf16[4,896,128]{2,1,0:T(8,128)(2,1)S(1)}, u32[]{:S(2)}, u32[]{:S(2)}) collective-permute-start(bf16[4,896,128]{2,1,0:T(8,128)(2,1)S(1)} %all_to_all.36.refs_1_), channel_id=1, source_target_pairs={{0,4},{4,0},{1,5},{5,1},{2,6},{6,2},{3,7},{7,3},{8,12},{12,8},{9,1... | collective-permute-start | bytes 2752520 | tf_op jit(solution)/shard_map/ppermute | solution.py:675

commit v12 on v11

--- a/solution.py
+++ b/solution.py
@@ -43,9 +43,15 @@
         return up(self.wide + 2, 8)
 
 
-def call(body, outs, args, scratch=(), smem=0, far=0, sems=0, mib=8, flops=0, beside=False, out_far=0):
-    specs = [pl.BlockSpec(memory_space=pltpu.SMEM)] * smem
-    specs += [pl.BlockSpec(memory_space=pltpu.VMEM)] * (len(args) - smem - far)
+def here():
+    return lax.axis_index("row"), lax.axis_index("col")
+
+
+def call(body, outs, args, scratch=(), placed=False, far=0, sems=0, mib=8, flops=0, beside=False, out_far=0):
+    inner = body
+    if placed:
+        body = lambda *refs: inner(here(), *refs)
+    specs = [pl.BlockSpec(memory_space=pltpu.VMEM)] * (len(args) - far)
     specs += [pl.BlockSpec(memory_space=pltpu.HBM)] * far
     near = len(args) - far
     args = [*args[:near], *(pltpu.with_memory_space_constraint(a, pltpu.HBM) for a in args[near:])]
@@ -718,7 +724,8 @@
 
 
 def placed_body(rows, swapped, *refs):
-    place, block, first, second, sems = refs[0], refs[1], *refs[-3:]
+    block, first, second, sems = refs[0], *refs[-3:]
+    place = here()
 
     def move(target):
         copies = [
@@ -741,18 +748,18 @@
         move(second)
 
 
-def placed(place, block, swapped, rows, so_far):
+def deliver(block, swapped, rows, so_far):
     anywhere = pl.BlockSpec(memory_space=pl.ANY)
     shape = (rows * block.shape[0], LANES)
     return pl.pallas_call(
         functools.partial(placed_body, rows, swapped),
         out_shape=[jax.ShapeDtypeStruct(shape, BF16)] * 2,
-        in_specs=[pl.BlockSpec(memory_space=pltpu.SMEM)] + [anywhere] * (1 + len(so_far)),
+        in_specs=[anywhere] * (1 + len(so_far)),
         out_specs=[anywhere, anywhere],
-        input_output_aliases={2 + k: k for k in range(len(so_far))},
+        input_output_aliases={1 + k: k for k in range(len(so_far))},
         scratch_shapes=[pltpu.SemaphoreType.DMA((block.shape[0],))],
         compiler_params=pltpu.CompilerParams(vmem_limit_bytes=1 << 20),
-    )(place, block, *so_far)
+    )(block, *so_far)
 
 
 def on_device(features, conv_first, conv_second, out_grad):
@@ -762,7 +769,6 @@
     across = lax.axis_size("col")
     peers = 2 * across
     factor = 1.0 / math.sqrt(size.cells * FRAMES * lax.axis_size("tm") * peers)
-    place = jnp.stack([lax.axis_index("row"), lax.axis_index("col")]).astype(jnp.int32)
     taps = conv_first.shape
     first = conv_first.reshape(-1, LANES)
     second = conv_second.reshape(-1, LANES)
@@ -778,8 +784,8 @@
     pay, stats, cols, features_near, grad_near = call(
         part(start_body, size),
         [((edge, LANES), BF16), stat, flat, (features.shape, BF16), (features.shape, BF16)],
-        [place, features, out_grad],
-        smem=1,
+        [features, out_grad],
+        placed=True,
         far=2,
         sems=2 * FRAMES,
     )
@@ -787,18 +793,18 @@
     (slots,) = call(
         part(slots_body, size, (1, 2), across),
         [((across, lines, LANES), BF16)],
-        [place, cols, row_got, stats],
+        [cols, row_got, stats],
         [flat],
-        smem=1,
+        placed=True,
     )
     col_got = lax.all_to_all(slots, "col", 0, 0)
     block = ((size.rows(1), LANES), BF16)
     act_first, grad, norm_first = call(
         part(act_first_body, size, across),
         [block, ((size.rows(2), LANES), BF16), stat],
-        [place, features_near, grad_near, row_got, col_got],
+        [features_near, grad_near, row_got, col_got],
         [frame],
-        smem=1,
+        placed=True,
     )
     grad_after = later(grad, -1)
     act_before = later(act_first, 1)
@@ -816,9 +822,9 @@
     hidden, slots = call(
         part(hidden_body, size, across),
         [(features.shape, BF16), ((peers, up(span + PARTS, 16), LANES), BF16)],
-        [place, act_before, sums, first],
+        [act_before, sums, first],
         [*conv_scratch(size, 1, wide, FRAMES), ((2, span, LANES), F32)],
-        smem=1,
+        placed=True,
         mib=12,
         flops=2 * work,
     )
@@ -842,9 +848,9 @@
     act_second, q, z = call(
         part(act_second_body, size, across),
         [block, field, field],
-        [place, hidden, got, grad_act, norm_second],
+        [hidden, got, grad_act, norm_second],
         [frame, field, field],
-        smem=1,
+        placed=True,
         sems=2 * FRAMES,
         beside=True,
         out_far=2,
@@ -864,9 +870,9 @@
     both, give, grad_second = call(
         part(first_term_body, size, across),
         [((2, *first.shape), F32), (first.shape, BF16), block],
-        [place, got, norm_second, q, z, act_before, act_first, second_term],
+        [got, norm_second, q, z, act_before, act_first, second_term],
         [*conv_scratch(size, 1, wide), turned, *[block] * 3, field, field],
-        smem=1,
+        placed=True,
         far=5,
         sems=2 * FRAMES + 4,
         mib=20,
@@ -883,8 +889,8 @@
     (slots,) = call(
         joined_body,
         [((across, by_col, LANES), BF16)],
-        [place, both, row_swap(give)],
-        smem=1,
+        [both, row_swap(give)],
+        placed=True,
     )
     slots = lax.all_to_all(slots, "col", 0, 0)
     slots, grad_second_after = lax.optimization_barrier((slots, grad_second_after))
@@ -920,8 +926,8 @@
     done = jnp.concatenate([done, parts], 0)
     mine = lax.all_to_all(jnp.broadcast_to(done[None], (across, *done.shape)), "col", 0, 0)
     theirs = row_swap(mine)
-    so_far = placed(place, mine, 0, by_col, [])
-    first_grad, second_grad = placed(place, theirs, 1, by_col, so_far)
+    so_far = deliver(mine, 0, by_col, [])
+    first_grad, second_grad = deliver(theirs, 1, by_col, so_far)
     (feature_grad,) = call(
         part(feature_grad_body, size, peers),
         [(features.shape, BF16)],

time: 113 us -> 110 us (0.973)
  Pallas kernels: 32 us -> 28.1 us
    pallas_call x16, Pallas kernels: 29 us -> 26.2 us  [call(): pl.pallas_call(body, out_shape=shapes[:kept] + [pltpu.HBM(o.shape, o.dtyp...]
    unnamed x16 -> x20, local copies, waits for them, and re-layouts: 2.35 us -> 1.92 us
  transfers between devices with their start and end apart: 13 -> 13, of which waited for: 9 -> 11; matrix products, arithmetic and copies ran while one was open for 0% -> 0% of each run, Pallas kernels for 17% -> 17%
where the time goes in v12:
time: 110 us; the launch traced here: 109 us
  starting transfers between devices  31.5 us (29%)
  Pallas kernels  28.1 us (26%)
  waiting for transfers between devices  23.2 us (21%)
  blocking collectives  23 us (21%)
  local copies, waits for them, and re-layouts  2.05 us (2%)
    pallas_call x16, Pallas kernels, call(): pl.pallas_call(body, out_shape=shapes[:kept] + [pltpu.HBM(o.shape, o.dtyp...  26.2 us
    all_to_all x1, blocking collectives, on_device(): lax.all_to_all(jnp.broadcast_to(done[None], (across, *done.shape)), 'col'...  12.6 us
    ppermute x4, starting transfers between devices, later(): return lax.ppermute(values, 'tm', pairs)  11.8 us
    all_to_all x1, blocking collectives, on_device(): col_got = lax.all_to_all(slots, 'col', 0, 0)  10.4 us
    ppermute x4, waiting for transfers between devices, later(): return lax.ppermute(values, 'tm', pairs)  7.92 us
    all_to_all x2, starting transfers between devices, on_device(): got = lax.all_to_all(slots, ('row', 'col'), 0, 0)  6.73 us
    all_to_all x1, starting transfers between devices, on_device(): got = lax.all_to_all(slots, 'tm', 0, 0)  5.18 us
    ppermute x4, waiting for transfers between devices, row_swap(): return lax.ppermute(values, 'row', [(0, 1), (1, 0)])  4.9 us
  transfers between devices with their start and end apart: 13, of which 11 were waited for; matrix products, arithmetic and copies ran while one was open for 0% of the time, Pallas kernels for 17%

profile of v12, /device:TPU:0, one launch (start us, length us, event | category | flops | bytes accessed | tf_op | source)
XLA Modules:
  0.0 108.8 jit_solution(12487688106860827744)
XLA Ops:
  3.3 10.4 %all_to_all.35.refs_3_ = bf16[4,176,128]{2,1,0:T(8,128)(2,1)S(1)} all-to-all(bf16[4,176,128]{2,1,0:T(8,128)(2,1)S(1)} %shard_map.76), channel_id=1, replica_groups=mesh['tm'=4,'row'=2,'col'=4] {'col'}, dimensions={0} | all-to-all | bytes 360448 | tf_op jit(solution)/shard_map/all_to_all | solution.py:800
  14.5 3.5 %collective-permute-start.1 = (bf16[1248,128]{1,0:T(8,128)(2,1)S(1)}, bf16[1248,128]{1,0:T(8,128)(2,1)S(1)}, u32[]{:S(2)}, u32[]{:S(2)}) collective-permute-start(bf16[1248,128]{1,0:T(8,128)(2,1)S(1)} %get-tuple-element.40.own.refs_5_), channel_id=1, source_target_pairs={{0,8},{8,16},{16,24},{1,9},{9,17},{17,25},{2,10},{10,18},{18,26},{... | collective-permute-start | bytes 958472 | tf_op jit(solution)/shard_map/ppermute | solution.py:687
  18.0 1.3 %collective-permute-start.2 = (bf16[1472,128]{1,0:T(8,128)(2,1)S(1)}, bf16[1472,128]{1,0:T(8,128)(2,1)S(1)}, u32[]{:S(2)}, u32[]{:S(2)}) collective-permute-start(bf16[1472,128]{1,0:T(8,128)(2,1)S(1)} %get-tuple-element.43.near), channel_id=1, source_target_pairs={{8,0},{16,8},{24,16},{9,1},{17,9},{25,17},{10,2},{18,10},{26,18},{... | collective-permute-start | bytes 1130504 | tf_op jit(solution)/shard_map/ppermute | solution.py:687
  21.3 2.3 %collective-permute-done.1.refs_0_.refs_4_ = bf16[1248,128]{1,0:T(8,128)(2,1)S(1)} collective-permute-done((bf16[1248,128]{1,0:T(8,128)(2,1)S(1)}, bf16[1248,128]{1,0:T(8,128)(2,1)S(1)}, u32[]{:S(2)}, u32[]{:S(2)}) %collective-permute-start.1) | collective-permute-done | bytes 319520 | tf_op jit(solution)/shard_map/ppermute | solution.py:687
  23.6 1.7 %shard_map.79 = (bf16[2,16,32,128]{3,2,1,0:T(8,128)(2,1)S(1)}, bf16[8,96,128]{2,1,0:T(8,128)(2,1)}) custom-call(bf16[1248,128]{1,0:T(8,128)(2,1)S(1)} %collective-permute-done.1.refs_0_.refs_4_, f32[2,512,128]{2,1,0:T(8,128)S(1)} %shard_map.78.refs_1_, bf16[3456,128]{1,0:T(8,128)(2,1)S(1)} %bitcast.6), custom_call_target="tpu_custom_call" | custom-call | flops 1811939328 | bytes 2187264 | tf_op jit(solution)/shard_map/pallas_call | solution.py:65
  25.4 3.4 %all-to-all-start.1 = ((bf16[8,96,128]{2,1,0:T(8,128)(2,1)}), bf16[8,96,128]{2,1,0:T(8,128)(2,1)S(1)}, u32[]{:S(2)}, u32[]{:S(2)}) async-start(bf16[8,96,128]{2,1,0:T(8,128)(2,1)} %get-tuple-element.42), calls=%async_computation.1 | async-start | bytes 393216 | tf_op jit(solution)/shard_map/all_to_all | solution.py:831
  29.0 3.5 %shard_map.80.grad_act.refs_2_ = f32[2,18,40,128]{3,2,1,0:T(8,128)S(1)} custom-call(bf16[1472,128]{1,0:T(8,128)(2,1)S(1)} %get-tuple-element.43.near, bf16[1472,128]{1,0:T(8,128)(2,1)S(1)} %collective-permute-done.2.far, bf16[3456,128]{1,0:T(8,128)(2,1)} %bitcast.8), custom_call_target="tpu_custom_call" | custom-call | flops 1811939328 | bytes 2375680 | tf_op jit(solution)/shard_map/pallas_call | solution.py:65
  32.5 2.1 %all-to-all-done.1.got.refs_1_ = bf16[8,96,128]{2,1,0:T(8,128)(2,1)S(1)} async-done(((bf16[8,96,128]{2,1,0:T(8,128)(2,1)}), bf16[8,96,128]{2,1,0:T(8,128)(2,1)S(1)}, u32[]{:S(2)}, u32[]{:S(2)}) %all-to-all-start.1) | async-done | bytes 196640 | tf_op jit(solution)/shard_map/all_to_all | solution.py:831
  35.9 3.3 %all-to-all-start.2 = ((f32[8,8,128]{2,1,0:T(8,128)}), f32[8,8,128]{2,1,0:T(8,128)S(1)}, u32[]{:S(2)}, u32[]{:S(2)}) async-start(f32[8,8,128]{2,1,0:T(8,128)} %get-tuple-element.44), calls=%async_computation.2 | async-start | bytes 65536 | tf_op jit(solution)/shard_map/all_to_all | solution.py:858
  39.2 1.7 %shard_map.82 = (bf16[1248,128]{1,0:T(8,128)(2,1)S(1)}, f32[2,18,40,128]{3,2,1,0:T(8,128)}, f32[2,18,40,128]{3,2,1,0:T(8,128)}) custom-call(bf16[2,16,32,128]{3,2,1,0:T(8,128)(2,1)S(1)} %get-tuple-element.41.hidden.refs_0_, bf16[8,96,128]{2,1,0:T(8,128)(2,1)S(1)} %all-to-all-done.1.got.refs_1_, f32[2,18,40,128]{3,2,1,0:T(8,128)S(1)} %shard_map.80.grad_act.refs_2_, ...), custom_call_target="tpu_custom_call" | custom-call | tf_op jit(solution)/shard_map/pallas_call | solution.py:65
  40.9 2.4 %shard_map.83.refs_6_ = f32[3456,128]{1,0:T(8,128)} custom-call(bf16[1472,128]{1,0:T(8,128)(2,1)S(1)} %get-tuple-element.43.near, bf16[1472,128]{1,0:T(8,128)(2,1)S(1)} %collective-permute-done.2.far, bf16[1248,128]{1,0:T(8,128)(2,1)S(1)} %get-tuple-element.55.act.far), custom_call_target="tpu_custom_call" | custom-call | tf_op jit(solution)/shard_map/pallas_call | solution.py:65
  44.0 3.8 %shard_map.84 = (f32[2,3456,128]{2,1,0:T(8,128)S(1)}, bf16[3456,128]{1,0:T(8,128)(2,1)S(1)}, bf16[1248,128]{1,0:T(8,128)(2,1)}) custom-call(f32[8,8,128]{2,1,0:T(8,128)S(1)} %all-to-all-done.2.refs_0_, f32[8,128]{1,0:T(8,128)S(1)} %get-tuple-element.45.refs_3_.refs_1_, f32[2,18,40,128]{3,2,1,0:T(8,128)} %get-tuple-element.46.refs_2_, ...), custom_call_target="tpu_custom_call" | custom-call | flops 905969664 | bytes 8663040 | tf_op jit(solution)/shard_map/pallas_call | solution.py:65
  47.9 2.4 %collective-permute-done.3.refs_1_ = bf16[3456,128]{1,0:T(8,128)(2,1)S(1)} collective-permute-done((bf16[3456,128]{1,0:T(8,128)(2,1)S(1)}, bf16[3456,128]{1,0:T(8,128)(2,1)S(1)}, u32[]{:S(2)}, u32[]{:S(2)}) %collective-permute-start.3) | collective-permute-done | bytes 884768 | tf_op jit(solution)/shard_map/ppermute | solution.py:681
  51.4 3.6 %all-to-all-start.3 = ((bf16[4,864,128]{2,1,0:T(8,128)(2,1)}), bf16[4,864,128]{2,1,0:T(8,128)(2,1)S(1)}, u32[]{:S(2)}, u32[]{:S(2)}) async-start(bf16[4,864,128]{2,1,0:T(8,128)(2,1)} %shard_map.85), calls=%async_computation.3 | async-start | bytes 1769472 | tf_op jit(solution)/shard_map/all_to_all | solution.py:895
  55.0 1.3 %collective-permute-start.4 = (bf16[1248,128]{1,0:T(8,128)(2,1)}, bf16[1248,128]{1,0:T(8,128)(2,1)S(1)}, u32[]{:S(2)}, u32[]{:S(2)}) collective-permute-start(bf16[1248,128]{1,0:T(8,128)(2,1)} %get-tuple-element.53.near), channel_id=1, source_target_pairs={{8,0},{16,8},{24,16},{9,1},{17,9},{25,17},{10,2},{18,10},{26,18},{... | collective-permute-start | bytes 958472 | tf_op jit(solution)/shard_map/ppermute | solution.py:687
  56.3 5.7 %collective-permute-start.5 = (bf16[1248,128]{1,0:T(8,128)(2,1)S(1)}, bf16[1248,128]{1,0:T(8,128)(2,1)}, u32[]{:S(2)}, u32[]{:S(2)}) collective-permute-start(bf16[1248,128]{1,0:T(8,128)(2,1)S(1)} %get-tuple-element.55.act.far), channel_id=1, source_target_pairs={{0,8},{8,16},{16,24},{1,9},{9,17},{17,25},{2,10},{10,18},{18,26},{... | collective-permute-start | bytes 958472 | tf_op jit(solution)/shard_map/ppermute | solution.py:687
  62.0 5.4 %collective-permute-done.4.far = bf16[1248,128]{1,0:T(8,128)(2,1)S(1)} collective-permute-done((bf16[1248,128]{1,0:T(8,128)(2,1)}, bf16[1248,128]{1,0:T(8,128)(2,1)S(1)}, u32[]{:S(2)}, u32[]{:S(2)}) %collective-permute-start.4) | collective-permute-done | bytes 319520 | tf_op jit(solution)/shard_map/ppermute | solution.py:687
  69.0 5.2 %all-to-all-start.4 = ((bf16[4,224,128]{2,1,0:T(8,128)(2,1)}), bf16[4,224,128]{2,1,0:T(8,128)(2,1)S(1)}, u32[]{:S(2)}, u32[]{:S(2)}) async-start(bf16[4,224,128]{2,1,0:T(8,128)(2,1)} %shard_map.86), calls=%async_computation.4 | async-start | bytes 458752 | tf_op jit(solution)/shard_map/all_to_all | solution.py:904
  74.2 3.4 %shard_map.87 = bf16[2,16,32,128]{3,2,1,0:T(8,128)(2,1)} custom-call(bf16[1248,128]{1,0:T(8,128)(2,1)} %collective-permute-done.5.near, bf16[1248,128]{1,0:T(8,128)(2,1)S(1)} %get-tuple-element.55.act.far, bf16[3456,128]{1,0:T(8,128)(2,1)S(1)} %bitcast.9, bf16[2,16,32,128]{3,2,1,0:T(8,128)(2,1)S(1)} %copy-done.1), custom_call_target="tpu_custom_call" | custom-call | flops 905969664 | bytes 2048000 | tf_op jit(solution)/shard_map/pallas_call | solution.py:65
  77.6 4.3 %all-to-all-done.4.got = bf16[4,224,128]{2,1,0:T(8,128)(2,1)S(1)} async-done(((bf16[4,224,128]{2,1,0:T(8,128)(2,1)}), bf16[4,224,128]{2,1,0:T(8,128)(2,1)S(1)}, u32[]{:S(2)}, u32[]{:S(2)}) %all-to-all-start.4) | async-done | bytes 229408 | tf_op jit(solution)/shard_map/all_to_all | solution.py:904
  82.6 3.4 %all-to-all-start.5 = ((bf16[4,224,128]{2,1,0:T(8,128)(2,1)}), bf16[4,224,128]{2,1,0:T(8,128)(2,1)S(1)}, u32[]{:S(2)}, u32[]{:S(2)}) async-start(bf16[4,224,128]{2,1,0:T(8,128)(2,1)} %shard_map.89), calls=%async_computation.5 | async-start | bytes 458752 | tf_op jit(solution)/shard_map/all_to_all | solution.py:923
  86.0 1.9 %shard_map.88 = (f32[2,512,128]{2,1,0:T(8,128)S(1)}, f32[8,128]{1,0:T(8,128)S(1)}) custom-call(bf16[1248,128]{1,0:T(8,128)(2,1)S(1)} %copy-done.7, bf16[1248,128]{1,0:T(8,128)(2,1)S(1)} %copy-done.9, bf16[3456,128]{1,0:T(8,128)(2,1)S(1)} %bitcast.7, bf16[2,16,32,128]{3,2,1,0:T(8,128)(2,1)S(1)} %copy-done.1, f32[8,128]{1,0:T(8,128)S(1)} %get-tuple-element.57.norm), custom_call_target="tpu_custom_call" | custom-call | flops 905969664 | bytes 2318336 | tf_op jit(solution)/shard_map/pallas_call | solution.py:65
  89.2 3.3 %all-to-all-done.5 = bf16[4,224,128]{2,1,0:T(8,128)(2,1)S(1)} async-done(((bf16[4,224,128]{2,1,0:T(8,128)(2,1)}), bf16[4,224,128]{2,1,0:T(8,128)(2,1)S(1)}, u32[]{:S(2)}, u32[]{:S(2)}) %all-to-all-start.5) | async-done | bytes 229408 | tf_op jit(solution)/shard_map/all_to_all | solution.py:923
  92.6 12.6 %all_to_all.36.refs_0_ = bf16[4,896,128]{2,1,0:T(8,128)(2,1)S(1)} all-to-all(bf16[4,896,128]{2,1,0:T(8,128)(2,1)S(1)} %broadcast_in_dim.2), channel_id=1, replica_groups=mesh['tm'=4,'row'=2,'col'=4] {'col'}, dimensions={0} | all-to-all | bytes 1835008 | tf_op jit(solution)/shard_map/all_to_all | solution.py:927
  (48 shorter events, 15.8 us)
Async XLA Ops:
  1.9 1.4 %collective-permute-start = (bf16[224,128]{1,0:T(8,128)(2,1)S(1)}, bf16[224,128]{1,0:T(8,128)(2,1)S(1)}, u32[]{:S(2)}, u32[]{:S(2)}) collective-permute-start(bf16[224,128]{1,0:T(8,128)(2,1)S(1)} %get-tuple-element.37), channel_id=1, source_target_pairs={{0,4},{4,0},{1,5},{5,1},{2,6},{6,2},{3,7},{7,3},{8,12},{12,8},{9,1... | collective-permute-start | bytes 172040 | tf_op jit(solution)/shard_map/ppermute | solution.py:681
  14.5 10.9 %copy-start = (bf16[1248,128]{1,0:T(8,128)(2,1)}, bf16[1248,128]{1,0:T(8,128)(2,1)S(1)}, u32[]{:S(2)}) copy-start(bf16[1248,128]{1,0:T(8,128)(2,1)S(1)} %get-tuple-element.40.own.refs_5_) | copy-start | bytes 958468
  14.5 9.2 %collective-permute-start.1 = (bf16[1248,128]{1,0:T(8,128)(2,1)S(1)}, bf16[1248,128]{1,0:T(8,128)(2,1)S(1)}, u32[]{:S(2)}, u32[]{:S(2)}) collective-permute-start(bf16[1248,128]{1,0:T(8,128)(2,1)S(1)} %get-tuple-element.40.own.refs_5_), channel_id=1, source_target_pairs={{0,8},{8,16},{16,24},{1,9},{9,17},{17,25},{2,10},{10,18},{18,26},{... | collective-permute-start | bytes 958472 | tf_op jit(solution)/shard_map/ppermute | solution.py:687
  18.0 11.0 %collective-permute-start.2 = (bf16[1472,128]{1,0:T(8,128)(2,1)S(1)}, bf16[1472,128]{1,0:T(8,128)(2,1)S(1)}, u32[]{:S(2)}, u32[]{:S(2)}) collective-permute-start(bf16[1472,128]{1,0:T(8,128)(2,1)S(1)} %get-tuple-element.43.near), channel_id=1, source_target_pairs={{8,0},{16,8},{24,16},{9,1},{17,9},{25,17},{10,2},{18,10},{26,18},{... | collective-permute-start | bytes 1130504 | tf_op jit(solution)/shard_map/ppermute | solution.py:687
  19.3 1.2 %copy-start.3 = (bf16[3,3,3,128,128]{4,3,2,1,0:T(8,128)(2,1)S(1)}, bf16[3,3,3,128,128]{4,3,2,1,0:T(8,128)(2,1)}, u32[]{:S(2)}) copy-start(bf16[3,3,3,128,128]{4,3,2,1,0:T(8,128)(2,1)} %param.5) | copy-start | bytes 2654212
  23.6 1.7 %copy-start.5 = (bf16[1248,128]{1,0:T(8,128)(2,1)}, bf16[1248,128]{1,0:T(8,128)(2,1)S(1)}, u32[]{:S(2)}) copy-start(bf16[1248,128]{1,0:T(8,128)(2,1)S(1)} %collective-permute-done.1.refs_0_.refs_4_) | copy-start | bytes 958468
  25.4 9.3 %all-to-all-start.1 = ((bf16[8,96,128]{2,1,0:T(8,128)(2,1)}), bf16[8,96,128]{2,1,0:T(8,128)(2,1)S(1)}, u32[]{:S(2)}, u32[]{:S(2)}) async-start(bf16[8,96,128]{2,1,0:T(8,128)(2,1)} %get-tuple-element.42), calls=%async_computation.1 | async-start | bytes 393216 | tf_op jit(solution)/shard_map/all_to_all | solution.py:831
  35.9 8.1 %all-to-all-start.2 = ((f32[8,8,128]{2,1,0:T(8,128)}), f32[8,8,128]{2,1,0:T(8,128)S(1)}, u32[]{:S(2)}, u32[]{:S(2)}) async-start(f32[8,8,128]{2,1,0:T(8,128)} %get-tuple-element.44), calls=%async_computation.2 | async-start | bytes 65536 | tf_op jit(solution)/shard_map/all_to_all | solution.py:858
  47.7 2.5 %collective-permute-start.3 = (bf16[3456,128]{1,0:T(8,128)(2,1)S(1)}, bf16[3456,128]{1,0:T(8,128)(2,1)S(1)}, u32[]{:S(2)}, u32[]{:S(2)}) collective-permute-start(bf16[3456,128]{1,0:T(8,128)(2,1)S(1)} %get-tuple-element.52), channel_id=1, source_target_pairs={{0,4},{4,0},{1,5},{5,1},{2,6},{6,2},{3,7},{7,3},{8,12},{12,8},{9,1... | collective-permute-start | bytes 2654216 | tf_op jit(solution)/shard_map/ppermute | solution.py:681
  50.2 23.9 %copy-start.1 = (bf16[2,16,32,128]{3,2,1,0:T(8,128)(2,1)S(1)}, bf16[2,16,32,128]{3,2,1,0:T(8,128)(2,1)}, u32[]{:S(2)}) copy-start(bf16[2,16,32,128]{3,2,1,0:T(8,128)(2,1)} %features.5) | copy-start | bytes 786436
  50.2 23.9 %copy-start.6 = (bf16[3,3,3,128,128]{4,3,2,1,0:T(8,128)(2,1)S(1)}, bf16[3,3,3,128,128]{4,3,2,1,0:T(8,128)(2,1)}, u32[]{:S(2)}) copy-start(bf16[3,3,3,128,128]{4,3,2,1,0:T(8,128)(2,1)} %param.6) | copy-start | bytes 2654212
  51.4 34.6 %copy-start.4 = (bf16[3,3,3,128,128]{4,3,2,1,0:T(8,128)(2,1)S(1)}, bf16[3,3,3,128,128]{4,3,2,1,0:T(8,128)(2,1)}, u32[]{:S(2)}) copy-start(bf16[3,3,3,128,128]{4,3,2,1,0:T(8,128)(2,1)} %param.5) | copy-start | bytes 2654212
  51.4 16.8 %all-to-all-start.3 = ((bf16[4,864,128]{2,1,0:T(8,128)(2,1)}), bf16[4,864,128]{2,1,0:T(8,128)(2,1)S(1)}, u32[]{:S(2)}, u32[]{:S(2)}) async-start(bf16[4,864,128]{2,1,0:T(8,128)(2,1)} %shard_map.85), calls=%async_computation.3 | async-start | bytes 1769472 | tf_op jit(solution)/shard_map/all_to_all | solution.py:895
  55.0 12.4 %collective-permute-start.4 = (bf16[1248,128]{1,0:T(8,128)(2,1)}, bf16[1248,128]{1,0:T(8,128)(2,1)S(1)}, u32[]{:S(2)}, u32[]{:S(2)}) collective-permute-start(bf16[1248,128]{1,0:T(8,128)(2,1)} %get-tuple-element.53.near), channel_id=1, source_target_pairs={{8,0},{16,8},{24,16},{9,1},{17,9},{25,17},{10,2},{18,10},{26,18},{... | collective-permute-start | bytes 958472 | tf_op jit(solution)/shard_map/ppermute | solution.py:687
  56.3 17.8 %collective-permute-start.5 = (bf16[1248,128]{1,0:T(8,128)(2,1)S(1)}, bf16[1248,128]{1,0:T(8,128)(2,1)}, u32[]{:S(2)}, u32[]{:S(2)}) collective-permute-start(bf16[1248,128]{1,0:T(8,128)(2,1)S(1)} %get-tuple-element.55.act.far), channel_id=1, source_target_pairs={{0,8},{8,16},{16,24},{1,9},{9,17},{17,25},{2,10},{10,18},{18,26},{... | collective-permute-start | bytes 958472 | tf_op jit(solution)/shard_map/ppermute | solution.py:687
  67.4 0.7 copy-start.8
  69.0 17.1 %copy-start.7 = (bf16[1248,128]{1,0:T(8,128)(2,1)S(1)}, bf16[1248,128]{1,0:T(8,128)(2,1)}, u32[]{:S(2)}) copy-start(bf16[1248,128]{1,0:T(8,128)(2,1)} %get-tuple-element.53.near) | copy-start | bytes 958468
  69.0 17.1 %copy-start.9 = (bf16[1248,128]{1,0:T(8,128)(2,1)S(1)}, bf16[1248,128]{1,0:T(8,128)(2,1)}, u32[]{:S(2)}) copy-start(bf16[1248,128]{1,0:T(8,128)(2,1)} %copy-done.8) | copy-start | bytes 958468
  69.0 12.9 %all-to-all-start.4 = ((bf16[4,224,128]{2,1,0:T(8,128)(2,1)}), bf16[4,224,128]{2,1,0:T(8,128)(2,1)S(1)}, u32[]{:S(2)}, u32[]{:S(2)}) async-start(bf16[4,224,128]{2,1,0:T(8,128)(2,1)} %shard_map.86), calls=%async_computation.4 | async-start | bytes 458752 | tf_op jit(solution)/shard_map/all_to_all | solution.py:904
  82.6 9.9 %all-to-all-start.5 = ((bf16[4,224,128]{2,1,0:T(8,128)(2,1)}), bf16[4,224,128]{2,1,0:T(8,128)(2,1)S(1)}, u32[]{:S(2)}, u32[]{:S(2)}) async-start(bf16[4,224,128]{2,1,0:T(8,128)(2,1)} %shard_map.89), calls=%async_computation.5 | async-start | bytes 458752 | tf_op jit(solution)/shard_map/all_to_all | solution.py:923
  86.0 19.2 %copy-start.2 = (bf16[2,16,32,128]{3,2,1,0:T(8,128)(2,1)S(1)}, bf16[2,16,32,128]{3,2,1,0:T(8,128)(2,1)}, u32[]{:S(2)}) copy-start(bf16[2,16,32,128]{3,2,1,0:T(8,128)(2,1)} %out_grad.1) | copy-start | bytes 786436
  87.9 1.2 %collective-permute-start.6 = (f32[8,128]{1,0:T(8,128)S(1)}, f32[8,128]{1,0:T(8,128)S(1)}, u32[]{:S(2)}, u32[]{:S(2)}) collective-permute-start(f32[8,128]{1,0:T(8,128)S(1)} %get-tuple-element.61), channel_id=1, source_target_pairs={{0,4},{4,0},{1,5},{5,1},{2,6},{6,2},{3,7},{7,3},{8,12},{12,8},{9,1... | collective-permute-start | bytes 12296 | tf_op jit(solution)/shard_map/ppermute | solution.py:681
  105.3 2.5 %collective-permute-start.7 = (bf16[4,896,128]{2,1,0:T(8,128)(2,1)S(1)}, bf16[4,896,128]{2,1,0:T(8,128)(2,1)S(1)}, u32[]{:S(2)}, u32[]{:S(2)}) collective-permute-start(bf16[4,896,128]{2,1,0:T(8,128)(2,1)S(1)} %all_to_all.36.refs_0_), channel_id=1, source_target_pairs={{0,4},{4,0},{1,5},{5,1},{2,6},{6,2},{3,7},{7,3},{8,12},{12,8},{9,1... | collective-permute-start | bytes 2752520 | tf_op jit(solution)/shard_map/ppermute | solution.py:681

commit v13 on v12

--- a/solution.py
+++ b/solution.py
@@ -448,14 +448,26 @@
     return up(max(FRAMES * size.wide, FRAMES * size.stride(1)), 16)
 
 
-def sums_second_body(size, across, hidden, got, grad_act, norm, slots):
+def sums_second_body(
+    size, across, got, hidden_far, grad_far, norm, slots, hidden, grad_act, sems
+):
     high, wide = size.high, size.wide
+    pairs = ((hidden_far, hidden), (grad_far, grad_act))
+    copies = [
+        pltpu.make_async_copy(source.at[f], target.at[f], sems.at[2 * f + k])
+        for f in range(FRAMES)
+        for k, (source, target) in enumerate(pairs)
+    ]
+    for copy in copies:
+        copy.start()
     at = span_second(size)
     blocks = [join3(got[peer, at : at + PARTS]) for peer in range(got.shape[0])]
     found = concluded(blocks, size.cells)
     norm[...] = found
     firsts, seconds = [], []
     for f in range(FRAMES):
+        copies[2 * f].wait()
+        copies[2 * f + 1].wait()
         own = hidden[f].astype(F32)
         normed = (own - found[f : f + 1][None]) * found[FRAMES + f : FRAMES + f + 1][None]
         sigmoid = logistic(normed)
@@ -648,7 +660,12 @@
         out[f] = total.astype(BF16)
 
 
-def back_first_body(size, near, far, kernel, features, norm, q, sums, x, frame):
+def back_first_body(
+    size, near, kernel, features, norm, after, q, sums, x, frame, far, sems
+):
+    copy = pltpu.make_async_copy(after, far, sems.at[0])
+    copy.start()
+    copy.wait()
     spread_all(size, 1, 1, size.wide, near, far, x, frame)
     grads = convolved(x, kernel, True)
     firsts, seconds = [], []
@@ -843,7 +860,10 @@
     norm_second, slots = call(
         part(sums_second_body, size, across),
         [stat, ((peers, STATS, LANES), F32)],
-        [hidden, got, grad_act],
+        [got, hidden, grad_act],
+        [(features.shape, BF16), field],
+        far=2,
+        sems=2 * FRAMES,
     )
     act_second, q, z = call(
         part(act_second_body, size, across),
@@ -913,8 +933,10 @@
     q, sums = call(
         part(back_first_body, size),
         [((FRAMES, size.cells, LANES), F32), stat],
-        [grad_second, grad_second_after, first, features, norm_first],
-        conv_scratch(size, 1, wide),
+        [grad_second, first, features, norm_first, grad_second_after],
+        [*conv_scratch(size, 1, wide), block],
+        far=1,
+        sems=1,
         mib=14,
         flops=work,
     )

time: 110 us -> 113 us (1.027)
  waiting for transfers between devices: 23.2 us -> 20.2 us
  local copies, waits for them, and re-layouts: 2.05 us -> 4.01 us
  Pallas kernels: 28.1 us -> 30 us
  starting transfers between devices: 31.5 us -> 33 us
    unnamed x20 -> x24, local copies, waits for them, and re-layouts: 1.92 us -> 3.87 us
    pallas_call x16, Pallas kernels: 26.2 us -> 28.1 us  [call(): pl.pallas_call(body, out_shape=shapes[:kept] + [pltpu.HBM(o.shape, o.dtyp...]
    all_to_all x2, waiting for transfers between devices: 2.73 us -> 1.42 us  [on_device(): got = lax.all_to_all(slots, ('row', 'col'), 0, 0)]
  transfers between devices with their start and end apart: 13 -> 13, of which waited for: 11 -> 9; matrix products, arithmetic and copies ran while one was open for 0% -> 0% of each run, Pallas kernels for 17% -> 17%
where the time goes in v13:
time: 113 us; the launch traced here: 112 us
  starting transfers between devices  33 us (29%)
  Pallas kernels  30 us (27%)
  blocking collectives  23.8 us (21%)
  waiting for transfers between devices  20.2 us (18%)
  local copies, waits for them, and re-layouts  4.01 us (4%)
    pallas_call x16, Pallas kernels, call(): pl.pallas_call(body, out_shape=shapes[:kept] + [pltpu.HBM(o.shape, o.dtyp...  28.1 us
    all_to_all x1, blocking collectives, on_device(): lax.all_to_all(jnp.broadcast_to(done[None], (across, *done.shape)), 'col'...  13.5 us
    ppermute x4, starting transfers between devices, later(): return lax.ppermute(values, 'tm', pairs)  11.8 us
    all_to_all x1, blocking collectives, on_device(): col_got = lax.all_to_all(slots, 'col', 0, 0)  10.4 us
    ppermute x4, waiting for transfers between devices, later(): return lax.ppermute(values, 'tm', pairs)  7.52 us
    all_to_all x2, starting transfers between devices, on_device(): got = lax.all_to_all(slots, ('row', 'col'), 0, 0)  6.75 us
    all_to_all x1, starting transfers between devices, on_device(): got = lax.all_to_all(slots, 'tm', 0, 0)  5.84 us
    ppermute x4, waiting for transfers between devices, row_swap(): return lax.ppermute(values, 'row', [(0, 1), (1, 0)])  4.6 us
  transfers between devices with their start and end apart: 13, of which 9 were waited for; matrix products, arithmetic and copies ran while one was open for 0% of the time, Pallas kernels for 17%

profile of v13, /device:TPU:0, one launch (start us, length us, event | category | flops | bytes accessed | tf_op | source)
XLA Modules:
  0.0 112.1 jit_solution(4825334298153663258)
XLA Ops:
  3.3 10.4 %all_to_all.35.refs_3_ = bf16[4,176,128]{2,1,0:T(8,128)(2,1)S(1)} all-to-all(bf16[4,176,128]{2,1,0:T(8,128)(2,1)S(1)} %shard_map.76), channel_id=1, replica_groups=mesh['tm'=4,'row'=2,'col'=4] {'col'}, dimensions={0} | all-to-all | bytes 360448 | tf_op jit(solution)/shard_map/all_to_all | solution.py:817
  14.5 3.5 %collective-permute-start.1 = (bf16[1248,128]{1,0:T(8,128)(2,1)S(1)}, bf16[1248,128]{1,0:T(8,128)(2,1)S(1)}, u32[]{:S(2)}, u32[]{:S(2)}) collective-permute-start(bf16[1248,128]{1,0:T(8,128)(2,1)S(1)} %get-tuple-element.40.own.refs_5_), channel_id=1, source_target_pairs={{0,8},{8,16},{16,24},{1,9},{9,17},{17,25},{2,10},{10,18},{18,26},{... | collective-permute-start | bytes 958472 | tf_op jit(solution)/shard_map/ppermute | solution.py:704
  18.0 1.3 %collective-permute-start.2 = (bf16[1472,128]{1,0:T(8,128)(2,1)S(1)}, bf16[1472,128]{1,0:T(8,128)(2,1)S(1)}, u32[]{:S(2)}, u32[]{:S(2)}) collective-permute-start(bf16[1472,128]{1,0:T(8,128)(2,1)S(1)} %get-tuple-element.43.near), channel_id=1, source_target_pairs={{8,0},{16,8},{24,16},{9,1},{17,9},{25,17},{10,2},{18,10},{26,18},{... | collective-permute-start | bytes 1130504 | tf_op jit(solution)/shard_map/ppermute | solution.py:704
  21.3 2.3 %collective-permute-done.1.refs_0_.refs_4_ = bf16[1248,128]{1,0:T(8,128)(2,1)S(1)} collective-permute-done((bf16[1248,128]{1,0:T(8,128)(2,1)S(1)}, bf16[1248,128]{1,0:T(8,128)(2,1)S(1)}, u32[]{:S(2)}, u32[]{:S(2)}) %collective-permute-start.1) | collective-permute-done | bytes 319520 | tf_op jit(solution)/shard_map/ppermute | solution.py:704
  23.6 1.7 %shard_map.79 = (bf16[2,16,32,128]{3,2,1,0:T(8,128)(2,1)S(1)}, bf16[8,96,128]{2,1,0:T(8,128)(2,1)}) custom-call(bf16[1248,128]{1,0:T(8,128)(2,1)S(1)} %collective-permute-done.1.refs_0_.refs_4_, f32[2,512,128]{2,1,0:T(8,128)S(1)} %shard_map.78.refs_1_, bf16[3456,128]{1,0:T(8,128)(2,1)S(1)} %bitcast.6), custom_call_target="tpu_custom_call" | custom-call | flops 1811939328 | bytes 2187264 | tf_op jit(solution)/shard_map/pallas_call | solution.py:65
  26.1 3.4 %all-to-all-start.1 = ((bf16[8,96,128]{2,1,0:T(8,128)(2,1)}), bf16[8,96,128]{2,1,0:T(8,128)(2,1)S(1)}, u32[]{:S(2)}, u32[]{:S(2)}) async-start(bf16[8,96,128]{2,1,0:T(8,128)(2,1)} %get-tuple-element.41), calls=%async_computation.1 | async-start | bytes 393216 | tf_op jit(solution)/shard_map/all_to_all | solution.py:848
  29.5 3.6 %shard_map.80.grad_far.refs_2_ = f32[2,18,40,128]{3,2,1,0:T(8,128)S(1)} custom-call(bf16[1472,128]{1,0:T(8,128)(2,1)S(1)} %get-tuple-element.43.near, bf16[1472,128]{1,0:T(8,128)(2,1)S(1)} %collective-permute-done.2.far, bf16[3456,128]{1,0:T(8,128)(2,1)} %bitcast.8), custom_call_target="tpu_custom_call" | custom-call | flops 1811939328 | bytes 2375680 | tf_op jit(solution)/shard_map/pallas_call | solution.py:65
  34.0 1.4 %all-to-all-done.1.got.refs_1_ = bf16[8,96,128]{2,1,0:T(8,128)(2,1)S(1)} async-done(((bf16[8,96,128]{2,1,0:T(8,128)(2,1)}), bf16[8,96,128]{2,1,0:T(8,128)(2,1)S(1)}, u32[]{:S(2)}, u32[]{:S(2)}) %all-to-all-start.1) | async-done | bytes 196640 | tf_op jit(solution)/shard_map/all_to_all | solution.py:848
  35.4 2.0 %shard_map.81 = (f32[8,128]{1,0:T(8,128)S(1)}, f32[8,8,128]{2,1,0:T(8,128)}) custom-call(bf16[8,96,128]{2,1,0:T(8,128)(2,1)S(1)} %all-to-all-done.1.got.refs_1_, bf16[2,16,32,128]{3,2,1,0:T(8,128)(2,1)} %copy-done.5, f32[2,18,40,128]{3,2,1,0:T(8,128)} %copy-done), custom_call_target="tpu_custom_call" | custom-call | bytes 1232896 | tf_op jit(solution)/shard_map/pallas_call | solution.py:65
  37.4 3.4 %all-to-all-start.2 = ((f32[8,8,128]{2,1,0:T(8,128)}), f32[8,8,128]{2,1,0:T(8,128)S(1)}, u32[]{:S(2)}, u32[]{:S(2)}) async-start(f32[8,8,128]{2,1,0:T(8,128)} %get-tuple-element.44), calls=%async_computation.2 | async-start | bytes 65536 | tf_op jit(solution)/shard_map/all_to_all | solution.py:878
  41.9 1.7 %shard_map.82 = (bf16[1248,128]{1,0:T(8,128)(2,1)S(1)}, f32[2,18,40,128]{3,2,1,0:T(8,128)}, f32[2,18,40,128]{3,2,1,0:T(8,128)}) custom-call(bf16[2,16,32,128]{3,2,1,0:T(8,128)(2,1)S(1)} %copy-done.6, bf16[8,96,128]{2,1,0:T(8,128)(2,1)S(1)} %all-to-all-done.1.got.refs_1_, f32[2,18,40,128]{3,2,1,0:T(8,128)S(1)} %copy-done.1, ...), custom_call_target="tpu_custom_call" | custom-call | tf_op jit(solution)/shard_map/pallas_call | solution.py:65
  43.6 2.4 %shard_map.83.refs_6_ = f32[3456,128]{1,0:T(8,128)} custom-call(bf16[1472,128]{1,0:T(8,128)(2,1)S(1)} %get-tuple-element.43.near, bf16[1472,128]{1,0:T(8,128)(2,1)S(1)} %collective-permute-done.2.far, bf16[1248,128]{1,0:T(8,128)(2,1)S(1)} %get-tuple-element.55.act.far), custom_call_target="tpu_custom_call" | custom-call | tf_op jit(solution)/shard_map/pallas_call | solution.py:65
  46.1 3.8 %shard_map.84 = (f32[2,3456,128]{2,1,0:T(8,128)S(1)}, bf16[3456,128]{1,0:T(8,128)(2,1)S(1)}, bf16[1248,128]{1,0:T(8,128)(2,1)}) custom-call(f32[8,8,128]{2,1,0:T(8,128)S(1)} %all-to-all-done.2.refs_0_, f32[8,128]{1,0:T(8,128)S(1)} %get-tuple-element.45.refs_3_.refs_1_, f32[2,18,40,128]{3,2,1,0:T(8,128)} %get-tuple-element.46.refs_2_, ...), custom_call_target="tpu_custom_call" | custom-call | flops 905969664 | bytes 8663040 | tf_op jit(solution)/shard_map/pallas_call | solution.py:65
  50.3 2.1 %collective-permute-done.3.refs_1_ = bf16[3456,128]{1,0:T(8,128)(2,1)S(1)} collective-permute-done((bf16[3456,128]{1,0:T(8,128)(2,1)S(1)}, bf16[3456,128]{1,0:T(8,128)(2,1)S(1)}, u32[]{:S(2)}, u32[]{:S(2)}) %collective-permute-start.3) | collective-permute-done | bytes 884768 | tf_op jit(solution)/shard_map/ppermute | solution.py:698
  53.5 4.2 %all-to-all-start.3 = ((bf16[4,864,128]{2,1,0:T(8,128)(2,1)}), bf16[4,864,128]{2,1,0:T(8,128)(2,1)S(1)}, u32[]{:S(2)}, u32[]{:S(2)}) async-start(bf16[4,864,128]{2,1,0:T(8,128)(2,1)} %shard_map.85), calls=%async_computation.3 | async-start | bytes 1769472 | tf_op jit(solution)/shard_map/all_to_all | solution.py:915
  59.0 5.8 %collective-permute-start.5 = (bf16[1248,128]{1,0:T(8,128)(2,1)S(1)}, bf16[1248,128]{1,0:T(8,128)(2,1)}, u32[]{:S(2)}, u32[]{:S(2)}) collective-permute-start(bf16[1248,128]{1,0:T(8,128)(2,1)S(1)} %get-tuple-element.55.act.far), channel_id=1, source_target_pairs={{0,8},{8,16},{16,24},{1,9},{9,17},{17,25},{2,10},{10,18},{18,26},{... | collective-permute-start | bytes 958472 | tf_op jit(solution)/shard_map/ppermute | solution.py:704
  64.7 5.2 %collective-permute-done.4.after = bf16[1248,128]{1,0:T(8,128)(2,1)} collective-permute-done((bf16[1248,128]{1,0:T(8,128)(2,1)}, bf16[1248,128]{1,0:T(8,128)(2,1)}, u32[]{:S(2)}, u32[]{:S(2)}) %collective-permute-start.4) | collective-permute-done | bytes 319520 | tf_op jit(solution)/shard_map/ppermute | solution.py:704
  70.7 5.8 %all-to-all-start.4 = ((bf16[4,224,128]{2,1,0:T(8,128)(2,1)}), bf16[4,224,128]{2,1,0:T(8,128)(2,1)S(1)}, u32[]{:S(2)}, u32[]{:S(2)}) async-start(bf16[4,224,128]{2,1,0:T(8,128)(2,1)} %shard_map.86), calls=%async_computation.4 | async-start | bytes 458752 | tf_op jit(solution)/shard_map/all_to_all | solution.py:924
  76.6 3.4 %shard_map.87 = bf16[2,16,32,128]{3,2,1,0:T(8,128)(2,1)} custom-call(bf16[1248,128]{1,0:T(8,128)(2,1)} %collective-permute-done.5.near, bf16[1248,128]{1,0:T(8,128)(2,1)S(1)} %get-tuple-element.55.act.far, bf16[3456,128]{1,0:T(8,128)(2,1)S(1)} %bitcast.9, bf16[2,16,32,128]{3,2,1,0:T(8,128)(2,1)S(1)} %copy-done.3), custom_call_target="tpu_custom_call" | custom-call | flops 905969664 | bytes 2048000 | tf_op jit(solution)/shard_map/pallas_call | solution.py:65
  80.0 4.3 %all-to-all-done.4.got = bf16[4,224,128]{2,1,0:T(8,128)(2,1)S(1)} async-done(((bf16[4,224,128]{2,1,0:T(8,128)(2,1)}), bf16[4,224,128]{2,1,0:T(8,128)(2,1)S(1)}, u32[]{:S(2)}, u32[]{:S(2)}) %all-to-all-start.4) | async-done | bytes 229408 | tf_op jit(solution)/shard_map/all_to_all | solution.py:924
  85.0 3.4 %all-to-all-start.5 = ((bf16[4,224,128]{2,1,0:T(8,128)(2,1)}), bf16[4,224,128]{2,1,0:T(8,128)(2,1)S(1)}, u32[]{:S(2)}, u32[]{:S(2)}) async-start(bf16[4,224,128]{2,1,0:T(8,128)(2,1)} %shard_map.89), calls=%async_computation.5 | async-start | bytes 458752 | tf_op jit(solution)/shard_map/all_to_all | solution.py:945
  88.5 2.9 %shard_map.88 = (f32[2,512,128]{2,1,0:T(8,128)S(1)}, f32[8,128]{1,0:T(8,128)S(1)}) custom-call(bf16[1248,128]{1,0:T(8,128)(2,1)S(1)} %copy-done.11, bf16[3456,128]{1,0:T(8,128)(2,1)S(1)} %bitcast.7, bf16[2,16,32,128]{3,2,1,0:T(8,128)(2,1)S(1)} %copy-done.3, f32[8,128]{1,0:T(8,128)S(1)} %get-tuple-element.57.norm, bf16[1248,128]{1,0:T(8,128)(2,1)} %collective-permute-done.4.after), custom_call_target="tpu_custom_call" | custom-call | flops 905969664 | bytes 2318336 | tf_op jit(solution)/shard_map/pallas_call | solution.py:65
  92.6 2.3 %all-to-all-done.5 = bf16[4,224,128]{2,1,0:T(8,128)(2,1)S(1)} async-done(((bf16[4,224,128]{2,1,0:T(8,128)(2,1)}), bf16[4,224,128]{2,1,0:T(8,128)(2,1)S(1)}, u32[]{:S(2)}, u32[]{:S(2)}) %all-to-all-start.5) | async-done | bytes 229408 | tf_op jit(solution)/shard_map/all_to_all | solution.py:945
  95.1 13.5 %all_to_all.36.refs_0_ = bf16[4,896,128]{2,1,0:T(8,128)(2,1)S(1)} all-to-all(bf16[4,896,128]{2,1,0:T(8,128)(2,1)S(1)} %broadcast_in_dim.2), channel_id=1, replica_groups=mesh['tm'=4,'row'=2,'col'=4] {'col'}, dimensions={0} | all-to-all | bytes 1835008 | tf_op jit(solution)/shard_map/all_to_all | solution.py:949
  (52 shorter events, 17.3 us)
Async XLA Ops:
  1.9 1.4 %collective-permute-start = (bf16[224,128]{1,0:T(8,128)(2,1)S(1)}, bf16[224,128]{1,0:T(8,128)(2,1)S(1)}, u32[]{:S(2)}, u32[]{:S(2)}) collective-permute-start(bf16[224,128]{1,0:T(8,128)(2,1)S(1)} %get-tuple-element.37), channel_id=1, source_target_pairs={{0,4},{4,0},{1,5},{5,1},{2,6},{6,2},{3,7},{7,3},{8,12},{12,8},{9,1... | collective-permute-start | bytes 172040 | tf_op jit(solution)/shard_map/ppermute | solution.py:698
  14.5 10.9 %copy-start.2 = (bf16[1248,128]{1,0:T(8,128)(2,1)}, bf16[1248,128]{1,0:T(8,128)(2,1)S(1)}, u32[]{:S(2)}) copy-start(bf16[1248,128]{1,0:T(8,128)(2,1)S(1)} %get-tuple-element.40.own.refs_5_) | copy-start | bytes 958468
  14.5 9.2 %collective-permute-start.1 = (bf16[1248,128]{1,0:T(8,128)(2,1)S(1)}, bf16[1248,128]{1,0:T(8,128)(2,1)S(1)}, u32[]{:S(2)}, u32[]{:S(2)}) collective-permute-start(bf16[1248,128]{1,0:T(8,128)(2,1)S(1)} %get-tuple-element.40.own.refs_5_), channel_id=1, source_target_pairs={{0,8},{8,16},{16,24},{1,9},{9,17},{17,25},{2,10},{10,18},{18,26},{... | collective-permute-start | bytes 958472 | tf_op jit(solution)/shard_map/ppermute | solution.py:704
  18.0 11.5 %collective-permute-start.2 = (bf16[1472,128]{1,0:T(8,128)(2,1)S(1)}, bf16[1472,128]{1,0:T(8,128)(2,1)S(1)}, u32[]{:S(2)}, u32[]{:S(2)}) collective-permute-start(bf16[1472,128]{1,0:T(8,128)(2,1)S(1)} %get-tuple-element.43.near), channel_id=1, source_target_pairs={{8,0},{16,8},{24,16},{9,1},{17,9},{25,17},{10,2},{18,10},{26,18},{... | collective-permute-start | bytes 1130504 | tf_op jit(solution)/shard_map/ppermute | solution.py:704
  19.3 1.2 %copy-start.7 = (bf16[3,3,3,128,128]{4,3,2,1,0:T(8,128)(2,1)S(1)}, bf16[3,3,3,128,128]{4,3,2,1,0:T(8,128)(2,1)}, u32[]{:S(2)}) copy-start(bf16[3,3,3,128,128]{4,3,2,1,0:T(8,128)(2,1)} %param.5) | copy-start | bytes 2654212
  23.6 2.5 %copy-start.9 = (bf16[1248,128]{1,0:T(8,128)(2,1)}, bf16[1248,128]{1,0:T(8,128)(2,1)S(1)}, u32[]{:S(2)}) copy-start(bf16[1248,128]{1,0:T(8,128)(2,1)S(1)} %collective-permute-done.1.refs_0_.refs_4_) | copy-start | bytes 958468
  26.1 9.3 %all-to-all-start.1 = ((bf16[8,96,128]{2,1,0:T(8,128)(2,1)}), bf16[8,96,128]{2,1,0:T(8,128)(2,1)S(1)}, u32[]{:S(2)}, u32[]{:S(2)}) async-start(bf16[8,96,128]{2,1,0:T(8,128)(2,1)} %get-tuple-element.41), calls=%async_computation.1 | async-start | bytes 393216 | tf_op jit(solution)/shard_map/all_to_all | solution.py:848
  29.5 11.3 %copy-start.6 = (bf16[2,16,32,128]{3,2,1,0:T(8,128)(2,1)S(1)}, bf16[2,16,32,128]{3,2,1,0:T(8,128)(2,1)}, u32[]{:S(2)}) copy-start(bf16[2,16,32,128]{3,2,1,0:T(8,128)(2,1)} %copy-done.5) | copy-start | bytes 786436
  33.1 0.9 copy-start
  37.4 8.6 %all-to-all-start.2 = ((f32[8,8,128]{2,1,0:T(8,128)}), f32[8,8,128]{2,1,0:T(8,128)S(1)}, u32[]{:S(2)}, u32[]{:S(2)}) async-start(f32[8,8,128]{2,1,0:T(8,128)} %get-tuple-element.44), calls=%async_computation.2 | async-start | bytes 65536 | tf_op jit(solution)/shard_map/all_to_all | solution.py:878
  40.8 1.1 copy-start.1
  49.9 2.5 %collective-permute-start.3 = (bf16[3456,128]{1,0:T(8,128)(2,1)S(1)}, bf16[3456,128]{1,0:T(8,128)(2,1)S(1)}, u32[]{:S(2)}, u32[]{:S(2)}) collective-permute-start(bf16[3456,128]{1,0:T(8,128)(2,1)S(1)} %get-tuple-element.52), channel_id=1, source_target_pairs={{0,4},{4,0},{1,5},{5,1},{2,6},{6,2},{3,7},{7,3},{8,12},{12,8},{9,1... | collective-permute-start | bytes 2654216 | tf_op jit(solution)/shard_map/ppermute | solution.py:698
  52.3 24.2 %copy-start.3 = (bf16[2,16,32,128]{3,2,1,0:T(8,128)(2,1)S(1)}, bf16[2,16,32,128]{3,2,1,0:T(8,128)(2,1)}, u32[]{:S(2)}) copy-start(bf16[2,16,32,128]{3,2,1,0:T(8,128)(2,1)} %features.5) | copy-start | bytes 786436
  52.3 24.2 %copy-start.10 = (bf16[3,3,3,128,128]{4,3,2,1,0:T(8,128)(2,1)S(1)}, bf16[3,3,3,128,128]{4,3,2,1,0:T(8,128)(2,1)}, u32[]{:S(2)}) copy-start(bf16[3,3,3,128,128]{4,3,2,1,0:T(8,128)(2,1)} %param.6) | copy-start | bytes 2654212
  53.5 35.0 %copy-start.8 = (bf16[3,3,3,128,128]{4,3,2,1,0:T(8,128)(2,1)S(1)}, bf16[3,3,3,128,128]{4,3,2,1,0:T(8,128)(2,1)}, u32[]{:S(2)}) copy-start(bf16[3,3,3,128,128]{4,3,2,1,0:T(8,128)(2,1)} %param.5) | copy-start | bytes 2654212
  53.5 16.5 %all-to-all-start.3 = ((bf16[4,864,128]{2,1,0:T(8,128)(2,1)}), bf16[4,864,128]{2,1,0:T(8,128)(2,1)S(1)}, u32[]{:S(2)}, u32[]{:S(2)}) async-start(bf16[4,864,128]{2,1,0:T(8,128)(2,1)} %shard_map.85), calls=%async_computation.3 | async-start | bytes 1769472 | tf_op jit(solution)/shard_map/all_to_all | solution.py:915
  57.7 12.2 %collective-permute-start.4 = (bf16[1248,128]{1,0:T(8,128)(2,1)}, bf16[1248,128]{1,0:T(8,128)(2,1)}, u32[]{:S(2)}, u32[]{:S(2)}) collective-permute-start(bf16[1248,128]{1,0:T(8,128)(2,1)} %get-tuple-element.53.near), channel_id=1, source_target_pairs={{8,0},{16,8},{24,16},{9,1},{17,9},{25,17},{10,2},{18,10},{26,18},{... | collective-permute-start | bytes 958472 | tf_op jit(solution)/shard_map/ppermute | solution.py:704
  59.0 17.6 %collective-permute-start.5 = (bf16[1248,128]{1,0:T(8,128)(2,1)S(1)}, bf16[1248,128]{1,0:T(8,128)(2,1)}, u32[]{:S(2)}, u32[]{:S(2)}) collective-permute-start(bf16[1248,128]{1,0:T(8,128)(2,1)S(1)} %get-tuple-element.55.act.far), channel_id=1, source_target_pairs={{0,8},{8,16},{16,24},{1,9},{9,17},{17,25},{2,10},{10,18},{18,26},{... | collective-permute-start | bytes 958472 | tf_op jit(solution)/shard_map/ppermute | solution.py:704
  70.7 17.7 %copy-start.11 = (bf16[1248,128]{1,0:T(8,128)(2,1)S(1)}, bf16[1248,128]{1,0:T(8,128)(2,1)}, u32[]{:S(2)}) copy-start(bf16[1248,128]{1,0:T(8,128)(2,1)} %get-tuple-element.53.near) | copy-start | bytes 958468
  70.7 13.6 %all-to-all-start.4 = ((bf16[4,224,128]{2,1,0:T(8,128)(2,1)}), bf16[4,224,128]{2,1,0:T(8,128)(2,1)S(1)}, u32[]{:S(2)}, u32[]{:S(2)}) async-start(bf16[4,224,128]{2,1,0:T(8,128)(2,1)} %shard_map.86), calls=%async_computation.4 | async-start | bytes 458752 | tf_op jit(solution)/shard_map/all_to_all | solution.py:924
  85.0 9.9 %all-to-all-start.5 = ((bf16[4,224,128]{2,1,0:T(8,128)(2,1)}), bf16[4,224,128]{2,1,0:T(8,128)(2,1)S(1)}, u32[]{:S(2)}, u32[]{:S(2)}) async-start(bf16[4,224,128]{2,1,0:T(8,128)(2,1)} %shard_map.89), calls=%async_computation.5 | async-start | bytes 458752 | tf_op jit(solution)/shard_map/all_to_all | solution.py:945
  88.5 20.1 %copy-start.4 = (bf16[2,16,32,128]{3,2,1,0:T(8,128)(2,1)S(1)}, bf16[2,16,32,128]{3,2,1,0:T(8,128)(2,1)}, u32[]{:S(2)}) copy-start(bf16[2,16,32,128]{3,2,1,0:T(8,128)(2,1)} %out_grad.1) | copy-start | bytes 786436
  91.3 1.2 %collective-permute-start.6 = (f32[8,128]{1,0:T(8,128)S(1)}, f32[8,128]{1,0:T(8,128)S(1)}, u32[]{:S(2)}, u32[]{:S(2)}) collective-permute-start(f32[8,128]{1,0:T(8,128)S(1)} %get-tuple-element.61), channel_id=1, source_target_pairs={{0,4},{4,0},{1,5},{5,1},{2,6},{6,2},{3,7},{7,3},{8,12},{12,8},{9,1... | collective-permute-start | bytes 12296 | tf_op jit(solution)/shard_map/ppermute | solution.py:698
  108.5 2.5 %collective-permute-start.7 = (bf16[4,896,128]{2,1,0:T(8,128)(2,1)S(1)}, bf16[4,896,128]{2,1,0:T(8,128)(2,1)S(1)}, u32[]{:S(2)}, u32[]{:S(2)}) collective-permute-start(bf16[4,896,128]{2,1,0:T(8,128)(2,1)S(1)} %all_to_all.36.refs_0_), channel_id=1, source_target_pairs={{0,4},{4,0},{1,5},{5,1},{2,6},{6,2},{3,7},{7,3},{8,12},{12,8},{9,1... | collective-permute-start | bytes 2752520 | tf_op jit(solution)/shard_map/ppermute | solution.py:698
  (1 other events, 0.7 us)

commit v14 on v12

--- a/solution.py
+++ b/solution.py
@@ -648,7 +648,12 @@
         out[f] = total.astype(BF16)
 
 
-def back_first_body(size, near, far, kernel, features, norm, q, sums, x, frame):
+def back_first_body(
+    size, near, kernel, features, norm, after, q, sums, x, frame, far, sems
+):
+    copy = pltpu.make_async_copy(after, far, sems.at[0])
+    copy.start()
+    copy.wait()
     spread_all(size, 1, 1, size.wide, near, far, x, frame)
     grads = convolved(x, kernel, True)
     firsts, seconds = [], []
@@ -913,8 +918,10 @@
     q, sums = call(
         part(back_first_body, size),
         [((FRAMES, size.cells, LANES), F32), stat],
-        [grad_second, grad_second_after, first, features, norm_first],
-        conv_scratch(size, 1, wide),
+        [grad_second, first, features, norm_first, grad_second_after],
+        [*conv_scratch(size, 1, wide), block],
+        far=1,
+        sems=1,
         mib=14,
         flops=work,
     )

time: 110 us -> 111 us (level)
  transfers between devices with their start and end apart: 13 -> 13, of which waited for: 11 -> 11; matrix products, arithmetic and copies ran while one was open for 0% -> 0% of each run, Pallas kernels for 17% -> 18%
where the time goes in v14:
time: 111 us; the launch traced here: 110 us
  starting transfers between devices  32.1 us (29%)
  Pallas kernels  29.1 us (26%)
  blocking collectives  23.8 us (21%)
  waiting for transfers between devices  22.3 us (20%)
  local copies, waits for them, and re-layouts  1.33 us (1%)
    pallas_call x16, Pallas kernels, call(): pl.pallas_call(body, out_shape=shapes[:kept] + [pltpu.HBM(o.shape, o.dtyp...  27.2 us
    all_to_all x1, blocking collectives, on_device(): lax.all_to_all(jnp.broadcast_to(done[None], (across, *done.shape)), 'col'...  13.5 us
    ppermute x4, starting transfers between devices, later(): return lax.ppermute(values, 'tm', pairs)  11.8 us
    all_to_all x1, blocking collectives, on_device(): col_got = lax.all_to_all(slots, 'col', 0, 0)  10.4 us
    ppermute x4, waiting for transfers between devices, later(): return lax.ppermute(values, 'tm', pairs)  8.02 us
    all_to_all x2, starting transfers between devices, on_device(): got = lax.all_to_all(slots, ('row', 'col'), 0, 0)  6.73 us
    all_to_all x1, starting transfers between devices, on_device(): got = lax.all_to_all(slots, 'tm', 0, 0)  5.79 us
    ppermute x4, waiting for transfers between devices, row_swap(): return lax.ppermute(values, 'row', [(0, 1), (1, 0)])  4.9 us
  transfers between devices with their start and end apart: 13, of which 11 were waited for; matrix products, arithmetic and copies ran while one was open for 0% of the time, Pallas kernels for 18%

profile of v14, /device:TPU:0, one launch (start us, length us, event | category | flops | bytes accessed | tf_op | source)
XLA Modules:
  0.0 109.7 jit_solution(11075748073877958182)
XLA Ops:
  3.3 10.4 %all_to_all.35.refs_3_ = bf16[4,176,128]{2,1,0:T(8,128)(2,1)S(1)} all-to-all(bf16[4,176,128]{2,1,0:T(8,128)(2,1)S(1)} %shard_map.76), channel_id=1, replica_groups=mesh['tm'=4,'row'=2,'col'=4] {'col'}, dimensions={0} | all-to-all | bytes 360448 | tf_op jit(solution)/shard_map/all_to_all | solution.py:805
  14.5 3.5 %collective-permute-start.1 = (bf16[1248,128]{1,0:T(8,128)(2,1)S(1)}, bf16[1248,128]{1,0:T(8,128)(2,1)S(1)}, u32[]{:S(2)}, u32[]{:S(2)}) collective-permute-start(bf16[1248,128]{1,0:T(8,128)(2,1)S(1)} %get-tuple-element.40.own.refs_5_), channel_id=1, source_target_pairs={{0,8},{8,16},{16,24},{1,9},{9,17},{17,25},{2,10},{10,18},{18,26},{... | collective-permute-start | bytes 958472 | tf_op jit(solution)/shard_map/ppermute | solution.py:692
  18.0 1.3 %collective-permute-start.2 = (bf16[1472,128]{1,0:T(8,128)(2,1)S(1)}, bf16[1472,128]{1,0:T(8,128)(2,1)S(1)}, u32[]{:S(2)}, u32[]{:S(2)}) collective-permute-start(bf16[1472,128]{1,0:T(8,128)(2,1)S(1)} %get-tuple-element.43.near), channel_id=1, source_target_pairs={{8,0},{16,8},{24,16},{9,1},{17,9},{25,17},{10,2},{18,10},{26,18},{... | collective-permute-start | bytes 1130504 | tf_op jit(solution)/shard_map/ppermute | solution.py:692
  21.3 2.3 %collective-permute-done.1.refs_0_.refs_4_ = bf16[1248,128]{1,0:T(8,128)(2,1)S(1)} collective-permute-done((bf16[1248,128]{1,0:T(8,128)(2,1)S(1)}, bf16[1248,128]{1,0:T(8,128)(2,1)S(1)}, u32[]{:S(2)}, u32[]{:S(2)}) %collective-permute-start.1) | collective-permute-done | bytes 319520 | tf_op jit(solution)/shard_map/ppermute | solution.py:692
  23.6 1.7 %shard_map.79 = (bf16[2,16,32,128]{3,2,1,0:T(8,128)(2,1)S(1)}, bf16[8,96,128]{2,1,0:T(8,128)(2,1)}) custom-call(bf16[1248,128]{1,0:T(8,128)(2,1)S(1)} %collective-permute-done.1.refs_0_.refs_4_, f32[2,512,128]{2,1,0:T(8,128)S(1)} %shard_map.78.refs_1_, bf16[3456,128]{1,0:T(8,128)(2,1)S(1)} %bitcast.6), custom_call_target="tpu_custom_call" | custom-call | flops 1811939328 | bytes 2187264 | tf_op jit(solution)/shard_map/pallas_call | solution.py:65
  25.4 3.4 %all-to-all-start.1 = ((bf16[8,96,128]{2,1,0:T(8,128)(2,1)}), bf16[8,96,128]{2,1,0:T(8,128)(2,1)S(1)}, u32[]{:S(2)}, u32[]{:S(2)}) async-start(bf16[8,96,128]{2,1,0:T(8,128)(2,1)} %get-tuple-element.42), calls=%async_computation.1 | async-start | bytes 393216 | tf_op jit(solution)/shard_map/all_to_all | solution.py:836
  29.0 3.5 %shard_map.80.grad_act.refs_2_ = f32[2,18,40,128]{3,2,1,0:T(8,128)S(1)} custom-call(bf16[1472,128]{1,0:T(8,128)(2,1)S(1)} %get-tuple-element.43.near, bf16[1472,128]{1,0:T(8,128)(2,1)S(1)} %collective-permute-done.2.far, bf16[3456,128]{1,0:T(8,128)(2,1)} %bitcast.8), custom_call_target="tpu_custom_call" | custom-call | flops 1811939328 | bytes 2375680 | tf_op jit(solution)/shard_map/pallas_call | solution.py:65
  32.5 2.1 %all-to-all-done.1.got.refs_1_ = bf16[8,96,128]{2,1,0:T(8,128)(2,1)S(1)} async-done(((bf16[8,96,128]{2,1,0:T(8,128)(2,1)}), bf16[8,96,128]{2,1,0:T(8,128)(2,1)S(1)}, u32[]{:S(2)}, u32[]{:S(2)}) %all-to-all-start.1) | async-done | bytes 196640 | tf_op jit(solution)/shard_map/all_to_all | solution.py:836
  35.9 3.3 %all-to-all-start.2 = ((f32[8,8,128]{2,1,0:T(8,128)}), f32[8,8,128]{2,1,0:T(8,128)S(1)}, u32[]{:S(2)}, u32[]{:S(2)}) async-start(f32[8,8,128]{2,1,0:T(8,128)} %get-tuple-element.44), calls=%async_computation.2 | async-start | bytes 65536 | tf_op jit(solution)/shard_map/all_to_all | solution.py:863
  39.2 1.7 %shard_map.82 = (bf16[1248,128]{1,0:T(8,128)(2,1)S(1)}, f32[2,18,40,128]{3,2,1,0:T(8,128)}, f32[2,18,40,128]{3,2,1,0:T(8,128)}) custom-call(bf16[2,16,32,128]{3,2,1,0:T(8,128)(2,1)S(1)} %get-tuple-element.41.hidden.refs_0_, bf16[8,96,128]{2,1,0:T(8,128)(2,1)S(1)} %all-to-all-done.1.got.refs_1_, f32[2,18,40,128]{3,2,1,0:T(8,128)S(1)} %shard_map.80.grad_act.refs_2_, ...), custom_call_target="tpu_custom_call" | custom-call | tf_op jit(solution)/shard_map/pallas_call | solution.py:65
  40.9 2.5 %shard_map.83.refs_6_ = f32[3456,128]{1,0:T(8,128)} custom-call(bf16[1472,128]{1,0:T(8,128)(2,1)S(1)} %get-tuple-element.43.near, bf16[1472,128]{1,0:T(8,128)(2,1)S(1)} %collective-permute-done.2.far, bf16[1248,128]{1,0:T(8,128)(2,1)S(1)} %get-tuple-element.55.act.far), custom_call_target="tpu_custom_call" | custom-call | tf_op jit(solution)/shard_map/pallas_call | solution.py:65
  44.0 3.8 %shard_map.84 = (f32[2,3456,128]{2,1,0:T(8,128)S(1)}, bf16[3456,128]{1,0:T(8,128)(2,1)S(1)}, bf16[1248,128]{1,0:T(8,128)(2,1)}) custom-call(f32[8,8,128]{2,1,0:T(8,128)S(1)} %all-to-all-done.2.refs_0_, f32[8,128]{1,0:T(8,128)S(1)} %get-tuple-element.45.refs_3_.refs_1_, f32[2,18,40,128]{3,2,1,0:T(8,128)} %get-tuple-element.46.refs_2_, ...), custom_call_target="tpu_custom_call" | custom-call | flops 905969664 | bytes 8663040 | tf_op jit(solution)/shard_map/pallas_call | solution.py:65
  47.9 2.4 %collective-permute-done.3.refs_1_ = bf16[3456,128]{1,0:T(8,128)(2,1)S(1)} collective-permute-done((bf16[3456,128]{1,0:T(8,128)(2,1)S(1)}, bf16[3456,128]{1,0:T(8,128)(2,1)S(1)}, u32[]{:S(2)}, u32[]{:S(2)}) %collective-permute-start.3) | collective-permute-done | bytes 884768 | tf_op jit(solution)/shard_map/ppermute | solution.py:686
  51.4 3.7 %all-to-all-start.3 = ((bf16[4,864,128]{2,1,0:T(8,128)(2,1)}), bf16[4,864,128]{2,1,0:T(8,128)(2,1)S(1)}, u32[]{:S(2)}, u32[]{:S(2)}) async-start(bf16[4,864,128]{2,1,0:T(8,128)(2,1)} %shard_map.85), calls=%async_computation.3 | async-start | bytes 1769472 | tf_op jit(solution)/shard_map/all_to_all | solution.py:900
  55.0 1.3 %collective-permute-start.4 = (bf16[1248,128]{1,0:T(8,128)(2,1)}, bf16[1248,128]{1,0:T(8,128)(2,1)}, u32[]{:S(2)}, u32[]{:S(2)}) collective-permute-start(bf16[1248,128]{1,0:T(8,128)(2,1)} %get-tuple-element.53.near), channel_id=1, source_target_pairs={{8,0},{16,8},{24,16},{9,1},{17,9},{25,17},{10,2},{18,10},{26,18},{... | collective-permute-start | bytes 958472 | tf_op jit(solution)/shard_map/ppermute | solution.py:692
  56.3 5.7 %collective-permute-start.5 = (bf16[1248,128]{1,0:T(8,128)(2,1)S(1)}, bf16[1248,128]{1,0:T(8,128)(2,1)}, u32[]{:S(2)}, u32[]{:S(2)}) collective-permute-start(bf16[1248,128]{1,0:T(8,128)(2,1)S(1)} %get-tuple-element.55.act.far), channel_id=1, source_target_pairs={{0,8},{8,16},{16,24},{1,9},{9,17},{17,25},{2,10},{10,18},{18,26},{... | collective-permute-start | bytes 958472 | tf_op jit(solution)/shard_map/ppermute | solution.py:692
  62.1 5.5 %collective-permute-done.4.after = bf16[1248,128]{1,0:T(8,128)(2,1)} collective-permute-done((bf16[1248,128]{1,0:T(8,128)(2,1)}, bf16[1248,128]{1,0:T(8,128)(2,1)}, u32[]{:S(2)}, u32[]{:S(2)}) %collective-permute-start.4) | collective-permute-done | bytes 319520 | tf_op jit(solution)/shard_map/ppermute | solution.py:692
  68.3 5.8 %all-to-all-start.4 = ((bf16[4,224,128]{2,1,0:T(8,128)(2,1)}), bf16[4,224,128]{2,1,0:T(8,128)(2,1)S(1)}, u32[]{:S(2)}, u32[]{:S(2)}) async-start(bf16[4,224,128]{2,1,0:T(8,128)(2,1)} %shard_map.86), calls=%async_computation.4 | async-start | bytes 458752 | tf_op jit(solution)/shard_map/all_to_all | solution.py:909
  74.2 3.4 %shard_map.87 = bf16[2,16,32,128]{3,2,1,0:T(8,128)(2,1)} custom-call(bf16[1248,128]{1,0:T(8,128)(2,1)} %collective-permute-done.5.near, bf16[1248,128]{1,0:T(8,128)(2,1)S(1)} %get-tuple-element.55.act.far, bf16[3456,128]{1,0:T(8,128)(2,1)S(1)} %bitcast.9, bf16[2,16,32,128]{3,2,1,0:T(8,128)(2,1)S(1)} %copy-done.1), custom_call_target="tpu_custom_call" | custom-call | flops 905969664 | bytes 2048000 | tf_op jit(solution)/shard_map/pallas_call | solution.py:65
  77.6 4.3 %all-to-all-done.4.got = bf16[4,224,128]{2,1,0:T(8,128)(2,1)S(1)} async-done(((bf16[4,224,128]{2,1,0:T(8,128)(2,1)}), bf16[4,224,128]{2,1,0:T(8,128)(2,1)S(1)}, u32[]{:S(2)}, u32[]{:S(2)}) %all-to-all-start.4) | async-done | bytes 229408 | tf_op jit(solution)/shard_map/all_to_all | solution.py:909
  82.6 3.4 %all-to-all-start.5 = ((bf16[4,224,128]{2,1,0:T(8,128)(2,1)}), bf16[4,224,128]{2,1,0:T(8,128)(2,1)S(1)}, u32[]{:S(2)}, u32[]{:S(2)}) async-start(bf16[4,224,128]{2,1,0:T(8,128)(2,1)} %shard_map.89), calls=%async_computation.5 | async-start | bytes 458752 | tf_op jit(solution)/shard_map/all_to_all | solution.py:930
  86.0 2.9 %shard_map.88 = (f32[2,512,128]{2,1,0:T(8,128)S(1)}, f32[8,128]{1,0:T(8,128)S(1)}) custom-call(bf16[1248,128]{1,0:T(8,128)(2,1)S(1)} %copy-done.7, bf16[3456,128]{1,0:T(8,128)(2,1)S(1)} %bitcast.7, bf16[2,16,32,128]{3,2,1,0:T(8,128)(2,1)S(1)} %copy-done.1, f32[8,128]{1,0:T(8,128)S(1)} %get-tuple-element.57.norm, bf16[1248,128]{1,0:T(8,128)(2,1)} %collective-permute-done.4.after), custom_call_target="tpu_custom_call" | custom-call | flops 905969664 | bytes 2318336 | tf_op jit(solution)/shard_map/pallas_call | solution.py:65
  90.1 2.3 %all-to-all-done.5 = bf16[4,224,128]{2,1,0:T(8,128)(2,1)S(1)} async-done(((bf16[4,224,128]{2,1,0:T(8,128)(2,1)}), bf16[4,224,128]{2,1,0:T(8,128)(2,1)S(1)}, u32[]{:S(2)}, u32[]{:S(2)}) %all-to-all-start.5) | async-done | bytes 229408 | tf_op jit(solution)/shard_map/all_to_all | solution.py:930
  92.6 13.5 %all_to_all.36.refs_0_ = bf16[4,896,128]{2,1,0:T(8,128)(2,1)S(1)} all-to-all(bf16[4,896,128]{2,1,0:T(8,128)(2,1)S(1)} %broadcast_in_dim.2), channel_id=1, replica_groups=mesh['tm'=4,'row'=2,'col'=4] {'col'}, dimensions={0} | all-to-all | bytes 1835008 | tf_op jit(solution)/shard_map/all_to_all | solution.py:934
  (44 shorter events, 15.0 us)
Async XLA Ops:
  1.9 1.4 %collective-permute-start = (bf16[224,128]{1,0:T(8,128)(2,1)S(1)}, bf16[224,128]{1,0:T(8,128)(2,1)S(1)}, u32[]{:S(2)}, u32[]{:S(2)}) collective-permute-start(bf16[224,128]{1,0:T(8,128)(2,1)S(1)} %get-tuple-element.37), channel_id=1, source_target_pairs={{0,4},{4,0},{1,5},{5,1},{2,6},{6,2},{3,7},{7,3},{8,12},{12,8},{9,1... | collective-permute-start | bytes 172040 | tf_op jit(solution)/shard_map/ppermute | solution.py:686
  14.5 10.9 %copy-start = (bf16[1248,128]{1,0:T(8,128)(2,1)}, bf16[1248,128]{1,0:T(8,128)(2,1)S(1)}, u32[]{:S(2)}) copy-start(bf16[1248,128]{1,0:T(8,128)(2,1)S(1)} %get-tuple-element.40.own.refs_5_) | copy-start | bytes 958468
  14.5 9.2 %collective-permute-start.1 = (bf16[1248,128]{1,0:T(8,128)(2,1)S(1)}, bf16[1248,128]{1,0:T(8,128)(2,1)S(1)}, u32[]{:S(2)}, u32[]{:S(2)}) collective-permute-start(bf16[1248,128]{1,0:T(8,128)(2,1)S(1)} %get-tuple-element.40.own.refs_5_), channel_id=1, source_target_pairs={{0,8},{8,16},{16,24},{1,9},{9,17},{17,25},{2,10},{10,18},{18,26},{... | collective-permute-start | bytes 958472 | tf_op jit(solution)/shard_map/ppermute | solution.py:692
  18.0 11.0 %collective-permute-start.2 = (bf16[1472,128]{1,0:T(8,128)(2,1)S(1)}, bf16[1472,128]{1,0:T(8,128)(2,1)S(1)}, u32[]{:S(2)}, u32[]{:S(2)}) collective-permute-start(bf16[1472,128]{1,0:T(8,128)(2,1)S(1)} %get-tuple-element.43.near), channel_id=1, source_target_pairs={{8,0},{16,8},{24,16},{9,1},{17,9},{25,17},{10,2},{18,10},{26,18},{... | collective-permute-start | bytes 1130504 | tf_op jit(solution)/shard_map/ppermute | solution.py:692
  19.3 1.2 %copy-start.3 = (bf16[3,3,3,128,128]{4,3,2,1,0:T(8,128)(2,1)S(1)}, bf16[3,3,3,128,128]{4,3,2,1,0:T(8,128)(2,1)}, u32[]{:S(2)}) copy-start(bf16[3,3,3,128,128]{4,3,2,1,0:T(8,128)(2,1)} %param.5) | copy-start | bytes 2654212
  23.6 1.7 %copy-start.5 = (bf16[1248,128]{1,0:T(8,128)(2,1)}, bf16[1248,128]{1,0:T(8,128)(2,1)S(1)}, u32[]{:S(2)}) copy-start(bf16[1248,128]{1,0:T(8,128)(2,1)S(1)} %collective-permute-done.1.refs_0_.refs_4_) | copy-start | bytes 958468
  25.4 9.3 %all-to-all-start.1 = ((bf16[8,96,128]{2,1,0:T(8,128)(2,1)}), bf16[8,96,128]{2,1,0:T(8,128)(2,1)S(1)}, u32[]{:S(2)}, u32[]{:S(2)}) async-start(bf16[8,96,128]{2,1,0:T(8,128)(2,1)} %get-tuple-element.42), calls=%async_computation.1 | async-start | bytes 393216 | tf_op jit(solution)/shard_map/all_to_all | solution.py:836
  35.9 8.1 %all-to-all-start.2 = ((f32[8,8,128]{2,1,0:T(8,128)}), f32[8,8,128]{2,1,0:T(8,128)S(1)}, u32[]{:S(2)}, u32[]{:S(2)}) async-start(f32[8,8,128]{2,1,0:T(8,128)} %get-tuple-element.44), calls=%async_computation.2 | async-start | bytes 65536 | tf_op jit(solution)/shard_map/all_to_all | solution.py:863
  47.7 2.5 %collective-permute-start.3 = (bf16[3456,128]{1,0:T(8,128)(2,1)S(1)}, bf16[3456,128]{1,0:T(8,128)(2,1)S(1)}, u32[]{:S(2)}, u32[]{:S(2)}) collective-permute-start(bf16[3456,128]{1,0:T(8,128)(2,1)S(1)} %get-tuple-element.52), channel_id=1, source_target_pairs={{0,4},{4,0},{1,5},{5,1},{2,6},{6,2},{3,7},{7,3},{8,12},{12,8},{9,1... | collective-permute-start | bytes 2654216 | tf_op jit(solution)/shard_map/ppermute | solution.py:686
  50.2 23.9 %copy-start.1 = (bf16[2,16,32,128]{3,2,1,0:T(8,128)(2,1)S(1)}, bf16[2,16,32,128]{3,2,1,0:T(8,128)(2,1)}, u32[]{:S(2)}) copy-start(bf16[2,16,32,128]{3,2,1,0:T(8,128)(2,1)} %features.5) | copy-start | bytes 786436
  50.2 23.9 %copy-start.6 = (bf16[3,3,3,128,128]{4,3,2,1,0:T(8,128)(2,1)S(1)}, bf16[3,3,3,128,128]{4,3,2,1,0:T(8,128)(2,1)}, u32[]{:S(2)}) copy-start(bf16[3,3,3,128,128]{4,3,2,1,0:T(8,128)(2,1)} %param.6) | copy-start | bytes 2654212
  51.4 34.6 %copy-start.4 = (bf16[3,3,3,128,128]{4,3,2,1,0:T(8,128)(2,1)S(1)}, bf16[3,3,3,128,128]{4,3,2,1,0:T(8,128)(2,1)}, u32[]{:S(2)}) copy-start(bf16[3,3,3,128,128]{4,3,2,1,0:T(8,128)(2,1)} %param.5) | copy-start | bytes 2654212
  51.4 16.2 %all-to-all-start.3 = ((bf16[4,864,128]{2,1,0:T(8,128)(2,1)}), bf16[4,864,128]{2,1,0:T(8,128)(2,1)S(1)}, u32[]{:S(2)}, u32[]{:S(2)}) async-start(bf16[4,864,128]{2,1,0:T(8,128)(2,1)} %shard_map.85), calls=%async_computation.3 | async-start | bytes 1769472 | tf_op jit(solution)/shard_map/all_to_all | solution.py:900
  55.0 12.5 %collective-permute-start.4 = (bf16[1248,128]{1,0:T(8,128)(2,1)}, bf16[1248,128]{1,0:T(8,128)(2,1)}, u32[]{:S(2)}, u32[]{:S(2)}) collective-permute-start(bf16[1248,128]{1,0:T(8,128)(2,1)} %get-tuple-element.53.near), channel_id=1, source_target_pairs={{8,0},{16,8},{24,16},{9,1},{17,9},{25,17},{10,2},{18,10},{26,18},{... | collective-permute-start | bytes 958472 | tf_op jit(solution)/shard_map/ppermute | solution.py:692
  56.3 17.8 %collective-permute-start.5 = (bf16[1248,128]{1,0:T(8,128)(2,1)S(1)}, bf16[1248,128]{1,0:T(8,128)(2,1)}, u32[]{:S(2)}, u32[]{:S(2)}) collective-permute-start(bf16[1248,128]{1,0:T(8,128)(2,1)S(1)} %get-tuple-element.55.act.far), channel_id=1, source_target_pairs={{0,8},{8,16},{16,24},{1,9},{9,17},{17,25},{2,10},{10,18},{18,26},{... | collective-permute-start | bytes 958472 | tf_op jit(solution)/shard_map/ppermute | solution.py:692
  68.3 17.7 %copy-start.7 = (bf16[1248,128]{1,0:T(8,128)(2,1)S(1)}, bf16[1248,128]{1,0:T(8,128)(2,1)}, u32[]{:S(2)}) copy-start(bf16[1248,128]{1,0:T(8,128)(2,1)} %get-tuple-element.53.near) | copy-start | bytes 958468
  68.3 13.5 %all-to-all-start.4 = ((bf16[4,224,128]{2,1,0:T(8,128)(2,1)}), bf16[4,224,128]{2,1,0:T(8,128)(2,1)S(1)}, u32[]{:S(2)}, u32[]{:S(2)}) async-start(bf16[4,224,128]{2,1,0:T(8,128)(2,1)} %shard_map.86), calls=%async_computation.4 | async-start | bytes 458752 | tf_op jit(solution)/shard_map/all_to_all | solution.py:909
  82.6 9.9 %all-to-all-start.5 = ((bf16[4,224,128]{2,1,0:T(8,128)(2,1)}), bf16[4,224,128]{2,1,0:T(8,128)(2,1)S(1)}, u32[]{:S(2)}, u32[]{:S(2)}) async-start(bf16[4,224,128]{2,1,0:T(8,128)(2,1)} %shard_map.89), calls=%async_computation.5 | async-start | bytes 458752 | tf_op jit(solution)/shard_map/all_to_all | solution.py:930
  86.0 20.1 %copy-start.2 = (bf16[2,16,32,128]{3,2,1,0:T(8,128)(2,1)S(1)}, bf16[2,16,32,128]{3,2,1,0:T(8,128)(2,1)}, u32[]{:S(2)}) copy-start(bf16[2,16,32,128]{3,2,1,0:T(8,128)(2,1)} %out_grad.1) | copy-start | bytes 786436
  88.9 1.2 %collective-permute-start.6 = (f32[8,128]{1,0:T(8,128)S(1)}, f32[8,128]{1,0:T(8,128)S(1)}, u32[]{:S(2)}, u32[]{:S(2)}) collective-permute-start(f32[8,128]{1,0:T(8,128)S(1)} %get-tuple-element.61), channel_id=1, source_target_pairs={{0,4},{4,0},{1,5},{5,1},{2,6},{6,2},{3,7},{7,3},{8,12},{12,8},{9,1... | collective-permute-start | bytes 12296 | tf_op jit(solution)/shard_map/ppermute | solution.py:686
  106.1 2.5 %collective-permute-start.7 = (bf16[4,896,128]{2,1,0:T(8,128)(2,1)S(1)}, bf16[4,896,128]{2,1,0:T(8,128)(2,1)S(1)}, u32[]{:S(2)}, u32[]{:S(2)}) collective-permute-start(bf16[4,896,128]{2,1,0:T(8,128)(2,1)S(1)} %all_to_all.36.refs_0_), channel_id=1, source_target_pairs={{0,4},{4,0},{1,5},{5,1},{2,6},{6,2},{3,7},{7,3},{8,12},{12,8},{9,1... | collective-permute-start | bytes 2752520 | tf_op jit(solution)/shard_map/ppermute | solution.py:686

commit v15 on v12

--- a/solution.py
+++ b/solution.py
@@ -893,7 +893,6 @@
         placed=True,
     )
     slots = lax.all_to_all(slots, "col", 0, 0)
-    slots, grad_second_after = lax.optimization_barrier((slots, grad_second_after))
     share = up(by_col, 16 * along) // along
     (slots,) = call(
         shared_body,
@@ -918,7 +917,7 @@
         mib=14,
         flops=work,
     )
-    got, result = lax.optimization_barrier((got, result))
+    got, result, q = lax.optimization_barrier((got, result, q))
     (slots,) = call(part(finished_body, factor), [((along, share, LANES), BF16)], [got])
     done = lax.all_to_all(slots, "tm", 0, 0).reshape(-1, LANES)[:by_col]
     parts = sum_parts(sums + row_swap(sums))

time: 110 us -> 110 us (level)
    all_to_all x1, waiting for transfers between devices: 0.01 us -> 5.98 us  [on_device(): slots = lax.all_to_all(slots, 'col', 0, 0)]
    ppermute x4, waiting for transfers between devices: 7.92 us -> 2.57 us  [later(): return lax.ppermute(values, 'tm', pairs)]
    all_to_all x1, waiting for transfers between devices: 4.3 us -> 1.46 us  [on_device(): got = lax.all_to_all(slots, 'tm', 0, 0)]
    all_to_all x1, waiting for transfers between devices: 3.33 us -> 5.52 us  [on_device(): done = lax.all_to_all(slots, 'tm', 0, 0).reshape(-1, LANES)[:by_col]]
  transfers between devices with their start and end apart: 13 -> 13, of which waited for: 11 -> 11; matrix products, arithmetic and copies ran while one was open for 0% -> 0% of each run, Pallas kernels for 17% -> 18%
where the time goes in v15:
time: 110 us; the launch traced here: 109 us
  starting transfers between devices  31.8 us (29%)
  Pallas kernels  29.1 us (26%)
  waiting for transfers between devices  23.1 us (21%)
  blocking collectives  23.1 us (21%)
  local copies, waits for them, and re-layouts  1.33 us (1%)
    pallas_call x16, Pallas kernels, call(): pl.pallas_call(body, out_shape=shapes[:kept] + [pltpu.HBM(o.shape, o.dtyp...  27.2 us
    all_to_all x1, blocking collectives, on_device(): lax.all_to_all(jnp.broadcast_to(done[None], (across, *done.shape)), 'col'...  12.7 us
    ppermute x4, starting transfers between devices, later(): return lax.ppermute(values, 'tm', pairs)  11.2 us
    all_to_all x1, blocking collectives, on_device(): col_got = lax.all_to_all(slots, 'col', 0, 0)  10.4 us
    all_to_all x2, starting transfers between devices, on_device(): got = lax.all_to_all(slots, ('row', 'col'), 0, 0)  6.73 us
    all_to_all x1, waiting for transfers between devices, on_device(): slots = lax.all_to_all(slots, 'col', 0, 0)  5.98 us
    all_to_all x1, starting transfers between devices, on_device(): got = lax.all_to_all(slots, 'tm', 0, 0)  5.91 us
    all_to_all x1, waiting for transfers between devices, on_device(): done = lax.all_to_all(slots, 'tm', 0, 0).reshape(-1, LANES)[:by_col]  5.52 us
  transfers between devices with their start and end apart: 13, of which 11 were waited for; matrix products, arithmetic and copies ran while one was open for 0% of the time, Pallas kernels for 18%

profile of v15, /device:TPU:0, one launch (start us, length us, event | category | flops | bytes accessed | tf_op | source)
XLA Modules:
  0.0 109.4 jit_solution(1619389287690794051)
XLA Ops:
  3.3 10.4 %all_to_all.35.refs_3_ = bf16[4,176,128]{2,1,0:T(8,128)(2,1)S(1)} all-to-all(bf16[4,176,128]{2,1,0:T(8,128)(2,1)S(1)} %shard_map.76), channel_id=1, replica_groups=mesh['tm'=4,'row'=2,'col'=4] {'col'}, dimensions={0} | all-to-all | bytes 360448 | tf_op jit(solution)/shard_map/all_to_all | solution.py:800
  14.5 3.5 %collective-permute-start.1 = (bf16[1248,128]{1,0:T(8,128)(2,1)S(1)}, bf16[1248,128]{1,0:T(8,128)(2,1)S(1)}, u32[]{:S(2)}, u32[]{:S(2)}) collective-permute-start(bf16[1248,128]{1,0:T(8,128)(2,1)S(1)} %get-tuple-element.39.own.refs_5_), channel_id=1, source_target_pairs={{0,8},{8,16},{16,24},{1,9},{9,17},{17,25},{2,10},{10,18},{18,26},{... | collective-permute-start | bytes 958472 | tf_op jit(solution)/shard_map/ppermute | solution.py:687
  18.0 1.3 %collective-permute-start.2 = (bf16[1472,128]{1,0:T(8,128)(2,1)S(1)}, bf16[1472,128]{1,0:T(8,128)(2,1)S(1)}, u32[]{:S(2)}, u32[]{:S(2)}) collective-permute-start(bf16[1472,128]{1,0:T(8,128)(2,1)S(1)} %get-tuple-element.42.near), channel_id=1, source_target_pairs={{8,0},{16,8},{24,16},{9,1},{17,9},{25,17},{10,2},{18,10},{26,18},{... | collective-permute-start | bytes 1130504 | tf_op jit(solution)/shard_map/ppermute | solution.py:687
  21.3 2.3 %collective-permute-done.1.refs_0_.refs_4_ = bf16[1248,128]{1,0:T(8,128)(2,1)S(1)} collective-permute-done((bf16[1248,128]{1,0:T(8,128)(2,1)S(1)}, bf16[1248,128]{1,0:T(8,128)(2,1)S(1)}, u32[]{:S(2)}, u32[]{:S(2)}) %collective-permute-start.1) | collective-permute-done | bytes 319520 | tf_op jit(solution)/shard_map/ppermute | solution.py:687
  23.6 1.7 %shard_map.79 = (bf16[2,16,32,128]{3,2,1,0:T(8,128)(2,1)S(1)}, bf16[8,96,128]{2,1,0:T(8,128)(2,1)}) custom-call(bf16[1248,128]{1,0:T(8,128)(2,1)S(1)} %collective-permute-done.1.refs_0_.refs_4_, f32[2,512,128]{2,1,0:T(8,128)S(1)} %shard_map.78.refs_1_, bf16[3456,128]{1,0:T(8,128)(2,1)S(1)} %bitcast.6), custom_call_target="tpu_custom_call" | custom-call | flops 1811939328 | bytes 2187264 | tf_op jit(solution)/shard_map/pallas_call | solution.py:65
  25.4 3.4 %all-to-all-start.1 = ((bf16[8,96,128]{2,1,0:T(8,128)(2,1)}), bf16[8,96,128]{2,1,0:T(8,128)(2,1)S(1)}, u32[]{:S(2)}, u32[]{:S(2)}) async-start(bf16[8,96,128]{2,1,0:T(8,128)(2,1)} %get-tuple-element.41), calls=%async_computation.1 | async-start | bytes 393216 | tf_op jit(solution)/shard_map/all_to_all | solution.py:831
  29.0 3.5 %shard_map.80.grad_act.refs_2_ = f32[2,18,40,128]{3,2,1,0:T(8,128)S(1)} custom-call(bf16[1472,128]{1,0:T(8,128)(2,1)S(1)} %get-tuple-element.42.near, bf16[1472,128]{1,0:T(8,128)(2,1)S(1)} %collective-permute-done.2.far, bf16[3456,128]{1,0:T(8,128)(2,1)} %bitcast.8), custom_call_target="tpu_custom_call" | custom-call | flops 1811939328 | bytes 2375680 | tf_op jit(solution)/shard_map/pallas_call | solution.py:65
  32.5 2.1 %all-to-all-done.1.got.refs_1_ = bf16[8,96,128]{2,1,0:T(8,128)(2,1)S(1)} async-done(((bf16[8,96,128]{2,1,0:T(8,128)(2,1)}), bf16[8,96,128]{2,1,0:T(8,128)(2,1)S(1)}, u32[]{:S(2)}, u32[]{:S(2)}) %all-to-all-start.1) | async-done | bytes 196640 | tf_op jit(solution)/shard_map/all_to_all | solution.py:831
  35.9 3.3 %all-to-all-start.2 = ((f32[8,8,128]{2,1,0:T(8,128)}), f32[8,8,128]{2,1,0:T(8,128)S(1)}, u32[]{:S(2)}, u32[]{:S(2)}) async-start(f32[8,8,128]{2,1,0:T(8,128)} %get-tuple-element.43), calls=%async_computation.2 | async-start | bytes 65536 | tf_op jit(solution)/shard_map/all_to_all | solution.py:858
  39.2 1.7 %shard_map.82 = (bf16[1248,128]{1,0:T(8,128)(2,1)S(1)}, f32[2,18,40,128]{3,2,1,0:T(8,128)}, f32[2,18,40,128]{3,2,1,0:T(8,128)}) custom-call(bf16[2,16,32,128]{3,2,1,0:T(8,128)(2,1)S(1)} %get-tuple-element.40.hidden.refs_0_, bf16[8,96,128]{2,1,0:T(8,128)(2,1)S(1)} %all-to-all-done.1.got.refs_1_, f32[2,18,40,128]{3,2,1,0:T(8,128)S(1)} %shard_map.80.grad_act.refs_2_, ...), custom_call_target="tpu_custom_call" | custom-call | tf_op jit(solution)/shard_map/pallas_call | solution.py:65
  40.9 2.5 %shard_map.83.refs_6_ = f32[3456,128]{1,0:T(8,128)} custom-call(bf16[1472,128]{1,0:T(8,128)(2,1)S(1)} %get-tuple-element.42.near, bf16[1472,128]{1,0:T(8,128)(2,1)S(1)} %collective-permute-done.2.far, bf16[1248,128]{1,0:T(8,128)(2,1)S(1)} %get-tuple-element.52.act.far), custom_call_target="tpu_custom_call" | custom-call | tf_op jit(solution)/shard_map/pallas_call | solution.py:65
  43.9 3.8 %shard_map.84 = (f32[2,3456,128]{2,1,0:T(8,128)S(1)}, bf16[3456,128]{1,0:T(8,128)(2,1)S(1)}, bf16[1248,128]{1,0:T(8,128)(2,1)}) custom-call(f32[8,8,128]{2,1,0:T(8,128)S(1)} %all-to-all-done.2.refs_0_, f32[8,128]{1,0:T(8,128)S(1)} %get-tuple-element.44.refs_3_.refs_1_, f32[2,18,40,128]{3,2,1,0:T(8,128)} %get-tuple-element.45.refs_2_, ...), custom_call_target="tpu_custom_call" | custom-call | flops 905969664 | bytes 8663040 | tf_op jit(solution)/shard_map/pallas_call | solution.py:65
  47.9 2.4 %collective-permute-done.3.refs_1_ = bf16[3456,128]{1,0:T(8,128)(2,1)S(1)} collective-permute-done((bf16[3456,128]{1,0:T(8,128)(2,1)S(1)}, bf16[3456,128]{1,0:T(8,128)(2,1)S(1)}, u32[]{:S(2)}, u32[]{:S(2)}) %collective-permute-start.3) | collective-permute-done | bytes 884768 | tf_op jit(solution)/shard_map/ppermute | solution.py:681
  51.4 3.7 %all-to-all-start.3 = ((bf16[4,864,128]{2,1,0:T(8,128)(2,1)}), bf16[4,864,128]{2,1,0:T(8,128)(2,1)S(1)}, u32[]{:S(2)}, u32[]{:S(2)}) async-start(bf16[4,864,128]{2,1,0:T(8,128)(2,1)} %shard_map.85), calls=%async_computation.3 | async-start | bytes 1769472 | tf_op jit(solution)/shard_map/all_to_all | solution.py:895
  55.0 5.1 %collective-permute-start.4 = (bf16[1248,128]{1,0:T(8,128)(2,1)S(1)}, bf16[1248,128]{1,0:T(8,128)(2,1)}, u32[]{:S(2)}, u32[]{:S(2)}) collective-permute-start(bf16[1248,128]{1,0:T(8,128)(2,1)S(1)} %get-tuple-element.52.act.far), channel_id=1, source_target_pairs={{0,8},{8,16},{16,24},{1,9},{9,17},{17,25},{2,10},{10,18},{18,26},{... | collective-permute-start | bytes 958472 | tf_op jit(solution)/shard_map/ppermute | solution.py:687
  60.2 1.3 %collective-permute-start.5 = (bf16[1248,128]{1,0:T(8,128)(2,1)}, bf16[1248,128]{1,0:T(8,128)(2,1)}, u32[]{:S(2)}, u32[]{:S(2)}) collective-permute-start(bf16[1248,128]{1,0:T(8,128)(2,1)} %get-tuple-element.53.near), channel_id=1, source_target_pairs={{8,0},{16,8},{24,16},{9,1},{17,9},{25,17},{10,2},{18,10},{26,18},{... | collective-permute-start | bytes 958472 | tf_op jit(solution)/shard_map/ppermute | solution.py:687
  61.4 6.0 %all-to-all-done.3.got = bf16[4,864,128]{2,1,0:T(8,128)(2,1)S(1)} async-done(((bf16[4,864,128]{2,1,0:T(8,128)(2,1)}), bf16[4,864,128]{2,1,0:T(8,128)(2,1)S(1)}, u32[]{:S(2)}, u32[]{:S(2)}) %all-to-all-start.3) | async-done | bytes 884768 | tf_op jit(solution)/shard_map/all_to_all | solution.py:895
  68.2 5.9 %all-to-all-start.4 = ((bf16[4,224,128]{2,1,0:T(8,128)(2,1)}), bf16[4,224,128]{2,1,0:T(8,128)(2,1)S(1)}, u32[]{:S(2)}, u32[]{:S(2)}) async-start(bf16[4,224,128]{2,1,0:T(8,128)(2,1)} %shard_map.86), calls=%async_computation.4 | async-start | bytes 458752 | tf_op jit(solution)/shard_map/all_to_all | solution.py:903
  74.2 3.4 %shard_map.87 = bf16[2,16,32,128]{3,2,1,0:T(8,128)(2,1)} custom-call(bf16[1248,128]{1,0:T(8,128)(2,1)} %collective-permute-done.4.near, bf16[1248,128]{1,0:T(8,128)(2,1)S(1)} %get-tuple-element.52.act.far, bf16[3456,128]{1,0:T(8,128)(2,1)S(1)} %bitcast.9, bf16[2,16,32,128]{3,2,1,0:T(8,128)(2,1)S(1)} %copy-done.1), custom_call_target="tpu_custom_call" | custom-call | flops 905969664 | bytes 2048000 | tf_op jit(solution)/shard_map/pallas_call | solution.py:65
  77.6 2.8 %shard_map.88 = (f32[2,512,128]{2,1,0:T(8,128)S(1)}, f32[8,128]{1,0:T(8,128)S(1)}) custom-call(bf16[1248,128]{1,0:T(8,128)(2,1)S(1)} %copy-done.7, bf16[1248,128]{1,0:T(8,128)(2,1)} %collective-permute-done.5.far, bf16[3456,128]{1,0:T(8,128)(2,1)S(1)} %bitcast.7, bf16[2,16,32,128]{3,2,1,0:T(8,128)(2,1)S(1)} %copy-done.1, f32[8,128]{1,0:T(8,128)S(1)} %get-tuple-element.54.norm), custom_call_target="tpu_custom_call" | custom-call | flops 905969664 | bytes 2318336 | tf_op jit(solution)/shard_map/pallas_call | solution.py:65
  80.4 1.5 %all-to-all-done.4.got = bf16[4,224,128]{2,1,0:T(8,128)(2,1)S(1)} async-done(((bf16[4,224,128]{2,1,0:T(8,128)(2,1)}), bf16[4,224,128]{2,1,0:T(8,128)(2,1)S(1)}, u32[]{:S(2)}, u32[]{:S(2)}) %all-to-all-start.4) | async-done | bytes 229408 | tf_op jit(solution)/shard_map/all_to_all | solution.py:903
  82.6 3.6 %all-to-all-start.5 = ((bf16[4,224,128]{2,1,0:T(8,128)(2,1)}), bf16[4,224,128]{2,1,0:T(8,128)(2,1)S(1)}, u32[]{:S(2)}, u32[]{:S(2)}) async-start(bf16[4,224,128]{2,1,0:T(8,128)(2,1)} %shard_map.89), calls=%async_computation.5 | async-start | bytes 458752 | tf_op jit(solution)/shard_map/all_to_all | solution.py:922
  87.4 5.5 %all-to-all-done.5 = bf16[4,224,128]{2,1,0:T(8,128)(2,1)S(1)} async-done(((bf16[4,224,128]{2,1,0:T(8,128)(2,1)}), bf16[4,224,128]{2,1,0:T(8,128)(2,1)S(1)}, u32[]{:S(2)}, u32[]{:S(2)}) %all-to-all-start.5) | async-done | bytes 229408 | tf_op jit(solution)/shard_map/all_to_all | solution.py:922
  93.1 12.7 %all_to_all.36.refs_0_ = bf16[4,896,128]{2,1,0:T(8,128)(2,1)S(1)} all-to-all(bf16[4,896,128]{2,1,0:T(8,128)(2,1)S(1)} %broadcast_in_dim.2), channel_id=1, replica_groups=mesh['tm'=4,'row'=2,'col'=4] {'col'}, dimensions={0} | all-to-all | bytes 1835008 | tf_op jit(solution)/shard_map/all_to_all | solution.py:926
  (44 shorter events, 15.0 us)
Async XLA Ops:
  1.9 1.4 %collective-permute-start = (bf16[224,128]{1,0:T(8,128)(2,1)S(1)}, bf16[224,128]{1,0:T(8,128)(2,1)S(1)}, u32[]{:S(2)}, u32[]{:S(2)}) collective-permute-start(bf16[224,128]{1,0:T(8,128)(2,1)S(1)} %get-tuple-element.36), channel_id=1, source_target_pairs={{0,4},{4,0},{1,5},{5,1},{2,6},{6,2},{3,7},{7,3},{8,12},{12,8},{9,1... | collective-permute-start | bytes 172040 | tf_op jit(solution)/shard_map/ppermute | solution.py:681
  14.5 10.9 %copy-start = (bf16[1248,128]{1,0:T(8,128)(2,1)}, bf16[1248,128]{1,0:T(8,128)(2,1)S(1)}, u32[]{:S(2)}) copy-start(bf16[1248,128]{1,0:T(8,128)(2,1)S(1)} %get-tuple-element.39.own.refs_5_) | copy-start | bytes 958468
  14.5 9.2 %collective-permute-start.1 = (bf16[1248,128]{1,0:T(8,128)(2,1)S(1)}, bf16[1248,128]{1,0:T(8,128)(2,1)S(1)}, u32[]{:S(2)}, u32[]{:S(2)}) collective-permute-start(bf16[1248,128]{1,0:T(8,128)(2,1)S(1)} %get-tuple-element.39.own.refs_5_), channel_id=1, source_target_pairs={{0,8},{8,16},{16,24},{1,9},{9,17},{17,25},{2,10},{10,18},{18,26},{... | collective-permute-start | bytes 958472 | tf_op jit(solution)/shard_map/ppermute | solution.py:687
  18.0 11.0 %collective-permute-start.2 = (bf16[1472,128]{1,0:T(8,128)(2,1)S(1)}, bf16[1472,128]{1,0:T(8,128)(2,1)S(1)}, u32[]{:S(2)}, u32[]{:S(2)}) collective-permute-start(bf16[1472,128]{1,0:T(8,128)(2,1)S(1)} %get-tuple-element.42.near), channel_id=1, source_target_pairs={{8,0},{16,8},{24,16},{9,1},{17,9},{25,17},{10,2},{18,10},{26,18},{... | collective-permute-start | bytes 1130504 | tf_op jit(solution)/shard_map/ppermute | solution.py:687
  19.3 1.2 %copy-start.3 = (bf16[3,3,3,128,128]{4,3,2,1,0:T(8,128)(2,1)S(1)}, bf16[3,3,3,128,128]{4,3,2,1,0:T(8,128)(2,1)}, u32[]{:S(2)}) copy-start(bf16[3,3,3,128,128]{4,3,2,1,0:T(8,128)(2,1)} %param.5) | copy-start | bytes 2654212
  23.6 1.7 %copy-start.5 = (bf16[1248,128]{1,0:T(8,128)(2,1)}, bf16[1248,128]{1,0:T(8,128)(2,1)S(1)}, u32[]{:S(2)}) copy-start(bf16[1248,128]{1,0:T(8,128)(2,1)S(1)} %collective-permute-done.1.refs_0_.refs_4_) | copy-start | bytes 958468
  25.4 9.3 %all-to-all-start.1 = ((bf16[8,96,128]{2,1,0:T(8,128)(2,1)}), bf16[8,96,128]{2,1,0:T(8,128)(2,1)S(1)}, u32[]{:S(2)}, u32[]{:S(2)}) async-start(bf16[8,96,128]{2,1,0:T(8,128)(2,1)} %get-tuple-element.41), calls=%async_computation.1 | async-start | bytes 393216 | tf_op jit(solution)/shard_map/all_to_all | solution.py:831
  35.9 8.1 %all-to-all-start.2 = ((f32[8,8,128]{2,1,0:T(8,128)}), f32[8,8,128]{2,1,0:T(8,128)S(1)}, u32[]{:S(2)}, u32[]{:S(2)}) async-start(f32[8,8,128]{2,1,0:T(8,128)} %get-tuple-element.43), calls=%async_computation.2 | async-start | bytes 65536 | tf_op jit(solution)/shard_map/all_to_all | solution.py:858
  47.7 2.5 %collective-permute-start.3 = (bf16[3456,128]{1,0:T(8,128)(2,1)S(1)}, bf16[3456,128]{1,0:T(8,128)(2,1)S(1)}, u32[]{:S(2)}, u32[]{:S(2)}) collective-permute-start(bf16[3456,128]{1,0:T(8,128)(2,1)S(1)} %get-tuple-element.51), channel_id=1, source_target_pairs={{0,4},{4,0},{1,5},{5,1},{2,6},{6,2},{3,7},{7,3},{8,12},{12,8},{9,1... | collective-permute-start | bytes 2654216 | tf_op jit(solution)/shard_map/ppermute | solution.py:681
  50.2 23.9 %copy-start.1 = (bf16[2,16,32,128]{3,2,1,0:T(8,128)(2,1)S(1)}, bf16[2,16,32,128]{3,2,1,0:T(8,128)(2,1)}, u32[]{:S(2)}) copy-start(bf16[2,16,32,128]{3,2,1,0:T(8,128)(2,1)} %features.5) | copy-start | bytes 786436
  50.2 23.9 %copy-start.6 = (bf16[3,3,3,128,128]{4,3,2,1,0:T(8,128)(2,1)S(1)}, bf16[3,3,3,128,128]{4,3,2,1,0:T(8,128)(2,1)}, u32[]{:S(2)}) copy-start(bf16[3,3,3,128,128]{4,3,2,1,0:T(8,128)(2,1)} %param.6) | copy-start | bytes 2654212
  51.4 26.2 %copy-start.4 = (bf16[3,3,3,128,128]{4,3,2,1,0:T(8,128)(2,1)S(1)}, bf16[3,3,3,128,128]{4,3,2,1,0:T(8,128)(2,1)}, u32[]{:S(2)}) copy-start(bf16[3,3,3,128,128]{4,3,2,1,0:T(8,128)(2,1)} %param.5) | copy-start | bytes 2654212
  51.4 16.1 %all-to-all-start.3 = ((bf16[4,864,128]{2,1,0:T(8,128)(2,1)}), bf16[4,864,128]{2,1,0:T(8,128)(2,1)S(1)}, u32[]{:S(2)}, u32[]{:S(2)}) async-start(bf16[4,864,128]{2,1,0:T(8,128)(2,1)} %shard_map.85), calls=%async_computation.3 | async-start | bytes 1769472 | tf_op jit(solution)/shard_map/all_to_all | solution.py:895
  55.0 19.1 %collective-permute-start.4 = (bf16[1248,128]{1,0:T(8,128)(2,1)S(1)}, bf16[1248,128]{1,0:T(8,128)(2,1)}, u32[]{:S(2)}, u32[]{:S(2)}) collective-permute-start(bf16[1248,128]{1,0:T(8,128)(2,1)S(1)} %get-tuple-element.52.act.far), channel_id=1, source_target_pairs={{0,8},{8,16},{16,24},{1,9},{9,17},{17,25},{2,10},{10,18},{18,26},{... | collective-permute-start | bytes 958472 | tf_op jit(solution)/shard_map/ppermute | solution.py:687
  60.2 17.4 %collective-permute-start.5 = (bf16[1248,128]{1,0:T(8,128)(2,1)}, bf16[1248,128]{1,0:T(8,128)(2,1)}, u32[]{:S(2)}, u32[]{:S(2)}) collective-permute-start(bf16[1248,128]{1,0:T(8,128)(2,1)} %get-tuple-element.53.near), channel_id=1, source_target_pairs={{8,0},{16,8},{24,16},{9,1},{17,9},{25,17},{10,2},{18,10},{26,18},{... | collective-permute-start | bytes 958472 | tf_op jit(solution)/shard_map/ppermute | solution.py:687
  68.2 9.3 %copy-start.7 = (bf16[1248,128]{1,0:T(8,128)(2,1)S(1)}, bf16[1248,128]{1,0:T(8,128)(2,1)}, u32[]{:S(2)}) copy-start(bf16[1248,128]{1,0:T(8,128)(2,1)} %get-tuple-element.53.near) | copy-start | bytes 958468
  68.2 13.7 %all-to-all-start.4 = ((bf16[4,224,128]{2,1,0:T(8,128)(2,1)}), bf16[4,224,128]{2,1,0:T(8,128)(2,1)S(1)}, u32[]{:S(2)}, u32[]{:S(2)}) async-start(bf16[4,224,128]{2,1,0:T(8,128)(2,1)} %shard_map.86), calls=%async_computation.4 | async-start | bytes 458752 | tf_op jit(solution)/shard_map/all_to_all | solution.py:903
  77.6 28.2 %copy-start.2 = (bf16[2,16,32,128]{3,2,1,0:T(8,128)(2,1)S(1)}, bf16[2,16,32,128]{3,2,1,0:T(8,128)(2,1)}, u32[]{:S(2)}) copy-start(bf16[2,16,32,128]{3,2,1,0:T(8,128)(2,1)} %out_grad.1) | copy-start | bytes 786436
  82.6 10.3 %all-to-all-start.5 = ((bf16[4,224,128]{2,1,0:T(8,128)(2,1)}), bf16[4,224,128]{2,1,0:T(8,128)(2,1)S(1)}, u32[]{:S(2)}, u32[]{:S(2)}) async-start(bf16[4,224,128]{2,1,0:T(8,128)(2,1)} %shard_map.89), calls=%async_computation.5 | async-start | bytes 458752 | tf_op jit(solution)/shard_map/all_to_all | solution.py:922
  86.2 1.2 %collective-permute-start.6 = (f32[8,128]{1,0:T(8,128)S(1)}, f32[8,128]{1,0:T(8,128)S(1)}, u32[]{:S(2)}, u32[]{:S(2)}) collective-permute-start(f32[8,128]{1,0:T(8,128)S(1)} %get-tuple-element.59), channel_id=1, source_target_pairs={{0,4},{4,0},{1,5},{5,1},{2,6},{6,2},{3,7},{7,3},{8,12},{12,8},{9,1... | collective-permute-start | bytes 12296 | tf_op jit(solution)/shard_map/ppermute | solution.py:681
  105.8 2.5 %collective-permute-start.7 = (bf16[4,896,128]{2,1,0:T(8,128)(2,1)S(1)}, bf16[4,896,128]{2,1,0:T(8,128)(2,1)S(1)}, u32[]{:S(2)}, u32[]{:S(2)}) collective-permute-start(bf16[4,896,128]{2,1,0:T(8,128)(2,1)S(1)} %all_to_all.36.refs_0_), channel_id=1, source_target_pairs={{0,4},{4,0},{1,5},{5,1},{2,6},{6,2},{3,7},{7,3},{8,12},{12,8},{9,1... | collective-permute-start | bytes 2752520 | tf_op jit(solution)/shard_map/ppermute | solution.py:681

commit v16 on v12

--- a/solution.py
+++ b/solution.py
@@ -725,14 +725,18 @@
 
 def placed_body(rows, swapped, *refs):
     block, first, second, sems = refs[0], *refs[-3:]
+    half = rows // 2
     place = here()
 
     def move(target):
         copies = [
             pltpu.make_async_copy(
-                block.at[peer, pl.ds(0, rows)], target.at[pl.ds(peer * rows, rows)], sems.at[peer]
+                block.at[peer, pl.ds(part * half, half)],
+                target.at[pl.ds(peer * rows + part * half, half)],
+                sems.at[2 * peer + part],
             )
             for peer in range(block.shape[0])
+            for part in range(2)
         ]
         for copy in copies:
             copy.start()
@@ -757,7 +761,7 @@
         in_specs=[anywhere] * (1 + len(so_far)),
         out_specs=[anywhere, anywhere],
         input_output_aliases={1 + k: k for k in range(len(so_far))},
-        scratch_shapes=[pltpu.SemaphoreType.DMA((block.shape[0],))],
+        scratch_shapes=[pltpu.SemaphoreType.DMA((2 * block.shape[0],))],
         compiler_params=pltpu.CompilerParams(vmem_limit_bytes=1 << 20),
     )(block, *so_far)
 

time: 110 us -> 110 us (level)
  no operation moved by 1% of the time
where the time goes in v16:
time: 110 us; the launch traced here: 109 us
  starting transfers between devices  31.5 us (29%)
  Pallas kernels  28.1 us (26%)
  waiting for transfers between devices  23.2 us (21%)
  blocking collectives  23 us (21%)
  local copies, waits for them, and re-layouts  2.05 us (2%)
    pallas_call x16, Pallas kernels, call(): pl.pallas_call(body, out_shape=shapes[:kept] + [pltpu.HBM(o.shape, o.dtyp...  26.2 us
    all_to_all x1, blocking collectives, on_device(): lax.all_to_all(jnp.broadcast_to(done[None], (across, *done.shape)), 'col'...  12.6 us
    ppermute x4, starting transfers between devices, later(): return lax.ppermute(values, 'tm', pairs)  11.8 us
    all_to_all x1, blocking collectives, on_device(): col_got = lax.all_to_all(slots, 'col', 0, 0)  10.4 us
    ppermute x4, waiting for transfers between devices, later(): return lax.ppermute(values, 'tm', pairs)  7.92 us
    all_to_all x2, starting transfers between devices, on_device(): got = lax.all_to_all(slots, ('row', 'col'), 0, 0)  6.73 us
    all_to_all x1, starting transfers between devices, on_device(): got = lax.all_to_all(slots, 'tm', 0, 0)  5.18 us
    ppermute x4, waiting for transfers between devices, row_swap(): return lax.ppermute(values, 'row', [(0, 1), (1, 0)])  4.87 us
  transfers between devices with their start and end apart: 13, of which 11 were waited for; matrix products, arithmetic and copies ran while one was open for 0% of the time, Pallas kernels for 17%

profile of v16, /device:TPU:0, one launch (start us, length us, event | category | flops | bytes accessed | tf_op | source)
XLA Modules:
  0.0 108.9 jit_solution(962809591052733182)
XLA Ops:
  3.3 10.4 %all_to_all.35.refs_3_ = bf16[4,176,128]{2,1,0:T(8,128)(2,1)S(1)} all-to-all(bf16[4,176,128]{2,1,0:T(8,128)(2,1)S(1)} %shard_map.76), channel_id=1, replica_groups=mesh['tm'=4,'row'=2,'col'=4] {'col'}, dimensions={0} | all-to-all | bytes 360448 | tf_op jit(solution)/shard_map/all_to_all | solution.py:804
  14.5 3.5 %collective-permute-start.1 = (bf16[1248,128]{1,0:T(8,128)(2,1)S(1)}, bf16[1248,128]{1,0:T(8,128)(2,1)S(1)}, u32[]{:S(2)}, u32[]{:S(2)}) collective-permute-start(bf16[1248,128]{1,0:T(8,128)(2,1)S(1)} %get-tuple-element.40.own.refs_5_), channel_id=1, source_target_pairs={{0,8},{8,16},{16,24},{1,9},{9,17},{17,25},{2,10},{10,18},{18,26},{... | collective-permute-start | bytes 958472 | tf_op jit(solution)/shard_map/ppermute | solution.py:687
  18.0 1.3 %collective-permute-start.2 = (bf16[1472,128]{1,0:T(8,128)(2,1)S(1)}, bf16[1472,128]{1,0:T(8,128)(2,1)S(1)}, u32[]{:S(2)}, u32[]{:S(2)}) collective-permute-start(bf16[1472,128]{1,0:T(8,128)(2,1)S(1)} %get-tuple-element.43.near), channel_id=1, source_target_pairs={{8,0},{16,8},{24,16},{9,1},{17,9},{25,17},{10,2},{18,10},{26,18},{... | collective-permute-start | bytes 1130504 | tf_op jit(solution)/shard_map/ppermute | solution.py:687
  21.3 2.3 %collective-permute-done.1.refs_0_.refs_4_ = bf16[1248,128]{1,0:T(8,128)(2,1)S(1)} collective-permute-done((bf16[1248,128]{1,0:T(8,128)(2,1)S(1)}, bf16[1248,128]{1,0:T(8,128)(2,1)S(1)}, u32[]{:S(2)}, u32[]{:S(2)}) %collective-permute-start.1) | collective-permute-done | bytes 319520 | tf_op jit(solution)/shard_map/ppermute | solution.py:687
  23.6 1.7 %shard_map.79 = (bf16[2,16,32,128]{3,2,1,0:T(8,128)(2,1)S(1)}, bf16[8,96,128]{2,1,0:T(8,128)(2,1)}) custom-call(bf16[1248,128]{1,0:T(8,128)(2,1)S(1)} %collective-permute-done.1.refs_0_.refs_4_, f32[2,512,128]{2,1,0:T(8,128)S(1)} %shard_map.78.refs_1_, bf16[3456,128]{1,0:T(8,128)(2,1)S(1)} %bitcast.6), custom_call_target="tpu_custom_call" | custom-call | flops 1811939328 | bytes 2187264 | tf_op jit(solution)/shard_map/pallas_call | solution.py:65
  25.4 3.4 %all-to-all-start.1 = ((bf16[8,96,128]{2,1,0:T(8,128)(2,1)}), bf16[8,96,128]{2,1,0:T(8,128)(2,1)S(1)}, u32[]{:S(2)}, u32[]{:S(2)}) async-start(bf16[8,96,128]{2,1,0:T(8,128)(2,1)} %get-tuple-element.42), calls=%async_computation.1 | async-start | bytes 393216 | tf_op jit(solution)/shard_map/all_to_all | solution.py:835
  29.0 3.5 %shard_map.80.grad_act.refs_2_ = f32[2,18,40,128]{3,2,1,0:T(8,128)S(1)} custom-call(bf16[1472,128]{1,0:T(8,128)(2,1)S(1)} %get-tuple-element.43.near, bf16[1472,128]{1,0:T(8,128)(2,1)S(1)} %collective-permute-done.2.far, bf16[3456,128]{1,0:T(8,128)(2,1)} %bitcast.8), custom_call_target="tpu_custom_call" | custom-call | flops 1811939328 | bytes 2375680 | tf_op jit(solution)/shard_map/pallas_call | solution.py:65
  32.5 2.1 %all-to-all-done.1.got.refs_1_ = bf16[8,96,128]{2,1,0:T(8,128)(2,1)S(1)} async-done(((bf16[8,96,128]{2,1,0:T(8,128)(2,1)}), bf16[8,96,128]{2,1,0:T(8,128)(2,1)S(1)}, u32[]{:S(2)}, u32[]{:S(2)}) %all-to-all-start.1) | async-done | bytes 196640 | tf_op jit(solution)/shard_map/all_to_all | solution.py:835
  35.9 3.3 %all-to-all-start.2 = ((f32[8,8,128]{2,1,0:T(8,128)}), f32[8,8,128]{2,1,0:T(8,128)S(1)}, u32[]{:S(2)}, u32[]{:S(2)}) async-start(f32[8,8,128]{2,1,0:T(8,128)} %get-tuple-element.44), calls=%async_computation.2 | async-start | bytes 65536 | tf_op jit(solution)/shard_map/all_to_all | solution.py:862
  39.2 1.7 %shard_map.82 = (bf16[1248,128]{1,0:T(8,128)(2,1)S(1)}, f32[2,18,40,128]{3,2,1,0:T(8,128)}, f32[2,18,40,128]{3,2,1,0:T(8,128)}) custom-call(bf16[2,16,32,128]{3,2,1,0:T(8,128)(2,1)S(1)} %get-tuple-element.41.hidden.refs_0_, bf16[8,96,128]{2,1,0:T(8,128)(2,1)S(1)} %all-to-all-done.1.got.refs_1_, f32[2,18,40,128]{3,2,1,0:T(8,128)S(1)} %shard_map.80.grad_act.refs_2_, ...), custom_call_target="tpu_custom_call" | custom-call | tf_op jit(solution)/shard_map/pallas_call | solution.py:65
  40.9 2.4 %shard_map.83.refs_6_ = f32[3456,128]{1,0:T(8,128)} custom-call(bf16[1472,128]{1,0:T(8,128)(2,1)S(1)} %get-tuple-element.43.near, bf16[1472,128]{1,0:T(8,128)(2,1)S(1)} %collective-permute-done.2.far, bf16[1248,128]{1,0:T(8,128)(2,1)S(1)} %get-tuple-element.55.act.far), custom_call_target="tpu_custom_call" | custom-call | tf_op jit(solution)/shard_map/pallas_call | solution.py:65
  44.0 3.8 %shard_map.84 = (f32[2,3456,128]{2,1,0:T(8,128)S(1)}, bf16[3456,128]{1,0:T(8,128)(2,1)S(1)}, bf16[1248,128]{1,0:T(8,128)(2,1)}) custom-call(f32[8,8,128]{2,1,0:T(8,128)S(1)} %all-to-all-done.2.refs_0_, f32[8,128]{1,0:T(8,128)S(1)} %get-tuple-element.45.refs_3_.refs_1_, f32[2,18,40,128]{3,2,1,0:T(8,128)} %get-tuple-element.46.refs_2_, ...), custom_call_target="tpu_custom_call" | custom-call | flops 905969664 | bytes 8663040 | tf_op jit(solution)/shard_map/pallas_call | solution.py:65
  47.9 2.4 %collective-permute-done.3.refs_1_ = bf16[3456,128]{1,0:T(8,128)(2,1)S(1)} collective-permute-done((bf16[3456,128]{1,0:T(8,128)(2,1)S(1)}, bf16[3456,128]{1,0:T(8,128)(2,1)S(1)}, u32[]{:S(2)}, u32[]{:S(2)}) %collective-permute-start.3) | collective-permute-done | bytes 884768 | tf_op jit(solution)/shard_map/ppermute | solution.py:681
  51.4 3.6 %all-to-all-start.3 = ((bf16[4,864,128]{2,1,0:T(8,128)(2,1)}), bf16[4,864,128]{2,1,0:T(8,128)(2,1)S(1)}, u32[]{:S(2)}, u32[]{:S(2)}) async-start(bf16[4,864,128]{2,1,0:T(8,128)(2,1)} %shard_map.85), calls=%async_computation.3 | async-start | bytes 1769472 | tf_op jit(solution)/shard_map/all_to_all | solution.py:899
  55.0 1.3 %collective-permute-start.4 = (bf16[1248,128]{1,0:T(8,128)(2,1)}, bf16[1248,128]{1,0:T(8,128)(2,1)S(1)}, u32[]{:S(2)}, u32[]{:S(2)}) collective-permute-start(bf16[1248,128]{1,0:T(8,128)(2,1)} %get-tuple-element.53.near), channel_id=1, source_target_pairs={{8,0},{16,8},{24,16},{9,1},{17,9},{25,17},{10,2},{18,10},{26,18},{... | collective-permute-start | bytes 958472 | tf_op jit(solution)/shard_map/ppermute | solution.py:687
  56.3 5.7 %collective-permute-start.5 = (bf16[1248,128]{1,0:T(8,128)(2,1)S(1)}, bf16[1248,128]{1,0:T(8,128)(2,1)}, u32[]{:S(2)}, u32[]{:S(2)}) collective-permute-start(bf16[1248,128]{1,0:T(8,128)(2,1)S(1)} %get-tuple-element.55.act.far), channel_id=1, source_target_pairs={{0,8},{8,16},{16,24},{1,9},{9,17},{17,25},{2,10},{10,18},{18,26},{... | collective-permute-start | bytes 958472 | tf_op jit(solution)/shard_map/ppermute | solution.py:687
  62.0 5.4 %collective-permute-done.4.far = bf16[1248,128]{1,0:T(8,128)(2,1)S(1)} collective-permute-done((bf16[1248,128]{1,0:T(8,128)(2,1)}, bf16[1248,128]{1,0:T(8,128)(2,1)S(1)}, u32[]{:S(2)}, u32[]{:S(2)}) %collective-permute-start.4) | collective-permute-done | bytes 319520 | tf_op jit(solution)/shard_map/ppermute | solution.py:687
  69.0 5.2 %all-to-all-start.4 = ((bf16[4,224,128]{2,1,0:T(8,128)(2,1)}), bf16[4,224,128]{2,1,0:T(8,128)(2,1)S(1)}, u32[]{:S(2)}, u32[]{:S(2)}) async-start(bf16[4,224,128]{2,1,0:T(8,128)(2,1)} %shard_map.86), calls=%async_computation.4 | async-start | bytes 458752 | tf_op jit(solution)/shard_map/all_to_all | solution.py:908
  74.2 3.4 %shard_map.87 = bf16[2,16,32,128]{3,2,1,0:T(8,128)(2,1)} custom-call(bf16[1248,128]{1,0:T(8,128)(2,1)} %collective-permute-done.5.near, bf16[1248,128]{1,0:T(8,128)(2,1)S(1)} %get-tuple-element.55.act.far, bf16[3456,128]{1,0:T(8,128)(2,1)S(1)} %bitcast.9, bf16[2,16,32,128]{3,2,1,0:T(8,128)(2,1)S(1)} %copy-done.1), custom_call_target="tpu_custom_call" | custom-call | flops 905969664 | bytes 2048000 | tf_op jit(solution)/shard_map/pallas_call | solution.py:65
  77.6 4.3 %all-to-all-done.4.got = bf16[4,224,128]{2,1,0:T(8,128)(2,1)S(1)} async-done(((bf16[4,224,128]{2,1,0:T(8,128)(2,1)}), bf16[4,224,128]{2,1,0:T(8,128)(2,1)S(1)}, u32[]{:S(2)}, u32[]{:S(2)}) %all-to-all-start.4) | async-done | bytes 229408 | tf_op jit(solution)/shard_map/all_to_all | solution.py:908
  82.6 3.4 %all-to-all-start.5 = ((bf16[4,224,128]{2,1,0:T(8,128)(2,1)}), bf16[4,224,128]{2,1,0:T(8,128)(2,1)S(1)}, u32[]{:S(2)}, u32[]{:S(2)}) async-start(bf16[4,224,128]{2,1,0:T(8,128)(2,1)} %shard_map.89), calls=%async_computation.5 | async-start | bytes 458752 | tf_op jit(solution)/shard_map/all_to_all | solution.py:927
  86.0 1.9 %shard_map.88 = (f32[2,512,128]{2,1,0:T(8,128)S(1)}, f32[8,128]{1,0:T(8,128)S(1)}) custom-call(bf16[1248,128]{1,0:T(8,128)(2,1)S(1)} %copy-done.7, bf16[1248,128]{1,0:T(8,128)(2,1)S(1)} %copy-done.9, bf16[3456,128]{1,0:T(8,128)(2,1)S(1)} %bitcast.7, bf16[2,16,32,128]{3,2,1,0:T(8,128)(2,1)S(1)} %copy-done.1, f32[8,128]{1,0:T(8,128)S(1)} %get-tuple-element.57.norm), custom_call_target="tpu_custom_call" | custom-call | flops 905969664 | bytes 2318336 | tf_op jit(solution)/shard_map/pallas_call | solution.py:65
  89.2 3.3 %all-to-all-done.5 = bf16[4,224,128]{2,1,0:T(8,128)(2,1)S(1)} async-done(((bf16[4,224,128]{2,1,0:T(8,128)(2,1)}), bf16[4,224,128]{2,1,0:T(8,128)(2,1)S(1)}, u32[]{:S(2)}, u32[]{:S(2)}) %all-to-all-start.5) | async-done | bytes 229408 | tf_op jit(solution)/shard_map/all_to_all | solution.py:927
  92.6 12.6 %all_to_all.36.refs_0_ = bf16[4,896,128]{2,1,0:T(8,128)(2,1)S(1)} all-to-all(bf16[4,896,128]{2,1,0:T(8,128)(2,1)S(1)} %broadcast_in_dim.2), channel_id=1, replica_groups=mesh['tm'=4,'row'=2,'col'=4] {'col'}, dimensions={0} | all-to-all | bytes 1835008 | tf_op jit(solution)/shard_map/all_to_all | solution.py:931
  (48 shorter events, 15.8 us)
Async XLA Ops:
  1.9 1.4 %collective-permute-start = (bf16[224,128]{1,0:T(8,128)(2,1)S(1)}, bf16[224,128]{1,0:T(8,128)(2,1)S(1)}, u32[]{:S(2)}, u32[]{:S(2)}) collective-permute-start(bf16[224,128]{1,0:T(8,128)(2,1)S(1)} %get-tuple-element.37), channel_id=1, source_target_pairs={{0,4},{4,0},{1,5},{5,1},{2,6},{6,2},{3,7},{7,3},{8,12},{12,8},{9,1... | collective-permute-start | bytes 172040 | tf_op jit(solution)/shard_map/ppermute | solution.py:681
  14.5 10.9 %copy-start = (bf16[1248,128]{1,0:T(8,128)(2,1)}, bf16[1248,128]{1,0:T(8,128)(2,1)S(1)}, u32[]{:S(2)}) copy-start(bf16[1248,128]{1,0:T(8,128)(2,1)S(1)} %get-tuple-element.40.own.refs_5_) | copy-start | bytes 958468
  14.5 9.2 %collective-permute-start.1 = (bf16[1248,128]{1,0:T(8,128)(2,1)S(1)}, bf16[1248,128]{1,0:T(8,128)(2,1)S(1)}, u32[]{:S(2)}, u32[]{:S(2)}) collective-permute-start(bf16[1248,128]{1,0:T(8,128)(2,1)S(1)} %get-tuple-element.40.own.refs_5_), channel_id=1, source_target_pairs={{0,8},{8,16},{16,24},{1,9},{9,17},{17,25},{2,10},{10,18},{18,26},{... | collective-permute-start | bytes 958472 | tf_op jit(solution)/shard_map/ppermute | solution.py:687
  18.0 11.0 %collective-permute-start.2 = (bf16[1472,128]{1,0:T(8,128)(2,1)S(1)}, bf16[1472,128]{1,0:T(8,128)(2,1)S(1)}, u32[]{:S(2)}, u32[]{:S(2)}) collective-permute-start(bf16[1472,128]{1,0:T(8,128)(2,1)S(1)} %get-tuple-element.43.near), channel_id=1, source_target_pairs={{8,0},{16,8},{24,16},{9,1},{17,9},{25,17},{10,2},{18,10},{26,18},{... | collective-permute-start | bytes 1130504 | tf_op jit(solution)/shard_map/ppermute | solution.py:687
  19.3 1.2 %copy-start.3 = (bf16[3,3,3,128,128]{4,3,2,1,0:T(8,128)(2,1)S(1)}, bf16[3,3,3,128,128]{4,3,2,1,0:T(8,128)(2,1)}, u32[]{:S(2)}) copy-start(bf16[3,3,3,128,128]{4,3,2,1,0:T(8,128)(2,1)} %param.5) | copy-start | bytes 2654212
  23.6 1.7 %copy-start.5 = (bf16[1248,128]{1,0:T(8,128)(2,1)}, bf16[1248,128]{1,0:T(8,128)(2,1)S(1)}, u32[]{:S(2)}) copy-start(bf16[1248,128]{1,0:T(8,128)(2,1)S(1)} %collective-permute-done.1.refs_0_.refs_4_) | copy-start | bytes 958468
  25.4 9.3 %all-to-all-start.1 = ((bf16[8,96,128]{2,1,0:T(8,128)(2,1)}), bf16[8,96,128]{2,1,0:T(8,128)(2,1)S(1)}, u32[]{:S(2)}, u32[]{:S(2)}) async-start(bf16[8,96,128]{2,1,0:T(8,128)(2,1)} %get-tuple-element.42), calls=%async_computation.1 | async-start | bytes 393216 | tf_op jit(solution)/shard_map/all_to_all | solution.py:835
  35.9 8.1 %all-to-all-start.2 = ((f32[8,8,128]{2,1,0:T(8,128)}), f32[8,8,128]{2,1,0:T(8,128)S(1)}, u32[]{:S(2)}, u32[]{:S(2)}) async-start(f32[8,8,128]{2,1,0:T(8,128)} %get-tuple-element.44), calls=%async_computation.2 | async-start | bytes 65536 | tf_op jit(solution)/shard_map/all_to_all | solution.py:862
  47.7 2.5 %collective-permute-start.3 = (bf16[3456,128]{1,0:T(8,128)(2,1)S(1)}, bf16[3456,128]{1,0:T(8,128)(2,1)S(1)}, u32[]{:S(2)}, u32[]{:S(2)}) collective-permute-start(bf16[3456,128]{1,0:T(8,128)(2,1)S(1)} %get-tuple-element.52), channel_id=1, source_target_pairs={{0,4},{4,0},{1,5},{5,1},{2,6},{6,2},{3,7},{7,3},{8,12},{12,8},{9,1... | collective-permute-start | bytes 2654216 | tf_op jit(solution)/shard_map/ppermute | solution.py:681
  50.2 23.9 %copy-start.1 = (bf16[2,16,32,128]{3,2,1,0:T(8,128)(2,1)S(1)}, bf16[2,16,32,128]{3,2,1,0:T(8,128)(2,1)}, u32[]{:S(2)}) copy-start(bf16[2,16,32,128]{3,2,1,0:T(8,128)(2,1)} %features.5) | copy-start | bytes 786436
  50.2 23.9 %copy-start.6 = (bf16[3,3,3,128,128]{4,3,2,1,0:T(8,128)(2,1)S(1)}, bf16[3,3,3,128,128]{4,3,2,1,0:T(8,128)(2,1)}, u32[]{:S(2)}) copy-start(bf16[3,3,3,128,128]{4,3,2,1,0:T(8,128)(2,1)} %param.6) | copy-start | bytes 2654212
  51.4 34.6 %copy-start.4 = (bf16[3,3,3,128,128]{4,3,2,1,0:T(8,128)(2,1)S(1)}, bf16[3,3,3,128,128]{4,3,2,1,0:T(8,128)(2,1)}, u32[]{:S(2)}) copy-start(bf16[3,3,3,128,128]{4,3,2,1,0:T(8,128)(2,1)} %param.5) | copy-start | bytes 2654212
  51.4 16.8 %all-to-all-start.3 = ((bf16[4,864,128]{2,1,0:T(8,128)(2,1)}), bf16[4,864,128]{2,1,0:T(8,128)(2,1)S(1)}, u32[]{:S(2)}, u32[]{:S(2)}) async-start(bf16[4,864,128]{2,1,0:T(8,128)(2,1)} %shard_map.85), calls=%async_computation.3 | async-start | bytes 1769472 | tf_op jit(solution)/shard_map/all_to_all | solution.py:899
  55.0 12.4 %collective-permute-start.4 = (bf16[1248,128]{1,0:T(8,128)(2,1)}, bf16[1248,128]{1,0:T(8,128)(2,1)S(1)}, u32[]{:S(2)}, u32[]{:S(2)}) collective-permute-start(bf16[1248,128]{1,0:T(8,128)(2,1)} %get-tuple-element.53.near), channel_id=1, source_target_pairs={{8,0},{16,8},{24,16},{9,1},{17,9},{25,17},{10,2},{18,10},{26,18},{... | collective-permute-start | bytes 958472 | tf_op jit(solution)/shard_map/ppermute | solution.py:687
  56.3 17.8 %collective-permute-start.5 = (bf16[1248,128]{1,0:T(8,128)(2,1)S(1)}, bf16[1248,128]{1,0:T(8,128)(2,1)}, u32[]{:S(2)}, u32[]{:S(2)}) collective-permute-start(bf16[1248,128]{1,0:T(8,128)(2,1)S(1)} %get-tuple-element.55.act.far), channel_id=1, source_target_pairs={{0,8},{8,16},{16,24},{1,9},{9,17},{17,25},{2,10},{10,18},{18,26},{... | collective-permute-start | bytes 958472 | tf_op jit(solution)/shard_map/ppermute | solution.py:687
  67.4 0.7 copy-start.8
  69.0 17.1 %copy-start.7 = (bf16[1248,128]{1,0:T(8,128)(2,1)S(1)}, bf16[1248,128]{1,0:T(8,128)(2,1)}, u32[]{:S(2)}) copy-start(bf16[1248,128]{1,0:T(8,128)(2,1)} %get-tuple-element.53.near) | copy-start | bytes 958468
  69.0 17.1 %copy-start.9 = (bf16[1248,128]{1,0:T(8,128)(2,1)S(1)}, bf16[1248,128]{1,0:T(8,128)(2,1)}, u32[]{:S(2)}) copy-start(bf16[1248,128]{1,0:T(8,128)(2,1)} %copy-done.8) | copy-start | bytes 958468
  69.0 12.9 %all-to-all-start.4 = ((bf16[4,224,128]{2,1,0:T(8,128)(2,1)}), bf16[4,224,128]{2,1,0:T(8,128)(2,1)S(1)}, u32[]{:S(2)}, u32[]{:S(2)}) async-start(bf16[4,224,128]{2,1,0:T(8,128)(2,1)} %shard_map.86), calls=%async_computation.4 | async-start | bytes 458752 | tf_op jit(solution)/shard_map/all_to_all | solution.py:908
  82.6 9.9 %all-to-all-start.5 = ((bf16[4,224,128]{2,1,0:T(8,128)(2,1)}), bf16[4,224,128]{2,1,0:T(8,128)(2,1)S(1)}, u32[]{:S(2)}, u32[]{:S(2)}) async-start(bf16[4,224,128]{2,1,0:T(8,128)(2,1)} %shard_map.89), calls=%async_computation.5 | async-start | bytes 458752 | tf_op jit(solution)/shard_map/all_to_all | solution.py:927
  86.0 19.2 %copy-start.2 = (bf16[2,16,32,128]{3,2,1,0:T(8,128)(2,1)S(1)}, bf16[2,16,32,128]{3,2,1,0:T(8,128)(2,1)}, u32[]{:S(2)}) copy-start(bf16[2,16,32,128]{3,2,1,0:T(8,128)(2,1)} %out_grad.1) | copy-start | bytes 786436
  87.9 1.2 %collective-permute-start.6 = (f32[8,128]{1,0:T(8,128)S(1)}, f32[8,128]{1,0:T(8,128)S(1)}, u32[]{:S(2)}, u32[]{:S(2)}) collective-permute-start(f32[8,128]{1,0:T(8,128)S(1)} %get-tuple-element.61), channel_id=1, source_target_pairs={{0,4},{4,0},{1,5},{5,1},{2,6},{6,2},{3,7},{7,3},{8,12},{12,8},{9,1... | collective-permute-start | bytes 12296 | tf_op jit(solution)/shard_map/ppermute | solution.py:681
  105.3 2.5 %collective-permute-start.7 = (bf16[4,896,128]{2,1,0:T(8,128)(2,1)S(1)}, bf16[4,896,128]{2,1,0:T(8,128)(2,1)S(1)}, u32[]{:S(2)}, u32[]{:S(2)}) collective-permute-start(bf16[4,896,128]{2,1,0:T(8,128)(2,1)S(1)} %all_to_all.36.refs_0_), channel_id=1, source_target_pairs={{0,4},{4,0},{1,5},{5,1},{2,6},{6,2},{3,7},{7,3},{8,12},{12,8},{9,1... | collective-permute-start | bytes 2752520 | tf_op jit(solution)/shard_map/ppermute | solution.py:681
